TPU v7x, 128 devices: a whole 4x4x4 slice. The times are simulated.
128 devices in a mesh: nodes: 16 (over x, z), cols: 8 (over y, core).
Axes of the slice: x: 4, y: 4, z: 4, core: 2. Of those that a mesh axis runs over, the one named last changes fastest.
Arguments:
- node_feats: bfloat16 [32768, 256], P(('nodes', 'cols')), may hold values from -6 to 6
- tile_row: int32 [16, 2816], P('nodes', 'cols'), may hold values from 0 to 15, as said below
- tile_col: int32 [16, 2816], P('nodes', 'cols'), may hold values from 0 to 31
- tile_bits: int32 [16, 2816, 16, 128], P('nodes', 'cols'), may hold values from 0 to 255, as said below
- w_self: bfloat16 [256, 256], replicated, may hold values from -0.375 to 0.375
- w_neigh: bfloat16 [256, 256], replicated, may hold values from -1.5 to 1.5
- bias: float32 [256], replicated, may hold values from -3 to 3
- cotangent: bfloat16 [32768, 256], P(('nodes', 'cols')), may hold values from -6 to 6
Outputs:
- layer_out: bfloat16 [32768, 256], P(('nodes', 'cols'))
- feat_grad: bfloat16 [32768, 256], P(('nodes', 'cols'))
- self_grad: float32 [256, 256], replicated
- neigh_grad: float32 [256, 256], replicated
- bias_grad: float32 [256], replicated
Inputs may be any that keep to these rules, and one draw needn't show every extreme that they name: `tile_row`: destination row block of a tile within its nodes group; in every nodes group at least one block carries no tile. `tile_col`: source row block of a tile within its cols index; a block may carry several tiles. `tile_bits`: bit j of word (w, a) of a tile is its edge from destination row a to source column 8 w + j; bits above the eighth are zero; some destination rows have no edge in any tile.
All inputs are finite; a program needn't handle non-finite values.
Results may differ from a plain program's by a relative error of at most 0.0075.
Values may be sent and summed in bfloat16 or wider, within the bound.
No kernel may reach another device: no remote copies, remote signals or barrier semaphores. Data moves between devices by JAX's collectives and lax.ppermute only.
A program may use at most 64 MiB of HBM per device.

v0:
```python
import math

import jax
import jax.numpy as jnp
from jax import lax
from jax.sharding import PartitionSpec as P


def unpack_tiles(packed):
    shifts = jnp.arange(8, dtype=jnp.int32)
    edge_flags = jnp.right_shift(packed[:, :, None, :], shifts[None, None, :, None]) & 1
    return edge_flags.reshape(packed.shape[0], 128, 128)


def shards(node_feats, tile_row, tile_col, tile_bits, w_self, w_neigh, bias, cotangent):
    rows_dev = node_feats.shape[0]
    width_in = node_feats.shape[1]
    node_count = lax.axis_size("nodes")
    col_count = lax.axis_size("cols")
    per_dev = rows_dev // 128
    dest_count = col_count * per_dev
    source_count = node_count * per_dev
    tile_count = tile_row.shape[1]
    tile_group = math.gcd(tile_count, 32)
    group_count = tile_count // tile_group
    rows_here = tile_row[0].reshape(group_count, tile_group)
    cols_here = tile_col[0].reshape(group_count, tile_group)
    packed_here = tile_bits[0].reshape(group_count, tile_group, 16, 128)
    source = lax.all_gather(node_feats, "nodes", axis=0, tiled=True)
    source_blocks = source.reshape(source_count, 128, width_in)

    def forward_step(totals, tile_set):
        summed, degree = totals
        rows_blk, cols_blk, packed_blk = tile_set
        edge_flags = unpack_tiles(packed_blk)
        bits_blk = edge_flags.astype(jnp.bfloat16)
        picked = source_blocks[cols_blk]
        products = jnp.einsum("tba,tbf->taf", bits_blk, picked, preferred_element_type=jnp.float32)
        summed = summed.at[rows_blk].add(products)
        degree = degree.at[rows_blk].add(jnp.sum(edge_flags, axis=1).astype(jnp.float32))
        return ((summed, degree), None)

    initial = (
        jnp.zeros((dest_count, 128, width_in), jnp.float32),
        jnp.zeros((dest_count, 128), jnp.float32),
    )
    (partial_sum, degree_part), _ = lax.scan(
        forward_step, initial, (rows_here, cols_here, packed_here)
    )
    summed, degree = (
        lax.psum_scatter(
            partial_sum.reshape(dest_count * 128, width_in), "cols", scatter_dimension=0, tiled=True
        ),
        lax.psum_scatter(
            degree_part.reshape(dest_count * 128), "cols", scatter_dimension=0, tiled=True
        ),
    )
    degree = jnp.maximum(degree, 1.0)
    neigh_mean = (summed / degree[:, None]).astype(jnp.bfloat16)
    preact = (
        jnp.dot(node_feats, w_self, preferred_element_type=jnp.float32)
        + jnp.dot(neigh_mean, w_neigh, preferred_element_type=jnp.float32)
        + bias
    )
    sigmoid_pre = jax.nn.sigmoid(preact)
    layer_out = (preact * sigmoid_pre).astype(jnp.bfloat16)
    pre_grad = (
        cotangent.astype(jnp.float32) * sigmoid_pre * (1.0 + preact * (1.0 - sigmoid_pre))
    ).astype(jnp.bfloat16)
    self_term = jnp.dot(node_feats.T, pre_grad, preferred_element_type=jnp.float32)
    neigh_term = jnp.dot(neigh_mean.T, pre_grad, preferred_element_type=jnp.float32)
    bias_term = jnp.sum(pre_grad.astype(jnp.float32), axis=0)
    self_grad, neigh_grad, bias_grad = lax.psum(
        (self_term, neigh_term, bias_term), ("nodes", "cols")
    )
    mean_grad = (
        jnp.dot(pre_grad, w_neigh.T, preferred_element_type=jnp.float32) / degree[:, None]
    ).astype(jnp.bfloat16)
    dest_grad = lax.all_gather(mean_grad, "cols", axis=0, tiled=True)
    grad_blocks = dest_grad.reshape(dest_count, 128, width_in)

    def backward_step(src_grad, tile_set):
        rows_blk, cols_blk, packed_blk = tile_set
        bits_blk = unpack_tiles(packed_blk).astype(jnp.bfloat16)
        picked = grad_blocks[rows_blk]
        products = jnp.einsum("tba,taf->tbf", bits_blk, picked, preferred_element_type=jnp.float32)
        return (src_grad.at[cols_blk].add(products), None)

    src_total, _ = lax.scan(
        backward_step,
        jnp.zeros((source_count, 128, width_in), jnp.float32),
        (rows_here, cols_here, packed_here),
    )
    src_total = src_total.reshape(source_count * 128, width_in)
    src_grad = lax.psum_scatter(src_total, "nodes", scatter_dimension=0, tiled=True)
    feat_grad = (jnp.dot(pre_grad, w_self.T, preferred_element_type=jnp.float32) + src_grad).astype(
        jnp.bfloat16
    )
    return (layer_out, feat_grad, self_grad, neigh_grad, bias_grad)


def solution(mesh):
    return jax.shard_map(
        shards,
        mesh=mesh,
        in_specs=(
            P(("nodes", "cols"), None),
            P("nodes", "cols"),
            P("nodes", "cols"),
            P("nodes", "cols", None, None),
            P(),
            P(),
            P(),
            P(("nodes", "cols"), None),
        ),
        out_specs=(P(("nodes", "cols"), None), P(("nodes", "cols"), None), P(), P(), P()),
        check_vma=False,
    )
```

profile of v0, /device:TPU:0, one launch (start us, length us, event | category | flops | bytes accessed | tf_op | source)
XLA Modules:
  0.0 557.0 jit_solution(13627646105467495376)
XLA Ops:
  9.5 48.4 %all-gather.3.cloned.1.call-done = bf16[4096,256]{1,0:T(8,128)(2,1)} async-done(((bf16[256,256]{1,0:T(8,128)(2,1)}), bf16[4096,256]{1,0:T(8,128)(2,1)}) %all-gather.3.cloned.1.call-update) | async-done | bytes 2097168 | tf_op jit(solution)/shard_map/all_gather | solution.py:29
  58.1 182.1 %while.22 = (s32[]{:T(128)}, f32[16,128,256]{2,1,0:T(8,128)S(1)}, f32[16,128]{1,0:T(8,128)S(1)}, s32[11,32]{1,0:T(8,128)S(1)}, s32[11,32,16,128]{3,2,1,0:T(8,128...) while((s32[]{:T(128)}, f32[16,128,256]{2,1,0:T(8,128)S(1)}, ...), condition=%wide.region_4.5_spmd, body=%wide.region_0.4_spmd.sunk | while | flops 272635072 | bytes 24165348 | solution.py:47
  83.8 6.5 %scatter_fusion = f32[16,128,256]{2,1,0:T(8,128)S(1)} fusion(f32[16,128,256]{2,1,0:T(8,128)S(1)} %get-tuple-element.232, s32[32]{0:T(128)S(1)} %get-tuple-element.213, f32[32,128,256]{2,1,0:T(8,128)} %fusion.56), kind=kCustom, calls=%fused_computation.2.clone.1 | custom fusion | flops 1048576 | bytes 12583040 | tf_op jit(solution)/shard_map/while/body/eval_jaxpr/scatter-add | solution.py:39
  150.0 6.5 %scatter_fusion = f32[16,128,256]{2,1,0:T(8,128)S(1)} fusion(f32[16,128,256]{2,1,0:T(8,128)S(1)} %get-tuple-element.232, s32[32]{0:T(128)S(1)} %get-tuple-element.213, f32[32,128,256]{2,1,0:T(8,128)} %fusion.56), kind=kCustom, calls=%fused_computation.2.clone.1 | custom fusion | flops 1048576 | bytes 12583040 | tf_op jit(solution)/shard_map/while/body/eval_jaxpr/scatter-add | solution.py:39
  183.1 6.5 %scatter_fusion = f32[16,128,256]{2,1,0:T(8,128)S(1)} fusion(f32[16,128,256]{2,1,0:T(8,128)S(1)} %get-tuple-element.232, s32[32]{0:T(128)S(1)} %get-tuple-element.213, f32[32,128,256]{2,1,0:T(8,128)} %fusion.56), kind=kCustom, calls=%fused_computation.2.clone.1 | custom fusion | flops 1048576 | bytes 12583040 | tf_op jit(solution)/shard_map/while/body/eval_jaxpr/scatter-add | solution.py:39
  216.2 6.5 %scatter_fusion = f32[16,128,256]{2,1,0:T(8,128)S(1)} fusion(f32[16,128,256]{2,1,0:T(8,128)S(1)} %get-tuple-element.232, s32[32]{0:T(128)S(1)} %get-tuple-element.213, f32[32,128,256]{2,1,0:T(8,128)} %fusion.56), kind=kCustom, calls=%fused_computation.2.clone.1 | custom fusion | flops 1048576 | bytes 12583040 | tf_op jit(solution)/shard_map/while/body/eval_jaxpr/scatter-add | solution.py:39
  232.8 6.5 %scatter_fusion = f32[16,128,256]{2,1,0:T(8,128)S(1)} fusion(f32[16,128,256]{2,1,0:T(8,128)S(1)} %get-tuple-element.232, s32[32]{0:T(128)S(1)} %get-tuple-element.213, f32[32,128,256]{2,1,0:T(8,128)} %fusion.56), kind=kCustom, calls=%fused_computation.2.clone.1 | custom fusion | flops 1048576 | bytes 12583040 | tf_op jit(solution)/shard_map/while/body/eval_jaxpr/scatter-add | solution.py:39
  243.1 13.8 %all-reduce = f32[2048]{0:T(1024)S(1)} all-reduce(f32[2048]{0:T(1024)S(1)} %bitcast.96), channel_id=3, replica_groups=mesh['nodes'=16,'cols'=8] {'cols'}, use_global_device_ids=true, to_apply=%region_6.7.clone | all-reduce | flops 2048 | bytes 16384
  257.0 17.7 %reduce-scatter.3.cloned.1.call-done = f32[256,256]{1,0:T(8,128)} async-done(((f32[2048,256]{1,0:T(8,128)}), f32[256,256]{1,0:T(8,128)}) %reduce-scatter.3.cloned.1.call-update) | async-done | bytes 262160 | tf_op jit(solution)/shard_map/reduce_scatter | solution.py:51
  280.3 20.2 %all-gather.5.cloned.1.call-done = bf16[2048,256]{1,0:T(8,128)(2,1)} async-done(((bf16[256,256]{1,0:T(8,128)(2,1)}), bf16[2048,256]{1,0:T(8,128)(2,1)}) %all-gather.5.cloned.1.call-update) | async-done | bytes 1048592 | tf_op jit(solution)/shard_map/all_gather | solution.py:79
  302.9 166.3 %while.23 = (s32[]{:T(128)}, f32[32,128,256]{2,1,0:T(8,128)}, s32[11,32]{1,0:T(8,128)}, s32[11,32,16,128]{3,2,1,0:T(8,128)}, s32[11,32]{1,0:T(8,128)}, /*index=5*/bf16[16,128,256]{2,1,0:T(8,128)(2,1)S(1)}, s32[]{:T(128)}) while((s32[]{:T(128)}, f32[32,128,256]{2,1,0:T(8,128)}, s32[11,32]{1,0:T(8,128)}, s32[11,32,16,128]{3,2,1,0:T(8,128)}, ...), condition=%wide.region_9.10_spmd, body=%wide.region_7.9_spmd.sunk | while | flops 271058112 | bytes 23862236 | solution.py:89
  308.1 10.0 %scatter_fusion.1 = f32[32,128,256]{2,1,0:T(8,128)} fusion(f32[32,128,256]{2,1,0:T(8,128)} %get-tuple-element.255, s32[32]{0:T(128)S(1)} %get-tuple-element.221, f32[32,128,256]{2,1,0:T(8,128)} %fusion.60), kind=kCustom, calls=%fused_computation.4.clone.1 | custom fusion | flops 1048576 | bytes 12583040 | tf_op jit(solution)/shard_map/while/body/eval_jaxpr/scatter-add | solution.py:87
  323.3 10.0 %scatter_fusion.1 = f32[32,128,256]{2,1,0:T(8,128)} fusion(f32[32,128,256]{2,1,0:T(8,128)} %get-tuple-element.255, s32[32]{0:T(128)S(1)} %get-tuple-element.221, f32[32,128,256]{2,1,0:T(8,128)} %fusion.60), kind=kCustom, calls=%fused_computation.4.clone.1 | custom fusion | flops 1048576 | bytes 12583040 | tf_op jit(solution)/shard_map/while/body/eval_jaxpr/scatter-add | solution.py:87
  338.5 9.9 %scatter_fusion.1 = f32[32,128,256]{2,1,0:T(8,128)} fusion(f32[32,128,256]{2,1,0:T(8,128)} %get-tuple-element.255, s32[32]{0:T(128)S(1)} %get-tuple-element.221, f32[32,128,256]{2,1,0:T(8,128)} %fusion.60), kind=kCustom, calls=%fused_computation.4.clone.1 | custom fusion | flops 1048576 | bytes 12583040 | tf_op jit(solution)/shard_map/while/body/eval_jaxpr/scatter-add | solution.py:87
  353.6 9.8 %scatter_fusion.1 = f32[32,128,256]{2,1,0:T(8,128)} fusion(f32[32,128,256]{2,1,0:T(8,128)} %get-tuple-element.255, s32[32]{0:T(128)S(1)} %get-tuple-element.221, f32[32,128,256]{2,1,0:T(8,128)} %fusion.60), kind=kCustom, calls=%fused_computation.4.clone.1 | custom fusion | flops 1048576 | bytes 12583040 | tf_op jit(solution)/shard_map/while/body/eval_jaxpr/scatter-add | solution.py:87
  368.6 9.9 %scatter_fusion.1 = f32[32,128,256]{2,1,0:T(8,128)} fusion(f32[32,128,256]{2,1,0:T(8,128)} %get-tuple-element.255, s32[32]{0:T(128)S(1)} %get-tuple-element.221, f32[32,128,256]{2,1,0:T(8,128)} %fusion.60), kind=kCustom, calls=%fused_computation.4.clone.1 | custom fusion | flops 1048576 | bytes 12583040 | tf_op jit(solution)/shard_map/while/body/eval_jaxpr/scatter-add | solution.py:87
  383.7 10.0 %scatter_fusion.1 = f32[32,128,256]{2,1,0:T(8,128)} fusion(f32[32,128,256]{2,1,0:T(8,128)} %get-tuple-element.255, s32[32]{0:T(128)S(1)} %get-tuple-element.221, f32[32,128,256]{2,1,0:T(8,128)} %fusion.60), kind=kCustom, calls=%fused_computation.4.clone.1 | custom fusion | flops 1048576 | bytes 12583040 | tf_op jit(solution)/shard_map/while/body/eval_jaxpr/scatter-add | solution.py:87
  398.8 9.9 %scatter_fusion.1 = f32[32,128,256]{2,1,0:T(8,128)} fusion(f32[32,128,256]{2,1,0:T(8,128)} %get-tuple-element.255, s32[32]{0:T(128)S(1)} %get-tuple-element.221, f32[32,128,256]{2,1,0:T(8,128)} %fusion.60), kind=kCustom, calls=%fused_computation.4.clone.1 | custom fusion | flops 1048576 | bytes 12583040 | tf_op jit(solution)/shard_map/while/body/eval_jaxpr/scatter-add | solution.py:87
  414.0 9.9 %scatter_fusion.1 = f32[32,128,256]{2,1,0:T(8,128)} fusion(f32[32,128,256]{2,1,0:T(8,128)} %get-tuple-element.255, s32[32]{0:T(128)S(1)} %get-tuple-element.221, f32[32,128,256]{2,1,0:T(8,128)} %fusion.60), kind=kCustom, calls=%fused_computation.4.clone.1 | custom fusion | flops 1048576 | bytes 12583040 | tf_op jit(solution)/shard_map/while/body/eval_jaxpr/scatter-add | solution.py:87
  429.1 9.9 %scatter_fusion.1 = f32[32,128,256]{2,1,0:T(8,128)} fusion(f32[32,128,256]{2,1,0:T(8,128)} %get-tuple-element.255, s32[32]{0:T(128)S(1)} %get-tuple-element.221, f32[32,128,256]{2,1,0:T(8,128)} %fusion.60), kind=kCustom, calls=%fused_computation.4.clone.1 | custom fusion | flops 1048576 | bytes 12583040 | tf_op jit(solution)/shard_map/while/body/eval_jaxpr/scatter-add | solution.py:87
  444.2 9.9 %scatter_fusion.1 = f32[32,128,256]{2,1,0:T(8,128)} fusion(f32[32,128,256]{2,1,0:T(8,128)} %get-tuple-element.255, s32[32]{0:T(128)S(1)} %get-tuple-element.221, f32[32,128,256]{2,1,0:T(8,128)} %fusion.60), kind=kCustom, calls=%fused_computation.4.clone.1 | custom fusion | flops 1048576 | bytes 12583040 | tf_op jit(solution)/shard_map/while/body/eval_jaxpr/scatter-add | solution.py:87
  459.2 9.9 %scatter_fusion.1 = f32[32,128,256]{2,1,0:T(8,128)} fusion(f32[32,128,256]{2,1,0:T(8,128)} %get-tuple-element.255, s32[32]{0:T(128)S(1)} %get-tuple-element.221, f32[32,128,256]{2,1,0:T(8,128)} %fusion.60), kind=kCustom, calls=%fused_computation.4.clone.1 | custom fusion | flops 1048576 | bytes 12583040 | tf_op jit(solution)/shard_map/while/body/eval_jaxpr/scatter-add | solution.py:87
  469.8 65.9 %psum.23 = f32[256]{0:T(256)} all-reduce(f32[256]{0:T(256)S(1)} %copy-done.7), channel_id=1, replica_groups=mesh['nodes'=16,'cols'=8] {'nodes','cols'}, use_global_device_ids=true, to_apply=%region_14.15 | all-reduce | flops 256 | bytes 2048 | tf_op jit(solution)/shard_map/psum | solution.py:73
  537.5 9.4 %reduce-scatter.5.cloned.1.call-done = f32[256,256]{1,0:T(8,128)} async-done(((f32[4096,256]{1,0:T(8,128)}), f32[256,256]{1,0:T(8,128)}) %reduce-scatter.5.cloned.1.call-update) | async-done | bytes 262160 | tf_op jit(solution)/shard_map/reduce_scatter | solution.py:95
  (234 shorter events, 224.6 us)
Async XLA Ops:
  7.2 267.6 %copy-start = (bf16[256,256]{1,0:T(8,128)(2,1)S(1)}, bf16[256,256]{1,0:T(8,128)(2,1)}, u32[]{:S(2)}) copy-start(bf16[256,256]{1,0:T(8,128)(2,1)} %param.17) | copy-start | bytes 393220
  7.2 50.7 %all-gather.3.cloned.1.call-start = ((), (), s32[]{:S(2)}) async-start(), calls=%async_computation.2 | async-start | bytes 2228224 | tf_op jit(solution)/shard_map/all_gather | solution.py:29
  7.9 266.8 %reduce-scatter.3.cloned.1.call-start = ((), (), s32[]{:S(2)}) async-start(), calls=%async_computation.3 | async-start | bytes 2359296 | tf_op jit(solution)/shard_map/reduce_scatter | solution.py:51
  240.2 1.4 copy-start.1
  240.3 2.0 copy-start.5
  240.3 2.0 copy-start.6
  240.3 1.4 copy-start.11
  240.3 2.6 copy-start.3
  240.3 2.6 copy-start.4
  240.3 34.4 %copy-start.9 = (bf16[256,256]{1,0:T(8,128)(2,1)S(1)}, bf16[256,256]{1,0:T(8,128)(2,1)}, u32[]{:S(2)}) copy-start(bf16[256,256]{1,0:T(8,128)(2,1)} %param.19) | copy-start | bytes 393220
  240.3 34.4 %copy-start.10 = (f32[256]{0:T(256)S(1)}, f32[256]{0:T(256)}, u32[]{:S(2)}) copy-start(f32[256]{0:T(256)} %param.18) | copy-start | bytes 3076
  241.6 58.8 %all-gather.5.cloned.1.call-start = ((), (), s32[]{:S(2)}) async-start(), calls=%async_computation.4 | async-start | bytes 1179648 | tf_op jit(solution)/shard_map/all_gather | solution.py:79
  274.7 4.5 copy-start.8
  278.2 257.5 %all-reduce.4.cloned.1.call-start = ((), (), s32[]{:S(2)}) async-start(), calls=%async_computation.6 | async-start | bytes 1048576 | tf_op jit(solution)/shard_map/psum | solution.py:73
  280.2 266.7 %reduce-scatter.5.cloned.1.call-start = ((), (), s32[]{:S(2)}) async-start(), calls=%async_computation.5 | async-start | bytes 4456448 | tf_op jit(solution)/shard_map/reduce_scatter | solution.py:95
  300.5 2.4 copy-start.2
  469.2 0.7 copy-start.7
Sparse Core Ops, SparseCore 0:
  10.2 47.7 all-gather.2
  241.7 32.9 reduce-scatter.2
  278.3 22.0 all-gather.4
  305.8 144.7 all-reduce.3
  469.3 77.5 reduce-scatter.4
where the time goes:
time: 560 us; the launch traced here: 557 us
  other arithmetic  200 us (36%)
  waiting for transfers between devices  96.4 us (17%)
  matrix products  85.6 us (15%)
  blocking collectives  79.7 us (14%)
  local copies, waits for them, and re-layouts  79.4 us (14%)
  between operations  14.6 us (3%)
    scatter-add x11, other arithmetic, backward_step(): return (src_grad.at[cols_blk].add(products), None)  109 us
    scatter-add x11, other arithmetic, forward_step(): summed = summed.at[rows_blk].add(products)  71.1 us
    psum x1, blocking collectives, shards(): lax.psum((self_term, neigh_term, bias_term), ('nodes', 'cols'))  65.9 us
    all_gather x1, waiting for transfers between devices, shards(): source = lax.all_gather(node_feats, 'nodes', axis=0, tiled=True)  48.4 us
    dot_general x11, matrix products, forward_step(): jnp.einsum('tba,tbf->taf', bits_blk, picked, preferred_element_type=jnp.f...  48.1 us
    gather x11, local copies, waits for them, and re-layouts, forward_step(): picked = source_blocks[cols_blk]  39.8 us
    dot_general x11, matrix products, backward_step(): jnp.einsum('tba,taf->tbf', bits_blk, picked, preferred_element_type=jnp.f...  30.1 us
    shift_right_arithmetic x66, local copies, waits for them, and re-layouts, unpack_tiles(): jnp.right_shift(packed[:, :, None, :], shifts[None, None, :, None]) & 1  23.4 us
  transfers between devices with their start and end apart: 5, of which 4 were waited for; matrix products, arithmetic and copies ran while one was open for 31% of the time, Pallas kernels for 0%

commit v1 on v0

v1 whole, which is shorter than its diff:
```python
import jax
import jax.numpy as jnp
from jax import lax
from jax.experimental import pallas as pl
from jax.experimental.pallas import tpu as pltpu
from jax.sharding import PartitionSpec as P

BF = jnp.bfloat16
F32 = jnp.float32


def build_kernel(row_ref, col_ref, bits_ref, at_ref, deg_ref, acc):
    step = pl.program_id(0)
    tiles = bits_ref.shape[0]
    slots = acc.shape[0]
    dests = at_ref.shape[1] // 128

    @pl.when(step == 0)
    def _():
        deg_ref[...] = jnp.zeros_like(deg_ref)

        def clear(s, carry):
            acc[s] = jnp.zeros((128, 128), F32)
            return carry

        lax.fori_loop(0, slots, clear, 0)
        shifts = lax.broadcasted_iota(jnp.int32, (8, 128), 0)

        def add_tile(t, carry):
            slot = col_ref[t] * dests + row_ref[t]
            for w in range(16):
                word = jnp.broadcast_to(bits_ref[t, w : w + 1, :], (8, 128))
                flag = (jnp.right_shift(word, shifts) & 1).astype(F32)
                acc[slot, 8 * w : 8 * w + 8, :] += flag
            return carry

        lax.fori_loop(0, tiles, add_tile, 0)

    for r in range(dests):
        block = acc[step * dests + r]
        at_ref[:, r * 128 : (r + 1) * 128] = block.astype(BF)
        deg_ref[:, r * 128 : (r + 1) * 128] += jnp.sum(block, axis=0, keepdims=True)


def build(rows, cols, bits, source_blocks, dest_blocks):
    tiles = bits.shape[0]
    return pl.pallas_call(
        build_kernel,
        out_shape=(
            jax.ShapeDtypeStruct((source_blocks * 128, dest_blocks * 128), BF),
            jax.ShapeDtypeStruct((1, dest_blocks * 128), F32),
        ),
        grid_spec=pltpu.PrefetchScalarGridSpec(
            num_scalar_prefetch=2,
            grid=(source_blocks,),
            in_specs=[pl.BlockSpec((tiles, 16, 128), lambda i, *_: (0, 0, 0))],
            out_specs=(
                pl.BlockSpec((128, dest_blocks * 128), lambda i, *_: (i, 0)),
                pl.BlockSpec((1, dest_blocks * 128), lambda i, *_: (0, 0)),
            ),
            scratch_shapes=[pltpu.VMEM((source_blocks * dest_blocks, 128, 128), F32)],
        ),
        compiler_params=pltpu.CompilerParams(vmem_limit_bytes=56 << 20),
        cost_estimate=pl.CostEstimate(flops=0, bytes_accessed=60 << 20, transcendentals=0),
        name="build",
    )(rows, cols, bits)


def forward_kernel(place_ref, xt_ref, at_ref, keep_ref, give_ref, acc):
    step = pl.program_id(0)
    width = xt_ref.shape[2]
    part = jnp.dot(xt_ref[0], at_ref[0:width, :], preferred_element_type=F32)
    for k in range(1, xt_ref.shape[0]):
        part += jnp.dot(
            xt_ref[k], at_ref[k * width : (k + 1) * width, :], preferred_element_type=F32
        )

    @pl.when(step == 0)
    def _():
        acc[...] = part

    @pl.when(step > 0)
    def _():
        acc[...] += part

    @pl.when(step == pl.num_programs(0) - 1)
    def _():
        y = place_ref[0]
        core = place_ref[1]
        for k in range(4):
            chunk = 2 * lax.rem(y + k, 4)
            mine = pl.multiple_of((chunk + core) * width, width)
            other = pl.multiple_of((chunk + 1 - core) * width, width)
            keep_ref[k] = acc[:, pl.ds(mine, width)]
            give_ref[k] = acc[:, pl.ds(other, width)].astype(BF)


def forward(place, xt, at):
    nodes, width_in, rows = xt.shape
    dest = at.shape[1]
    per = 2
    return pl.pallas_call(
        forward_kernel,
        out_shape=(
            jax.ShapeDtypeStruct((4, width_in, rows), F32),
            jax.ShapeDtypeStruct((4, width_in, rows), BF),
        ),
        grid_spec=pltpu.PrefetchScalarGridSpec(
            num_scalar_prefetch=1,
            grid=(nodes // per,),
            in_specs=[
                pl.BlockSpec((per, width_in, rows), lambda i, *_: (i, 0, 0)),
                pl.BlockSpec((per * rows, dest), lambda i, *_: (i, 0)),
            ],
            out_specs=(
                pl.BlockSpec((4, width_in, rows), lambda i, *_: (0, 0, 0)),
                pl.BlockSpec((4, width_in, rows), lambda i, *_: (0, 0, 0)),
            ),
            scratch_shapes=[pltpu.VMEM((width_in, dest), F32)],
        ),
        cost_estimate=pl.CostEstimate(
            flops=2 * nodes * rows * dest * width_in, bytes_accessed=20 << 20, transcendentals=0
        ),
        name="forward",
    )(place, xt, at)


def backward_kernel(g_ref, at_ref, out_ref):
    out_ref[...] = jnp.dot(at_ref[...], g_ref[...], preferred_element_type=F32).astype(BF)


def backward(g, at):
    source, dest = at.shape
    width = g.shape[1]
    rows = 512
    return pl.pallas_call(
        backward_kernel,
        out_shape=jax.ShapeDtypeStruct((source, width), BF),
        grid=(source // rows,),
        in_specs=[
            pl.BlockSpec((dest, width), lambda i: (0, 0)),
            pl.BlockSpec((rows, dest), lambda i: (i, 0)),
        ],
        out_specs=pl.BlockSpec((rows, width), lambda i: (i, 0)),
        cost_estimate=pl.CostEstimate(
            flops=2 * source * dest * width, bytes_accessed=20 << 20, transcendentals=0
        ),
        name="backward",
    )(g, at)


def dot_on(a, b, da, db):
    return lax.dot_general(a, b, (((da,), (db,)), ((), ())), preferred_element_type=F32)


def middle_kernel(
    own_ref, r1_ref, r2_ref, r3_ref, deg_ref, x_ref, ws_ref, wn_ref, bias_ref, cot_ref,
    out_ref, pre_ref, mean_ref, grad_ref,
):
    degree = jnp.maximum(jnp.sum(deg_ref[...], axis=0, keepdims=True), 1.0)
    summed = own_ref[0] + r1_ref[...].astype(F32) + r2_ref[...].astype(F32)
    summed += r3_ref[...].astype(F32)
    mean_t = (summed / degree).astype(BF)
    mean_ref[...] = mean_t
    preact = (
        jnp.dot(x_ref[...], ws_ref[...], preferred_element_type=F32)
        + dot_on(mean_t, wn_ref[...], 0, 0)
        + bias_ref[...]
    )
    sig = 1.0 / (1.0 + jnp.exp(-preact))
    out_ref[...] = (preact * sig).astype(BF)
    pre_grad = (cot_ref[...].astype(F32) * sig * (1.0 + preact * (1.0 - sig))).astype(BF)
    pre_ref[...] = pre_grad
    grad_t = dot_on(wn_ref[...], pre_grad, 1, 1) / degree
    grad_ref[...] = grad_t.T.astype(BF)


def middle(own, r1, r2, r3, deg, x, ws, wn, bias, cot):
    n = x.shape[0]
    shape = jax.ShapeDtypeStruct((n, n), BF)
    return pl.pallas_call(
        middle_kernel,
        out_shape=(shape, shape, shape, shape),
        cost_estimate=pl.CostEstimate(
            flops=6 * n * n * n, bytes_accessed=2 << 20, transcendentals=n * n
        ),
        name="middle",
    )(own, r1, r2, r3, deg, x, ws, wn, bias, cot)


def weights_kernel(x_ref, pre_ref, mean_ref, ws_ref, part_ref, self_ref):
    pre_grad = pre_ref[...]
    self_grad = dot_on(x_ref[...], pre_grad, 0, 0)
    neigh_grad = jnp.dot(mean_ref[...], pre_grad, preferred_element_type=F32)
    bias_grad = jnp.sum(pre_grad.astype(F32), axis=0, keepdims=True)
    first = lax.broadcasted_iota(jnp.int32, (8, 1), 0) == 0
    bias_rows = jnp.where(first, bias_grad, 0.0)
    for c in range(8):
        grad = self_grad if c < 4 else neigh_grad
        part_ref[c, 0:64, :] = grad[(c % 4) * 64 : (c % 4) * 64 + 64, :]
        part_ref[c, 64:72, :] = bias_rows
    self_ref[...] = dot_on(pre_grad, ws_ref[...], 1, 1)


def weights(x, pre_grad, mean_t, ws):
    n = x.shape[0]
    return pl.pallas_call(
        weights_kernel,
        out_shape=(
            jax.ShapeDtypeStruct((8, 72, n), F32),
            jax.ShapeDtypeStruct((n, n), F32),
        ),
        cost_estimate=pl.CostEstimate(
            flops=6 * n * n * n, bytes_accessed=2 << 20, transcendentals=0
        ),
        name="weights",
    )(x, pre_grad, mean_t, ws)


def finish_kernel(parts_ref, self_ref, out_ref):
    total = self_ref[...]
    for k in range(parts_ref.shape[0]):
        total += parts_ref[k].astype(F32)
    out_ref[...] = total.astype(BF)


def finish(parts, self_part):
    return pl.pallas_call(
        finish_kernel,
        out_shape=jax.ShapeDtypeStruct(self_part.shape, BF),
        cost_estimate=pl.CostEstimate(flops=1 << 20, bytes_accessed=2 << 20, transcendentals=0),
        name="finish",
    )(parts, self_part)


def swap(x, axis):
    return lax.all_to_all(x, axis, 0, 0, tiled=True)


def spread(x, axis):
    count = lax.axis_size(axis)
    return swap(jnp.broadcast_to(x[None], (count, *x.shape)), axis)


def along_y(step):
    return [(2 * y + c, 2 * ((y + step) % 4) + c) for y in range(4) for c in range(2)]


def shards(node_feats, tile_row, tile_col, tile_bits, w_self, w_neigh, bias, cotangent):
    nodes = lax.axis_size("nodes")
    cols = lax.axis_size("cols")
    rows_dev, width = node_feats.shape
    me = lax.axis_index("cols")
    y, core = me // 2, me % 2
    place = jnp.stack([y, core]).astype(jnp.int32)
    partner = [(i, i ^ 1) for i in range(8)]

    xt_all = spread(node_feats.T, "nodes")
    at, degree = build(
        tile_row[0], tile_col[0], tile_bits[0], nodes * rows_dev // 128, cols * rows_dev // 128
    )
    degrees = swap(degree.reshape(cols, rows_dev), "cols")

    keep, give = forward(place, xt_all, at)
    taken = lax.ppermute(give, "cols", partner)
    both = keep + taken.astype(F32)
    send = both[1:].astype(BF)
    got = [lax.ppermute(send[k - 1], "cols", along_y(k)) for k in (1, 2, 3)]
    layer_out, pre_grad, mean_t, mean_grad = middle(
        both[:1], *got, degrees, node_feats, w_self, w_neigh, bias.reshape(1, -1), cotangent
    )
    others = [mean_grad] + [lax.ppermute(mean_grad, "cols", along_y(k)) for k in (1, 2, 3)]
    same_core = jnp.stack(others)
    other_core = lax.ppermute(same_core, "cols", partner)
    pair = jnp.where(core == 0, jnp.stack([same_core, other_core], 1), jnp.stack([other_core, same_core], 1))
    order = (y - jnp.arange(4)) % 4
    grads = pair[order].reshape(cols * rows_dev, width)

    part, self_part = weights(node_feats, pre_grad, mean_t, w_self)
    part = jnp.sum(swap(part, "cols"), axis=0)
    bias_sum = part[64:72]
    fine = jnp.concatenate(
        [part[:64].reshape(nodes, 4, width), jnp.broadcast_to(bias_sum[None, :4], (nodes, 4, width))], 1
    )
    fine = jnp.sum(swap(fine, "nodes"), axis=0)
    coarse = spread(fine, "nodes")
    bias_grad = coarse[0, 4]
    coarse = coarse[:, :4].reshape(64, width)
    whole = spread(coarse, "cols").reshape(2, width, width)

    src = backward(grads, at)
    parts = swap(src.reshape(nodes, rows_dev, width), "nodes")
    feat_grad = finish(parts, self_part)
    return (layer_out, feat_grad, whole[0], whole[1], bias_grad)


def solution(mesh):
    return jax.shard_map(
        shards,
        mesh=mesh,
        in_specs=(
            P(("nodes", "cols"), None),
            P("nodes", "cols"),
            P("nodes", "cols"),
            P("nodes", "cols", None, None),
            P(),
            P(),
            P(),
            P(("nodes", "cols"), None),
        ),
        out_specs=(P(("nodes", "cols"), None), P(("nodes", "cols"), None), P(), P(), P()),
        check_vma=False,
    )
```

time: 560 us -> 183 us (0.33)
  other arithmetic: 200 us -> 4.42 us
  matrix products: 85.6 us -> 0 us
  local copies, waits for them, and re-layouts: 79.4 us -> 11.8 us
  blocking collectives: 79.7 us -> 19.2 us
  Pallas kernels: 0 us -> 57.9 us
  waiting for transfers between devices: 96.4 us -> 54.1 us
  starting transfers between devices: 0.2 us -> 33.2 us
  between operations: 14.6 us -> 0.88 us
    scatter-add x33 -> x0, other arithmetic: 188 us -> none  [the longest x11 109 us: backward_step(): return (src_grad.at[cols_blk].add(products), None)]
    dot_general x28 -> x0, matrix products: 85.6 us -> none  [the longest x11 48.1 us: forward_step(): jnp.einsum('tba,tbf->taf', bits_blk, picked, preferred_element_type=jnp.f...]
    all_gather x2 -> x0, waiting for transfers between devices: 68.6 us -> none  [the longest x1 48.4 us: shards(): source = lax.all_gather(node_feats, 'nodes', axis=0, tiled=True)]
    psum x1 -> x0, blocking collectives: 65.9 us -> none  [shards(): lax.psum((self_term, neigh_term, bias_term), ('nodes', 'cols'))]
    pallas_call x0 -> x6, Pallas kernels: none -> 57.9 us  [the longest x1 25.1 us: build(): pl.pallas_call(build_kernel, out_shape=(jax.ShapeDtypeStruct((source_bloc...]
    gather x22 -> x1, local copies, waits for them, and re-layouts: 47.3 us -> 1.61 us  [shards(): grads = pair[order].reshape(cols * rows_dev, width)]
    all_to_all x0 -> x5, waiting for transfers between devices: none -> 40.5 us  [swap(): return lax.all_to_all(x, axis, 0, 0, tiled=True)]
    reduce_scatter x2 -> x0, waiting for transfers between devices: 27.1 us -> none  [the longest x1 17.7 us: shards(): lax.psum_scatter(partial_sum.reshape(dest_count * 128, width_in), 'cols',...]
  transfers between devices with their start and end apart: 5 -> 13, of which waited for: 4 -> 7; matrix products, arithmetic and copies ran while one was open for 31% -> 5% of each run, Pallas kernels for 0% -> 20%
where the time goes in v1:
time: 183 us; the launch traced here: 182 us
  Pallas kernels  57.9 us (32%)
  waiting for transfers between devices  54.1 us (30%)
  starting transfers between devices  33.2 us (18%)
  blocking collectives  19.2 us (10%)
  local copies, waits for them, and re-layouts  11.8 us (6%)
  other arithmetic  4.42 us (2%)
    all_to_all x5, waiting for transfers between devices, swap(): return lax.all_to_all(x, axis, 0, 0, tiled=True)  40.5 us
    pallas_call x1, Pallas kernels, build(): pl.pallas_call(build_kernel, out_shape=(jax.ShapeDtypeStruct((source_bloc...  25.1 us
    all_to_all x5, starting transfers between devices, swap(): return lax.all_to_all(x, axis, 0, 0, tiled=True)  22.4 us
    all_to_all x2, blocking collectives, swap(): return lax.all_to_all(x, axis, 0, 0, tiled=True)  19.2 us
    pallas_call x1, Pallas kernels, forward(): pl.pallas_call(forward_kernel, out_shape=(jax.ShapeDtypeStruct((4, width_...  13.6 us
    pallas_call x1, Pallas kernels, backward(): pl.pallas_call(backward_kernel, out_shape=jax.ShapeDtypeStruct((source, w...  11.7 us
    ppermute x3, waiting for transfers between devices, shards(): lax.ppermute(mean_grad, 'cols', along_y(k))  11.4 us
    ppermute x3, starting transfers between devices, shards(): got = [lax.ppermute(send[k - 1], 'cols', along_y(k)) for k in (1, 2, 3)]  5.89 us
  transfers between devices with their start and end apart: 13, of which 7 were waited for; matrix products, arithmetic and copies ran while one was open for 5% of the time, Pallas kernels for 20%

profile of v1, /device:TPU:0, one launch (start us, length us, event | category | flops | bytes accessed | tf_op | source)
XLA Modules:
  0.0 181.5 jit_solution(17688063762132051684)
XLA Ops:
  1.6 1.5 broadcast_in_dim.10
  3.2 8.1 %all-to-all-start = ((bf16[16,256,256]{2,1,0:T(8,128)(2,1)}), bf16[16,256,256]{2,1,0:T(8,128)(2,1)S(1)}, u32[]{:S(2)}, u32[]{:S(2)}) async-start(bf16[16,256,256]{2,1,0:T(8,128)(2,1)} %broadcast_in_dim.10), calls=%async_computation | async-start | bytes 4194304 | tf_op jit(solution)/shard_map/all_to_all | solution.py:237
  12.5 25.1 %build.1 = (bf16[4096,2048]{1,0:T(8,128)(2,1)}, f32[1,2048]{1,0:T(1,128)}) custom-call(s32[352]{0:T(512)} %reduce.row_ref, s32[352]{0:T(512)} %reduce.1.col_ref, s32[352,16,128]{2,1,0:T(8,128)} %bitcast.31), custom_call_target="tpu_custom_call" | custom-call | bytes 62914560 | tf_op jit(solution)/shard_map/build/pallas_call | solution.py:47
  38.2 3.5 %all-to-all-done.xt_ref = bf16[16,256,256]{2,1,0:T(8,128)(2,1)S(1)} async-done(((bf16[16,256,256]{2,1,0:T(8,128)(2,1)}), bf16[16,256,256]{2,1,0:T(8,128)(2,1)S(1)}, u32[]{:S(2)}, u32[]{:S(2)}) %all-to-all-start) | async-done | bytes 2097184 | tf_op jit(solution)/shard_map/all_to_all | solution.py:237
  43.0 13.6 %forward.1 = (f32[4,256,256]{2,1,0:T(8,128)}, bf16[4,256,256]{2,1,0:T(8,128)(2,1)}) custom-call(s32[2]{0:T(128)} %pad_add_fusion.place_ref, bf16[16,256,256]{2,1,0:T(8,128)(2,1)} %copy-done.1, bf16[4096,2048]{1,0:T(8,128)(2,1)} %get-tuple-element.15.at_ref), custom_call_target="tpu_custom_call" | custom-call | flops 4294967296 | bytes 20971520 | tf_op jit(solution)/shard_map/forward/pallas_call | solution.py:102
  56.6 2.1 %collective-permute-done = bf16[4,256,256]{2,1,0:T(8,128)(2,1)S(1)} collective-permute-done((bf16[4,256,256]{2,1,0:T(8,128)(2,1)}, bf16[4,256,256]{2,1,0:T(8,128)(2,1)S(1)}, u32[]{:S(2)}, u32[]{:S(2)}) %collective-permute-start) | collective-permute-done | bytes 524320 | tf_op jit(solution)/shard_map/ppermute | solution.py:265
  60.2 1.6 collective-permute-start.1
  61.8 2.9 %collective-permute-start.2 = (bf16[256,256]{1,0:T(8,128)(2,1)S(1)}, bf16[256,256]{1,0:T(8,128)(2,1)S(1)}, u32[]{:S(2)}, u32[]{:S(2)}) collective-permute-start(bf16[256,256]{1,0:T(8,128)(2,1)S(1)} %get-tuple-element.32), channel_id=1, source_target_pairs={{0,4},{1,5},{2,6},{3,7},{4,0},{5,1},{6,2},{7,3},{8,12},{9,13},{10,... | collective-permute-start | bytes 393224 | tf_op jit(solution)/shard_map/ppermute | solution.py:268
  66.1 7.7 %all_to_all.41 = f32[8,1,256]{2,1,0:T(1,128)S(1)} all-to-all(f32[8,1,256]{2,1,0:T(1,128)S(1)} %bitcast.41), channel_id=1, replica_groups=mesh['nodes'=16,'cols'=8] {'cols'}, dimensions={0} | all-to-all | bytes 16384 | tf_op jit(solution)/shard_map/all_to_all | solution.py:237
  75.8 2.7 %middle.1 = (bf16[256,256]{1,0:T(8,128)(2,1)}, bf16[256,256]{1,0:T(8,128)(2,1)}, bf16[256,256]{1,0:T(8,128)(2,1)}, bf16[256,256]{1,0:T(8,128)(2,1)}) custom-call(f32[1,256,256]{2,1,0:T(8,128)} %slice.51.own_ref, bf16[256,256]{1,0:T(8,128)(2,1)} %copy-done.2, bf16[256,256]{1,0:T(8,128)(2,1)} %copy-done.3, bf16[256,256]{1,0:T(8,128)(2,1)} %copy-done.4, ...), custom_call_target="tpu_custom_call" | custom-call | flops 100663296 | bytes 2097152 | tf_op jit(solution)/shard_map/middle/pallas_call | solution.py:181
  78.5 2.2 %weights.1 = (f32[8,72,256]{2,1,0:T(8,128)}, f32[256,256]{1,0:T(8,128)}) custom-call(bf16[256,256]{1,0:T(8,128)(2,1)} %x_ref.3, bf16[256,256]{1,0:T(8,128)(2,1)} %get-tuple-element.21.pre_ref, bf16[256,256]{1,0:T(8,128)(2,1)} %get-tuple-element.22.mean_ref, bf16[256,256]{1,0:T(8,128)(2,1)} %ws_ref.3), custom_call_target="tpu_custom_call" | custom-call | flops 100663296 | bytes 2097152 | tf_op jit(solution)/shard_map/weights/pallas_call | solution.py:207
  80.7 3.5 %all-to-all-start.3 = ((f32[8,72,256]{2,1,0:T(8,128)}), f32[8,72,256]{2,1,0:T(8,128)S(1)}, u32[]{:S(2)}, u32[]{:S(2)}) async-start(f32[8,72,256]{2,1,0:T(8,128)} %get-tuple-element.24), calls=%async_computation.3 | async-start | bytes 1179648 | tf_op jit(solution)/shard_map/all_to_all | solution.py:237
  84.2 3.2 %collective-permute-start.6 = (bf16[256,256]{1,0:T(8,128)(2,1)}, bf16[256,256]{1,0:T(8,128)(2,1)S(1)}, u32[]{:S(2)}, u32[]{:S(2)}) collective-permute-start(bf16[256,256]{1,0:T(8,128)(2,1)} %get-tuple-element.20), channel_id=1, source_target_pairs={{0,6},{1,7},{2,0},{3,1},{4,2},{5,3},{6,4},{7,5},{8,14},{9,15},{10,... | collective-permute-start | bytes 393224 | tf_op jit(solution)/shard_map/ppermute | solution.py:272
  89.1 7.9 %collective-permute-done.6 = bf16[256,256]{1,0:T(8,128)(2,1)S(1)} collective-permute-done((bf16[256,256]{1,0:T(8,128)(2,1)}, bf16[256,256]{1,0:T(8,128)(2,1)S(1)}, u32[]{:S(2)}, u32[]{:S(2)}) %collective-permute-start.6) | collective-permute-done | bytes 131104 | tf_op jit(solution)/shard_map/ppermute | solution.py:272
  98.5 2.0 %collective-permute-done.4 = bf16[256,256]{1,0:T(8,128)(2,1)S(1)} collective-permute-done((bf16[256,256]{1,0:T(8,128)(2,1)}, bf16[256,256]{1,0:T(8,128)(2,1)S(1)}, u32[]{:S(2)}, u32[]{:S(2)}) %collective-permute-start.4) | collective-permute-done | bytes 131104 | tf_op jit(solution)/shard_map/ppermute | solution.py:272
  101.8 11.5 %all_to_all.42 = f32[16,8,256]{2,1,0:T(8,128)S(1)} all-to-all(f32[16,8,256]{2,1,0:T(8,128)S(1)} %pad_maximum_fusion.1), channel_id=1, replica_groups=mesh['nodes'=16,'cols'=8] {'nodes'}, dimensions={0} | all-to-all | bytes 262144 | tf_op jit(solution)/shard_map/all_to_all | solution.py:237
  114.0 3.5 %all-to-all-start.5 = ((f32[16,8,256]{2,1,0:T(8,128)}), f32[16,8,256]{2,1,0:T(8,128)S(1)}, u32[]{:S(2)}, u32[]{:S(2)}) async-start(f32[16,8,256]{2,1,0:T(8,128)} %broadcast_in_dim.12), calls=%async_computation.5 | async-start | bytes 262144 | tf_op jit(solution)/shard_map/all_to_all | solution.py:237
  117.6 7.8 %all-to-all-done.5 = f32[16,8,256]{2,1,0:T(8,128)S(1)} async-done(((f32[16,8,256]{2,1,0:T(8,128)}), f32[16,8,256]{2,1,0:T(8,128)S(1)}, u32[]{:S(2)}, u32[]{:S(2)}) %all-to-all-start.5) | async-done | bytes 131104 | tf_op jit(solution)/shard_map/all_to_all | solution.py:237
  126.2 3.5 %all-to-all-start.6 = ((f32[8,64,256]{2,1,0:T(8,128)}), f32[8,64,256]{2,1,0:T(8,128)S(1)}, u32[]{:S(2)}, u32[]{:S(2)}) async-start(f32[8,64,256]{2,1,0:T(8,128)} %broadcast_in_dim.14), calls=%async_computation.6 | async-start | bytes 1048576 | tf_op jit(solution)/shard_map/all_to_all | solution.py:237
  129.9 1.6 gather_fusion
  131.5 11.7 %backward.1 = bf16[4096,256]{1,0:T(8,128)(2,1)} custom-call(bf16[2048,256]{1,0:T(8,128)(2,1)} %bitcast.30, bf16[4096,2048]{1,0:T(8,128)(2,1)} %get-tuple-element.15.at_ref), custom_call_target="tpu_custom_call" | custom-call | flops 4294967296 | bytes 20971520 | tf_op jit(solution)/shard_map/backward/pallas_call | solution.py:136
  143.2 3.7 %all-to-all-start.2 = ((bf16[16,256,256]{2,1,0:T(8,128)(2,1)}), bf16[16,256,256]{2,1,0:T(8,128)(2,1)S(1)}, u32[]{:S(2)}, u32[]{:S(2)}) async-start(bf16[16,256,256]{2,1,0:T(8,128)(2,1)} %bitcast.29), calls=%async_computation.2 | async-start | bytes 4194304 | tf_op jit(solution)/shard_map/all_to_all | solution.py:237
  148.4 29.3 %all-to-all-done.2.parts_ref = bf16[16,256,256]{2,1,0:T(8,128)(2,1)S(1)} async-done(((bf16[16,256,256]{2,1,0:T(8,128)(2,1)}), bf16[16,256,256]{2,1,0:T(8,128)(2,1)S(1)}, u32[]{:S(2)}, u32[]{:S(2)}) %all-to-all-start.2) | async-done | bytes 2097184 | tf_op jit(solution)/shard_map/all_to_all | solution.py:237
  179.0 2.5 %finish.1 = bf16[256,256]{1,0:T(8,128)(2,1)} custom-call(bf16[16,256,256]{2,1,0:T(8,128)(2,1)} %copy-done, f32[256,256]{1,0:T(8,128)} %get-tuple-element.23.self_ref), custom_call_target="tpu_custom_call" | custom-call | flops 1048576 | bytes 2097152 | tf_op jit(solution)/shard_map/finish/pallas_call | solution.py:228
  (53 shorter events, 17.8 us)
Async XLA Ops:
  3.2 8.1 %copy-start.6 = (s32[1,352]{1,0:T(1,128)S(1)}, s32[1,352]{1,0:T(1,128)}, u32[]{:S(2)}) copy-start(s32[1,352]{1,0:T(1,128)} %param.9) | copy-start | bytes 4228
  3.2 8.7 %copy-start.7 = (s32[1,352]{1,0:T(1,128)S(1)}, s32[1,352]{1,0:T(1,128)}, u32[]{:S(2)}) copy-start(s32[1,352]{1,0:T(1,128)} %param.10) | copy-start | bytes 4228
  3.2 38.5 %all-to-all-start = ((bf16[16,256,256]{2,1,0:T(8,128)(2,1)}), bf16[16,256,256]{2,1,0:T(8,128)(2,1)S(1)}, u32[]{:S(2)}, u32[]{:S(2)}) async-start(bf16[16,256,256]{2,1,0:T(8,128)(2,1)} %broadcast_in_dim.10), calls=%async_computation | async-start | bytes 4194304 | tf_op jit(solution)/shard_map/all_to_all | solution.py:237
  41.7 1.3 copy-start.1
  56.6 9.4 %copy-start.5 = (f32[1,2048]{1,0:T(1,128)S(1)}, f32[1,2048]{1,0:T(1,128)}, u32[]{:S(2)}) copy-start(f32[1,2048]{1,0:T(1,128)} %get-tuple-element.18) | copy-start | bytes 24580
  56.6 2.1 %collective-permute-start = (bf16[4,256,256]{2,1,0:T(8,128)(2,1)}, bf16[4,256,256]{2,1,0:T(8,128)(2,1)S(1)}, u32[]{:S(2)}, u32[]{:S(2)}) collective-permute-start(bf16[4,256,256]{2,1,0:T(8,128)(2,1)} %get-tuple-element.17), channel_id=1, source_target_pairs={{0,1},{1,0},{2,3},{3,2},{4,5},{5,4},{6,7},{7,6},{8,9},{9,8},{10,11... | collective-permute-start | bytes 1572872 | tf_op jit(solution)/shard_map/ppermute | solution.py:265
  60.2 14.9 %collective-permute-start.1 = (bf16[256,256]{1,0:T(8,128)(2,1)S(1)}, bf16[256,256]{1,0:T(8,128)(2,1)S(1)}, u32[]{:S(2)}, u32[]{:S(2)}) collective-permute-start(bf16[256,256]{1,0:T(8,128)(2,1)S(1)} %get-tuple-element.33), channel_id=1, source_target_pairs={{0,2},{1,3},{2,4},{3,5},{4,6},{5,7},{6,0},{7,1},{8,10},{9,11},{10,... | collective-permute-start | bytes 393224 | tf_op jit(solution)/shard_map/ppermute | solution.py:268
  61.8 13.2 %collective-permute-start.2 = (bf16[256,256]{1,0:T(8,128)(2,1)S(1)}, bf16[256,256]{1,0:T(8,128)(2,1)S(1)}, u32[]{:S(2)}, u32[]{:S(2)}) collective-permute-start(bf16[256,256]{1,0:T(8,128)(2,1)S(1)} %get-tuple-element.32), channel_id=1, source_target_pairs={{0,4},{1,5},{2,6},{3,7},{4,0},{5,1},{6,2},{7,3},{8,12},{9,13},{10,... | collective-permute-start | bytes 393224 | tf_op jit(solution)/shard_map/ppermute | solution.py:268
  64.7 10.3 %collective-permute-start.3 = (bf16[256,256]{1,0:T(8,128)(2,1)S(1)}, bf16[256,256]{1,0:T(8,128)(2,1)S(1)}, u32[]{:S(2)}, u32[]{:S(2)}) collective-permute-start(bf16[256,256]{1,0:T(8,128)(2,1)S(1)} %get-tuple-element.31), channel_id=1, source_target_pairs={{0,6},{1,7},{2,0},{3,1},{4,2},{5,3},{6,4},{7,5},{8,14},{9,15},{10,... | collective-permute-start | bytes 393224 | tf_op jit(solution)/shard_map/ppermute | solution.py:268
  75.0 0.7 copy-start.2
  75.0 0.7 copy-start.3
  75.1 0.7 copy-start.4
  80.7 20.9 %all-to-all-start.3 = ((f32[8,72,256]{2,1,0:T(8,128)}), f32[8,72,256]{2,1,0:T(8,128)S(1)}, u32[]{:S(2)}, u32[]{:S(2)}) async-start(f32[8,72,256]{2,1,0:T(8,128)} %get-tuple-element.24), calls=%async_computation.3 | async-start | bytes 1179648 | tf_op jit(solution)/shard_map/all_to_all | solution.py:237
  84.2 12.8 %collective-permute-start.6 = (bf16[256,256]{1,0:T(8,128)(2,1)}, bf16[256,256]{1,0:T(8,128)(2,1)S(1)}, u32[]{:S(2)}, u32[]{:S(2)}) collective-permute-start(bf16[256,256]{1,0:T(8,128)(2,1)} %get-tuple-element.20), channel_id=1, source_target_pairs={{0,6},{1,7},{2,0},{3,1},{4,2},{5,3},{6,4},{7,5},{8,14},{9,15},{10,... | collective-permute-start | bytes 393224 | tf_op jit(solution)/shard_map/ppermute | solution.py:272
  87.4 11.1 %collective-permute-start.5 = (bf16[256,256]{1,0:T(8,128)(2,1)}, bf16[256,256]{1,0:T(8,128)(2,1)S(1)}, u32[]{:S(2)}, u32[]{:S(2)}) collective-permute-start(bf16[256,256]{1,0:T(8,128)(2,1)} %get-tuple-element.20), channel_id=1, source_target_pairs={{0,4},{1,5},{2,6},{3,7},{4,0},{5,1},{6,2},{7,3},{8,12},{9,13},{10,... | collective-permute-start | bytes 393224 | tf_op jit(solution)/shard_map/ppermute | solution.py:272
  88.2 12.3 %collective-permute-start.4 = (bf16[256,256]{1,0:T(8,128)(2,1)}, bf16[256,256]{1,0:T(8,128)(2,1)S(1)}, u32[]{:S(2)}, u32[]{:S(2)}) collective-permute-start(bf16[256,256]{1,0:T(8,128)(2,1)} %get-tuple-element.20), channel_id=1, source_target_pairs={{0,2},{1,3},{2,4},{3,5},{4,6},{5,7},{6,0},{7,1},{8,10},{9,11},{10,... | collective-permute-start | bytes 393224 | tf_op jit(solution)/shard_map/ppermute | solution.py:272
  101.5 28.2 %collective-permute-start.7 = (bf16[4,256,256]{2,1,0:T(8,128)(2,1)S(1)}, bf16[4,256,256]{2,1,0:T(8,128)(2,1)S(1)}, u32[]{:S(2)}, u32[]{:S(2)}) collective-permute-start(bf16[4,256,256]{2,1,0:T(8,128)(2,1)S(1)} %get-tuple-element.30), channel_id=1, source_target_pairs={{0,1},{1,0},{2,3},{3,2},{4,5},{5,4},{6,7},{7,6},{8,9},{9,8},{10,11... | collective-permute-start | bytes 1572872 | tf_op jit(solution)/shard_map/ppermute | solution.py:274
  114.0 11.3 %all-to-all-start.5 = ((f32[16,8,256]{2,1,0:T(8,128)}), f32[16,8,256]{2,1,0:T(8,128)S(1)}, u32[]{:S(2)}, u32[]{:S(2)}) async-start(f32[16,8,256]{2,1,0:T(8,128)} %broadcast_in_dim.12), calls=%async_computation.5 | async-start | bytes 262144 | tf_op jit(solution)/shard_map/all_to_all | solution.py:237
  126.2 17.0 %all-to-all-start.6 = ((f32[8,64,256]{2,1,0:T(8,128)}), f32[8,64,256]{2,1,0:T(8,128)S(1)}, u32[]{:S(2)}, u32[]{:S(2)}) async-start(f32[8,64,256]{2,1,0:T(8,128)} %broadcast_in_dim.14), calls=%async_computation.6 | async-start | bytes 1048576 | tf_op jit(solution)/shard_map/all_to_all | solution.py:237
  143.2 34.4 %all-to-all-start.2 = ((bf16[16,256,256]{2,1,0:T(8,128)(2,1)}), bf16[16,256,256]{2,1,0:T(8,128)(2,1)S(1)}, u32[]{:S(2)}, u32[]{:S(2)}) async-start(bf16[16,256,256]{2,1,0:T(8,128)(2,1)} %bitcast.29), calls=%async_computation.2 | async-start | bytes 4194304 | tf_op jit(solution)/shard_map/all_to_all | solution.py:237
  177.6 1.3 copy-start

commit v2 on v1

v2 whole, which is shorter than its diff:
```python
import jax
import jax.numpy as jnp
from jax import lax
from jax.experimental import pallas as pl
from jax.experimental.pallas import tpu as pltpu
from jax.sharding import PartitionSpec as P

BF = jnp.bfloat16
F32 = jnp.float32
EXACT = 256


def params(mib):
    return pltpu.CompilerParams(vmem_limit_bytes=mib << 20)


def in_hbm(shape, kind):
    return pltpu.HBM(shape, kind)


def cost(flops, moved, transcendentals=0):
    return pl.CostEstimate(flops=flops, bytes_accessed=moved, transcendentals=transcendentals)


def prepare_kernel(x_ref, out_ref, flipped):
    @pl.when(pl.program_id(0) == 0)
    def _():
        flipped[...] = x_ref[...].T

    for k in range(out_ref.shape[0]):
        out_ref[k] = flipped[...]


def prepare(x, copies):
    rows, width = x.shape
    per = 4
    return pl.pallas_call(
        prepare_kernel,
        out_shape=in_hbm((copies, width, rows), BF),
        grid=(copies // per,),
        in_specs=[pl.BlockSpec((rows, width), lambda i: (0, 0))],
        out_specs=pl.BlockSpec((per, width, rows), lambda i: (i, 0, 0)),
        scratch_shapes=[pltpu.VMEM((width, rows), BF)],
        compiler_params=params(8),
        cost_estimate=cost(0, 2 << 20),
        name="prepare",
    )(x)


def build_kernel(row_ref, col_ref, bits_ref, at_ref, deg_ref, deg8, count, spill):
    sources = at_ref.shape[0] - 1
    dests = at_ref.shape[1]
    tiles = bits_ref.shape[0]
    for r in range(dests):
        deg8[r] = jnp.zeros((8, 128), F32)

    def clear(k, carry):
        for r in range(dests):
            at_ref[k, r] = jnp.zeros((128, 128), BF)
            count[k * dests + r] = 0
        return carry

    lax.fori_loop(0, sources, clear, 0)
    at_ref[sources, 0] = jnp.zeros((128, 128), BF)
    spill[0] = -1
    shifts = lax.broadcasted_iota(jnp.int32, (8, 128), 0)

    def add_tile(t, carry):
        row = row_ref[0, t]
        col = col_ref[0, t]
        slot = col * dests + row
        seen = count[slot]
        count[slot] = seen + 1
        full = seen >= EXACT
        spill[0] = jnp.where(full, slot, spill[0])
        to_col = jnp.where(full, sources, col)
        to_row = jnp.where(full, 0, row)
        total = None
        for i in range(8):
            flags = []
            for w in (2 * i, 2 * i + 1):
                word = jnp.broadcast_to(bits_ref[t, w : w + 1, :], (8, 128))
                flags.append((jnp.right_shift(word, shifts) & 1).astype(F32))
            pair = flags[0] + flags[1]
            total = pair if total is None else total + pair
            at_ref[to_col, to_row, 16 * i : 16 * i + 16, :] += jnp.concatenate(flags, 0).astype(BF)
        deg8[row] += total
        return carry

    lax.fori_loop(0, tiles, add_tile, 0, unroll=2)

    @pl.when(spill[0] >= 0)
    def _():
        slot = spill[0]
        col = lax.div(slot, dests)
        row = lax.rem(slot, dests)
        whole = at_ref[col, row].astype(F32) + at_ref[sources, 0].astype(F32)
        at_ref[col, row] = whole.astype(BF)

    for r in range(dests):
        deg_ref[:, r * 128 : (r + 1) * 128] = jnp.sum(deg8[r], axis=0, keepdims=True)


def build(rows, cols, bits, sources, dests):
    assert bits.shape[0] <= 2 * EXACT
    smem = pl.BlockSpec(memory_space=pltpu.SMEM)
    vmem = pl.BlockSpec(memory_space=pltpu.VMEM)
    return pl.pallas_call(
        build_kernel,
        out_shape=(
            in_hbm((sources + 1, dests, 128, 128), BF),
            jax.ShapeDtypeStruct((1, dests * 128), F32),
        ),
        in_specs=[smem, smem, vmem],
        out_specs=(vmem, vmem),
        scratch_shapes=[
            pltpu.VMEM((dests, 8, 128), F32),
            pltpu.SMEM((sources * dests,), jnp.int32),
            pltpu.SMEM((1,), jnp.int32),
        ],
        compiler_params=params(24),
        cost_estimate=cost(0, 30 << 20),
        name="build",
    )(rows, cols, bits)


def forward_kernel(place_ref, xt_ref, at_ref, out_ref, joined):
    @pl.when(pl.program_id(0) == 0)
    def _():
        for n in range(xt_ref.shape[0]):
            rows = xt_ref.shape[2]
            joined[:, n * rows : (n + 1) * rows] = xt_ref[n]

    blocks = [
        jnp.concatenate([at_ref[k, r] for r in range(at_ref.shape[1])], axis=1)
        for k in range(at_ref.shape[0])
    ]
    part = jnp.dot(joined[...], jnp.concatenate(blocks, axis=0), preferred_element_type=F32)
    out_ref[0] = part.astype(out_ref.dtype)


def forward(place, xt, at, kind):
    nodes, width, rows = xt.shape
    sources = at.shape[0] - 1
    per = rows // 128

    def chunk(j, place):
        return (0, 2 * lax.rem(place[0] + j, 4) + place[1], 0, 0)

    return pl.pallas_call(
        forward_kernel,
        out_shape=jax.ShapeDtypeStruct((4, width, rows), kind),
        grid_spec=pltpu.PrefetchScalarGridSpec(
            num_scalar_prefetch=1,
            grid=(4,),
            in_specs=[
                pl.BlockSpec((nodes, width, rows), lambda j, *_: (0, 0, 0)),
                pl.BlockSpec((sources, per, 128, 128), chunk),
            ],
            out_specs=pl.BlockSpec((1, width, rows), lambda j, *_: (j, 0, 0)),
            scratch_shapes=[pltpu.VMEM((width, nodes * rows), BF)],
        ),
        compiler_params=params(50),
        cost_estimate=cost(8 * nodes * rows * rows * width, 10 << 20),
        name="forward",
    )(place, xt, at)


def backward_kernel(place_ref, *refs):
    parts, at_ref, out_ref, grads = refs[:8], refs[8], refs[9], refs[10]
    rows = parts[0].shape[0]

    @pl.when(pl.program_id(0) == 0)
    def _():
        for k in range(4):
            chunk = 2 * lax.rem(place_ref[0] + 4 - k, 4)
            own = pl.multiple_of((chunk + place_ref[1]) * rows, rows)
            other = pl.multiple_of((chunk + 1 - place_ref[1]) * rows, rows)
            grads[pl.ds(own, rows), :] = parts[k][...]
            grads[pl.ds(other, rows), :] = parts[4 + k][...]

    for k in range(at_ref.shape[0]):
        block = jnp.concatenate([at_ref[k, r] for r in range(at_ref.shape[1])], axis=1)
        got = jnp.dot(block, grads[...], preferred_element_type=F32)
        out_ref[k * 128 : (k + 1) * 128, :] = got.astype(BF)


def backward(place, parts, at):
    sources, dests = at.shape[0] - 1, at.shape[1]
    rows, width = parts[0].shape
    per = 8
    return pl.pallas_call(
        backward_kernel,
        out_shape=in_hbm((sources * 128, width), BF),
        grid_spec=pltpu.PrefetchScalarGridSpec(
            num_scalar_prefetch=1,
            grid=(sources // per,),
            in_specs=[pl.BlockSpec((rows, width), lambda i, *_: (0, 0))] * 8
            + [pl.BlockSpec((per, dests, 128, 128), lambda i, *_: (i, 0, 0, 0))],
            out_specs=pl.BlockSpec((per * 128, width), lambda i, *_: (i, 0)),
            scratch_shapes=[pltpu.VMEM((dests * 128, width), BF)],
        ),
        compiler_params=params(50),
        cost_estimate=cost(2 * sources * 128 * dests * 128 * width, 20 << 20),
        name="backward",
    )(place, *parts, at)


def dot_on(a, b, da, db):
    return lax.dot_general(a, b, (((da,), (db,)), ((), ())), preferred_element_type=F32)


def middle_kernel(
    keep_ref, taken_ref, r1_ref, r2_ref, r3_ref, deg_ref, x_ref, ws_ref, wn_ref, bias_ref, cot_ref,
    out_ref, pre_ref, mean_ref, grad_ref,
):
    degree = jnp.maximum(deg_ref[...], 1.0)
    summed = keep_ref[0] + taken_ref[0].astype(F32) + r1_ref[...].astype(F32)
    summed += r2_ref[...].astype(F32) + r3_ref[...].astype(F32)
    mean_t = (summed / degree).astype(BF)
    mean_ref[...] = mean_t
    preact = (
        jnp.dot(x_ref[...], ws_ref[...], preferred_element_type=F32)
        + dot_on(mean_t, wn_ref[...], 0, 0)
        + bias_ref[...]
    )
    sig = 1.0 / (1.0 + jnp.exp(-preact))
    out_ref[...] = (preact * sig).astype(BF)
    pre_grad = (cot_ref[...].astype(F32) * sig * (1.0 + preact * (1.0 - sig))).astype(BF)
    pre_ref[...] = pre_grad
    grad_t = dot_on(wn_ref[...], pre_grad, 1, 1) / degree
    grad_ref[...] = grad_t.T.astype(BF)


def middle(keep, taken, got, deg, x, ws, wn, bias, cot):
    n = x.shape[0]
    shape = jax.ShapeDtypeStruct((n, n), BF)
    whole = pl.BlockSpec((n, n), lambda i: (0, 0))
    first = pl.BlockSpec((1, n, n), lambda i: (0, 0, 0))
    return pl.pallas_call(
        middle_kernel,
        out_shape=(shape, shape, shape, shape),
        grid=(1,),
        in_specs=[first, first, whole, whole, whole]
        + [pl.BlockSpec(deg.shape, lambda i: (0, 0)), whole, whole, whole]
        + [pl.BlockSpec((1, n), lambda i: (0, 0)), whole],
        out_specs=(whole, whole, whole, whole),
        compiler_params=params(16),
        cost_estimate=cost(6 * n * n * n, 2 << 20, n * n),
        name="middle",
    )(keep, taken, *got, deg, x, ws, wn, bias, cot)


def weights_kernel(x_ref, pre_ref, mean_ref, ws_ref, part_ref, self_ref):
    pre_grad = pre_ref[...]
    self_grad = dot_on(x_ref[...], pre_grad, 0, 0)
    neigh_grad = jnp.dot(mean_ref[...], pre_grad, preferred_element_type=F32)
    bias_grad = jnp.sum(pre_grad.astype(F32), axis=0, keepdims=True)
    first = lax.broadcasted_iota(jnp.int32, (8, 1), 0) == 0
    bias_rows = jnp.where(first, bias_grad, 0.0)
    for c in range(16):
        grad = self_grad if c < 8 else neigh_grad
        part_ref[c, 0:32, :] = grad[(c % 8) * 32 : (c % 8) * 32 + 32, :]
        part_ref[c, 32:40, :] = bias_rows
    self_ref[...] = dot_on(pre_grad, ws_ref[...], 1, 1)


def weights(x, pre_grad, mean_t, ws):
    n = x.shape[0]
    return pl.pallas_call(
        weights_kernel,
        out_shape=(
            in_hbm((16, 40, n), F32),
            jax.ShapeDtypeStruct((n, n), F32),
        ),
        compiler_params=params(16),
        cost_estimate=cost(6 * n * n * n, 2 << 20),
        name="weights",
    )(x, pre_grad, mean_t, ws)


def finish_kernel(parts_ref, self_ref, out_ref):
    total = self_ref[...]
    for k in range(parts_ref.shape[0]):
        total += parts_ref[k].astype(F32)
    out_ref[...] = total.astype(BF)


def finish(parts, self_part):
    return pl.pallas_call(
        finish_kernel,
        out_shape=jax.ShapeDtypeStruct(self_part.shape, BF),
        compiler_params=params(16),
        cost_estimate=cost(1 << 20, 2 << 20),
        name="finish",
    )(parts, self_part)


def assemble_kernel(spot_ref, *refs):
    planes, outs = refs[:4], refs[4:]
    rows = 2 * outs[0].shape[0] // 16
    for kx in range(4):
        x = lax.rem(spot_ref[0] + 4 - kx, 4)
        for kz in range(4):
            z = lax.rem(spot_ref[1] + 4 - kz, 4)
            place = pl.multiple_of((4 * lax.rem(x, 2) + z) * rows, rows)
            for half in range(2):

                @pl.when(lax.div(x, 2) == half)
                def _():
                    outs[half][pl.ds(place, rows), :] = planes[kx][kz, 0:rows, :]


def assemble(spot, planes):
    width = planes[0].shape[2]
    shape = jax.ShapeDtypeStruct((width, width), F32)
    vmem = pl.BlockSpec(memory_space=pltpu.VMEM)
    return pl.pallas_call(
        assemble_kernel,
        out_shape=(shape, shape),
        in_specs=[pl.BlockSpec(memory_space=pltpu.SMEM)] + [vmem] * 4,
        out_specs=(vmem, vmem),
        compiler_params=params(16),
        cost_estimate=cost(0, 2 << 20),
        name="assemble",
    )(spot, *planes)


def swap(x, axis):
    return lax.all_to_all(x, axis, 0, 0, tiled=True)


def along_y(step):
    return [(2 * y + c, 2 * ((y + step) % 4) + c) for y in range(4) for c in range(2)]


def send_node(x, dx, dz):
    moves = [
        (4 * i + j, 4 * ((i + dx) % 4) + (j + dz) % 4) for i in range(4) for j in range(4)
    ]
    return lax.ppermute(x, "nodes", moves)


PARTNER = [(i, i ^ 1) for i in range(8)]


def send_y(x, step):
    return lax.ppermute(x, "cols", along_y(step))


def send_core(x):
    return lax.ppermute(x, "cols", PARTNER)


def shards(node_feats, tile_row, tile_col, tile_bits, w_self, w_neigh, bias, cotangent):
    nodes = lax.axis_size("nodes")
    cols = lax.axis_size("cols")
    rows_dev, width = node_feats.shape
    me = lax.axis_index("cols")
    y, core = me // 2, me % 2
    mine = jnp.stack([y, core]).astype(jnp.int32)
    theirs = jnp.stack([y, 1 - core]).astype(jnp.int32)
    node = lax.axis_index("nodes")
    spot = jnp.stack([node // 4, node % 4]).astype(jnp.int32)

    ready = prepare(node_feats, nodes)
    tile_row, tile_col, ready = lax.optimization_barrier((tile_row, tile_col, ready))
    xt_all = swap(ready, "nodes")
    at, degree = build(
        tile_row, tile_col, tile_bits[0], nodes * rows_dev // 128, cols * rows_dev // 128
    )
    degree = degree + send_core(degree)
    degree = degree + send_y(degree, 1) + send_y(degree, 2) + send_y(degree, 3)
    degree = lax.dynamic_slice_in_dim(degree, me * rows_dev, rows_dev, 1)
    xt_all, degree, mine, theirs = lax.optimization_barrier((xt_all, degree, mine, theirs))

    give = forward(theirs, xt_all, at, BF)
    taken = send_core(give)
    keep = forward(mine, xt_all, at, F32)
    both = (keep[1:] + taken[1:].astype(F32)).astype(BF)
    got = [send_y(both[k - 1], k) for k in (1, 2, 3)]
    layer_out, pre_grad, mean_t, mean_grad = middle(
        keep, taken, got, degree, node_feats, w_self, w_neigh, bias.reshape(1, -1), cotangent
    )
    same_core = [mean_grad] + [send_y(mean_grad, k) for k in (1, 2, 3)]
    other_core = [send_core(g) for g in same_core]

    part, self_part = weights(node_feats, pre_grad, mean_t, w_self)
    part = jnp.sum(swap(part, "nodes"), axis=0)

    src = backward(mine, same_core + other_core, at)
    src, part = lax.optimization_barrier((src, part))
    parts = swap(src.reshape(nodes, rows_dev, width), "nodes")

    part = part + send_core(part)
    part = part + send_y(part, 1) + send_y(part, 2) + send_y(part, 3)
    line = jnp.stack([part] + [send_node(part, 0, k) for k in (1, 2, 3)])
    plane = [line] + [send_node(line, k, 0) for k in (1, 2, 3)]
    self_grad, neigh_grad = assemble(spot, plane)
    bias_grad = part[32]

    feat_grad = finish(parts, self_part)
    return (layer_out, feat_grad, self_grad, neigh_grad, bias_grad)


def solution(mesh):
    return jax.shard_map(
        shards,
        mesh=mesh,
        in_specs=(
            P(("nodes", "cols"), None),
            P("nodes", "cols"),
            P("nodes", "cols"),
            P("nodes", "cols", None, None),
            P(),
            P(),
            P(),
            P(("nodes", "cols"), None),
        ),
        out_specs=(P(("nodes", "cols"), None), P(("nodes", "cols"), None), P(), P(), P()),
        check_vma=False,
    )
```

time: 183 us -> 140 us (0.77)
  blocking collectives: 19.2 us -> 0 us
  Pallas kernels: 57.9 us -> 44.2 us
  starting transfers between devices: 33.2 us -> 44.5 us
  waiting for transfers between devices: 54.1 us -> 45.1 us
  local copies, waits for them, and re-layouts: 11.8 us -> 3.34 us
  other arithmetic: 4.42 us -> 0.33 us
    all_to_all x5 -> x3, waiting for transfers between devices: 40.5 us -> 4.2 us  [swap(): return lax.all_to_all(x, axis, 0, 0, tiled=True)]
    ppermute x8 -> x25, waiting for transfers between devices: 13.6 us -> 40.9 us  [the longest x6 18.8 us: send_node(): return lax.ppermute(x, 'nodes', moves)]
    all_to_all x2 -> x0, blocking collectives: 19.2 us -> none  [swap(): return lax.all_to_all(x, axis, 0, 0, tiled=True)]
    ppermute x8 -> x25, starting transfers between devices: 10.8 us -> 27.9 us  [the longest x12 16.9 us: send_y(): return lax.ppermute(x, 'cols', along_y(step))]
    pallas_call x5 -> x8, Pallas kernels: 55.4 us -> 43.3 us  [the longest x1 14.6 us: build(): pl.pallas_call(build_kernel, out_shape=(in_hbm((sources + 1, dests, 128,...]
    all_to_all x5 -> x3, starting transfers between devices: 22.4 us -> 16.7 us  [swap(): return lax.all_to_all(x, axis, 0, 0, tiled=True)]
    broadcast_in_dim x5 -> x0, local copies, waits for them, and re-layouts: 3.08 us -> none  [the longest x4 3.07 us: spread(): return swap(jnp.broadcast_to(x[None], (count, *x.shape)), axis)]
    another operation x3, other arithmetic: 2.94 us -> 0.16 us  [the longest x1 0.08 us: shards(): mine = jnp.stack([y, core]).astype(jnp.int32)]
  transfers between devices with their start and end apart: 13 -> 28, of which waited for: 7 -> 18; matrix products, arithmetic and copies ran while one was open for 5% -> 1% of each run, Pallas kernels for 20% -> 24%
where the time goes in v2:
time: 140 us; the launch traced here: 138 us
  waiting for transfers between devices  45.1 us (32%)
  starting transfers between devices  44.5 us (32%)
  Pallas kernels  44.2 us (32%)
  local copies, waits for them, and re-layouts  3.34 us (2%)
    ppermute x6, waiting for transfers between devices, send_node(): return lax.ppermute(x, 'nodes', moves)  18.8 us
    ppermute x12, waiting for transfers between devices, send_y(): return lax.ppermute(x, 'cols', along_y(step))  18.4 us
    ppermute x12, starting transfers between devices, send_y(): return lax.ppermute(x, 'cols', along_y(step))  16.9 us
    all_to_all x3, starting transfers between devices, swap(): return lax.all_to_all(x, axis, 0, 0, tiled=True)  16.7 us
    pallas_call x1, Pallas kernels, build(): pl.pallas_call(build_kernel, out_shape=(in_hbm((sources + 1, dests, 128,...  14.6 us
    pallas_call x2, Pallas kernels, forward(): pl.pallas_call(forward_kernel, out_shape=jax.ShapeDtypeStruct((4, width,...  12.7 us
    pallas_call x1, Pallas kernels, backward(): pl.pallas_call(backward_kernel, out_shape=in_hbm((sources * 128, width),...  10.3 us
    ppermute x6, starting transfers between devices, send_node(): return lax.ppermute(x, 'nodes', moves)  10.1 us
  transfers between devices with their start and end apart: 28, of which 18 were waited for; matrix products, arithmetic and copies ran while one was open for 1% of the time, Pallas kernels for 24%

profile of v2, /device:TPU:0, one launch (start us, length us, event | category | flops | bytes accessed | tf_op | source)
XLA Modules:
  0.0 138.3 jit_solution(15625583935627876896)
XLA Ops:
  1.5 2.0 %prepare.1 = bf16[16,256,256]{2,1,0:T(8,128)(2,1)} custom-call(bf16[256,256]{1,0:T(8,128)(2,1)S(1)} %copy-done.1), custom_call_target="tpu_custom_call" | custom-call | bytes 2097152 | tf_op jit(solution)/shard_map/prepare/pallas_call | solution.py:37
  3.5 8.1 %all-to-all-start = ((bf16[16,256,256]{2,1,0:T(8,128)(2,1)}), bf16[16,256,256]{2,1,0:T(8,128)(2,1)S(1)}, u32[]{:S(2)}, u32[]{:S(2)}) async-start(bf16[16,256,256]{2,1,0:T(8,128)(2,1)} %prepare.1), calls=%async_computation | async-start | bytes 4194304 | tf_op jit(solution)/shard_map/all_to_all | solution.py:330
  11.6 1.8 %copy-done = s32[1,352,16,128]{3,2,1,0:T(8,128)S(1)} copy-done((s32[1,352,16,128]{3,2,1,0:T(8,128)S(1)}, s32[1,352,16,128]{3,2,1,0:T(8,128)}, u32[]{:S(2)}) %copy-start) | copy-done | bytes 2883608
  13.5 14.6 %build.1 = (bf16[33,16,128,128]{3,2,1,0:T(8,128)(2,1)}, f32[1,2048]{1,0:T(1,128)S(1)}) custom-call(s32[1,352]{1,0:T(1,128)S(1)} %copy-done.6, s32[1,352]{1,0:T(1,128)S(1)} %copy-done.7, s32[352,16,128]{2,1,0:T(8,128)S(1)} %bitcast.19), custom_call_target="tpu_custom_call" | custom-call | bytes 31457280 | tf_op jit(solution)/shard_map/build/pallas_call | solution.py:108
  29.2 3.1 %collective-permute-start.3 = (f32[1,2048]{1,0:T(1,128)S(1)}, f32[1,2048]{1,0:T(1,128)S(1)}, u32[]{:S(2)}, u32[]{:S(2)}) collective-permute-start(f32[1,2048]{1,0:T(1,128)S(1)} %add.39), channel_id=1, source_target_pairs={{0,6},{1,7},{2,0},{3,1},{4,2},{5,3},{6,4},{7,5},{8,14},{9,15},{10,... | collective-permute-start | bytes 24584 | tf_op jit(solution)/shard_map/ppermute | solution.py:348
  34.0 3.5 %collective-permute-done.2 = f32[1,2048]{1,0:T(1,128)S(1)} collective-permute-done((f32[1,2048]{1,0:T(1,128)S(1)}, f32[1,2048]{1,0:T(1,128)S(1)}, u32[]{:S(2)}, u32[]{:S(2)}) %collective-permute-start.2) | collective-permute-done | bytes 8224 | tf_op jit(solution)/shard_map/ppermute | solution.py:348
  37.8 4.2 %all-to-all-done.xt_ref = bf16[16,256,256]{2,1,0:T(8,128)(2,1)S(1)} async-done(((bf16[16,256,256]{2,1,0:T(8,128)(2,1)}), bf16[16,256,256]{2,1,0:T(8,128)(2,1)S(1)}, u32[]{:S(2)}, u32[]{:S(2)}) %all-to-all-start) | async-done | bytes 2097184 | tf_op jit(solution)/shard_map/all_to_all | solution.py:330
  42.0 6.4 %forward.3 = bf16[4,256,256]{2,1,0:T(8,128)(2,1)S(1)} custom-call(s32[2]{0:T(128)S(1)} %get-tuple-element.31.place_ref, bf16[16,256,256]{2,1,0:T(8,128)(2,1)S(1)} %all-to-all-done.xt_ref, bf16[33,16,128,128]{3,2,1,0:T(8,128)(2,1)} %get-tuple-element.30.at_ref.refs_8_), custom_call_target="tpu_custom_call" | custom-call | flops 2147483648 | bytes 10485760 | tf_op jit(solution)/shard_map/forward/pallas_call | solution.py:150
  48.5 6.4 %forward.2.keep_ref = f32[4,256,256]{2,1,0:T(8,128)S(1)} custom-call(s32[2]{0:T(128)S(1)} %get-tuple-element.28.place_ref, bf16[16,256,256]{2,1,0:T(8,128)(2,1)S(1)} %all-to-all-done.xt_ref, bf16[33,16,128,128]{3,2,1,0:T(8,128)(2,1)} %get-tuple-element.30.at_ref.refs_8_), custom_call_target="tpu_custom_call" | custom-call | flops 2147483648 | bytes 10485760 | tf_op jit(solution)/shard_map/forward/pallas_call | solution.py:150
  55.0 3.1 %collective-permute-start.7 = (bf16[256,256]{1,0:T(8,128)(2,1)S(1)}, bf16[256,256]{1,0:T(8,128)(2,1)S(1)}, u32[]{:S(2)}, u32[]{:S(2)}) collective-permute-start(bf16[256,256]{1,0:T(8,128)(2,1)S(1)} %get-tuple-element.43), channel_id=1, source_target_pairs={{0,6},{1,7},{2,0},{3,1},{4,2},{5,3},{6,4},{7,5},{8,14},{9,15},{10,... | collective-permute-start | bytes 393224 | tf_op jit(solution)/shard_map/ppermute | solution.py:348
  59.7 4.6 %collective-permute-done.7.r3_ref = bf16[256,256]{1,0:T(8,128)(2,1)S(1)} collective-permute-done((bf16[256,256]{1,0:T(8,128)(2,1)S(1)}, bf16[256,256]{1,0:T(8,128)(2,1)S(1)}, u32[]{:S(2)}, u32[]{:S(2)}) %collective-permute-start.7) | collective-permute-done | bytes 131104 | tf_op jit(solution)/shard_map/ppermute | solution.py:348
  66.0 2.1 %collective-permute-done.5.r1_ref = bf16[256,256]{1,0:T(8,128)(2,1)S(1)} collective-permute-done((bf16[256,256]{1,0:T(8,128)(2,1)S(1)}, bf16[256,256]{1,0:T(8,128)(2,1)S(1)}, u32[]{:S(2)}, u32[]{:S(2)}) %collective-permute-start.5) | collective-permute-done | bytes 131104 | tf_op jit(solution)/shard_map/ppermute | solution.py:348
  72.3 3.6 %all-to-all-start.1 = ((f32[16,40,256]{2,1,0:T(8,128)}), f32[16,40,256]{2,1,0:T(8,128)S(1)}, u32[]{:S(2)}, u32[]{:S(2)}) async-start(f32[16,40,256]{2,1,0:T(8,128)} %get-tuple-element.37), calls=%async_computation.1 | async-start | bytes 1310720 | tf_op jit(solution)/shard_map/all_to_all | solution.py:330
  80.3 10.3 %backward.1 = bf16[4096,256]{1,0:T(8,128)(2,1)} custom-call(s32[2]{0:T(128)S(1)} %get-tuple-element.28.place_ref, bf16[256,256]{1,0:T(8,128)(2,1)S(1)} %get-tuple-element.34.refs_0_, bf16[256,256]{1,0:T(8,128)(2,1)S(1)} %collective-permute-done.8.refs_1_, bf16[256,256]{1,0:T(8,128)(2,1)S(1)} %collective-permute-done.9.refs_2_, ...), custom_call_target="tpu_custom_call" | custom-call | flops 4294967296 | bytes 20971520 | tf_op jit(solution)/shard_map/backward/pallas_call | solution.py:192
  90.6 4.9 %all-to-all-start.2 = ((bf16[16,256,256]{2,1,0:T(8,128)(2,1)}), bf16[16,256,256]{2,1,0:T(8,128)(2,1)S(1)}, u32[]{:S(2)}, u32[]{:S(2)}) async-start(bf16[16,256,256]{2,1,0:T(8,128)(2,1)} %bitcast.21), calls=%async_computation.2 | async-start | bytes 4194304 | tf_op jit(solution)/shard_map/all_to_all | solution.py:330
  96.8 2.7 %collective-permute-start.18 = (f32[40,256]{1,0:T(8,128)S(1)}, f32[40,256]{1,0:T(8,128)S(1)}, u32[]{:S(2)}, u32[]{:S(2)}) collective-permute-start(f32[40,256]{1,0:T(8,128)S(1)} %add.47), channel_id=1, source_target_pairs={{0,6},{1,7},{2,0},{3,1},{4,2},{5,3},{6,4},{7,5},{8,14},{9,15},{10,... | collective-permute-start | bytes 122888 | tf_op jit(solution)/shard_map/ppermute | solution.py:348
  102.4 2.7 %collective-permute-done.17 = f32[40,256]{1,0:T(8,128)S(1)} collective-permute-done((f32[40,256]{1,0:T(8,128)S(1)}, f32[40,256]{1,0:T(8,128)S(1)}, u32[]{:S(2)}, u32[]{:S(2)}) %collective-permute-start.17) | collective-permute-done | bytes 40992 | tf_op jit(solution)/shard_map/ppermute | solution.py:348
  106.3 3.1 %collective-permute-start.21 = (f32[40,256]{1,0:T(8,128)S(1)}, f32[40,256]{1,0:T(8,128)S(1)}, u32[]{:S(2)}, u32[]{:S(2)}) collective-permute-start(f32[40,256]{1,0:T(8,128)S(1)} %add_add_fusion), channel_id=1, source_target_pairs={{0,24},{8,0},{16,8},{24,16},{32,56},{40,32},{48,40},{56,48},{64,88... | collective-permute-start | bytes 122888 | tf_op jit(solution)/shard_map/ppermute | solution.py:341
  111.1 6.0 %collective-permute-done.21 = f32[40,256]{1,0:T(8,128)S(1)} collective-permute-done((f32[40,256]{1,0:T(8,128)S(1)}, f32[40,256]{1,0:T(8,128)S(1)}, u32[]{:S(2)}, u32[]{:S(2)}) %collective-permute-start.21) | collective-permute-done | bytes 40992 | tf_op jit(solution)/shard_map/ppermute | solution.py:341
  117.1 5.2 %collective-permute-done.19 = f32[40,256]{1,0:T(8,128)S(1)} collective-permute-done((f32[40,256]{1,0:T(8,128)S(1)}, f32[40,256]{1,0:T(8,128)S(1)}, u32[]{:S(2)}, u32[]{:S(2)}) %collective-permute-start.19) | collective-permute-done | bytes 40992 | tf_op jit(solution)/shard_map/ppermute | solution.py:341
  122.3 4.3 %collective-permute-start.24 = (f32[4,40,256]{2,1,0:T(8,128)S(1)}, f32[4,40,256]{2,1,0:T(8,128)S(1)}, u32[]{:S(2)}, u32[]{:S(2)}) collective-permute-start(f32[4,40,256]{2,1,0:T(8,128)S(1)} %pad_maximum_fusion.refs_0_), channel_id=1, source_target_pairs={{0,96},{8,104},{16,112},{24,120},{32,0},{40,8},{48,16},{56,24},{64... | collective-permute-start | bytes 491528 | tf_op jit(solution)/shard_map/ppermute | solution.py:341
  128.2 4.0 %collective-permute-done.24.refs_3_ = f32[4,40,256]{2,1,0:T(8,128)S(1)} collective-permute-done((f32[4,40,256]{2,1,0:T(8,128)S(1)}, f32[4,40,256]{2,1,0:T(8,128)S(1)}, u32[]{:S(2)}, u32[]{:S(2)}) %collective-permute-start.24) | collective-permute-done | bytes 163872 | tf_op jit(solution)/shard_map/ppermute | solution.py:341
  132.2 2.0 %collective-permute-done.23.refs_2_ = f32[4,40,256]{2,1,0:T(8,128)S(1)} collective-permute-done((f32[4,40,256]{2,1,0:T(8,128)S(1)}, f32[4,40,256]{2,1,0:T(8,128)S(1)}, u32[]{:S(2)}, u32[]{:S(2)}) %collective-permute-start.23) | collective-permute-done | bytes 163872 | tf_op jit(solution)/shard_map/ppermute | solution.py:341
  134.1 1.7 %collective-permute-done.22.refs_1_ = f32[4,40,256]{2,1,0:T(8,128)S(1)} collective-permute-done((f32[4,40,256]{2,1,0:T(8,128)S(1)}, f32[4,40,256]{2,1,0:T(8,128)S(1)}, u32[]{:S(2)}, u32[]{:S(2)}) %collective-permute-start.22) | collective-permute-done | bytes 163872 | tf_op jit(solution)/shard_map/ppermute | solution.py:341
  (70 shorter events, 27.5 us)
Async XLA Ops:
  3.5 38.5 %all-to-all-start = ((bf16[16,256,256]{2,1,0:T(8,128)(2,1)}), bf16[16,256,256]{2,1,0:T(8,128)(2,1)S(1)}, u32[]{:S(2)}, u32[]{:S(2)}) async-start(bf16[16,256,256]{2,1,0:T(8,128)(2,1)} %prepare.1), calls=%async_computation | async-start | bytes 4194304 | tf_op jit(solution)/shard_map/all_to_all | solution.py:330
  29.2 4.8 %collective-permute-start.3 = (f32[1,2048]{1,0:T(1,128)S(1)}, f32[1,2048]{1,0:T(1,128)S(1)}, u32[]{:S(2)}, u32[]{:S(2)}) collective-permute-start(f32[1,2048]{1,0:T(1,128)S(1)} %add.39), channel_id=1, source_target_pairs={{0,6},{1,7},{2,0},{3,1},{4,2},{5,3},{6,4},{7,5},{8,14},{9,15},{10,... | collective-permute-start | bytes 24584 | tf_op jit(solution)/shard_map/ppermute | solution.py:348
  32.3 5.2 %collective-permute-start.2 = (f32[1,2048]{1,0:T(1,128)S(1)}, f32[1,2048]{1,0:T(1,128)S(1)}, u32[]{:S(2)}, u32[]{:S(2)}) collective-permute-start(f32[1,2048]{1,0:T(1,128)S(1)} %add.39), channel_id=1, source_target_pairs={{0,4},{1,5},{2,6},{3,7},{4,0},{5,1},{6,2},{7,3},{8,12},{9,13},{10,... | collective-permute-start | bytes 24584 | tf_op jit(solution)/shard_map/ppermute | solution.py:348
  32.9 4.9 %collective-permute-start.1 = (f32[1,2048]{1,0:T(1,128)S(1)}, f32[1,2048]{1,0:T(1,128)S(1)}, u32[]{:S(2)}, u32[]{:S(2)}) collective-permute-start(f32[1,2048]{1,0:T(1,128)S(1)} %add.39), channel_id=1, source_target_pairs={{0,2},{1,3},{2,4},{3,5},{4,6},{5,7},{6,0},{7,1},{8,10},{9,11},{10,... | collective-permute-start | bytes 24584 | tf_op jit(solution)/shard_map/ppermute | solution.py:348
  48.4 6.5 %collective-permute-start.4 = (bf16[4,256,256]{2,1,0:T(8,128)(2,1)S(1)}, bf16[4,256,256]{2,1,0:T(8,128)(2,1)S(1)}, u32[]{:S(2)}, u32[]{:S(2)}) collective-permute-start(bf16[4,256,256]{2,1,0:T(8,128)(2,1)S(1)} %forward.3), channel_id=1, source_target_pairs={{0,1},{1,0},{2,3},{3,2},{4,5},{5,4},{6,7},{7,6},{8,9},{9,8},{10,11... | collective-permute-start | bytes 1572872 | tf_op jit(solution)/shard_map/ppermute | solution.py:352
  55.0 9.3 %collective-permute-start.7 = (bf16[256,256]{1,0:T(8,128)(2,1)S(1)}, bf16[256,256]{1,0:T(8,128)(2,1)S(1)}, u32[]{:S(2)}, u32[]{:S(2)}) collective-permute-start(bf16[256,256]{1,0:T(8,128)(2,1)S(1)} %get-tuple-element.43), channel_id=1, source_target_pairs={{0,6},{1,7},{2,0},{3,1},{4,2},{5,3},{6,4},{7,5},{8,14},{9,15},{10,... | collective-permute-start | bytes 393224 | tf_op jit(solution)/shard_map/ppermute | solution.py:348
  58.1 7.9 %collective-permute-start.6 = (bf16[256,256]{1,0:T(8,128)(2,1)S(1)}, bf16[256,256]{1,0:T(8,128)(2,1)S(1)}, u32[]{:S(2)}, u32[]{:S(2)}) collective-permute-start(bf16[256,256]{1,0:T(8,128)(2,1)S(1)} %get-tuple-element.44), channel_id=1, source_target_pairs={{0,4},{1,5},{2,6},{3,7},{4,0},{5,1},{6,2},{7,3},{8,12},{9,13},{10,... | collective-permute-start | bytes 393224 | tf_op jit(solution)/shard_map/ppermute | solution.py:348
  58.8 9.3 %collective-permute-start.5 = (bf16[256,256]{1,0:T(8,128)(2,1)S(1)}, bf16[256,256]{1,0:T(8,128)(2,1)S(1)}, u32[]{:S(2)}, u32[]{:S(2)}) collective-permute-start(bf16[256,256]{1,0:T(8,128)(2,1)S(1)} %get-tuple-element.45), channel_id=1, source_target_pairs={{0,2},{1,3},{2,4},{3,5},{4,6},{5,7},{6,0},{7,1},{8,10},{9,11},{10,... | collective-permute-start | bytes 393224 | tf_op jit(solution)/shard_map/ppermute | solution.py:348
  69.2 6.9 %collective-permute-start.10 = (bf16[256,256]{1,0:T(8,128)(2,1)S(1)}, bf16[256,256]{1,0:T(8,128)(2,1)S(1)}, u32[]{:S(2)}, u32[]{:S(2)}) collective-permute-start(bf16[256,256]{1,0:T(8,128)(2,1)S(1)} %get-tuple-element.34.refs_0_), channel_id=1, source_target_pairs={{0,6},{1,7},{2,0},{3,1},{4,2},{5,3},{6,4},{7,5},{8,14},{9,15},{10,... | collective-permute-start | bytes 393224 | tf_op jit(solution)/shard_map/ppermute | solution.py:348
  69.8 7.4 %collective-permute-start.9 = (bf16[256,256]{1,0:T(8,128)(2,1)S(1)}, bf16[256,256]{1,0:T(8,128)(2,1)S(1)}, u32[]{:S(2)}, u32[]{:S(2)}) collective-permute-start(bf16[256,256]{1,0:T(8,128)(2,1)S(1)} %get-tuple-element.34.refs_0_), channel_id=1, source_target_pairs={{0,4},{1,5},{2,6},{3,7},{4,0},{5,1},{6,2},{7,3},{8,12},{9,13},{10,... | collective-permute-start | bytes 393224 | tf_op jit(solution)/shard_map/ppermute | solution.py:348
  70.4 8.5 %collective-permute-start.8 = (bf16[256,256]{1,0:T(8,128)(2,1)S(1)}, bf16[256,256]{1,0:T(8,128)(2,1)S(1)}, u32[]{:S(2)}, u32[]{:S(2)}) collective-permute-start(bf16[256,256]{1,0:T(8,128)(2,1)S(1)} %get-tuple-element.34.refs_0_), channel_id=1, source_target_pairs={{0,2},{1,3},{2,4},{3,5},{4,6},{5,7},{6,0},{7,1},{8,10},{9,11},{10,... | collective-permute-start | bytes 393224 | tf_op jit(solution)/shard_map/ppermute | solution.py:348
  72.3 18.2 %all-to-all-start.1 = ((f32[16,40,256]{2,1,0:T(8,128)}), f32[16,40,256]{2,1,0:T(8,128)S(1)}, u32[]{:S(2)}, u32[]{:S(2)}) async-start(f32[16,40,256]{2,1,0:T(8,128)} %get-tuple-element.37), calls=%async_computation.1 | async-start | bytes 1310720 | tf_op jit(solution)/shard_map/all_to_all | solution.py:330
  75.9 3.0 %collective-permute-start.11 = (bf16[256,256]{1,0:T(8,128)(2,1)S(1)}, bf16[256,256]{1,0:T(8,128)(2,1)S(1)}, u32[]{:S(2)}, u32[]{:S(2)}) collective-permute-start(bf16[256,256]{1,0:T(8,128)(2,1)S(1)} %get-tuple-element.34.refs_0_), channel_id=1, source_target_pairs={{0,1},{1,0},{2,3},{3,2},{4,5},{5,4},{6,7},{7,6},{8,9},{9,8},{10,11... | collective-permute-start | bytes 393224 | tf_op jit(solution)/shard_map/ppermute | solution.py:352
  76.0 2.9 %collective-permute-start.14 = (bf16[256,256]{1,0:T(8,128)(2,1)S(1)}, bf16[256,256]{1,0:T(8,128)(2,1)S(1)}, u32[]{:S(2)}, u32[]{:S(2)}) collective-permute-start(bf16[256,256]{1,0:T(8,128)(2,1)S(1)} %collective-permute-done.10.refs_3_), channel_id=1, source_target_pairs={{0,1},{1,0},{2,3},{3,2},{4,5},{5,4},{6,7},{7,6},{8,9},{9,8},{10,11... | collective-permute-start | bytes 393224 | tf_op jit(solution)/shard_map/ppermute | solution.py:352
  90.6 46.8 %all-to-all-start.2 = ((bf16[16,256,256]{2,1,0:T(8,128)(2,1)}), bf16[16,256,256]{2,1,0:T(8,128)(2,1)S(1)}, u32[]{:S(2)}, u32[]{:S(2)}) async-start(bf16[16,256,256]{2,1,0:T(8,128)(2,1)} %bitcast.21), calls=%async_computation.2 | async-start | bytes 4194304 | tf_op jit(solution)/shard_map/all_to_all | solution.py:330
  96.8 5.5 %collective-permute-start.18 = (f32[40,256]{1,0:T(8,128)S(1)}, f32[40,256]{1,0:T(8,128)S(1)}, u32[]{:S(2)}, u32[]{:S(2)}) collective-permute-start(f32[40,256]{1,0:T(8,128)S(1)} %add.47), channel_id=1, source_target_pairs={{0,6},{1,7},{2,0},{3,1},{4,2},{5,3},{6,4},{7,5},{8,14},{9,15},{10,... | collective-permute-start | bytes 122888 | tf_op jit(solution)/shard_map/ppermute | solution.py:348
  99.5 5.5 %collective-permute-start.17 = (f32[40,256]{1,0:T(8,128)S(1)}, f32[40,256]{1,0:T(8,128)S(1)}, u32[]{:S(2)}, u32[]{:S(2)}) collective-permute-start(f32[40,256]{1,0:T(8,128)S(1)} %add.47), channel_id=1, source_target_pairs={{0,4},{1,5},{2,6},{3,7},{4,0},{5,1},{6,2},{7,3},{8,12},{9,13},{10,... | collective-permute-start | bytes 122888 | tf_op jit(solution)/shard_map/ppermute | solution.py:348
  101.0 5.2 %collective-permute-start.16 = (f32[40,256]{1,0:T(8,128)S(1)}, f32[40,256]{1,0:T(8,128)S(1)}, u32[]{:S(2)}, u32[]{:S(2)}) collective-permute-start(f32[40,256]{1,0:T(8,128)S(1)} %add.47), channel_id=1, source_target_pairs={{0,2},{1,3},{2,4},{3,5},{4,6},{5,7},{6,0},{7,1},{8,10},{9,11},{10,... | collective-permute-start | bytes 122888 | tf_op jit(solution)/shard_map/ppermute | solution.py:348
  106.3 10.8 %collective-permute-start.21 = (f32[40,256]{1,0:T(8,128)S(1)}, f32[40,256]{1,0:T(8,128)S(1)}, u32[]{:S(2)}, u32[]{:S(2)}) collective-permute-start(f32[40,256]{1,0:T(8,128)S(1)} %add_add_fusion), channel_id=1, source_target_pairs={{0,24},{8,0},{16,8},{24,16},{32,56},{40,32},{48,40},{56,48},{64,88... | collective-permute-start | bytes 122888 | tf_op jit(solution)/shard_map/ppermute | solution.py:341
  109.4 7.7 %collective-permute-start.20 = (f32[40,256]{1,0:T(8,128)S(1)}, f32[40,256]{1,0:T(8,128)S(1)}, u32[]{:S(2)}, u32[]{:S(2)}) collective-permute-start(f32[40,256]{1,0:T(8,128)S(1)} %add_add_fusion), channel_id=1, source_target_pairs={{0,16},{8,24},{16,0},{24,8},{32,48},{40,56},{48,32},{56,40},{64,80... | collective-permute-start | bytes 122888 | tf_op jit(solution)/shard_map/ppermute | solution.py:341
  110.2 12.0 %collective-permute-start.19 = (f32[40,256]{1,0:T(8,128)S(1)}, f32[40,256]{1,0:T(8,128)S(1)}, u32[]{:S(2)}, u32[]{:S(2)}) collective-permute-start(f32[40,256]{1,0:T(8,128)S(1)} %add_add_fusion), channel_id=1, source_target_pairs={{0,8},{8,16},{16,24},{24,0},{32,40},{40,48},{48,56},{56,32},{64,72... | collective-permute-start | bytes 122888 | tf_op jit(solution)/shard_map/ppermute | solution.py:341
  122.3 9.9 %collective-permute-start.24 = (f32[4,40,256]{2,1,0:T(8,128)S(1)}, f32[4,40,256]{2,1,0:T(8,128)S(1)}, u32[]{:S(2)}, u32[]{:S(2)}) collective-permute-start(f32[4,40,256]{2,1,0:T(8,128)S(1)} %pad_maximum_fusion.refs_0_), channel_id=1, source_target_pairs={{0,96},{8,104},{16,112},{24,120},{32,0},{40,8},{48,16},{56,24},{64... | collective-permute-start | bytes 491528 | tf_op jit(solution)/shard_map/ppermute | solution.py:341
  126.5 7.6 %collective-permute-start.23 = (f32[4,40,256]{2,1,0:T(8,128)S(1)}, f32[4,40,256]{2,1,0:T(8,128)S(1)}, u32[]{:S(2)}, u32[]{:S(2)}) collective-permute-start(f32[4,40,256]{2,1,0:T(8,128)S(1)} %pad_maximum_fusion.refs_0_), channel_id=1, source_target_pairs={{0,64},{8,72},{16,80},{24,88},{32,96},{40,104},{48,112},{56,120},{... | collective-permute-start | bytes 491528 | tf_op jit(solution)/shard_map/ppermute | solution.py:341
  126.6 9.3 %collective-permute-start.22 = (f32[4,40,256]{2,1,0:T(8,128)S(1)}, f32[4,40,256]{2,1,0:T(8,128)S(1)}, u32[]{:S(2)}, u32[]{:S(2)}) collective-permute-start(f32[4,40,256]{2,1,0:T(8,128)S(1)} %pad_maximum_fusion.refs_0_), channel_id=1, source_target_pairs={{0,32},{8,40},{16,48},{24,56},{32,64},{40,72},{48,80},{56,88},{64,... | collective-permute-start | bytes 491528 | tf_op jit(solution)/shard_map/ppermute | solution.py:341
  (13 other events, 90.5 us)

commit v3 on v2

--- a/solution.py
+++ b/solution.py
@@ -22,27 +22,16 @@
     return pl.CostEstimate(flops=flops, bytes_accessed=moved, transcendentals=transcendentals)
 
 
-def prepare_kernel(x_ref, out_ref, flipped):
-    @pl.when(pl.program_id(0) == 0)
-    def _():
-        flipped[...] = x_ref[...].T
-
-    for k in range(out_ref.shape[0]):
-        out_ref[k] = flipped[...]
-
-
-def prepare(x, copies):
-    rows, width = x.shape
-    per = 4
+def prepare_kernel(x_ref, out_ref):
+    out_ref[...] = x_ref[...].T
+
+
+def prepare(x):
     return pl.pallas_call(
         prepare_kernel,
-        out_shape=in_hbm((copies, width, rows), BF),
-        grid=(copies // per,),
-        in_specs=[pl.BlockSpec((rows, width), lambda i: (0, 0))],
-        out_specs=pl.BlockSpec((per, width, rows), lambda i: (i, 0, 0)),
-        scratch_shapes=[pltpu.VMEM((width, rows), BF)],
+        out_shape=jax.ShapeDtypeStruct(x.shape[::-1], BF),
         compiler_params=params(8),
-        cost_estimate=cost(0, 2 << 20),
+        cost_estimate=cost(0, 1 << 18),
         name="prepare",
     )(x)
 
@@ -108,7 +97,7 @@
     return pl.pallas_call(
         build_kernel,
         out_shape=(
-            in_hbm((sources + 1, dests, 128, 128), BF),
+            jax.ShapeDtypeStruct((sources + 1, dests, 128, 128), BF),
             jax.ShapeDtypeStruct((1, dests * 128), F32),
         ),
         in_specs=[smem, smem, vmem],
@@ -124,12 +113,17 @@
     )(rows, cols, bits)
 
 
-def forward_kernel(place_ref, xt_ref, at_ref, out_ref, joined):
+def forward_kernel(place_ref, *refs):
+    planes, at_ref, out_ref, joined = refs[:4], refs[4], refs[5], refs[6]
+    rows = planes[0].shape[2]
+
     @pl.when(pl.program_id(0) == 0)
     def _():
-        for n in range(xt_ref.shape[0]):
-            rows = xt_ref.shape[2]
-            joined[:, n * rows : (n + 1) * rows] = xt_ref[n]
+        for kx in range(4):
+            x = lax.rem(place_ref[2] + 4 - kx, 4)
+            for kz in range(4):
+                n = 4 * x + lax.rem(place_ref[3] + 4 - kz, 4)
+                joined[:, pl.ds(pl.multiple_of(n * rows, rows), rows)] = planes[kz][kx]
 
     blocks = [
         jnp.concatenate([at_ref[k, r] for r in range(at_ref.shape[1])], axis=1)
@@ -139,8 +133,8 @@
     out_ref[0] = part.astype(out_ref.dtype)
 
 
-def forward(place, xt, at, kind):
-    nodes, width, rows = xt.shape
+def forward(place, planes, at, kind):
+    lines, width, rows = planes[0].shape
     sources = at.shape[0] - 1
     per = rows // 128
 
@@ -153,17 +147,15 @@
         grid_spec=pltpu.PrefetchScalarGridSpec(
             num_scalar_prefetch=1,
             grid=(4,),
-            in_specs=[
-                pl.BlockSpec((nodes, width, rows), lambda j, *_: (0, 0, 0)),
-                pl.BlockSpec((sources, per, 128, 128), chunk),
-            ],
+            in_specs=[pl.BlockSpec((lines, width, rows), lambda j, *_: (0, 0, 0))] * 4
+            + [pl.BlockSpec((sources, per, 128, 128), chunk)],
             out_specs=pl.BlockSpec((1, width, rows), lambda j, *_: (j, 0, 0)),
-            scratch_shapes=[pltpu.VMEM((width, nodes * rows), BF)],
+            scratch_shapes=[pltpu.VMEM((width, sources * 128), BF)],
         ),
-        compiler_params=params(50),
-        cost_estimate=cost(8 * nodes * rows * rows * width, 10 << 20),
+        compiler_params=params(20),
+        cost_estimate=cost(8 * sources * 128 * rows * width, 10 << 20),
         name="forward",
-    )(place, xt, at)
+    )(place, *planes, at)
 
 
 def backward_kernel(place_ref, *refs):
@@ -200,7 +192,7 @@
             out_specs=pl.BlockSpec((per * 128, width), lambda i, *_: (i, 0)),
             scratch_shapes=[pltpu.VMEM((dests * 128, width), BF)],
         ),
-        compiler_params=params(50),
+        compiler_params=params(20),
         cost_estimate=cost(2 * sources * 128 * dests * 128 * width, 20 << 20),
         name="backward",
     )(place, *parts, at)
@@ -211,7 +203,7 @@
 
 
 def middle_kernel(
-    keep_ref, taken_ref, r1_ref, r2_ref, r3_ref, deg_ref, x_ref, ws_ref, wn_ref, bias_ref, cot_ref,
+    place_ref, keep_ref, taken_ref, r1_ref, r2_ref, r3_ref, deg_ref, x_ref, ws_ref, wn_ref, bias_ref, cot_ref,
     out_ref, pre_ref, mean_ref, grad_ref,
 ):
     degree = jnp.maximum(deg_ref[...], 1.0)
@@ -232,51 +224,63 @@
     grad_ref[...] = grad_t.T.astype(BF)
 
 
-def middle(keep, taken, got, deg, x, ws, wn, bias, cot):
+def middle(place, keep, taken, got, deg, x, ws, wn, bias, cot):
     n = x.shape[0]
     shape = jax.ShapeDtypeStruct((n, n), BF)
-    whole = pl.BlockSpec((n, n), lambda i: (0, 0))
-    first = pl.BlockSpec((1, n, n), lambda i: (0, 0, 0))
+    whole = pl.BlockSpec((n, n), lambda i, *_: (0, 0))
+    first = pl.BlockSpec((1, n, n), lambda i, *_: (0, 0, 0))
     return pl.pallas_call(
         middle_kernel,
         out_shape=(shape, shape, shape, shape),
-        grid=(1,),
-        in_specs=[first, first, whole, whole, whole]
-        + [pl.BlockSpec(deg.shape, lambda i: (0, 0)), whole, whole, whole]
-        + [pl.BlockSpec((1, n), lambda i: (0, 0)), whole],
-        out_specs=(whole, whole, whole, whole),
+        grid_spec=pltpu.PrefetchScalarGridSpec(
+            num_scalar_prefetch=1,
+            grid=(1,),
+            in_specs=[first, first, whole, whole, whole]
+            + [pl.BlockSpec((1, n), lambda i, place: (0, 2 * place[0] + place[1]))]
+            + [whole, whole, whole, pl.BlockSpec((1, n), lambda i, *_: (0, 0)), whole],
+            out_specs=(whole, whole, whole, whole),
+        ),
         compiler_params=params(16),
         cost_estimate=cost(6 * n * n * n, 2 << 20, n * n),
         name="middle",
-    )(keep, taken, *got, deg, x, ws, wn, bias, cot)
-
-
-def weights_kernel(x_ref, pre_ref, mean_ref, ws_ref, part_ref, self_ref):
+    )(place, keep, taken, *got, deg, x, ws, wn, bias, cot)
+
+
+def weights_kernel(place_ref, x_ref, pre_ref, mean_ref, ws_ref, keep_ref, give_ref, self_ref):
+    n = x_ref.shape[0]
     pre_grad = pre_ref[...]
-    self_grad = dot_on(x_ref[...], pre_grad, 0, 0)
-    neigh_grad = jnp.dot(mean_ref[...], pre_grad, preferred_element_type=F32)
+    grads = (
+        dot_on(x_ref[...], pre_grad, 0, 0),
+        jnp.dot(mean_ref[...], pre_grad, preferred_element_type=F32),
+    )
     bias_grad = jnp.sum(pre_grad.astype(F32), axis=0, keepdims=True)
-    first = lax.broadcasted_iota(jnp.int32, (8, 1), 0) == 0
+    first = lax.broadcasted_iota(jnp.int32, (16, 1), 0) == 0
     bias_rows = jnp.where(first, bias_grad, 0.0)
-    for c in range(16):
-        grad = self_grad if c < 8 else neigh_grad
-        part_ref[c, 0:32, :] = grad[(c % 8) * 32 : (c % 8) * 32 + 32, :]
-        part_ref[c, 32:40, :] = bias_rows
+    for core in range(2):
+
+        @pl.when(place_ref[1] == core)
+        def _():
+            keep_ref[0:n, :] = grads[core]
+            give_ref[0:n, :] = grads[1 - core]
+
+    keep_ref[n : n + 16, :] = bias_rows
+    give_ref[n : n + 16, :] = bias_rows
     self_ref[...] = dot_on(pre_grad, ws_ref[...], 1, 1)
 
 
-def weights(x, pre_grad, mean_t, ws):
+def weights(place, x, pre_grad, mean_t, ws):
     n = x.shape[0]
+    half = jax.ShapeDtypeStruct((n + 16, n), F32)
+    vmem = pl.BlockSpec(memory_space=pltpu.VMEM)
     return pl.pallas_call(
         weights_kernel,
-        out_shape=(
-            in_hbm((16, 40, n), F32),
-            jax.ShapeDtypeStruct((n, n), F32),
-        ),
+        out_shape=(half, half, jax.ShapeDtypeStruct((n, n), F32)),
+        in_specs=[pl.BlockSpec(memory_space=pltpu.SMEM)] + [vmem] * 4,
+        out_specs=(vmem, vmem, vmem),
         compiler_params=params(16),
         cost_estimate=cost(6 * n * n * n, 2 << 20),
         name="weights",
-    )(x, pre_grad, mean_t, ws)
+    )(place, x, pre_grad, mean_t, ws)
 
 
 def finish_kernel(parts_ref, self_ref, out_ref):
@@ -296,36 +300,6 @@
     )(parts, self_part)
 
 
-def assemble_kernel(spot_ref, *refs):
-    planes, outs = refs[:4], refs[4:]
-    rows = 2 * outs[0].shape[0] // 16
-    for kx in range(4):
-        x = lax.rem(spot_ref[0] + 4 - kx, 4)
-        for kz in range(4):
-            z = lax.rem(spot_ref[1] + 4 - kz, 4)
-            place = pl.multiple_of((4 * lax.rem(x, 2) + z) * rows, rows)
-            for half in range(2):
-
-                @pl.when(lax.div(x, 2) == half)
-                def _():
-                    outs[half][pl.ds(place, rows), :] = planes[kx][kz, 0:rows, :]
-
-
-def assemble(spot, planes):
-    width = planes[0].shape[2]
-    shape = jax.ShapeDtypeStruct((width, width), F32)
-    vmem = pl.BlockSpec(memory_space=pltpu.VMEM)
-    return pl.pallas_call(
-        assemble_kernel,
-        out_shape=(shape, shape),
-        in_specs=[pl.BlockSpec(memory_space=pltpu.SMEM)] + [vmem] * 4,
-        out_specs=(vmem, vmem),
-        compiler_params=params(16),
-        cost_estimate=cost(0, 2 << 20),
-        name="assemble",
-    )(spot, *planes)
-
-
 def swap(x, axis):
     return lax.all_to_all(x, axis, 0, 0, tiled=True)
 
@@ -352,52 +326,65 @@
     return lax.ppermute(x, "cols", PARTNER)
 
 
+def total(x, send):
+    x = x.astype(BF)
+    one, two, three = (send(x, k).astype(F32) for k in (1, 2, 3))
+    return (x.astype(F32) + two) + (one + three)
+
+
+def send_x(x, step):
+    return send_node(x, step, 0)
+
+
+def send_z(x, step):
+    return send_node(x, 0, step)
+
+
 def shards(node_feats, tile_row, tile_col, tile_bits, w_self, w_neigh, bias, cotangent):
     nodes = lax.axis_size("nodes")
     cols = lax.axis_size("cols")
     rows_dev, width = node_feats.shape
-    me = lax.axis_index("cols")
+    me, node = lax.axis_index("cols"), lax.axis_index("nodes")
     y, core = me // 2, me % 2
-    mine = jnp.stack([y, core]).astype(jnp.int32)
-    theirs = jnp.stack([y, 1 - core]).astype(jnp.int32)
-    node = lax.axis_index("nodes")
-    spot = jnp.stack([node // 4, node % 4]).astype(jnp.int32)
-
-    ready = prepare(node_feats, nodes)
-    tile_row, tile_col, ready = lax.optimization_barrier((tile_row, tile_col, ready))
-    xt_all = swap(ready, "nodes")
+    mine = jnp.stack([y, core, node // 4, node % 4]).astype(jnp.int32)
+    theirs = jnp.stack([y, 1 - core, node // 4, node % 4]).astype(jnp.int32)
+
+    ready = prepare(node_feats)
+    line = jnp.stack([ready] + [send_x(ready, k) for k in (1, 2, 3)])
+    tile_row, tile_col, line, mine, theirs = lax.optimization_barrier(
+        (tile_row, tile_col, line, mine, theirs)
+    )
+    planes = [line] + [send_z(line, k) for k in (1, 2, 3)]
     at, degree = build(
         tile_row, tile_col, tile_bits[0], nodes * rows_dev // 128, cols * rows_dev // 128
     )
     degree = degree + send_core(degree)
     degree = degree + send_y(degree, 1) + send_y(degree, 2) + send_y(degree, 3)
-    degree = lax.dynamic_slice_in_dim(degree, me * rows_dev, rows_dev, 1)
-    xt_all, degree, mine, theirs = lax.optimization_barrier((xt_all, degree, mine, theirs))
-
-    give = forward(theirs, xt_all, at, BF)
+    *planes, degree = lax.optimization_barrier((*planes, degree))
+
+    give = forward(theirs, planes, at, BF)
     taken = send_core(give)
-    keep = forward(mine, xt_all, at, F32)
+    keep = forward(mine, planes, at, F32)
     both = (keep[1:] + taken[1:].astype(F32)).astype(BF)
     got = [send_y(both[k - 1], k) for k in (1, 2, 3)]
     layer_out, pre_grad, mean_t, mean_grad = middle(
-        keep, taken, got, degree, node_feats, w_self, w_neigh, bias.reshape(1, -1), cotangent
+        mine, keep, taken, got, degree, node_feats, w_self, w_neigh, bias.reshape(1, -1), cotangent
     )
     same_core = [mean_grad] + [send_y(mean_grad, k) for k in (1, 2, 3)]
     other_core = [send_core(g) for g in same_core]
 
-    part, self_part = weights(node_feats, pre_grad, mean_t, w_self)
-    part = jnp.sum(swap(part, "nodes"), axis=0)
+    part, give_part, self_part = weights(mine, node_feats, pre_grad, mean_t, w_self)
+    part = total(part + send_core(give_part), send_x)
 
     src = backward(mine, same_core + other_core, at)
     src, part = lax.optimization_barrier((src, part))
     parts = swap(src.reshape(nodes, rows_dev, width), "nodes")
 
-    part = part + send_core(part)
-    part = part + send_y(part, 1) + send_y(part, 2) + send_y(part, 3)
-    line = jnp.stack([part] + [send_node(part, 0, k) for k in (1, 2, 3)])
-    plane = [line] + [send_node(line, k, 0) for k in (1, 2, 3)]
-    self_grad, neigh_grad = assemble(spot, plane)
-    bias_grad = part[32]
+    part = total(total(part, send_z), send_y)
+    other = send_core(part)
+    bias_grad = part[width]
+    self_grad = jnp.where(core == 0, part[:width], other[:width])
+    neigh_grad = jnp.where(core == 0, other[:width], part[:width])
 
     feat_grad = finish(parts, self_part)
     return (layer_out, feat_grad, self_grad, neigh_grad, bias_grad)

time: 140 us -> 140 us (level)
  waiting for transfers between devices: 45.1 us -> 67.5 us
  Pallas kernels: 44.2 us -> 27.8 us
  starting transfers between devices: 44.5 us -> 36.7 us
    ppermute x6 -> x12, waiting for transfers between devices: 18.8 us -> 36.7 us  [send_node(): return lax.ppermute(x, 'nodes', moves)]
    all_to_all x3 -> x1, starting transfers between devices: 16.7 us -> 3.74 us  [swap(): return lax.all_to_all(x, axis, 0, 0, tiled=True)]
    ppermute x12, waiting for transfers between devices: 18.4 us -> 28.7 us  [send_y(): return lax.ppermute(x, 'cols', along_y(step))]
    pallas_call x4 -> x3, Pallas kernels: 19.2 us -> 9.75 us  [the longest x1 8.65 us: build(): pl.pallas_call(build_kernel, out_shape=(jax.ShapeDtypeStruct((sources + 1...]
    ppermute x6 -> x12, starting transfers between devices: 10.1 us -> 18.5 us  [send_node(): return lax.ppermute(x, 'nodes', moves)]
    all_to_all x3 -> x1, waiting for transfers between devices: 4.2 us -> 0.01 us  [swap(): return lax.all_to_all(x, axis, 0, 0, tiled=True)]
    pallas_call x2, Pallas kernels: 12.7 us -> 8.68 us  [forward(): pl.pallas_call(forward_kernel, out_shape=jax.ShapeDtypeStruct((4, width,...]
    pallas_call x1, Pallas kernels: 10.3 us -> 6.76 us  [backward(): pl.pallas_call(backward_kernel, out_shape=in_hbm((sources * 128, width),...]
  transfers between devices with their start and end apart: 28 -> 33, of which waited for: 18 -> 20; matrix products, arithmetic and copies ran while one was open for 1% -> 1% of each run, Pallas kernels for 24% -> 14%
where the time goes in v3:
time: 140 us; the launch traced here: 139 us
  waiting for transfers between devices  67.5 us (48%)
  starting transfers between devices  36.7 us (26%)
  Pallas kernels  27.8 us (20%)
  local copies, waits for them, and re-layouts  4.7 us (3%)
    ppermute x12, waiting for transfers between devices, send_node(): return lax.ppermute(x, 'nodes', moves)  36.7 us
    ppermute x12, waiting for transfers between devices, send_y(): return lax.ppermute(x, 'cols', along_y(step))  28.7 us
    ppermute x12, starting transfers between devices, send_node(): return lax.ppermute(x, 'nodes', moves)  18.5 us
    ppermute x12, starting transfers between devices, send_y(): return lax.ppermute(x, 'cols', along_y(step))  14.1 us
    pallas_call x2, Pallas kernels, forward(): pl.pallas_call(forward_kernel, out_shape=jax.ShapeDtypeStruct((4, width,...  8.68 us
    pallas_call x1, Pallas kernels, build(): pl.pallas_call(build_kernel, out_shape=(jax.ShapeDtypeStruct((sources + 1...  8.65 us
    pallas_call x1, Pallas kernels, backward(): pl.pallas_call(backward_kernel, out_shape=in_hbm((sources * 128, width),...  6.76 us
    unnamed x18, local copies, waits for them, and re-layouts  4.11 us
  transfers between devices with their start and end apart: 33, of which 20 were waited for; matrix products, arithmetic and copies ran while one was open for 1% of the time, Pallas kernels for 14%

profile of v3, /device:TPU:0, one launch (start us, length us, event | category | flops | bytes accessed | tf_op | source)
XLA Modules:
  0.0 138.9 jit_solution(6780121039560325267)
XLA Ops:
  1.6 2.9 %collective-permute-start.2 = (bf16[256,256]{1,0:T(8,128)(2,1)S(1)}, bf16[256,256]{1,0:T(8,128)(2,1)S(1)}, u32[]{:S(2)}, u32[]{:S(2)}) collective-permute-start(bf16[256,256]{1,0:T(8,128)(2,1)S(1)} %prepare.1), channel_id=1, source_target_pairs={{0,96},{8,104},{16,112},{24,120},{32,0},{40,8},{48,16},{56,24},{64... | collective-permute-start | bytes 393224 | tf_op jit(solution)/shard_map/ppermute | solution.py:315
  6.3 3.8 %collective-permute-done.2 = bf16[256,256]{1,0:T(8,128)(2,1)S(1)} collective-permute-done((bf16[256,256]{1,0:T(8,128)(2,1)S(1)}, bf16[256,256]{1,0:T(8,128)(2,1)S(1)}, u32[]{:S(2)}, u32[]{:S(2)}) %collective-permute-start.2) | collective-permute-done | bytes 131104 | tf_op jit(solution)/shard_map/ppermute | solution.py:315
  10.1 2.3 %collective-permute-done.1 = bf16[256,256]{1,0:T(8,128)(2,1)S(1)} collective-permute-done((bf16[256,256]{1,0:T(8,128)(2,1)S(1)}, bf16[256,256]{1,0:T(8,128)(2,1)S(1)}, u32[]{:S(2)}, u32[]{:S(2)}) %collective-permute-start.1) | collective-permute-done | bytes 131104 | tf_op jit(solution)/shard_map/ppermute | solution.py:315
  13.9 4.1 %collective-permute-start.5 = (bf16[4,256,256]{2,1,0:T(8,128)(2,1)S(1)}, bf16[4,256,256]{2,1,0:T(8,128)(2,1)S(1)}, u32[]{:S(2)}, u32[]{:S(2)}) collective-permute-start(bf16[4,256,256]{2,1,0:T(8,128)(2,1)S(1)} %pad_maximum_fusion.refs_0_), channel_id=1, source_target_pairs={{0,24},{8,0},{16,8},{24,16},{32,56},{40,32},{48,40},{56,48},{64,88... | collective-permute-start | bytes 1572872 | tf_op jit(solution)/shard_map/ppermute | solution.py:315
  22.4 8.6 %build.1 = (bf16[33,16,128,128]{3,2,1,0:T(8,128)(2,1)S(1)}, f32[1,2048]{1,0:T(1,128)S(1)}) custom-call(s32[1,352]{1,0:T(1,128)S(1)} %copy-done.6, s32[1,352]{1,0:T(1,128)S(1)} %copy-done.7, s32[352,16,128]{2,1,0:T(8,128)S(1)} %bitcast.19), custom_call_target="tpu_custom_call" | custom-call | bytes 31457280 | tf_op jit(solution)/shard_map/build/pallas_call | solution.py:97
  32.3 3.1 %collective-permute-start.9 = (f32[1,2048]{1,0:T(1,128)S(1)}, f32[1,2048]{1,0:T(1,128)S(1)}, u32[]{:S(2)}, u32[]{:S(2)}) collective-permute-start(f32[1,2048]{1,0:T(1,128)S(1)} %add.57), channel_id=1, source_target_pairs={{0,6},{1,7},{2,0},{3,1},{4,2},{5,3},{6,4},{7,5},{8,14},{9,15},{10,... | collective-permute-start | bytes 24584 | tf_op jit(solution)/shard_map/ppermute | solution.py:322
  37.6 3.0 %collective-permute-done.8 = f32[1,2048]{1,0:T(1,128)S(1)} collective-permute-done((f32[1,2048]{1,0:T(1,128)S(1)}, f32[1,2048]{1,0:T(1,128)S(1)}, u32[]{:S(2)}, u32[]{:S(2)}) %collective-permute-start.8) | collective-permute-done | bytes 8224 | tf_op jit(solution)/shard_map/ppermute | solution.py:322
  43.8 4.3 %forward.3 = bf16[4,256,256]{2,1,0:T(8,128)(2,1)S(1)} custom-call(s32[4]{0:T(128)S(1)} %get-tuple-element.36.place_ref, bf16[4,256,256]{2,1,0:T(8,128)(2,1)S(1)} %pad_maximum_fusion.refs_0_, bf16[4,256,256]{2,1,0:T(8,128)(2,1)S(1)} %collective-permute-done.3.refs_1_, bf16[4,256,256]{2,1,0:T(8,128)(2,1)S(1)} %collective-permute-done.4.refs_2_, ...), custom_call_target="tpu_custom_call" | custom-call | flops 2147483648 | bytes 10485760 | tf_op jit(solution)/shard_map/forward/pallas_call | solution.py:144
  48.3 4.3 %forward.2.keep_ref = f32[4,256,256]{2,1,0:T(8,128)S(1)} custom-call(s32[4]{0:T(128)S(1)} %get-tuple-element.26.place_ref, bf16[4,256,256]{2,1,0:T(8,128)(2,1)S(1)} %pad_maximum_fusion.refs_0_, bf16[4,256,256]{2,1,0:T(8,128)(2,1)S(1)} %collective-permute-done.3.refs_1_, bf16[4,256,256]{2,1,0:T(8,128)(2,1)S(1)} %collective-permute-done.4.refs_2_, ...), custom_call_target="tpu_custom_call" | custom-call | flops 2147483648 | bytes 10485760 | tf_op jit(solution)/shard_map/forward/pallas_call | solution.py:144
  52.8 3.1 %collective-permute-start.13 = (bf16[256,256]{1,0:T(8,128)(2,1)S(1)}, bf16[256,256]{1,0:T(8,128)(2,1)S(1)}, u32[]{:S(2)}, u32[]{:S(2)}) collective-permute-start(bf16[256,256]{1,0:T(8,128)(2,1)S(1)} %get-tuple-element.49), channel_id=1, source_target_pairs={{0,6},{1,7},{2,0},{3,1},{4,2},{5,3},{6,4},{7,5},{8,14},{9,15},{10,... | collective-permute-start | bytes 393224 | tf_op jit(solution)/shard_map/ppermute | solution.py:322
  57.5 4.6 %collective-permute-done.13.r3_ref = bf16[256,256]{1,0:T(8,128)(2,1)S(1)} collective-permute-done((bf16[256,256]{1,0:T(8,128)(2,1)S(1)}, bf16[256,256]{1,0:T(8,128)(2,1)S(1)}, u32[]{:S(2)}, u32[]{:S(2)}) %collective-permute-start.13) | collective-permute-done | bytes 131104 | tf_op jit(solution)/shard_map/ppermute | solution.py:322
  63.8 2.1 %collective-permute-done.11.r1_ref = bf16[256,256]{1,0:T(8,128)(2,1)S(1)} collective-permute-done((bf16[256,256]{1,0:T(8,128)(2,1)S(1)}, bf16[256,256]{1,0:T(8,128)(2,1)S(1)}, u32[]{:S(2)}, u32[]{:S(2)}) %collective-permute-start.11) | collective-permute-done | bytes 131104 | tf_op jit(solution)/shard_map/ppermute | solution.py:322
  70.7 4.3 %collective-permute-done.16.refs_3_ = bf16[256,256]{1,0:T(8,128)(2,1)S(1)} collective-permute-done((bf16[256,256]{1,0:T(8,128)(2,1)S(1)}, bf16[256,256]{1,0:T(8,128)(2,1)S(1)}, u32[]{:S(2)}, u32[]{:S(2)}) %collective-permute-start.16) | collective-permute-done | bytes 131104 | tf_op jit(solution)/shard_map/ppermute | solution.py:322
  75.0 2.1 %collective-permute-done.15.refs_2_ = bf16[256,256]{1,0:T(8,128)(2,1)S(1)} collective-permute-done((bf16[256,256]{1,0:T(8,128)(2,1)S(1)}, bf16[256,256]{1,0:T(8,128)(2,1)S(1)}, u32[]{:S(2)}, u32[]{:S(2)}) %collective-permute-start.15) | collective-permute-done | bytes 131104 | tf_op jit(solution)/shard_map/ppermute | solution.py:322
  77.1 2.0 %collective-permute-done.14.refs_1_ = bf16[256,256]{1,0:T(8,128)(2,1)S(1)} collective-permute-done((bf16[256,256]{1,0:T(8,128)(2,1)S(1)}, bf16[256,256]{1,0:T(8,128)(2,1)S(1)}, u32[]{:S(2)}, u32[]{:S(2)}) %collective-permute-start.14) | collective-permute-done | bytes 131104 | tf_op jit(solution)/shard_map/ppermute | solution.py:322
  79.3 2.0 %collective-permute-start.23 = (bf16[272,256]{1,0:T(8,128)(2,1)S(1)}, bf16[272,256]{1,0:T(8,128)(2,1)S(1)}, u32[]{:S(2)}, u32[]{:S(2)}) collective-permute-start(bf16[272,256]{1,0:T(8,128)(2,1)S(1)} %add_convert_fusion.1), channel_id=1, source_target_pairs={{0,32},{8,40},{16,48},{24,56},{32,64},{40,72},{48,80},{56,88},{64,... | collective-permute-start | bytes 417800 | tf_op jit(solution)/shard_map/ppermute | solution.py:315
  81.7 6.8 %backward.1 = bf16[4096,256]{1,0:T(8,128)(2,1)} custom-call(s32[4]{0:T(128)S(1)} %get-tuple-element.26.place_ref, bf16[256,256]{1,0:T(8,128)(2,1)S(1)} %get-tuple-element.39.refs_0_, bf16[256,256]{1,0:T(8,128)(2,1)S(1)} %collective-permute-done.14.refs_1_, bf16[256,256]{1,0:T(8,128)(2,1)S(1)} %collective-permute-done.15.refs_2_, ...), custom_call_target="tpu_custom_call" | custom-call | flops 4294967296 | bytes 20971520 | tf_op jit(solution)/shard_map/backward/pallas_call | solution.py:184
  89.7 3.7 %all-to-all-start = ((bf16[16,256,256]{2,1,0:T(8,128)(2,1)}), bf16[16,256,256]{2,1,0:T(8,128)(2,1)S(1)}, u32[]{:S(2)}, u32[]{:S(2)}) async-start(bf16[16,256,256]{2,1,0:T(8,128)(2,1)} %bitcast.22), calls=%async_computation | async-start | bytes 4194304 | tf_op jit(solution)/shard_map/all_to_all | solution.py:304
  93.5 1.9 %collective-permute-start.26 = (bf16[272,256]{1,0:T(8,128)(2,1)S(1)}, bf16[272,256]{1,0:T(8,128)(2,1)S(1)}, u32[]{:S(2)}, u32[]{:S(2)}) collective-permute-start(bf16[272,256]{1,0:T(8,128)(2,1)S(1)} %add_add_fusion.1), channel_id=1, source_target_pairs={{0,8},{8,16},{16,24},{24,0},{32,40},{40,48},{48,56},{56,32},{64,72... | collective-permute-start | bytes 417800 | tf_op jit(solution)/shard_map/ppermute | solution.py:315
  95.4 2.7 %collective-permute-start.25 = (bf16[272,256]{1,0:T(8,128)(2,1)S(1)}, bf16[272,256]{1,0:T(8,128)(2,1)S(1)}, u32[]{:S(2)}, u32[]{:S(2)}) collective-permute-start(bf16[272,256]{1,0:T(8,128)(2,1)S(1)} %add_add_fusion.1), channel_id=1, source_target_pairs={{0,16},{8,24},{16,0},{24,8},{32,48},{40,56},{48,32},{56,40},{64,80... | collective-permute-start | bytes 417800 | tf_op jit(solution)/shard_map/ppermute | solution.py:315
  99.6 23.7 %collective-permute-done.26 = bf16[272,256]{1,0:T(8,128)(2,1)S(1)} collective-permute-done((bf16[272,256]{1,0:T(8,128)(2,1)S(1)}, bf16[272,256]{1,0:T(8,128)(2,1)S(1)}, u32[]{:S(2)}, u32[]{:S(2)}) %collective-permute-start.26) | collective-permute-done | bytes 139296 | tf_op jit(solution)/shard_map/ppermute | solution.py:315
  123.2 2.5 %collective-permute-done.25 = bf16[272,256]{1,0:T(8,128)(2,1)S(1)} collective-permute-done((bf16[272,256]{1,0:T(8,128)(2,1)S(1)}, bf16[272,256]{1,0:T(8,128)(2,1)S(1)}, u32[]{:S(2)}, u32[]{:S(2)}) %collective-permute-start.25) | collective-permute-done | bytes 139296 | tf_op jit(solution)/shard_map/ppermute | solution.py:315
  128.5 3.5 %collective-permute-done.30 = bf16[272,256]{1,0:T(8,128)(2,1)S(1)} collective-permute-done((bf16[272,256]{1,0:T(8,128)(2,1)S(1)}, bf16[272,256]{1,0:T(8,128)(2,1)S(1)}, u32[]{:S(2)}, u32[]{:S(2)}) %collective-permute-start.30) | collective-permute-done | bytes 139296 | tf_op jit(solution)/shard_map/ppermute | solution.py:322
  132.0 3.3 %collective-permute-done.29 = bf16[272,256]{1,0:T(8,128)(2,1)S(1)} collective-permute-done((bf16[272,256]{1,0:T(8,128)(2,1)S(1)}, bf16[272,256]{1,0:T(8,128)(2,1)S(1)}, u32[]{:S(2)}, u32[]{:S(2)}) %collective-permute-start.29) | collective-permute-done | bytes 139296 | tf_op jit(solution)/shard_map/ppermute | solution.py:322
  (80 shorter events, 33.2 us)
Async XLA Ops:
  1.6 8.5 %collective-permute-start.2 = (bf16[256,256]{1,0:T(8,128)(2,1)S(1)}, bf16[256,256]{1,0:T(8,128)(2,1)S(1)}, u32[]{:S(2)}, u32[]{:S(2)}) collective-permute-start(bf16[256,256]{1,0:T(8,128)(2,1)S(1)} %prepare.1), channel_id=1, source_target_pairs={{0,96},{8,104},{16,112},{24,120},{32,0},{40,8},{48,16},{56,24},{64... | collective-permute-start | bytes 393224 | tf_op jit(solution)/shard_map/ppermute | solution.py:315
  4.5 7.9 %collective-permute-start.1 = (bf16[256,256]{1,0:T(8,128)(2,1)S(1)}, bf16[256,256]{1,0:T(8,128)(2,1)S(1)}, u32[]{:S(2)}, u32[]{:S(2)}) collective-permute-start(bf16[256,256]{1,0:T(8,128)(2,1)S(1)} %prepare.1), channel_id=1, source_target_pairs={{0,64},{8,72},{16,80},{24,88},{32,96},{40,104},{48,112},{56,120},{... | collective-permute-start | bytes 393224 | tf_op jit(solution)/shard_map/ppermute | solution.py:315
  5.3 8.5 %collective-permute-start = (bf16[256,256]{1,0:T(8,128)(2,1)S(1)}, bf16[256,256]{1,0:T(8,128)(2,1)S(1)}, u32[]{:S(2)}, u32[]{:S(2)}) collective-permute-start(bf16[256,256]{1,0:T(8,128)(2,1)S(1)} %prepare.1), channel_id=1, source_target_pairs={{0,32},{8,40},{16,48},{24,56},{32,64},{40,72},{48,80},{56,88},{64,... | collective-permute-start | bytes 393224 | tf_op jit(solution)/shard_map/ppermute | solution.py:315
  13.9 28.1 %collective-permute-start.5 = (bf16[4,256,256]{2,1,0:T(8,128)(2,1)S(1)}, bf16[4,256,256]{2,1,0:T(8,128)(2,1)S(1)}, u32[]{:S(2)}, u32[]{:S(2)}) collective-permute-start(bf16[4,256,256]{2,1,0:T(8,128)(2,1)S(1)} %pad_maximum_fusion.refs_0_), channel_id=1, source_target_pairs={{0,24},{8,0},{16,8},{24,16},{32,56},{40,32},{48,40},{56,48},{64,88... | collective-permute-start | bytes 1572872 | tf_op jit(solution)/shard_map/ppermute | solution.py:315
  18.0 24.0 %collective-permute-start.4 = (bf16[4,256,256]{2,1,0:T(8,128)(2,1)S(1)}, bf16[4,256,256]{2,1,0:T(8,128)(2,1)S(1)}, u32[]{:S(2)}, u32[]{:S(2)}) collective-permute-start(bf16[4,256,256]{2,1,0:T(8,128)(2,1)S(1)} %pad_maximum_fusion.refs_0_), channel_id=1, source_target_pairs={{0,16},{8,24},{16,0},{24,8},{32,48},{40,56},{48,32},{56,40},{64,80... | collective-permute-start | bytes 1572872 | tf_op jit(solution)/shard_map/ppermute | solution.py:315
  18.0 25.8 %collective-permute-start.3 = (bf16[4,256,256]{2,1,0:T(8,128)(2,1)S(1)}, bf16[4,256,256]{2,1,0:T(8,128)(2,1)S(1)}, u32[]{:S(2)}, u32[]{:S(2)}) collective-permute-start(bf16[4,256,256]{2,1,0:T(8,128)(2,1)S(1)} %pad_maximum_fusion.refs_0_), channel_id=1, source_target_pairs={{0,8},{8,16},{16,24},{24,0},{32,40},{40,48},{48,56},{56,32},{64,72... | collective-permute-start | bytes 1572872 | tf_op jit(solution)/shard_map/ppermute | solution.py:315
  52.8 9.3 %collective-permute-start.13 = (bf16[256,256]{1,0:T(8,128)(2,1)S(1)}, bf16[256,256]{1,0:T(8,128)(2,1)S(1)}, u32[]{:S(2)}, u32[]{:S(2)}) collective-permute-start(bf16[256,256]{1,0:T(8,128)(2,1)S(1)} %get-tuple-element.49), channel_id=1, source_target_pairs={{0,6},{1,7},{2,0},{3,1},{4,2},{5,3},{6,4},{7,5},{8,14},{9,15},{10,... | collective-permute-start | bytes 393224 | tf_op jit(solution)/shard_map/ppermute | solution.py:322
  55.9 7.9 %collective-permute-start.12 = (bf16[256,256]{1,0:T(8,128)(2,1)S(1)}, bf16[256,256]{1,0:T(8,128)(2,1)S(1)}, u32[]{:S(2)}, u32[]{:S(2)}) collective-permute-start(bf16[256,256]{1,0:T(8,128)(2,1)S(1)} %get-tuple-element.50), channel_id=1, source_target_pairs={{0,4},{1,5},{2,6},{3,7},{4,0},{5,1},{6,2},{7,3},{8,12},{9,13},{10,... | collective-permute-start | bytes 393224 | tf_op jit(solution)/shard_map/ppermute | solution.py:322
  56.5 9.3 %collective-permute-start.11 = (bf16[256,256]{1,0:T(8,128)(2,1)S(1)}, bf16[256,256]{1,0:T(8,128)(2,1)S(1)}, u32[]{:S(2)}, u32[]{:S(2)}) collective-permute-start(bf16[256,256]{1,0:T(8,128)(2,1)S(1)} %get-tuple-element.51), channel_id=1, source_target_pairs={{0,2},{1,3},{2,4},{3,5},{4,6},{5,7},{6,0},{7,1},{8,10},{9,11},{10,... | collective-permute-start | bytes 393224 | tf_op jit(solution)/shard_map/ppermute | solution.py:322
  68.5 10.7 %collective-permute-start.21 = (f32[272,256]{1,0:T(8,128)S(1)}, f32[272,256]{1,0:T(8,128)S(1)}, u32[]{:S(2)}, u32[]{:S(2)}) collective-permute-start(f32[272,256]{1,0:T(8,128)S(1)} %get-tuple-element.43), channel_id=1, source_target_pairs={{0,1},{1,0},{2,3},{3,2},{4,5},{5,4},{6,7},{7,6},{8,9},{9,8},{10,11... | collective-permute-start | bytes 835592 | tf_op jit(solution)/shard_map/ppermute | solution.py:326
  68.6 6.4 %collective-permute-start.16 = (bf16[256,256]{1,0:T(8,128)(2,1)S(1)}, bf16[256,256]{1,0:T(8,128)(2,1)S(1)}, u32[]{:S(2)}, u32[]{:S(2)}) collective-permute-start(bf16[256,256]{1,0:T(8,128)(2,1)S(1)} %get-tuple-element.39.refs_0_), channel_id=1, source_target_pairs={{0,6},{1,7},{2,0},{3,1},{4,2},{5,3},{6,4},{7,5},{8,14},{9,15},{10,... | collective-permute-start | bytes 393224 | tf_op jit(solution)/shard_map/ppermute | solution.py:322
  69.3 7.8 %collective-permute-start.15 = (bf16[256,256]{1,0:T(8,128)(2,1)S(1)}, bf16[256,256]{1,0:T(8,128)(2,1)S(1)}, u32[]{:S(2)}, u32[]{:S(2)}) collective-permute-start(bf16[256,256]{1,0:T(8,128)(2,1)S(1)} %get-tuple-element.39.refs_0_), channel_id=1, source_target_pairs={{0,4},{1,5},{2,6},{3,7},{4,0},{5,1},{6,2},{7,3},{8,12},{9,13},{10,... | collective-permute-start | bytes 393224 | tf_op jit(solution)/shard_map/ppermute | solution.py:322
  69.9 9.3 %collective-permute-start.14 = (bf16[256,256]{1,0:T(8,128)(2,1)S(1)}, bf16[256,256]{1,0:T(8,128)(2,1)S(1)}, u32[]{:S(2)}, u32[]{:S(2)}) collective-permute-start(bf16[256,256]{1,0:T(8,128)(2,1)S(1)} %get-tuple-element.39.refs_0_), channel_id=1, source_target_pairs={{0,2},{1,3},{2,4},{3,5},{4,6},{5,7},{6,0},{7,1},{8,10},{9,11},{10,... | collective-permute-start | bytes 393224 | tf_op jit(solution)/shard_map/ppermute | solution.py:322
  70.7 8.6 %collective-permute-start.17 = (bf16[256,256]{1,0:T(8,128)(2,1)S(1)}, bf16[256,256]{1,0:T(8,128)(2,1)S(1)}, u32[]{:S(2)}, u32[]{:S(2)}) collective-permute-start(bf16[256,256]{1,0:T(8,128)(2,1)S(1)} %get-tuple-element.39.refs_0_), channel_id=1, source_target_pairs={{0,1},{1,0},{2,3},{3,2},{4,5},{5,4},{6,7},{7,6},{8,9},{9,8},{10,11... | collective-permute-start | bytes 393224 | tf_op jit(solution)/shard_map/ppermute | solution.py:326
  75.0 6.4 %collective-permute-start.20 = (bf16[256,256]{1,0:T(8,128)(2,1)S(1)}, bf16[256,256]{1,0:T(8,128)(2,1)S(1)}, u32[]{:S(2)}, u32[]{:S(2)}) collective-permute-start(bf16[256,256]{1,0:T(8,128)(2,1)S(1)} %collective-permute-done.16.refs_3_), channel_id=1, source_target_pairs={{0,1},{1,0},{2,3},{3,2},{4,5},{5,4},{6,7},{7,6},{8,9},{9,8},{10,11... | collective-permute-start | bytes 393224 | tf_op jit(solution)/shard_map/ppermute | solution.py:326
  79.3 9.2 %collective-permute-start.24 = (bf16[272,256]{1,0:T(8,128)(2,1)S(1)}, bf16[272,256]{1,0:T(8,128)(2,1)S(1)}, u32[]{:S(2)}, u32[]{:S(2)}) collective-permute-start(bf16[272,256]{1,0:T(8,128)(2,1)S(1)} %add_convert_fusion.1), channel_id=1, source_target_pairs={{0,96},{8,104},{16,112},{24,120},{32,0},{40,8},{48,16},{56,24},{64... | collective-permute-start | bytes 417800 | tf_op jit(solution)/shard_map/ppermute | solution.py:315
  79.3 10.3 %collective-permute-start.23 = (bf16[272,256]{1,0:T(8,128)(2,1)S(1)}, bf16[272,256]{1,0:T(8,128)(2,1)S(1)}, u32[]{:S(2)}, u32[]{:S(2)}) collective-permute-start(bf16[272,256]{1,0:T(8,128)(2,1)S(1)} %add_convert_fusion.1), channel_id=1, source_target_pairs={{0,32},{8,40},{16,48},{24,56},{32,64},{40,72},{48,80},{56,88},{64,... | collective-permute-start | bytes 417800 | tf_op jit(solution)/shard_map/ppermute | solution.py:315
  81.4 8.3 %collective-permute-start.22 = (bf16[272,256]{1,0:T(8,128)(2,1)S(1)}, bf16[272,256]{1,0:T(8,128)(2,1)S(1)}, u32[]{:S(2)}, u32[]{:S(2)}) collective-permute-start(bf16[272,256]{1,0:T(8,128)(2,1)S(1)} %add_convert_fusion.1), channel_id=1, source_target_pairs={{0,64},{8,72},{16,80},{24,88},{32,96},{40,104},{48,112},{56,120},{... | collective-permute-start | bytes 417800 | tf_op jit(solution)/shard_map/ppermute | solution.py:315
  89.7 48.2 %all-to-all-start = ((bf16[16,256,256]{2,1,0:T(8,128)(2,1)}), bf16[16,256,256]{2,1,0:T(8,128)(2,1)S(1)}, u32[]{:S(2)}, u32[]{:S(2)}) async-start(bf16[16,256,256]{2,1,0:T(8,128)(2,1)} %bitcast.22), calls=%async_computation | async-start | bytes 4194304 | tf_op jit(solution)/shard_map/all_to_all | solution.py:304
  93.5 29.7 %collective-permute-start.26 = (bf16[272,256]{1,0:T(8,128)(2,1)S(1)}, bf16[272,256]{1,0:T(8,128)(2,1)S(1)}, u32[]{:S(2)}, u32[]{:S(2)}) collective-permute-start(bf16[272,256]{1,0:T(8,128)(2,1)S(1)} %add_add_fusion.1), channel_id=1, source_target_pairs={{0,8},{8,16},{16,24},{24,0},{32,40},{40,48},{48,56},{56,32},{64,72... | collective-permute-start | bytes 417800 | tf_op jit(solution)/shard_map/ppermute | solution.py:315
  95.4 30.3 %collective-permute-start.25 = (bf16[272,256]{1,0:T(8,128)(2,1)S(1)}, bf16[272,256]{1,0:T(8,128)(2,1)S(1)}, u32[]{:S(2)}, u32[]{:S(2)}) collective-permute-start(bf16[272,256]{1,0:T(8,128)(2,1)S(1)} %add_add_fusion.1), channel_id=1, source_target_pairs={{0,16},{8,24},{16,0},{24,8},{32,48},{40,56},{48,32},{56,40},{64,80... | collective-permute-start | bytes 417800 | tf_op jit(solution)/shard_map/ppermute | solution.py:315
  98.1 27.7 %collective-permute-start.27 = (bf16[272,256]{1,0:T(8,128)(2,1)S(1)}, bf16[272,256]{1,0:T(8,128)(2,1)S(1)}, u32[]{:S(2)}, u32[]{:S(2)}) collective-permute-start(bf16[272,256]{1,0:T(8,128)(2,1)S(1)} %add_add_fusion.1), channel_id=1, source_target_pairs={{0,24},{8,0},{16,8},{24,16},{32,56},{40,32},{48,40},{56,48},{64,88... | collective-permute-start | bytes 417800 | tf_op jit(solution)/shard_map/ppermute | solution.py:315
  126.9 8.5 %collective-permute-start.29 = (bf16[272,256]{1,0:T(8,128)(2,1)S(1)}, bf16[272,256]{1,0:T(8,128)(2,1)S(1)}, u32[]{:S(2)}, u32[]{:S(2)}) collective-permute-start(bf16[272,256]{1,0:T(8,128)(2,1)S(1)} %add_convert_fusion), channel_id=1, source_target_pairs={{0,2},{1,3},{2,4},{3,5},{4,6},{5,7},{6,0},{7,1},{8,10},{9,11},{10,... | collective-permute-start | bytes 417800 | tf_op jit(solution)/shard_map/ppermute | solution.py:322
  127.9 7.5 %collective-permute-start.28 = (bf16[272,256]{1,0:T(8,128)(2,1)S(1)}, bf16[272,256]{1,0:T(8,128)(2,1)S(1)}, u32[]{:S(2)}, u32[]{:S(2)}) collective-permute-start(bf16[272,256]{1,0:T(8,128)(2,1)S(1)} %add_convert_fusion), channel_id=1, source_target_pairs={{0,4},{1,5},{2,6},{3,7},{4,0},{5,1},{6,2},{7,3},{8,12},{9,13},{10,... | collective-permute-start | bytes 417800 | tf_op jit(solution)/shard_map/ppermute | solution.py:322
  (18 other events, 127.9 us)

commit v4 on v3

--- a/solution.py
+++ b/solution.py
@@ -8,6 +8,7 @@
 BF = jnp.bfloat16
 F32 = jnp.float32
 EXACT = 256
+EXTRA = 16
 
 
 def params(mib):
@@ -36,10 +37,26 @@
     )(x)
 
 
-def build_kernel(row_ref, col_ref, bits_ref, at_ref, deg_ref, deg8, count, spill):
+def build_kernel(
+    rows_ref, cols_ref, bits_all, gate_ref, at_ref, deg_ref,
+    deg8, count, spill, row_ref, col_ref, bits_ref, sems,
+):
     sources = at_ref.shape[0] - 1
     dests = at_ref.shape[1]
     tiles = bits_ref.shape[0]
+    pieces = 4
+    each = tiles // pieces
+
+    def fetch(k):
+        part = pl.ds(k * each, each)
+        return pltpu.make_async_copy(bits_all.at[0, part], bits_ref.at[part], sems.at[2 + k])
+
+    copies = [
+        pltpu.make_async_copy(rows_ref, row_ref, sems.at[0]),
+        pltpu.make_async_copy(cols_ref, col_ref, sems.at[1]),
+    ] + [fetch(k) for k in range(pieces)]
+    for copy in copies:
+        copy.start()
     for r in range(dests):
         deg8[r] = jnp.zeros((8, 128), F32)
 
@@ -76,7 +93,11 @@
         deg8[row] += total
         return carry
 
-    lax.fori_loop(0, tiles, add_tile, 0, unroll=2)
+    copies[0].wait()
+    copies[1].wait()
+    for k in range(pieces):
+        copies[2 + k].wait()
+        lax.fori_loop(k * each, (k + 1) * each, add_tile, 0, unroll=2)
 
     @pl.when(spill[0] >= 0)
     def _():
@@ -90,9 +111,10 @@
         deg_ref[:, r * 128 : (r + 1) * 128] = jnp.sum(deg8[r], axis=0, keepdims=True)
 
 
-def build(rows, cols, bits, sources, dests):
-    assert bits.shape[0] <= 2 * EXACT
-    smem = pl.BlockSpec(memory_space=pltpu.SMEM)
+def build(rows, cols, bits, gate, sources, dests):
+    tiles = bits.shape[1]
+    assert tiles <= 2 * EXACT and tiles % 8 == 0
+    hbm = pl.BlockSpec(memory_space=pltpu.HBM)
     vmem = pl.BlockSpec(memory_space=pltpu.VMEM)
     return pl.pallas_call(
         build_kernel,
@@ -100,22 +122,27 @@
             jax.ShapeDtypeStruct((sources + 1, dests, 128, 128), BF),
             jax.ShapeDtypeStruct((1, dests * 128), F32),
         ),
-        in_specs=[smem, smem, vmem],
+        in_specs=[hbm, hbm, hbm, pl.BlockSpec(memory_space=pl.ANY)],
         out_specs=(vmem, vmem),
         scratch_shapes=[
             pltpu.VMEM((dests, 8, 128), F32),
             pltpu.SMEM((sources * dests,), jnp.int32),
             pltpu.SMEM((1,), jnp.int32),
+            pltpu.SMEM((1, tiles), jnp.int32),
+            pltpu.SMEM((1, tiles), jnp.int32),
+            pltpu.VMEM((tiles, 16, 128), jnp.int32),
+            pltpu.SemaphoreType.DMA((6,)),
         ],
         compiler_params=params(24),
         cost_estimate=cost(0, 30 << 20),
         name="build",
-    )(rows, cols, bits)
+    )(rows, cols, bits, gate)
 
 
 def forward_kernel(place_ref, *refs):
-    planes, at_ref, out_ref, joined = refs[:4], refs[4], refs[5], refs[6]
+    planes, at_ref, deg_ref, out_ref, joined = refs[:4], refs[4], refs[5], refs[6], refs[7]
     rows = planes[0].shape[2]
+    width = planes[0].shape[1]
 
     @pl.when(pl.program_id(0) == 0)
     def _():
@@ -130,10 +157,27 @@
         for k in range(at_ref.shape[0])
     ]
     part = jnp.dot(joined[...], jnp.concatenate(blocks, axis=0), preferred_element_type=F32)
-    out_ref[0] = part.astype(out_ref.dtype)
-
-
-def forward(place, planes, at, kind):
+    out_ref[0, 0:width, :] = part.astype(out_ref.dtype)
+    degree = deg_ref[...] if out_ref.dtype == F32 else two_rows(deg_ref[...])
+    out_ref[0, width:, :] = spaced(degree, out_ref.dtype)
+
+
+def two_rows(whole):
+    high = whole.astype(BF).astype(F32)
+    first = lax.broadcasted_iota(jnp.int32, (2, 1), 0) == 0
+    return jnp.where(first, high, whole - high)
+
+
+def spaced(rows, kind):
+    count, width = rows.shape
+    place = lax.broadcasted_iota(jnp.int32, (EXTRA, 1), 0)
+    out = jnp.zeros((EXTRA, width), F32)
+    for k in range(count):
+        out = jnp.where(place == k, rows[k : k + 1, :], out)
+    return out.astype(kind)
+
+
+def forward(place, planes, at, degree, kind):
     lines, width, rows = planes[0].shape
     sources = at.shape[0] - 1
     per = rows // 128
@@ -143,19 +187,20 @@
 
     return pl.pallas_call(
         forward_kernel,
-        out_shape=jax.ShapeDtypeStruct((4, width, rows), kind),
+        out_shape=jax.ShapeDtypeStruct((4, width + EXTRA, rows), kind),
         grid_spec=pltpu.PrefetchScalarGridSpec(
             num_scalar_prefetch=1,
             grid=(4,),
             in_specs=[pl.BlockSpec((lines, width, rows), lambda j, *_: (0, 0, 0))] * 4
-            + [pl.BlockSpec((sources, per, 128, 128), chunk)],
-            out_specs=pl.BlockSpec((1, width, rows), lambda j, *_: (j, 0, 0)),
+            + [pl.BlockSpec((sources, per, 128, 128), chunk)]
+            + [pl.BlockSpec((1, rows), lambda j, place: chunk(j, place)[:2])],
+            out_specs=pl.BlockSpec((1, width + EXTRA, rows), lambda j, *_: (j, 0, 0)),
             scratch_shapes=[pltpu.VMEM((width, sources * 128), BF)],
         ),
         compiler_params=params(20),
         cost_estimate=cost(8 * sources * 128 * rows * width, 10 << 20),
         name="forward",
-    )(place, *planes, at)
+    )(place, *planes, at, degree)
 
 
 def backward_kernel(place_ref, *refs):
@@ -202,13 +247,37 @@
     return lax.dot_general(a, b, (((da,), (db,)), ((), ())), preferred_element_type=F32)
 
 
+def mix_kernel(keep_ref, taken_ref, own_ref, *outs):
+    width = own_ref.shape[0] - EXTRA
+    own_ref[...] = keep_ref[0] + taken_ref[0].astype(F32)
+    for k, out_ref in enumerate(outs):
+        both = keep_ref[k + 1] + taken_ref[k + 1].astype(F32)
+        out_ref[0:width, :] = both[0:width].astype(BF)
+        degree = both[width : width + 1] + both[width + 1 : width + 2]
+        out_ref[width:, :] = spaced(two_rows(degree), BF)
+
+
+def mix(keep, taken):
+    shape = keep.shape[1:]
+    return pl.pallas_call(
+        mix_kernel,
+        out_shape=(jax.ShapeDtypeStruct(shape, F32),) + (jax.ShapeDtypeStruct(shape, BF),) * 3,
+        compiler_params=params(16),
+        cost_estimate=cost(1 << 18, 2 << 20),
+        name="mix",
+    )(keep, taken)
+
+
 def middle_kernel(
-    place_ref, keep_ref, taken_ref, r1_ref, r2_ref, r3_ref, deg_ref, x_ref, ws_ref, wn_ref, bias_ref, cot_ref,
+    own_ref, r1_ref, r2_ref, r3_ref, x_ref, ws_ref, wn_ref, bias_ref, cot_ref,
     out_ref, pre_ref, mean_ref, grad_ref,
 ):
-    degree = jnp.maximum(deg_ref[...], 1.0)
-    summed = keep_ref[0] + taken_ref[0].astype(F32) + r1_ref[...].astype(F32)
-    summed += r2_ref[...].astype(F32) + r3_ref[...].astype(F32)
+    width = x_ref.shape[1]
+    summed = (own_ref[...] + r2_ref[...].astype(F32)) + (
+        r1_ref[...].astype(F32) + r3_ref[...].astype(F32)
+    )
+    degree = jnp.maximum(summed[width : width + 1] + summed[width + 1 : width + 2], 1.0)
+    summed = summed[0:width]
     mean_t = (summed / degree).astype(BF)
     mean_ref[...] = mean_t
     preact = (
@@ -224,26 +293,16 @@
     grad_ref[...] = grad_t.T.astype(BF)
 
 
-def middle(place, keep, taken, got, deg, x, ws, wn, bias, cot):
+def middle(own, got, x, ws, wn, bias, cot):
     n = x.shape[0]
     shape = jax.ShapeDtypeStruct((n, n), BF)
-    whole = pl.BlockSpec((n, n), lambda i, *_: (0, 0))
-    first = pl.BlockSpec((1, n, n), lambda i, *_: (0, 0, 0))
     return pl.pallas_call(
         middle_kernel,
         out_shape=(shape, shape, shape, shape),
-        grid_spec=pltpu.PrefetchScalarGridSpec(
-            num_scalar_prefetch=1,
-            grid=(1,),
-            in_specs=[first, first, whole, whole, whole]
-            + [pl.BlockSpec((1, n), lambda i, place: (0, 2 * place[0] + place[1]))]
-            + [whole, whole, whole, pl.BlockSpec((1, n), lambda i, *_: (0, 0)), whole],
-            out_specs=(whole, whole, whole, whole),
-        ),
         compiler_params=params(16),
         cost_estimate=cost(6 * n * n * n, 2 << 20, n * n),
         name="middle",
-    )(place, keep, taken, *got, deg, x, ws, wn, bias, cot)
+    )(own, *got, x, ws, wn, bias, cot)
 
 
 def weights_kernel(place_ref, x_ref, pre_ref, mean_ref, ws_ref, keep_ref, give_ref, self_ref):
@@ -326,10 +385,9 @@
     return lax.ppermute(x, "cols", PARTNER)
 
 
-def total(x, send):
-    x = x.astype(BF)
-    one, two, three = (send(x, k).astype(F32) for k in (1, 2, 3))
-    return (x.astype(F32) + two) + (one + three)
+def add_terms(terms):
+    own, one, two, three = (x.astype(F32) for x in terms)
+    return (own + two) + (one + three)
 
 
 def send_x(x, step):
@@ -351,36 +409,39 @@
 
     ready = prepare(node_feats)
     line = jnp.stack([ready] + [send_x(ready, k) for k in (1, 2, 3)])
-    tile_row, tile_col, line, mine, theirs = lax.optimization_barrier(
-        (tile_row, tile_col, line, mine, theirs)
-    )
+    line, mine, theirs = lax.optimization_barrier((line, mine, theirs))
     planes = [line] + [send_z(line, k) for k in (1, 2, 3)]
     at, degree = build(
-        tile_row, tile_col, tile_bits[0], nodes * rows_dev // 128, cols * rows_dev // 128
-    )
-    degree = degree + send_core(degree)
-    degree = degree + send_y(degree, 1) + send_y(degree, 2) + send_y(degree, 3)
-    *planes, degree = lax.optimization_barrier((*planes, degree))
-
-    give = forward(theirs, planes, at, BF)
+        *(pltpu.with_memory_space_constraint(t, pltpu.HBM) for t in (tile_row, tile_col, tile_bits)),
+        line,
+        nodes * rows_dev // 128, cols * rows_dev // 128
+    )
+
+    give = forward(theirs, planes, at, degree, BF)
     taken = send_core(give)
-    keep = forward(mine, planes, at, F32)
-    both = (keep[1:] + taken[1:].astype(F32)).astype(BF)
-    got = [send_y(both[k - 1], k) for k in (1, 2, 3)]
+    keep = forward(mine, planes, at, degree, F32)
+    own, *sent = mix(keep, taken)
+    got = [send_y(sent[k - 1], k) for k in (1, 2, 3)]
     layer_out, pre_grad, mean_t, mean_grad = middle(
-        mine, keep, taken, got, degree, node_feats, w_self, w_neigh, bias.reshape(1, -1), cotangent
+        own, got, node_feats, w_self, w_neigh, bias.reshape(1, -1), cotangent
     )
     same_core = [mean_grad] + [send_y(mean_grad, k) for k in (1, 2, 3)]
-    other_core = [send_core(g) for g in same_core]
 
     part, give_part, self_part = weights(mine, node_feats, pre_grad, mean_t, w_self)
-    part = total(part + send_core(give_part), send_x)
-
-    src = backward(mine, same_core + other_core, at)
-    src, part = lax.optimization_barrier((src, part))
+    part = (part + send_core(give_part)).astype(BF)
+    terms = [part] + [send_x(part, k) for k in (1, 2, 3)]
+    far, terms = lax.optimization_barrier((same_core[2], terms))
+    other_core = [send_core(g) for g in (same_core[0], same_core[1], far, same_core[3])]
+
+    grads, terms = lax.optimization_barrier((same_core + other_core, terms))
+    part = add_terms(terms).astype(BF)
+    terms = [part] + [send_z(part, k) for k in (1, 2, 3)]
+    src = backward(mine, grads, at)
+    src, terms = lax.optimization_barrier((src, terms))
     parts = swap(src.reshape(nodes, rows_dev, width), "nodes")
 
-    part = total(total(part, send_z), send_y)
+    part = add_terms(terms).astype(BF)
+    part = add_terms([part] + [send_y(part, k) for k in (1, 2, 3)])
     other = send_core(part)
     bias_grad = part[width]
     self_grad = jnp.where(core == 0, part[:width], other[:width])

time: 140 us -> 130 us (0.929); the launches traced: 139 us -> 130 us
  waiting for transfers between devices: 67.5 us -> 63.3 us
  local copies, waits for them, and re-layouts: 4.7 us -> 1.5 us
    all_to_all x1, waiting for transfers between devices: 0.01 us -> 17.6 us  [swap(): return lax.all_to_all(x, axis, 0, 0, tiled=True)]
    ppermute x12 -> x9, waiting for transfers between devices: 28.7 us -> 17.6 us  [send_y(): return lax.ppermute(x, 'cols', along_y(step))]
    ppermute x12, waiting for transfers between devices: 36.7 us -> 25.9 us  [send_node(): return lax.ppermute(x, 'nodes', moves)]
    ppermute x12, starting transfers between devices: 18.5 us -> 14.2 us  [send_node(): return lax.ppermute(x, 'nodes', moves)]
    unnamed x18 -> x12, local copies, waits for them, and re-layouts: 4.11 us -> 0.93 us
    all_to_all x1, starting transfers between devices: 3.74 us -> 6.74 us  [swap(): return lax.all_to_all(x, axis, 0, 0, tiled=True)]
    ppermute x12 -> x9, starting transfers between devices: 14.1 us -> 14.7 us  [send_y(): return lax.ppermute(x, 'cols', along_y(step))]
    pallas_call x3 -> x4, Pallas kernels: 10.3 us -> 9.91 us  [the longest x2 8.71 us: forward(): pl.pallas_call(forward_kernel, out_shape=jax.ShapeDtypeStruct((4, width +...]
  transfers between devices with their start and end apart: 33 -> 29, of which waited for: 20 -> 19; matrix products, arithmetic and copies ran while one was open for 1% -> 1% of each run, Pallas kernels for 14% -> 15%
where the time goes in v4:
time: 130 us
  waiting for transfers between devices  63.3 us (49%)
  starting transfers between devices  36.5 us (28%)
  Pallas kernels  26.9 us (21%)
  local copies, waits for them, and re-layouts  1.5 us (1%)
    ppermute x12, waiting for transfers between devices, send_node(): return lax.ppermute(x, 'nodes', moves)  25.9 us
    all_to_all x1, waiting for transfers between devices, swap(): return lax.all_to_all(x, axis, 0, 0, tiled=True)  17.6 us
    ppermute x9, waiting for transfers between devices, send_y(): return lax.ppermute(x, 'cols', along_y(step))  17.6 us
    ppermute x9, starting transfers between devices, send_y(): return lax.ppermute(x, 'cols', along_y(step))  14.7 us
    ppermute x12, starting transfers between devices, send_node(): return lax.ppermute(x, 'nodes', moves)  14.2 us
    pallas_call x2, Pallas kernels, forward(): pl.pallas_call(forward_kernel, out_shape=jax.ShapeDtypeStruct((4, width +...  8.71 us
    pallas_call x1, Pallas kernels, build(): pl.pallas_call(build_kernel, out_shape=(jax.ShapeDtypeStruct((sources + 1...  8.24 us
    pallas_call x1, Pallas kernels, backward(): pl.pallas_call(backward_kernel, out_shape=in_hbm((sources * 128, width),...  6.74 us
  transfers between devices with their start and end apart: 29, of which 19 were waited for; matrix products, arithmetic and copies ran while one was open for 1% of the time, Pallas kernels for 15%

profile of v4, /device:TPU:0, one launch (start us, length us, event | category | flops | bytes accessed | tf_op | source)
XLA Modules:
  0.0 130.3 jit_solution(13480544453054203258)
XLA Ops:
  1.6 2.9 %collective-permute-start.2 = (bf16[256,256]{1,0:T(8,128)(2,1)S(1)}, bf16[256,256]{1,0:T(8,128)(2,1)S(1)}, u32[]{:S(2)}, u32[]{:S(2)}) collective-permute-start(bf16[256,256]{1,0:T(8,128)(2,1)S(1)} %prepare.1), channel_id=1, source_target_pairs={{0,96},{8,104},{16,112},{24,120},{32,0},{40,8},{48,16},{56,24},{64... | collective-permute-start | bytes 393224 | tf_op jit(solution)/shard_map/ppermute | solution.py:374
  6.3 3.8 %collective-permute-done.2 = bf16[256,256]{1,0:T(8,128)(2,1)S(1)} collective-permute-done((bf16[256,256]{1,0:T(8,128)(2,1)S(1)}, bf16[256,256]{1,0:T(8,128)(2,1)S(1)}, u32[]{:S(2)}, u32[]{:S(2)}) %collective-permute-start.2) | collective-permute-done | bytes 131104 | tf_op jit(solution)/shard_map/ppermute | solution.py:374
  10.1 2.3 %collective-permute-done.1 = bf16[256,256]{1,0:T(8,128)(2,1)S(1)} collective-permute-done((bf16[256,256]{1,0:T(8,128)(2,1)S(1)}, bf16[256,256]{1,0:T(8,128)(2,1)S(1)}, u32[]{:S(2)}, u32[]{:S(2)}) %collective-permute-start.1) | collective-permute-done | bytes 131104 | tf_op jit(solution)/shard_map/ppermute | solution.py:374
  13.9 4.1 %collective-permute-start.5 = (bf16[4,256,256]{2,1,0:T(8,128)(2,1)S(1)}, bf16[4,256,256]{2,1,0:T(8,128)(2,1)S(1)}, u32[]{:S(2)}, u32[]{:S(2)}) collective-permute-start(bf16[4,256,256]{2,1,0:T(8,128)(2,1)S(1)} %pad_maximum_fusion.gate_ref.refs_0_), channel_id=1, source_target_pairs={{0,24},{8,0},{16,8},{24,16},{32,56},{40,32},{48,40},{56,48},{64,88... | collective-permute-start | bytes 1572872 | tf_op jit(solution)/shard_map/ppermute | solution.py:374
  19.2 8.2 %build.1 = (bf16[33,16,128,128]{3,2,1,0:T(8,128)(2,1)S(1)}, f32[1,2048]{1,0:T(1,128)S(1)}) custom-call(s32[1,352]{1,0:T(1,128)} %rows_ref.1, s32[1,352]{1,0:T(1,128)} %cols_ref.1, s32[1,352,16,128]{3,2,1,0:T(8,128)} %bits_all.1, bf16[4,256,256]{2,1,0:T(8,128)(2,1)S(1)} %pad_maximum_fusion.gate_ref.refs_0_), custom_call_target="tpu_custom_call" | custom-call | bytes 31457280 | tf_op jit(solution)/shard_map/build/pallas_call | solution.py:119
  27.5 12.9 %collective-permute-done.5.refs_3_ = bf16[4,256,256]{2,1,0:T(8,128)(2,1)S(1)} collective-permute-done((bf16[4,256,256]{2,1,0:T(8,128)(2,1)S(1)}, bf16[4,256,256]{2,1,0:T(8,128)(2,1)S(1)}, u32[]{:S(2)}, u32[]{:S(2)}) %collective-permute-start.5) | collective-permute-done | bytes 524320 | tf_op jit(solution)/shard_map/ppermute | solution.py:374
  40.4 3.4 %collective-permute-done.3.refs_1_ = bf16[4,256,256]{2,1,0:T(8,128)(2,1)S(1)} collective-permute-done((bf16[4,256,256]{2,1,0:T(8,128)(2,1)S(1)}, bf16[4,256,256]{2,1,0:T(8,128)(2,1)S(1)}, u32[]{:S(2)}, u32[]{:S(2)}) %collective-permute-start.3) | collective-permute-done | bytes 524320 | tf_op jit(solution)/shard_map/ppermute | solution.py:374
  43.8 4.4 %forward.3 = bf16[4,272,256]{2,1,0:T(8,128)(2,1)S(1)} custom-call(s32[4]{0:T(128)S(1)} %get-tuple-element.47.place_ref, bf16[4,256,256]{2,1,0:T(8,128)(2,1)S(1)} %pad_maximum_fusion.gate_ref.refs_0_, bf16[4,256,256]{2,1,0:T(8,128)(2,1)S(1)} %collective-permute-done.3.refs_1_, bf16[4,256,256]{2,1,0:T(8,128)(2,1)S(1)} %collective-permute-done.4.refs_2_, ...), custom_call_target="tpu_custom_call" | custom-call | flops 2147483648 | bytes 10485760 | tf_op jit(solution)/shard_map/forward/pallas_call | solution.py:188
  48.3 4.4 %forward.2.keep_ref = f32[4,272,256]{2,1,0:T(8,128)S(1)} custom-call(s32[4]{0:T(128)S(1)} %get-tuple-element.43.place_ref, bf16[4,256,256]{2,1,0:T(8,128)(2,1)S(1)} %pad_maximum_fusion.gate_ref.refs_0_, bf16[4,256,256]{2,1,0:T(8,128)(2,1)S(1)} %collective-permute-done.3.refs_1_, bf16[4,256,256]{2,1,0:T(8,128)(2,1)S(1)} %collective-permute-done.4.refs_2_, ...), custom_call_target="tpu_custom_call" | custom-call | flops 2147483648 | bytes 10485760 | tf_op jit(solution)/shard_map/forward/pallas_call | solution.py:188
  52.8 1.6 %collective-permute-start.7 = (bf16[272,256]{1,0:T(8,128)(2,1)S(1)}, bf16[272,256]{1,0:T(8,128)(2,1)S(1)}, u32[]{:S(2)}, u32[]{:S(2)}) collective-permute-start(bf16[272,256]{1,0:T(8,128)(2,1)S(1)} %get-tuple-element.49), channel_id=1, source_target_pairs={{0,2},{1,3},{2,4},{3,5},{4,6},{5,7},{6,0},{7,1},{8,10},{9,11},{10,... | collective-permute-start | bytes 417800 | tf_op jit(solution)/shard_map/ppermute | solution.py:381
  54.5 2.9 %collective-permute-start.8 = (bf16[272,256]{1,0:T(8,128)(2,1)S(1)}, bf16[272,256]{1,0:T(8,128)(2,1)S(1)}, u32[]{:S(2)}, u32[]{:S(2)}) collective-permute-start(bf16[272,256]{1,0:T(8,128)(2,1)S(1)} %get-tuple-element.50), channel_id=1, source_target_pairs={{0,4},{1,5},{2,6},{3,7},{4,0},{5,1},{6,2},{7,3},{8,12},{9,13},{10,... | collective-permute-start | bytes 417800 | tf_op jit(solution)/shard_map/ppermute | solution.py:381
  58.7 1.5 %collective-permute-done.7.r1_ref = bf16[272,256]{1,0:T(8,128)(2,1)S(1)} collective-permute-done((bf16[272,256]{1,0:T(8,128)(2,1)S(1)}, bf16[272,256]{1,0:T(8,128)(2,1)S(1)}, u32[]{:S(2)}, u32[]{:S(2)}) %collective-permute-start.7) | collective-permute-done | bytes 139296 | tf_op jit(solution)/shard_map/ppermute | solution.py:381
  60.2 4.2 %collective-permute-done.8.r2_ref = bf16[272,256]{1,0:T(8,128)(2,1)S(1)} collective-permute-done((bf16[272,256]{1,0:T(8,128)(2,1)S(1)}, bf16[272,256]{1,0:T(8,128)(2,1)S(1)}, u32[]{:S(2)}, u32[]{:S(2)}) %collective-permute-start.8) | collective-permute-done | bytes 139296 | tf_op jit(solution)/shard_map/ppermute | solution.py:381
  66.6 2.2 %collective-permute-start.12 = (bf16[256,256]{1,0:T(8,128)(2,1)S(1)}, bf16[256,256]{1,0:T(8,128)(2,1)S(1)}, u32[]{:S(2)}, u32[]{:S(2)}) collective-permute-start(bf16[256,256]{1,0:T(8,128)(2,1)S(1)} %get-tuple-element.63.refs_0_), channel_id=1, source_target_pairs={{0,6},{1,7},{2,0},{3,1},{4,2},{5,3},{6,4},{7,5},{8,14},{9,15},{10,... | collective-permute-start | bytes 393224 | tf_op jit(solution)/shard_map/ppermute | solution.py:381
  69.4 1.6 %collective-permute-start.16 = (bf16[272,256]{1,0:T(8,128)(2,1)S(1)}, bf16[272,256]{1,0:T(8,128)(2,1)S(1)}, u32[]{:S(2)}, u32[]{:S(2)}) collective-permute-start(bf16[272,256]{1,0:T(8,128)(2,1)S(1)} %add_convert_fusion.2), channel_id=1, source_target_pairs={{0,32},{8,40},{16,48},{24,56},{32,64},{40,72},{48,80},{56,88},{64,... | collective-permute-start | bytes 417800 | tf_op jit(solution)/shard_map/ppermute | solution.py:374
  71.0 1.9 %collective-permute-start.11 = (bf16[256,256]{1,0:T(8,128)(2,1)S(1)}, bf16[256,256]{1,0:T(8,128)(2,1)S(1)}, u32[]{:S(2)}, u32[]{:S(2)}) collective-permute-start(bf16[256,256]{1,0:T(8,128)(2,1)S(1)} %get-tuple-element.63.refs_0_), channel_id=1, source_target_pairs={{0,4},{1,5},{2,6},{3,7},{4,0},{5,1},{6,2},{7,3},{8,12},{9,13},{10,... | collective-permute-start | bytes 393224 | tf_op jit(solution)/shard_map/ppermute | solution.py:381
  73.8 3.8 %collective-permute-done.11.refs_2_ = bf16[256,256]{1,0:T(8,128)(2,1)S(1)} collective-permute-done((bf16[256,256]{1,0:T(8,128)(2,1)S(1)}, bf16[256,256]{1,0:T(8,128)(2,1)S(1)}, u32[]{:S(2)}, u32[]{:S(2)}) %collective-permute-start.11) | collective-permute-done | bytes 131104 | tf_op jit(solution)/shard_map/ppermute | solution.py:381
  77.6 2.7 %collective-permute-done.10.refs_1_ = bf16[256,256]{1,0:T(8,128)(2,1)S(1)} collective-permute-done((bf16[256,256]{1,0:T(8,128)(2,1)S(1)}, bf16[256,256]{1,0:T(8,128)(2,1)S(1)}, u32[]{:S(2)}, u32[]{:S(2)}) %collective-permute-start.10) | collective-permute-done | bytes 131104 | tf_op jit(solution)/shard_map/ppermute | solution.py:381
  84.4 6.7 %backward.1 = bf16[4096,256]{1,0:T(8,128)(2,1)} custom-call(s32[4]{0:T(128)S(1)} %get-tuple-element.43.place_ref, bf16[256,256]{1,0:T(8,128)(2,1)S(1)} %get-tuple-element.63.refs_0_, bf16[256,256]{1,0:T(8,128)(2,1)S(1)} %collective-permute-done.10.refs_1_, bf16[256,256]{1,0:T(8,128)(2,1)S(1)} %collective-permute-done.11.refs_2_, ...), custom_call_target="tpu_custom_call" | custom-call | flops 4294967296 | bytes 20971520 | tf_op jit(solution)/shard_map/backward/pallas_call | solution.py:229
  91.3 1.9 %collective-permute-done.21 = bf16[272,256]{1,0:T(8,128)(2,1)S(1)} collective-permute-done((bf16[272,256]{1,0:T(8,128)(2,1)S(1)}, bf16[272,256]{1,0:T(8,128)(2,1)S(1)}, u32[]{:S(2)}, u32[]{:S(2)}) %collective-permute-start.21) | collective-permute-done | bytes 139296 | tf_op jit(solution)/shard_map/ppermute | solution.py:374
  93.2 6.7 %all-to-all-start = ((bf16[16,256,256]{2,1,0:T(8,128)(2,1)}), bf16[16,256,256]{2,1,0:T(8,128)(2,1)S(1)}, u32[]{:S(2)}, u32[]{:S(2)}) async-start(bf16[16,256,256]{2,1,0:T(8,128)(2,1)} %bitcast.14), calls=%async_computation | async-start | bytes 4194304 | tf_op jit(solution)/shard_map/all_to_all | solution.py:363
  102.1 1.8 %collective-permute-start.24 = (bf16[272,256]{1,0:T(8,128)(2,1)S(1)}, bf16[272,256]{1,0:T(8,128)(2,1)S(1)}, u32[]{:S(2)}, u32[]{:S(2)}) collective-permute-start(bf16[272,256]{1,0:T(8,128)(2,1)S(1)} %add_convert_fusion), channel_id=1, source_target_pairs={{0,4},{1,5},{2,6},{3,7},{4,0},{5,1},{6,2},{7,3},{8,12},{9,13},{10,... | collective-permute-start | bytes 417800 | tf_op jit(solution)/shard_map/ppermute | solution.py:381
  103.9 2.6 %collective-permute-done.26 = bf16[272,256]{1,0:T(8,128)(2,1)S(1)} collective-permute-done((bf16[272,256]{1,0:T(8,128)(2,1)S(1)}, bf16[272,256]{1,0:T(8,128)(2,1)S(1)}, u32[]{:S(2)}, u32[]{:S(2)}) %collective-permute-start.26) | collective-permute-done | bytes 139296 | tf_op jit(solution)/shard_map/ppermute | solution.py:381
  111.8 17.6 %all-to-all-done.parts_ref = bf16[16,256,256]{2,1,0:T(8,128)(2,1)S(1)} async-done(((bf16[16,256,256]{2,1,0:T(8,128)(2,1)}), bf16[16,256,256]{2,1,0:T(8,128)(2,1)S(1)}, u32[]{:S(2)}, u32[]{:S(2)}) %all-to-all-start) | async-done | bytes 2097184 | tf_op jit(solution)/shard_map/all_to_all | solution.py:363
  (63 shorter events, 23.3 us)
Async XLA Ops:
  1.6 8.5 %collective-permute-start.2 = (bf16[256,256]{1,0:T(8,128)(2,1)S(1)}, bf16[256,256]{1,0:T(8,128)(2,1)S(1)}, u32[]{:S(2)}, u32[]{:S(2)}) collective-permute-start(bf16[256,256]{1,0:T(8,128)(2,1)S(1)} %prepare.1), channel_id=1, source_target_pairs={{0,96},{8,104},{16,112},{24,120},{32,0},{40,8},{48,16},{56,24},{64... | collective-permute-start | bytes 393224 | tf_op jit(solution)/shard_map/ppermute | solution.py:374
  4.5 7.9 %collective-permute-start.1 = (bf16[256,256]{1,0:T(8,128)(2,1)S(1)}, bf16[256,256]{1,0:T(8,128)(2,1)S(1)}, u32[]{:S(2)}, u32[]{:S(2)}) collective-permute-start(bf16[256,256]{1,0:T(8,128)(2,1)S(1)} %prepare.1), channel_id=1, source_target_pairs={{0,64},{8,72},{16,80},{24,88},{32,96},{40,104},{48,112},{56,120},{... | collective-permute-start | bytes 393224 | tf_op jit(solution)/shard_map/ppermute | solution.py:374
  5.3 8.5 %collective-permute-start = (bf16[256,256]{1,0:T(8,128)(2,1)S(1)}, bf16[256,256]{1,0:T(8,128)(2,1)S(1)}, u32[]{:S(2)}, u32[]{:S(2)}) collective-permute-start(bf16[256,256]{1,0:T(8,128)(2,1)S(1)} %prepare.1), channel_id=1, source_target_pairs={{0,32},{8,40},{16,48},{24,56},{32,64},{40,72},{48,80},{56,88},{64,... | collective-permute-start | bytes 393224 | tf_op jit(solution)/shard_map/ppermute | solution.py:374
  13.9 26.5 %collective-permute-start.5 = (bf16[4,256,256]{2,1,0:T(8,128)(2,1)S(1)}, bf16[4,256,256]{2,1,0:T(8,128)(2,1)S(1)}, u32[]{:S(2)}, u32[]{:S(2)}) collective-permute-start(bf16[4,256,256]{2,1,0:T(8,128)(2,1)S(1)} %pad_maximum_fusion.gate_ref.refs_0_), channel_id=1, source_target_pairs={{0,24},{8,0},{16,8},{24,16},{32,56},{40,32},{48,40},{56,48},{64,88... | collective-permute-start | bytes 1572872 | tf_op jit(solution)/shard_map/ppermute | solution.py:374
  18.0 22.4 %collective-permute-start.4 = (bf16[4,256,256]{2,1,0:T(8,128)(2,1)S(1)}, bf16[4,256,256]{2,1,0:T(8,128)(2,1)S(1)}, u32[]{:S(2)}, u32[]{:S(2)}) collective-permute-start(bf16[4,256,256]{2,1,0:T(8,128)(2,1)S(1)} %pad_maximum_fusion.gate_ref.refs_0_), channel_id=1, source_target_pairs={{0,16},{8,24},{16,0},{24,8},{32,48},{40,56},{48,32},{56,40},{64,80... | collective-permute-start | bytes 1572872 | tf_op jit(solution)/shard_map/ppermute | solution.py:374
  18.0 25.8 %collective-permute-start.3 = (bf16[4,256,256]{2,1,0:T(8,128)(2,1)S(1)}, bf16[4,256,256]{2,1,0:T(8,128)(2,1)S(1)}, u32[]{:S(2)}, u32[]{:S(2)}) collective-permute-start(bf16[4,256,256]{2,1,0:T(8,128)(2,1)S(1)} %pad_maximum_fusion.gate_ref.refs_0_), channel_id=1, source_target_pairs={{0,8},{8,16},{16,24},{24,0},{32,40},{40,48},{48,56},{56,32},{64,72... | collective-permute-start | bytes 1572872 | tf_op jit(solution)/shard_map/ppermute | solution.py:374
  48.2 4.5 %collective-permute-start.6 = (bf16[4,272,256]{2,1,0:T(8,128)(2,1)S(1)}, bf16[4,272,256]{2,1,0:T(8,128)(2,1)S(1)}, u32[]{:S(2)}, u32[]{:S(2)}) collective-permute-start(bf16[4,272,256]{2,1,0:T(8,128)(2,1)S(1)} %forward.3), channel_id=1, source_target_pairs={{0,1},{1,0},{2,3},{3,2},{4,5},{5,4},{6,7},{7,6},{8,9},{9,8},{10,11... | collective-permute-start | bytes 1671176 | tf_op jit(solution)/shard_map/ppermute | solution.py:385
  52.8 7.4 %collective-permute-start.7 = (bf16[272,256]{1,0:T(8,128)(2,1)S(1)}, bf16[272,256]{1,0:T(8,128)(2,1)S(1)}, u32[]{:S(2)}, u32[]{:S(2)}) collective-permute-start(bf16[272,256]{1,0:T(8,128)(2,1)S(1)} %get-tuple-element.49), channel_id=1, source_target_pairs={{0,2},{1,3},{2,4},{3,5},{4,6},{5,7},{6,0},{7,1},{8,10},{9,11},{10,... | collective-permute-start | bytes 417800 | tf_op jit(solution)/shard_map/ppermute | solution.py:381
  54.5 9.9 %collective-permute-start.8 = (bf16[272,256]{1,0:T(8,128)(2,1)S(1)}, bf16[272,256]{1,0:T(8,128)(2,1)S(1)}, u32[]{:S(2)}, u32[]{:S(2)}) collective-permute-start(bf16[272,256]{1,0:T(8,128)(2,1)S(1)} %get-tuple-element.50), channel_id=1, source_target_pairs={{0,4},{1,5},{2,6},{3,7},{4,0},{5,1},{6,2},{7,3},{8,12},{9,13},{10,... | collective-permute-start | bytes 417800 | tf_op jit(solution)/shard_map/ppermute | solution.py:381
  57.4 7.0 %collective-permute-start.9 = (bf16[272,256]{1,0:T(8,128)(2,1)S(1)}, bf16[272,256]{1,0:T(8,128)(2,1)S(1)}, u32[]{:S(2)}, u32[]{:S(2)}) collective-permute-start(bf16[272,256]{1,0:T(8,128)(2,1)S(1)} %get-tuple-element.51), channel_id=1, source_target_pairs={{0,6},{1,7},{2,0},{3,1},{4,2},{5,3},{6,4},{7,5},{8,14},{9,15},{10,... | collective-permute-start | bytes 417800 | tf_op jit(solution)/shard_map/ppermute | solution.py:381
  66.6 6.3 %collective-permute-start.12 = (bf16[256,256]{1,0:T(8,128)(2,1)S(1)}, bf16[256,256]{1,0:T(8,128)(2,1)S(1)}, u32[]{:S(2)}, u32[]{:S(2)}) collective-permute-start(bf16[256,256]{1,0:T(8,128)(2,1)S(1)} %get-tuple-element.63.refs_0_), channel_id=1, source_target_pairs={{0,6},{1,7},{2,0},{3,1},{4,2},{5,3},{6,4},{7,5},{8,14},{9,15},{10,... | collective-permute-start | bytes 393224 | tf_op jit(solution)/shard_map/ppermute | solution.py:381
  68.9 11.4 %collective-permute-start.18 = (bf16[272,256]{1,0:T(8,128)(2,1)S(1)}, bf16[272,256]{1,0:T(8,128)(2,1)S(1)}, u32[]{:S(2)}, u32[]{:S(2)}) collective-permute-start(bf16[272,256]{1,0:T(8,128)(2,1)S(1)} %add_convert_fusion.2), channel_id=1, source_target_pairs={{0,96},{8,104},{16,112},{24,120},{32,0},{40,8},{48,16},{56,24},{64... | collective-permute-start | bytes 417800 | tf_op jit(solution)/shard_map/ppermute | solution.py:374
  69.0 11.9 %collective-permute-start.17 = (bf16[272,256]{1,0:T(8,128)(2,1)S(1)}, bf16[272,256]{1,0:T(8,128)(2,1)S(1)}, u32[]{:S(2)}, u32[]{:S(2)}) collective-permute-start(bf16[272,256]{1,0:T(8,128)(2,1)S(1)} %add_convert_fusion.2), channel_id=1, source_target_pairs={{0,64},{8,72},{16,80},{24,88},{32,96},{40,104},{48,112},{56,120},{... | collective-permute-start | bytes 417800 | tf_op jit(solution)/shard_map/ppermute | solution.py:374
  69.4 11.4 %collective-permute-start.16 = (bf16[272,256]{1,0:T(8,128)(2,1)S(1)}, bf16[272,256]{1,0:T(8,128)(2,1)S(1)}, u32[]{:S(2)}, u32[]{:S(2)}) collective-permute-start(bf16[272,256]{1,0:T(8,128)(2,1)S(1)} %add_convert_fusion.2), channel_id=1, source_target_pairs={{0,32},{8,40},{16,48},{24,56},{32,64},{40,72},{48,80},{56,88},{64,... | collective-permute-start | bytes 417800 | tf_op jit(solution)/shard_map/ppermute | solution.py:374
  71.0 6.6 %collective-permute-start.11 = (bf16[256,256]{1,0:T(8,128)(2,1)S(1)}, bf16[256,256]{1,0:T(8,128)(2,1)S(1)}, u32[]{:S(2)}, u32[]{:S(2)}) collective-permute-start(bf16[256,256]{1,0:T(8,128)(2,1)S(1)} %get-tuple-element.63.refs_0_), channel_id=1, source_target_pairs={{0,4},{1,5},{2,6},{3,7},{4,0},{5,1},{6,2},{7,3},{8,12},{9,13},{10,... | collective-permute-start | bytes 393224 | tf_op jit(solution)/shard_map/ppermute | solution.py:381
  72.9 7.4 %collective-permute-start.10 = (bf16[256,256]{1,0:T(8,128)(2,1)S(1)}, bf16[256,256]{1,0:T(8,128)(2,1)S(1)}, u32[]{:S(2)}, u32[]{:S(2)}) collective-permute-start(bf16[256,256]{1,0:T(8,128)(2,1)S(1)} %get-tuple-element.63.refs_0_), channel_id=1, source_target_pairs={{0,2},{1,3},{2,4},{3,5},{4,6},{5,7},{6,0},{7,1},{8,10},{9,11},{10,... | collective-permute-start | bytes 393224 | tf_op jit(solution)/shard_map/ppermute | solution.py:381
  77.6 3.3 %collective-permute-start.13 = (bf16[256,256]{1,0:T(8,128)(2,1)S(1)}, bf16[256,256]{1,0:T(8,128)(2,1)S(1)}, u32[]{:S(2)}, u32[]{:S(2)}) collective-permute-start(bf16[256,256]{1,0:T(8,128)(2,1)S(1)} %get-tuple-element.63.refs_0_), channel_id=1, source_target_pairs={{0,1},{1,0},{2,3},{3,2},{4,5},{5,4},{6,7},{7,6},{8,9},{9,8},{10,11... | collective-permute-start | bytes 393224 | tf_op jit(solution)/shard_map/ppermute | solution.py:385
  82.3 8.8 %collective-permute-start.23 = (bf16[272,256]{1,0:T(8,128)(2,1)S(1)}, bf16[272,256]{1,0:T(8,128)(2,1)S(1)}, u32[]{:S(2)}, u32[]{:S(2)}) collective-permute-start(bf16[272,256]{1,0:T(8,128)(2,1)S(1)} %add_convert_fusion.1), channel_id=1, source_target_pairs={{0,24},{8,0},{16,8},{24,16},{32,56},{40,32},{48,40},{56,48},{64,88... | collective-permute-start | bytes 417800 | tf_op jit(solution)/shard_map/ppermute | solution.py:374
  83.2 8.1 %collective-permute-start.22 = (bf16[272,256]{1,0:T(8,128)(2,1)S(1)}, bf16[272,256]{1,0:T(8,128)(2,1)S(1)}, u32[]{:S(2)}, u32[]{:S(2)}) collective-permute-start(bf16[272,256]{1,0:T(8,128)(2,1)S(1)} %add_convert_fusion.1), channel_id=1, source_target_pairs={{0,16},{8,24},{16,0},{24,8},{32,48},{40,56},{48,32},{56,40},{64,80... | collective-permute-start | bytes 417800 | tf_op jit(solution)/shard_map/ppermute | solution.py:374
  83.5 9.7 %collective-permute-start.21 = (bf16[272,256]{1,0:T(8,128)(2,1)S(1)}, bf16[272,256]{1,0:T(8,128)(2,1)S(1)}, u32[]{:S(2)}, u32[]{:S(2)}) collective-permute-start(bf16[272,256]{1,0:T(8,128)(2,1)S(1)} %add_convert_fusion.1), channel_id=1, source_target_pairs={{0,8},{8,16},{16,24},{24,0},{32,40},{40,48},{48,56},{56,32},{64,72... | collective-permute-start | bytes 417800 | tf_op jit(solution)/shard_map/ppermute | solution.py:374
  93.2 36.1 %all-to-all-start = ((bf16[16,256,256]{2,1,0:T(8,128)(2,1)}), bf16[16,256,256]{2,1,0:T(8,128)(2,1)S(1)}, u32[]{:S(2)}, u32[]{:S(2)}) async-start(bf16[16,256,256]{2,1,0:T(8,128)(2,1)} %bitcast.14), calls=%async_computation | async-start | bytes 4194304 | tf_op jit(solution)/shard_map/all_to_all | solution.py:363
  100.0 6.5 %collective-permute-start.26 = (bf16[272,256]{1,0:T(8,128)(2,1)S(1)}, bf16[272,256]{1,0:T(8,128)(2,1)S(1)}, u32[]{:S(2)}, u32[]{:S(2)}) collective-permute-start(bf16[272,256]{1,0:T(8,128)(2,1)S(1)} %add_convert_fusion), channel_id=1, source_target_pairs={{0,6},{1,7},{2,0},{3,1},{4,2},{5,3},{6,4},{7,5},{8,14},{9,15},{10,... | collective-permute-start | bytes 417800 | tf_op jit(solution)/shard_map/ppermute | solution.py:381
  100.7 7.2 %collective-permute-start.25 = (bf16[272,256]{1,0:T(8,128)(2,1)S(1)}, bf16[272,256]{1,0:T(8,128)(2,1)S(1)}, u32[]{:S(2)}, u32[]{:S(2)}) collective-permute-start(bf16[272,256]{1,0:T(8,128)(2,1)S(1)} %add_convert_fusion), channel_id=1, source_target_pairs={{0,2},{1,3},{2,4},{3,5},{4,6},{5,7},{6,0},{7,1},{8,10},{9,11},{10,... | collective-permute-start | bytes 417800 | tf_op jit(solution)/shard_map/ppermute | solution.py:381
  102.1 7.1 %collective-permute-start.24 = (bf16[272,256]{1,0:T(8,128)(2,1)S(1)}, bf16[272,256]{1,0:T(8,128)(2,1)S(1)}, u32[]{:S(2)}, u32[]{:S(2)}) collective-permute-start(bf16[272,256]{1,0:T(8,128)(2,1)S(1)} %add_convert_fusion), channel_id=1, source_target_pairs={{0,4},{1,5},{2,6},{3,7},{4,0},{5,1},{6,2},{7,3},{8,12},{9,13},{10,... | collective-permute-start | bytes 417800 | tf_op jit(solution)/shard_map/ppermute | solution.py:381
  (11 other events, 90.1 us)

commit v5 on v4

--- a/solution.py
+++ b/solution.py
@@ -23,14 +23,19 @@
     return pl.CostEstimate(flops=flops, bytes_accessed=moved, transcendentals=transcendentals)
 
 
-def prepare_kernel(x_ref, out_ref):
-    out_ref[...] = x_ref[...].T
+def prepare_kernel(x_ref, top_ref, low_ref):
+    half = top_ref.shape[0]
+    flipped = x_ref[...].T
+    top_ref[...] = flipped[:half]
+    low_ref[...] = flipped[half:]
 
 
 def prepare(x):
+    rows, width = x.shape
+    shape = jax.ShapeDtypeStruct((width // 2, rows), BF)
     return pl.pallas_call(
         prepare_kernel,
-        out_shape=jax.ShapeDtypeStruct(x.shape[::-1], BF),
+        out_shape=(shape, shape),
         compiler_params=params(8),
         cost_estimate=cost(0, 1 << 18),
         name="prepare",
@@ -140,9 +145,10 @@
 
 
 def forward_kernel(place_ref, *refs):
-    planes, at_ref, deg_ref, out_ref, joined = refs[:4], refs[4], refs[5], refs[6], refs[7]
-    rows = planes[0].shape[2]
-    width = planes[0].shape[1]
+    tops, lows = refs[:4], refs[4:8]
+    at_ref, deg_ref, out_ref, joined = refs[8:]
+    half, rows = tops[0].shape[1:]
+    width = 2 * half
 
     @pl.when(pl.program_id(0) == 0)
     def _():
@@ -150,7 +156,9 @@
             x = lax.rem(place_ref[2] + 4 - kx, 4)
             for kz in range(4):
                 n = 4 * x + lax.rem(place_ref[3] + 4 - kz, 4)
-                joined[:, pl.ds(pl.multiple_of(n * rows, rows), rows)] = planes[kz][kx]
+                lanes = pl.ds(pl.multiple_of(n * rows, rows), rows)
+                joined[0:half, lanes] = tops[kz][kx]
+                joined[half:width, lanes] = lows[kx][kz]
 
     blocks = [
         jnp.concatenate([at_ref[k, r] for r in range(at_ref.shape[1])], axis=1)
@@ -178,7 +186,8 @@
 
 
 def forward(place, planes, at, degree, kind):
-    lines, width, rows = planes[0].shape
+    lines, half, rows = planes[0].shape
+    width = 2 * half
     sources = at.shape[0] - 1
     per = rows // 128
 
@@ -191,7 +200,7 @@
         grid_spec=pltpu.PrefetchScalarGridSpec(
             num_scalar_prefetch=1,
             grid=(4,),
-            in_specs=[pl.BlockSpec((lines, width, rows), lambda j, *_: (0, 0, 0))] * 4
+            in_specs=[pl.BlockSpec((lines, half, rows), lambda j, *_: (0, 0, 0))] * 8
             + [pl.BlockSpec((sources, per, 128, 128), chunk)]
             + [pl.BlockSpec((1, rows), lambda j, place: chunk(j, place)[:2])],
             out_specs=pl.BlockSpec((1, width + EXTRA, rows), lambda j, *_: (j, 0, 0)),
@@ -407,13 +416,15 @@
     mine = jnp.stack([y, core, node // 4, node % 4]).astype(jnp.int32)
     theirs = jnp.stack([y, 1 - core, node // 4, node % 4]).astype(jnp.int32)
 
-    ready = prepare(node_feats)
-    line = jnp.stack([ready] + [send_x(ready, k) for k in (1, 2, 3)])
-    line, mine, theirs = lax.optimization_barrier((line, mine, theirs))
-    planes = [line] + [send_z(line, k) for k in (1, 2, 3)]
+    top, low = prepare(node_feats)
+    top = jnp.stack([top] + [send_x(top, k) for k in (1, 2, 3)])
+    low = jnp.stack([low] + [send_z(low, k) for k in (1, 2, 3)])
+    top, low, mine, theirs = lax.optimization_barrier((top, low, mine, theirs))
+    planes = [top] + [send_z(top, k) for k in (1, 2, 3)]
+    planes += [low] + [send_x(low, k) for k in (1, 2, 3)]
     at, degree = build(
         *(pltpu.with_memory_space_constraint(t, pltpu.HBM) for t in (tile_row, tile_col, tile_bits)),
-        line,
+        top,
         nodes * rows_dev // 128, cols * rows_dev // 128
     )
 
@@ -429,19 +440,17 @@
 
     part, give_part, self_part = weights(mine, node_feats, pre_grad, mean_t, w_self)
     part = (part + send_core(give_part)).astype(BF)
+    *same_core, part = lax.optimization_barrier((*same_core, part))
+    other_core = [send_core(g) for g in same_core]
     terms = [part] + [send_x(part, k) for k in (1, 2, 3)]
-    far, terms = lax.optimization_barrier((same_core[2], terms))
-    other_core = [send_core(g) for g in (same_core[0], same_core[1], far, same_core[3])]
-
-    grads, terms = lax.optimization_barrier((same_core + other_core, terms))
-    part = add_terms(terms).astype(BF)
-    terms = [part] + [send_z(part, k) for k in (1, 2, 3)]
-    src = backward(mine, grads, at)
+
+    src = backward(mine, same_core + other_core, at)
     src, terms = lax.optimization_barrier((src, terms))
     parts = swap(src.reshape(nodes, rows_dev, width), "nodes")
 
     part = add_terms(terms).astype(BF)
-    part = add_terms([part] + [send_y(part, k) for k in (1, 2, 3)])
+    part = add_terms([part] + [send_y(part, k) for k in (1, 2, 3)]).astype(BF)
+    part = add_terms([part] + [send_z(part, k) for k in (1, 2, 3)])
     other = send_core(part)
     bias_grad = part[width]
     self_grad = jnp.where(core == 0, part[:width], other[:width])

time: 130 us -> 127 us (0.977)
  waiting for transfers between devices: 63.3 us -> 50.7 us
  starting transfers between devices: 36.5 us -> 44.9 us
    all_to_all x1, waiting for transfers between devices: 17.6 us -> 0.01 us  [swap(): return lax.all_to_all(x, axis, 0, 0, tiled=True)]
    ppermute x12 -> x18, starting transfers between devices: 14.2 us -> 25.7 us  [send_node(): return lax.ppermute(x, 'nodes', moves)]
    ppermute x12 -> x18, waiting for transfers between devices: 25.9 us -> 29.5 us  [send_node(): return lax.ppermute(x, 'nodes', moves)]
    ppermute x9, waiting for transfers between devices: 17.6 us -> 20.2 us  [send_y(): return lax.ppermute(x, 'cols', along_y(step))]
    all_to_all x1, starting transfers between devices: 6.74 us -> 4.7 us  [swap(): return lax.all_to_all(x, axis, 0, 0, tiled=True)]
    ppermute x9, starting transfers between devices: 14.7 us -> 13.2 us  [send_y(): return lax.ppermute(x, 'cols', along_y(step))]
  transfers between devices with their start and end apart: 29 -> 35, of which waited for: 19 -> 16; matrix products, arithmetic and copies ran while one was open for 1% -> 1% of each run, Pallas kernels for 15% -> 15%
where the time goes in v5:
time: 127 us; the launch traced here: 126 us
  waiting for transfers between devices  50.7 us (40%)
  starting transfers between devices  44.9 us (35%)
  Pallas kernels  27 us (21%)
  local copies, waits for them, and re-layouts  1.5 us (1%)
    ppermute x18, waiting for transfers between devices, send_node(): return lax.ppermute(x, 'nodes', moves)  29.5 us
    ppermute x18, starting transfers between devices, send_node(): return lax.ppermute(x, 'nodes', moves)  25.7 us
    ppermute x9, waiting for transfers between devices, send_y(): return lax.ppermute(x, 'cols', along_y(step))  20.2 us
    ppermute x9, starting transfers between devices, send_y(): return lax.ppermute(x, 'cols', along_y(step))  13.2 us
    pallas_call x2, Pallas kernels, forward(): pl.pallas_call(forward_kernel, out_shape=jax.ShapeDtypeStruct((4, width +...  8.76 us
    pallas_call x1, Pallas kernels, build(): pl.pallas_call(build_kernel, out_shape=(jax.ShapeDtypeStruct((sources + 1...  8.24 us
    pallas_call x1, Pallas kernels, backward(): pl.pallas_call(backward_kernel, out_shape=in_hbm((sources * 128, width),...  6.76 us
    all_to_all x1, starting transfers between devices, swap(): return lax.all_to_all(x, axis, 0, 0, tiled=True)  4.7 us
  transfers between devices with their start and end apart: 35, of which 16 were waited for; matrix products, arithmetic and copies ran while one was open for 1% of the time, Pallas kernels for 15%

profile of v5, /device:TPU:0, one launch (start us, length us, event | category | flops | bytes accessed | tf_op | source)
XLA Modules:
  0.0 126.2 jit_solution(12244014517956700028)
XLA Ops:
  1.6 2.9 %collective-permute-start.2 = (bf16[128,256]{1,0:T(8,128)(2,1)S(1)}, bf16[128,256]{1,0:T(8,128)(2,1)S(1)}, u32[]{:S(2)}, u32[]{:S(2)}) collective-permute-start(bf16[128,256]{1,0:T(8,128)(2,1)S(1)} %get-tuple-element.34), channel_id=1, source_target_pairs={{0,96},{8,104},{16,112},{24,120},{32,0},{40,8},{48,16},{56,24},{64... | collective-permute-start | bytes 196616 | tf_op jit(solution)/shard_map/ppermute | solution.py:383
  6.2 4.0 %collective-permute-start.5 = (bf16[128,256]{1,0:T(8,128)(2,1)S(1)}, bf16[128,256]{1,0:T(8,128)(2,1)S(1)}, u32[]{:S(2)}, u32[]{:S(2)}) collective-permute-start(bf16[128,256]{1,0:T(8,128)(2,1)S(1)} %get-tuple-element.35), channel_id=1, source_target_pairs={{0,24},{8,0},{16,8},{24,16},{32,56},{40,32},{48,40},{56,48},{64,88... | collective-permute-start | bytes 196616 | tf_op jit(solution)/shard_map/ppermute | solution.py:383
  12.2 4.0 %collective-permute-done.4 = bf16[128,256]{1,0:T(8,128)(2,1)S(1)} collective-permute-done((bf16[128,256]{1,0:T(8,128)(2,1)S(1)}, bf16[128,256]{1,0:T(8,128)(2,1)S(1)}, u32[]{:S(2)}, u32[]{:S(2)}) %collective-permute-start.4) | collective-permute-done | bytes 65568 | tf_op jit(solution)/shard_map/ppermute | solution.py:383
  16.6 2.4 %collective-permute-start.11 = (bf16[4,128,256]{2,1,0:T(8,128)(2,1)S(1)}, bf16[4,128,256]{2,1,0:T(8,128)(2,1)S(1)}, u32[]{:S(2)}, u32[]{:S(2)}) collective-permute-start(bf16[4,128,256]{2,1,0:T(8,128)(2,1)S(1)} %pad_maximum_fusion.1.refs_4_), channel_id=1, source_target_pairs={{0,96},{8,104},{16,112},{24,120},{32,0},{40,8},{48,16},{56,24},{64... | collective-permute-start | bytes 786440 | tf_op jit(solution)/shard_map/ppermute | solution.py:383
  22.1 5.8 %collective-permute-done.11.refs_7_ = bf16[4,128,256]{2,1,0:T(8,128)(2,1)S(1)} collective-permute-done((bf16[4,128,256]{2,1,0:T(8,128)(2,1)S(1)}, bf16[4,128,256]{2,1,0:T(8,128)(2,1)S(1)}, u32[]{:S(2)}, u32[]{:S(2)}) %collective-permute-start.11) | collective-permute-done | bytes 262176 | tf_op jit(solution)/shard_map/ppermute | solution.py:383
  27.9 8.2 %build.1 = (bf16[33,16,128,128]{3,2,1,0:T(8,128)(2,1)S(1)}, f32[1,2048]{1,0:T(1,128)S(1)}) custom-call(s32[1,352]{1,0:T(1,128)} %rows_ref.1, s32[1,352]{1,0:T(1,128)} %cols_ref.1, s32[1,352,16,128]{3,2,1,0:T(8,128)} %bits_all.1, bf16[4,128,256]{2,1,0:T(8,128)(2,1)S(1)} %pad_maximum_fusion.gate_ref.refs_0_), custom_call_target="tpu_custom_call" | custom-call | bytes 31457280 | tf_op jit(solution)/shard_map/build/pallas_call | solution.py:124
  36.2 4.4 %forward.3 = bf16[4,272,256]{2,1,0:T(8,128)(2,1)S(1)} custom-call(s32[4]{0:T(128)S(1)} %get-tuple-element.41.place_ref, bf16[4,128,256]{2,1,0:T(8,128)(2,1)S(1)} %pad_maximum_fusion.gate_ref.refs_0_, bf16[4,128,256]{2,1,0:T(8,128)(2,1)S(1)} %collective-permute-done.6.refs_1_, bf16[4,128,256]{2,1,0:T(8,128)(2,1)S(1)} %collective-permute-done.7.refs_2_, ...), custom_call_target="tpu_custom_call" | custom-call | flops 2147483648 | bytes 10485760 | tf_op jit(solution)/shard_map/forward/pallas_call | solution.py:197
  40.8 4.4 %forward.2.keep_ref = f32[4,272,256]{2,1,0:T(8,128)S(1)} custom-call(s32[4]{0:T(128)S(1)} %get-tuple-element.36.place_ref, bf16[4,128,256]{2,1,0:T(8,128)(2,1)S(1)} %pad_maximum_fusion.gate_ref.refs_0_, bf16[4,128,256]{2,1,0:T(8,128)(2,1)S(1)} %collective-permute-done.6.refs_1_, bf16[4,128,256]{2,1,0:T(8,128)(2,1)S(1)} %collective-permute-done.7.refs_2_, ...), custom_call_target="tpu_custom_call" | custom-call | flops 2147483648 | bytes 10485760 | tf_op jit(solution)/shard_map/forward/pallas_call | solution.py:197
  45.3 1.6 %collective-permute-start.13 = (bf16[272,256]{1,0:T(8,128)(2,1)S(1)}, bf16[272,256]{1,0:T(8,128)(2,1)S(1)}, u32[]{:S(2)}, u32[]{:S(2)}) collective-permute-start(bf16[272,256]{1,0:T(8,128)(2,1)S(1)} %get-tuple-element.43), channel_id=1, source_target_pairs={{0,2},{1,3},{2,4},{3,5},{4,6},{5,7},{6,0},{7,1},{8,10},{9,11},{10,... | collective-permute-start | bytes 417800 | tf_op jit(solution)/shard_map/ppermute | solution.py:390
  46.9 2.9 %collective-permute-start.14 = (bf16[272,256]{1,0:T(8,128)(2,1)S(1)}, bf16[272,256]{1,0:T(8,128)(2,1)S(1)}, u32[]{:S(2)}, u32[]{:S(2)}) collective-permute-start(bf16[272,256]{1,0:T(8,128)(2,1)S(1)} %get-tuple-element.44), channel_id=1, source_target_pairs={{0,4},{1,5},{2,6},{3,7},{4,0},{5,1},{6,2},{7,3},{8,12},{9,13},{10,... | collective-permute-start | bytes 417800 | tf_op jit(solution)/shard_map/ppermute | solution.py:390
  52.7 4.2 %collective-permute-done.14.r2_ref = bf16[272,256]{1,0:T(8,128)(2,1)S(1)} collective-permute-done((bf16[272,256]{1,0:T(8,128)(2,1)S(1)}, bf16[272,256]{1,0:T(8,128)(2,1)S(1)}, u32[]{:S(2)}, u32[]{:S(2)}) %collective-permute-start.14) | collective-permute-done | bytes 139296 | tf_op jit(solution)/shard_map/ppermute | solution.py:390
  59.1 2.2 %collective-permute-start.18 = (bf16[256,256]{1,0:T(8,128)(2,1)S(1)}, bf16[256,256]{1,0:T(8,128)(2,1)S(1)}, u32[]{:S(2)}, u32[]{:S(2)}) collective-permute-start(bf16[256,256]{1,0:T(8,128)(2,1)S(1)} %get-tuple-element.52.refs_0_), channel_id=1, source_target_pairs={{0,6},{1,7},{2,0},{3,1},{4,2},{5,3},{6,4},{7,5},{8,14},{9,15},{10,... | collective-permute-start | bytes 393224 | tf_op jit(solution)/shard_map/ppermute | solution.py:390
  63.2 4.3 %collective-permute-done.18.refs_3_ = bf16[256,256]{1,0:T(8,128)(2,1)S(1)} collective-permute-done((bf16[256,256]{1,0:T(8,128)(2,1)S(1)}, bf16[256,256]{1,0:T(8,128)(2,1)S(1)}, u32[]{:S(2)}, u32[]{:S(2)}) %collective-permute-start.18) | collective-permute-done | bytes 131104 | tf_op jit(solution)/shard_map/ppermute | solution.py:390
  67.5 1.6 %collective-permute-done.17.refs_2_ = bf16[256,256]{1,0:T(8,128)(2,1)S(1)} collective-permute-done((bf16[256,256]{1,0:T(8,128)(2,1)S(1)}, bf16[256,256]{1,0:T(8,128)(2,1)S(1)}, u32[]{:S(2)}, u32[]{:S(2)}) %collective-permute-start.17) | collective-permute-done | bytes 131104 | tf_op jit(solution)/shard_map/ppermute | solution.py:390
  69.2 2.0 %collective-permute-done.16.refs_1_ = bf16[256,256]{1,0:T(8,128)(2,1)S(1)} collective-permute-done((bf16[256,256]{1,0:T(8,128)(2,1)S(1)}, bf16[256,256]{1,0:T(8,128)(2,1)S(1)}, u32[]{:S(2)}, u32[]{:S(2)}) %collective-permute-start.16) | collective-permute-done | bytes 131104 | tf_op jit(solution)/shard_map/ppermute | solution.py:390
  72.2 3.7 %collective-permute-start.26 = (bf16[272,256]{1,0:T(8,128)(2,1)S(1)}, bf16[272,256]{1,0:T(8,128)(2,1)S(1)}, u32[]{:S(2)}, u32[]{:S(2)}) collective-permute-start(bf16[272,256]{1,0:T(8,128)(2,1)S(1)} %add_convert_fusion.2), channel_id=1, source_target_pairs={{0,96},{8,104},{16,112},{24,120},{32,0},{40,8},{48,16},{56,24},{64... | collective-permute-start | bytes 417800 | tf_op jit(solution)/shard_map/ppermute | solution.py:383
  77.1 6.8 %backward.1 = bf16[4096,256]{1,0:T(8,128)(2,1)} custom-call(s32[4]{0:T(128)S(1)} %get-tuple-element.36.place_ref, bf16[256,256]{1,0:T(8,128)(2,1)S(1)} %get-tuple-element.52.refs_0_, bf16[256,256]{1,0:T(8,128)(2,1)S(1)} %collective-permute-done.16.refs_1_, bf16[256,256]{1,0:T(8,128)(2,1)S(1)} %collective-permute-done.17.refs_2_, ...), custom_call_target="tpu_custom_call" | custom-call | flops 4294967296 | bytes 20971520 | tf_op jit(solution)/shard_map/backward/pallas_call | solution.py:238
  84.0 1.7 %collective-permute-done.24 = bf16[272,256]{1,0:T(8,128)(2,1)S(1)} collective-permute-done((bf16[272,256]{1,0:T(8,128)(2,1)S(1)}, bf16[272,256]{1,0:T(8,128)(2,1)S(1)}, u32[]{:S(2)}, u32[]{:S(2)}) %collective-permute-start.24) | collective-permute-done | bytes 139296 | tf_op jit(solution)/shard_map/ppermute | solution.py:383
  85.7 4.7 %all-to-all-start = ((bf16[16,256,256]{2,1,0:T(8,128)(2,1)}), bf16[16,256,256]{2,1,0:T(8,128)(2,1)S(1)}, u32[]{:S(2)}, u32[]{:S(2)}) async-start(bf16[16,256,256]{2,1,0:T(8,128)(2,1)} %bitcast.19), calls=%async_computation | async-start | bytes 4194304 | tf_op jit(solution)/shard_map/all_to_all | solution.py:372
  93.7 3.0 %collective-permute-done.29 = bf16[272,256]{1,0:T(8,128)(2,1)S(1)} collective-permute-done((bf16[272,256]{1,0:T(8,128)(2,1)S(1)}, bf16[272,256]{1,0:T(8,128)(2,1)S(1)}, u32[]{:S(2)}, u32[]{:S(2)}) %collective-permute-start.29) | collective-permute-done | bytes 139296 | tf_op jit(solution)/shard_map/ppermute | solution.py:390
  96.7 3.5 %collective-permute-done.28 = bf16[272,256]{1,0:T(8,128)(2,1)S(1)} collective-permute-done((bf16[272,256]{1,0:T(8,128)(2,1)S(1)}, bf16[272,256]{1,0:T(8,128)(2,1)S(1)}, u32[]{:S(2)}, u32[]{:S(2)}) %collective-permute-start.28) | collective-permute-done | bytes 139296 | tf_op jit(solution)/shard_map/ppermute | solution.py:390
  100.3 3.1 %collective-permute-start.32 = (bf16[272,256]{1,0:T(8,128)(2,1)S(1)}, bf16[272,256]{1,0:T(8,128)(2,1)S(1)}, u32[]{:S(2)}, u32[]{:S(2)}) collective-permute-start(bf16[272,256]{1,0:T(8,128)(2,1)S(1)} %add_convert_fusion), channel_id=1, source_target_pairs={{0,24},{8,0},{16,8},{24,16},{32,56},{40,32},{48,40},{56,48},{64,88... | collective-permute-start | bytes 417800 | tf_op jit(solution)/shard_map/ppermute | solution.py:383
  103.4 2.3 %collective-permute-start.30 = (bf16[272,256]{1,0:T(8,128)(2,1)S(1)}, bf16[272,256]{1,0:T(8,128)(2,1)S(1)}, u32[]{:S(2)}, u32[]{:S(2)}) collective-permute-start(bf16[272,256]{1,0:T(8,128)(2,1)S(1)} %add_convert_fusion), channel_id=1, source_target_pairs={{0,16},{8,24},{16,0},{24,8},{32,48},{40,56},{48,32},{56,40},{64,80... | collective-permute-start | bytes 417800 | tf_op jit(solution)/shard_map/ppermute | solution.py:383
  105.7 15.4 %collective-permute-done.32 = bf16[272,256]{1,0:T(8,128)(2,1)S(1)} collective-permute-done((bf16[272,256]{1,0:T(8,128)(2,1)S(1)}, bf16[272,256]{1,0:T(8,128)(2,1)S(1)}, u32[]{:S(2)}, u32[]{:S(2)}) %collective-permute-start.32) | collective-permute-done | bytes 139296 | tf_op jit(solution)/shard_map/ppermute | solution.py:383
  (76 shorter events, 26.1 us)
Async XLA Ops:
  1.6 8.7 %collective-permute-start.2 = (bf16[128,256]{1,0:T(8,128)(2,1)S(1)}, bf16[128,256]{1,0:T(8,128)(2,1)S(1)}, u32[]{:S(2)}, u32[]{:S(2)}) collective-permute-start(bf16[128,256]{1,0:T(8,128)(2,1)S(1)} %get-tuple-element.34), channel_id=1, source_target_pairs={{0,96},{8,104},{16,112},{24,120},{32,0},{40,8},{48,16},{56,24},{64... | collective-permute-start | bytes 196616 | tf_op jit(solution)/shard_map/ppermute | solution.py:383
  4.5 7.1 %collective-permute-start.1 = (bf16[128,256]{1,0:T(8,128)(2,1)S(1)}, bf16[128,256]{1,0:T(8,128)(2,1)S(1)}, u32[]{:S(2)}, u32[]{:S(2)}) collective-permute-start(bf16[128,256]{1,0:T(8,128)(2,1)S(1)} %get-tuple-element.34), channel_id=1, source_target_pairs={{0,64},{8,72},{16,80},{24,88},{32,96},{40,104},{48,112},{56,120},{... | collective-permute-start | bytes 196616 | tf_op jit(solution)/shard_map/ppermute | solution.py:383
  5.3 6.3 %collective-permute-start = (bf16[128,256]{1,0:T(8,128)(2,1)S(1)}, bf16[128,256]{1,0:T(8,128)(2,1)S(1)}, u32[]{:S(2)}, u32[]{:S(2)}) collective-permute-start(bf16[128,256]{1,0:T(8,128)(2,1)S(1)} %get-tuple-element.34), channel_id=1, source_target_pairs={{0,32},{8,40},{16,48},{24,56},{32,64},{40,72},{48,80},{56,88},{64,... | collective-permute-start | bytes 196616 | tf_op jit(solution)/shard_map/ppermute | solution.py:383
  16.6 11.4 %collective-permute-start.11 = (bf16[4,128,256]{2,1,0:T(8,128)(2,1)S(1)}, bf16[4,128,256]{2,1,0:T(8,128)(2,1)S(1)}, u32[]{:S(2)}, u32[]{:S(2)}) collective-permute-start(bf16[4,128,256]{2,1,0:T(8,128)(2,1)S(1)} %pad_maximum_fusion.1.refs_4_), channel_id=1, source_target_pairs={{0,96},{8,104},{16,112},{24,120},{32,0},{40,8},{48,16},{56,24},{64... | collective-permute-start | bytes 786440 | tf_op jit(solution)/shard_map/ppermute | solution.py:383
  19.0 17.2 %collective-permute-start.10 = (bf16[4,128,256]{2,1,0:T(8,128)(2,1)S(1)}, bf16[4,128,256]{2,1,0:T(8,128)(2,1)S(1)}, u32[]{:S(2)}, u32[]{:S(2)}) collective-permute-start(bf16[4,128,256]{2,1,0:T(8,128)(2,1)S(1)} %pad_maximum_fusion.1.refs_4_), channel_id=1, source_target_pairs={{0,64},{8,72},{16,80},{24,88},{32,96},{40,104},{48,112},{56,120},{... | collective-permute-start | bytes 786440 | tf_op jit(solution)/shard_map/ppermute | solution.py:383
  20.5 15.7 %collective-permute-start.9 = (bf16[4,128,256]{2,1,0:T(8,128)(2,1)S(1)}, bf16[4,128,256]{2,1,0:T(8,128)(2,1)S(1)}, u32[]{:S(2)}, u32[]{:S(2)}) collective-permute-start(bf16[4,128,256]{2,1,0:T(8,128)(2,1)S(1)} %pad_maximum_fusion.1.refs_4_), channel_id=1, source_target_pairs={{0,32},{8,40},{16,48},{24,56},{32,64},{40,72},{48,80},{56,88},{64,... | collective-permute-start | bytes 786440 | tf_op jit(solution)/shard_map/ppermute | solution.py:383
  20.5 15.7 %collective-permute-start.8 = (bf16[4,128,256]{2,1,0:T(8,128)(2,1)S(1)}, bf16[4,128,256]{2,1,0:T(8,128)(2,1)S(1)}, u32[]{:S(2)}, u32[]{:S(2)}) collective-permute-start(bf16[4,128,256]{2,1,0:T(8,128)(2,1)S(1)} %pad_maximum_fusion.gate_ref.refs_0_), channel_id=1, source_target_pairs={{0,24},{8,0},{16,8},{24,16},{32,56},{40,32},{48,40},{56,48},{64,88... | collective-permute-start | bytes 786440 | tf_op jit(solution)/shard_map/ppermute | solution.py:383
  21.3 14.9 %collective-permute-start.7 = (bf16[4,128,256]{2,1,0:T(8,128)(2,1)S(1)}, bf16[4,128,256]{2,1,0:T(8,128)(2,1)S(1)}, u32[]{:S(2)}, u32[]{:S(2)}) collective-permute-start(bf16[4,128,256]{2,1,0:T(8,128)(2,1)S(1)} %pad_maximum_fusion.gate_ref.refs_0_), channel_id=1, source_target_pairs={{0,16},{8,24},{16,0},{24,8},{32,48},{40,56},{48,32},{56,40},{64,80... | collective-permute-start | bytes 786440 | tf_op jit(solution)/shard_map/ppermute | solution.py:383
  27.9 8.3 %collective-permute-start.6 = (bf16[4,128,256]{2,1,0:T(8,128)(2,1)S(1)}, bf16[4,128,256]{2,1,0:T(8,128)(2,1)S(1)}, u32[]{:S(2)}, u32[]{:S(2)}) collective-permute-start(bf16[4,128,256]{2,1,0:T(8,128)(2,1)S(1)} %pad_maximum_fusion.gate_ref.refs_0_), channel_id=1, source_target_pairs={{0,8},{8,16},{16,24},{24,0},{32,40},{40,48},{48,56},{56,32},{64,72... | collective-permute-start | bytes 786440 | tf_op jit(solution)/shard_map/ppermute | solution.py:383
  45.3 7.4 %collective-permute-start.13 = (bf16[272,256]{1,0:T(8,128)(2,1)S(1)}, bf16[272,256]{1,0:T(8,128)(2,1)S(1)}, u32[]{:S(2)}, u32[]{:S(2)}) collective-permute-start(bf16[272,256]{1,0:T(8,128)(2,1)S(1)} %get-tuple-element.43), channel_id=1, source_target_pairs={{0,2},{1,3},{2,4},{3,5},{4,6},{5,7},{6,0},{7,1},{8,10},{9,11},{10,... | collective-permute-start | bytes 417800 | tf_op jit(solution)/shard_map/ppermute | solution.py:390
  46.9 9.9 %collective-permute-start.14 = (bf16[272,256]{1,0:T(8,128)(2,1)S(1)}, bf16[272,256]{1,0:T(8,128)(2,1)S(1)}, u32[]{:S(2)}, u32[]{:S(2)}) collective-permute-start(bf16[272,256]{1,0:T(8,128)(2,1)S(1)} %get-tuple-element.44), channel_id=1, source_target_pairs={{0,4},{1,5},{2,6},{3,7},{4,0},{5,1},{6,2},{7,3},{8,12},{9,13},{10,... | collective-permute-start | bytes 417800 | tf_op jit(solution)/shard_map/ppermute | solution.py:390
  49.8 7.0 %collective-permute-start.15 = (bf16[272,256]{1,0:T(8,128)(2,1)S(1)}, bf16[272,256]{1,0:T(8,128)(2,1)S(1)}, u32[]{:S(2)}, u32[]{:S(2)}) collective-permute-start(bf16[272,256]{1,0:T(8,128)(2,1)S(1)} %get-tuple-element.45), channel_id=1, source_target_pairs={{0,6},{1,7},{2,0},{3,1},{4,2},{5,3},{6,4},{7,5},{8,14},{9,15},{10,... | collective-permute-start | bytes 417800 | tf_op jit(solution)/shard_map/ppermute | solution.py:390
  59.1 8.4 %collective-permute-start.18 = (bf16[256,256]{1,0:T(8,128)(2,1)S(1)}, bf16[256,256]{1,0:T(8,128)(2,1)S(1)}, u32[]{:S(2)}, u32[]{:S(2)}) collective-permute-start(bf16[256,256]{1,0:T(8,128)(2,1)S(1)} %get-tuple-element.52.refs_0_), channel_id=1, source_target_pairs={{0,6},{1,7},{2,0},{3,1},{4,2},{5,3},{6,4},{7,5},{8,14},{9,15},{10,... | collective-permute-start | bytes 393224 | tf_op jit(solution)/shard_map/ppermute | solution.py:390
  61.3 7.8 %collective-permute-start.17 = (bf16[256,256]{1,0:T(8,128)(2,1)S(1)}, bf16[256,256]{1,0:T(8,128)(2,1)S(1)}, u32[]{:S(2)}, u32[]{:S(2)}) collective-permute-start(bf16[256,256]{1,0:T(8,128)(2,1)S(1)} %get-tuple-element.52.refs_0_), channel_id=1, source_target_pairs={{0,4},{1,5},{2,6},{3,7},{4,0},{5,1},{6,2},{7,3},{8,12},{9,13},{10,... | collective-permute-start | bytes 393224 | tf_op jit(solution)/shard_map/ppermute | solution.py:390
  62.5 8.7 %collective-permute-start.16 = (bf16[256,256]{1,0:T(8,128)(2,1)S(1)}, bf16[256,256]{1,0:T(8,128)(2,1)S(1)}, u32[]{:S(2)}, u32[]{:S(2)}) collective-permute-start(bf16[256,256]{1,0:T(8,128)(2,1)S(1)} %get-tuple-element.52.refs_0_), channel_id=1, source_target_pairs={{0,2},{1,3},{2,4},{3,5},{4,6},{5,7},{6,0},{7,1},{8,10},{9,11},{10,... | collective-permute-start | bytes 393224 | tf_op jit(solution)/shard_map/ppermute | solution.py:390
  72.2 11.6 %collective-permute-start.26 = (bf16[272,256]{1,0:T(8,128)(2,1)S(1)}, bf16[272,256]{1,0:T(8,128)(2,1)S(1)}, u32[]{:S(2)}, u32[]{:S(2)}) collective-permute-start(bf16[272,256]{1,0:T(8,128)(2,1)S(1)} %add_convert_fusion.2), channel_id=1, source_target_pairs={{0,96},{8,104},{16,112},{24,120},{32,0},{40,8},{48,16},{56,24},{64... | collective-permute-start | bytes 417800 | tf_op jit(solution)/shard_map/ppermute | solution.py:383
  75.9 8.1 %collective-permute-start.25 = (bf16[272,256]{1,0:T(8,128)(2,1)S(1)}, bf16[272,256]{1,0:T(8,128)(2,1)S(1)}, u32[]{:S(2)}, u32[]{:S(2)}) collective-permute-start(bf16[272,256]{1,0:T(8,128)(2,1)S(1)} %add_convert_fusion.2), channel_id=1, source_target_pairs={{0,64},{8,72},{16,80},{24,88},{32,96},{40,104},{48,112},{56,120},{... | collective-permute-start | bytes 417800 | tf_op jit(solution)/shard_map/ppermute | solution.py:383
  76.2 9.5 %collective-permute-start.24 = (bf16[272,256]{1,0:T(8,128)(2,1)S(1)}, bf16[272,256]{1,0:T(8,128)(2,1)S(1)}, u32[]{:S(2)}, u32[]{:S(2)}) collective-permute-start(bf16[272,256]{1,0:T(8,128)(2,1)S(1)} %add_convert_fusion.2), channel_id=1, source_target_pairs={{0,32},{8,40},{16,48},{24,56},{32,64},{40,72},{48,80},{56,88},{64,... | collective-permute-start | bytes 417800 | tf_op jit(solution)/shard_map/ppermute | solution.py:383
  85.7 39.5 %all-to-all-start = ((bf16[16,256,256]{2,1,0:T(8,128)(2,1)}), bf16[16,256,256]{2,1,0:T(8,128)(2,1)S(1)}, u32[]{:S(2)}, u32[]{:S(2)}) async-start(bf16[16,256,256]{2,1,0:T(8,128)(2,1)} %bitcast.19), calls=%async_computation | async-start | bytes 4194304 | tf_op jit(solution)/shard_map/all_to_all | solution.py:372
  91.1 9.1 %collective-permute-start.28 = (bf16[272,256]{1,0:T(8,128)(2,1)S(1)}, bf16[272,256]{1,0:T(8,128)(2,1)S(1)}, u32[]{:S(2)}, u32[]{:S(2)}) collective-permute-start(bf16[272,256]{1,0:T(8,128)(2,1)S(1)} %add_convert_fusion.1), channel_id=1, source_target_pairs={{0,2},{1,3},{2,4},{3,5},{4,6},{5,7},{6,0},{7,1},{8,10},{9,11},{10,... | collective-permute-start | bytes 417800 | tf_op jit(solution)/shard_map/ppermute | solution.py:390
  92.6 7.7 %collective-permute-start.27 = (bf16[272,256]{1,0:T(8,128)(2,1)S(1)}, bf16[272,256]{1,0:T(8,128)(2,1)S(1)}, u32[]{:S(2)}, u32[]{:S(2)}) collective-permute-start(bf16[272,256]{1,0:T(8,128)(2,1)S(1)} %add_convert_fusion.1), channel_id=1, source_target_pairs={{0,4},{1,5},{2,6},{3,7},{4,0},{5,1},{6,2},{7,3},{8,12},{9,13},{10,... | collective-permute-start | bytes 417800 | tf_op jit(solution)/shard_map/ppermute | solution.py:390
  100.3 20.8 %collective-permute-start.32 = (bf16[272,256]{1,0:T(8,128)(2,1)S(1)}, bf16[272,256]{1,0:T(8,128)(2,1)S(1)}, u32[]{:S(2)}, u32[]{:S(2)}) collective-permute-start(bf16[272,256]{1,0:T(8,128)(2,1)S(1)} %add_convert_fusion), channel_id=1, source_target_pairs={{0,24},{8,0},{16,8},{24,16},{32,56},{40,32},{48,40},{56,48},{64,88... | collective-permute-start | bytes 417800 | tf_op jit(solution)/shard_map/ppermute | solution.py:383
  103.4 17.7 %collective-permute-start.31 = (bf16[272,256]{1,0:T(8,128)(2,1)S(1)}, bf16[272,256]{1,0:T(8,128)(2,1)S(1)}, u32[]{:S(2)}, u32[]{:S(2)}) collective-permute-start(bf16[272,256]{1,0:T(8,128)(2,1)S(1)} %add_convert_fusion), channel_id=1, source_target_pairs={{0,8},{8,16},{16,24},{24,0},{32,40},{40,48},{48,56},{56,32},{64,72... | collective-permute-start | bytes 417800 | tf_op jit(solution)/shard_map/ppermute | solution.py:383
  103.4 19.3 %collective-permute-start.30 = (bf16[272,256]{1,0:T(8,128)(2,1)S(1)}, bf16[272,256]{1,0:T(8,128)(2,1)S(1)}, u32[]{:S(2)}, u32[]{:S(2)}) collective-permute-start(bf16[272,256]{1,0:T(8,128)(2,1)S(1)} %add_convert_fusion), channel_id=1, source_target_pairs={{0,16},{8,24},{16,0},{24,8},{32,48},{40,56},{48,32},{56,40},{64,80... | collective-permute-start | bytes 417800 | tf_op jit(solution)/shard_map/ppermute | solution.py:383
  (17 other events, 137.0 us)

commit v6 on v5

--- a/solution.py
+++ b/solution.py
@@ -314,41 +314,29 @@
     )(own, *got, x, ws, wn, bias, cot)
 
 
-def weights_kernel(place_ref, x_ref, pre_ref, mean_ref, ws_ref, keep_ref, give_ref, self_ref):
+def weights_kernel(x_ref, pre_ref, mean_ref, ws_ref, part_ref, self_ref):
     n = x_ref.shape[0]
     pre_grad = pre_ref[...]
-    grads = (
-        dot_on(x_ref[...], pre_grad, 0, 0),
-        jnp.dot(mean_ref[...], pre_grad, preferred_element_type=F32),
-    )
+    part_ref[0:n, :] = dot_on(x_ref[...], pre_grad, 0, 0).astype(BF)
+    neigh_grad = jnp.dot(mean_ref[...], pre_grad, preferred_element_type=F32)
+    part_ref[n : 2 * n, :] = neigh_grad.astype(BF)
     bias_grad = jnp.sum(pre_grad.astype(F32), axis=0, keepdims=True)
-    first = lax.broadcasted_iota(jnp.int32, (16, 1), 0) == 0
-    bias_rows = jnp.where(first, bias_grad, 0.0)
-    for core in range(2):
-
-        @pl.when(place_ref[1] == core)
-        def _():
-            keep_ref[0:n, :] = grads[core]
-            give_ref[0:n, :] = grads[1 - core]
-
-    keep_ref[n : n + 16, :] = bias_rows
-    give_ref[n : n + 16, :] = bias_rows
+    part_ref[2 * n :, :] = spaced(bias_grad, BF)
     self_ref[...] = dot_on(pre_grad, ws_ref[...], 1, 1)
 
 
-def weights(place, x, pre_grad, mean_t, ws):
+def weights(x, pre_grad, mean_t, ws):
     n = x.shape[0]
-    half = jax.ShapeDtypeStruct((n + 16, n), F32)
-    vmem = pl.BlockSpec(memory_space=pltpu.VMEM)
     return pl.pallas_call(
         weights_kernel,
-        out_shape=(half, half, jax.ShapeDtypeStruct((n, n), F32)),
-        in_specs=[pl.BlockSpec(memory_space=pltpu.SMEM)] + [vmem] * 4,
-        out_specs=(vmem, vmem, vmem),
+        out_shape=(
+            jax.ShapeDtypeStruct((2 * n + EXTRA, n), BF),
+            jax.ShapeDtypeStruct((n, n), F32),
+        ),
         compiler_params=params(16),
         cost_estimate=cost(6 * n * n * n, 2 << 20),
         name="weights",
-    )(place, x, pre_grad, mean_t, ws)
+    )(x, pre_grad, mean_t, ws)
 
 
 def finish_kernel(parts_ref, self_ref, out_ref):
@@ -380,6 +368,11 @@
     moves = [
         (4 * i + j, 4 * ((i + dx) % 4) + (j + dz) % 4) for i in range(4) for j in range(4)
     ]
+    return lax.ppermute(x, "nodes", moves)
+
+
+def send_flip(x, bit):
+    moves = [(4 * i + j, 4 * (i ^ bit) + j) for i in range(4) for j in range(4)]
     return lax.ppermute(x, "nodes", moves)
 
 
@@ -419,7 +412,7 @@
     top, low = prepare(node_feats)
     top = jnp.stack([top] + [send_x(top, k) for k in (1, 2, 3)])
     low = jnp.stack([low] + [send_z(low, k) for k in (1, 2, 3)])
-    top, low, mine, theirs = lax.optimization_barrier((top, low, mine, theirs))
+    top, low, mine, theirs, zero = lax.optimization_barrier((top, low, mine, theirs, core == 0))
     planes = [top] + [send_z(top, k) for k in (1, 2, 3)]
     planes += [low] + [send_x(low, k) for k in (1, 2, 3)]
     at, degree = build(
@@ -438,23 +431,26 @@
     )
     same_core = [mean_grad] + [send_y(mean_grad, k) for k in (1, 2, 3)]
 
-    part, give_part, self_part = weights(mine, node_feats, pre_grad, mean_t, w_self)
-    part = (part + send_core(give_part)).astype(BF)
-    *same_core, part = lax.optimization_barrier((*same_core, part))
+    part, self_part = weights(node_feats, pre_grad, mean_t, w_self)
+    part = (part.astype(F32) + send_flip(part, 1).astype(F32)).astype(BF)
     other_core = [send_core(g) for g in same_core]
-    terms = [part] + [send_x(part, k) for k in (1, 2, 3)]
+    flipped = send_flip(part, 2)
 
     src = backward(mine, same_core + other_core, at)
-    src, terms = lax.optimization_barrier((src, terms))
+    src, part, flipped = lax.optimization_barrier((src, part, flipped))
     parts = swap(src.reshape(nodes, rows_dev, width), "nodes")
 
-    part = add_terms(terms).astype(BF)
+    part = (part.astype(F32) + flipped.astype(F32)).astype(BF)
+    halves = (part[:width], part[width : 2 * width])
+    kept = jnp.concatenate([jnp.where(zero, *halves), part[2 * width :]])
+    given = jnp.concatenate([jnp.where(zero, *halves[::-1]), part[2 * width :]])
+    part = (kept.astype(F32) + send_core(given).astype(F32)).astype(BF)
     part = add_terms([part] + [send_y(part, k) for k in (1, 2, 3)]).astype(BF)
     part = add_terms([part] + [send_z(part, k) for k in (1, 2, 3)])
     other = send_core(part)
     bias_grad = part[width]
-    self_grad = jnp.where(core == 0, part[:width], other[:width])
-    neigh_grad = jnp.where(core == 0, other[:width], part[:width])
+    self_grad = jnp.where(zero, part[:width], other[:width])
+    neigh_grad = jnp.where(zero, other[:width], part[:width])
 
     feat_grad = finish(parts, self_part)
     return (layer_out, feat_grad, self_grad, neigh_grad, bias_grad)

time: 127 us -> 127 us (level)
  starting transfers between devices: 44.9 us -> 46.6 us
  waiting for transfers between devices: 50.7 us -> 49 us
    ppermute x0 -> x2, starting transfers between devices: none -> 5.47 us  [send_flip(): return lax.ppermute(x, 'nodes', moves)]
    ppermute x18 -> x15, starting transfers between devices: 25.7 us -> 21 us  [send_node(): return lax.ppermute(x, 'nodes', moves)]
    ppermute x18 -> x15, waiting for transfers between devices: 29.5 us -> 25.8 us  [send_node(): return lax.ppermute(x, 'nodes', moves)]
    all_to_all x1, starting transfers between devices: 4.7 us -> 7.27 us  [swap(): return lax.all_to_all(x, axis, 0, 0, tiled=True)]
    ppermute x7, waiting for transfers between devices: 0.99 us -> 2.34 us  [send_core(): return lax.ppermute(x, 'cols', PARTNER)]
  transfers between devices with their start and end apart: 35 -> 34, of which waited for: 16 -> 16; matrix products, arithmetic and copies ran while one was open for 1% -> 1% of each run, Pallas kernels for 15% -> 15%
where the time goes in v6:
time: 127 us; the launch traced here: 126 us
  waiting for transfers between devices  49 us (39%)
  starting transfers between devices  46.6 us (37%)
  Pallas kernels  26.2 us (21%)
  local copies, waits for them, and re-layouts  1.5 us (1%)
  other arithmetic  1.33 us (1%)
    ppermute x15, waiting for transfers between devices, send_node(): return lax.ppermute(x, 'nodes', moves)  25.8 us
    ppermute x15, starting transfers between devices, send_node(): return lax.ppermute(x, 'nodes', moves)  21 us
    ppermute x9, waiting for transfers between devices, send_y(): return lax.ppermute(x, 'cols', along_y(step))  20.4 us
    ppermute x9, starting transfers between devices, send_y(): return lax.ppermute(x, 'cols', along_y(step))  12.6 us
    pallas_call x2, Pallas kernels, forward(): pl.pallas_call(forward_kernel, out_shape=jax.ShapeDtypeStruct((4, width +...  8.76 us
    pallas_call x1, Pallas kernels, build(): pl.pallas_call(build_kernel, out_shape=(jax.ShapeDtypeStruct((sources + 1...  8.24 us
    all_to_all x1, starting transfers between devices, swap(): return lax.all_to_all(x, axis, 0, 0, tiled=True)  7.27 us
    pallas_call x1, Pallas kernels, backward(): pl.pallas_call(backward_kernel, out_shape=in_hbm((sources * 128, width),...  6.76 us
  transfers between devices with their start and end apart: 34, of which 16 were waited for; matrix products, arithmetic and copies ran while one was open for 1% of the time, Pallas kernels for 15%

profile of v6, /device:TPU:0, one launch (start us, length us, event | category | flops | bytes accessed | tf_op | source)
XLA Modules:
  0.0 125.6 jit_solution(9148429290556742116)
XLA Ops:
  1.6 2.9 %collective-permute-start.2 = (bf16[128,256]{1,0:T(8,128)(2,1)S(1)}, bf16[128,256]{1,0:T(8,128)(2,1)S(1)}, u32[]{:S(2)}, u32[]{:S(2)}) collective-permute-start(bf16[128,256]{1,0:T(8,128)(2,1)S(1)} %get-tuple-element.27), channel_id=1, source_target_pairs={{0,96},{8,104},{16,112},{24,120},{32,0},{40,8},{48,16},{56,24},{64... | collective-permute-start | bytes 196616 | tf_op jit(solution)/shard_map/ppermute | solution.py:371
  6.2 4.0 %collective-permute-start.5 = (bf16[128,256]{1,0:T(8,128)(2,1)S(1)}, bf16[128,256]{1,0:T(8,128)(2,1)S(1)}, u32[]{:S(2)}, u32[]{:S(2)}) collective-permute-start(bf16[128,256]{1,0:T(8,128)(2,1)S(1)} %get-tuple-element.28), channel_id=1, source_target_pairs={{0,24},{8,0},{16,8},{24,16},{32,56},{40,32},{48,40},{56,48},{64,88... | collective-permute-start | bytes 196616 | tf_op jit(solution)/shard_map/ppermute | solution.py:371
  12.2 4.0 %collective-permute-done.4 = bf16[128,256]{1,0:T(8,128)(2,1)S(1)} collective-permute-done((bf16[128,256]{1,0:T(8,128)(2,1)S(1)}, bf16[128,256]{1,0:T(8,128)(2,1)S(1)}, u32[]{:S(2)}, u32[]{:S(2)}) %collective-permute-start.4) | collective-permute-done | bytes 65568 | tf_op jit(solution)/shard_map/ppermute | solution.py:371
  16.6 2.4 %collective-permute-start.11 = (bf16[4,128,256]{2,1,0:T(8,128)(2,1)S(1)}, bf16[4,128,256]{2,1,0:T(8,128)(2,1)S(1)}, u32[]{:S(2)}, u32[]{:S(2)}) collective-permute-start(bf16[4,128,256]{2,1,0:T(8,128)(2,1)S(1)} %pad_maximum_fusion.1.refs_4_), channel_id=1, source_target_pairs={{0,96},{8,104},{16,112},{24,120},{32,0},{40,8},{48,16},{56,24},{64... | collective-permute-start | bytes 786440 | tf_op jit(solution)/shard_map/ppermute | solution.py:371
  22.1 5.8 %collective-permute-done.11.refs_7_ = bf16[4,128,256]{2,1,0:T(8,128)(2,1)S(1)} collective-permute-done((bf16[4,128,256]{2,1,0:T(8,128)(2,1)S(1)}, bf16[4,128,256]{2,1,0:T(8,128)(2,1)S(1)}, u32[]{:S(2)}, u32[]{:S(2)}) %collective-permute-start.11) | collective-permute-done | bytes 262176 | tf_op jit(solution)/shard_map/ppermute | solution.py:371
  27.9 8.2 %build.1 = (bf16[33,16,128,128]{3,2,1,0:T(8,128)(2,1)S(1)}, f32[1,2048]{1,0:T(1,128)S(1)}) custom-call(s32[1,352]{1,0:T(1,128)} %rows_ref.1, s32[1,352]{1,0:T(1,128)} %cols_ref.1, s32[1,352,16,128]{3,2,1,0:T(8,128)} %bits_all.1, bf16[4,128,256]{2,1,0:T(8,128)(2,1)S(1)} %pad_maximum_fusion.gate_ref.refs_0_), custom_call_target="tpu_custom_call" | custom-call | bytes 31457280 | tf_op jit(solution)/shard_map/build/pallas_call | solution.py:124
  36.2 4.4 %forward.3 = bf16[4,272,256]{2,1,0:T(8,128)(2,1)S(1)} custom-call(s32[4]{0:T(128)S(1)} %get-tuple-element.34.place_ref, bf16[4,128,256]{2,1,0:T(8,128)(2,1)S(1)} %pad_maximum_fusion.gate_ref.refs_0_, bf16[4,128,256]{2,1,0:T(8,128)(2,1)S(1)} %collective-permute-done.6.refs_1_, bf16[4,128,256]{2,1,0:T(8,128)(2,1)S(1)} %collective-permute-done.7.refs_2_, ...), custom_call_target="tpu_custom_call" | custom-call | flops 2147483648 | bytes 10485760 | tf_op jit(solution)/shard_map/forward/pallas_call | solution.py:197
  40.8 4.4 %forward.2.keep_ref = f32[4,272,256]{2,1,0:T(8,128)S(1)} custom-call(s32[4]{0:T(128)S(1)} %get-tuple-element.29.place_ref, bf16[4,128,256]{2,1,0:T(8,128)(2,1)S(1)} %pad_maximum_fusion.gate_ref.refs_0_, bf16[4,128,256]{2,1,0:T(8,128)(2,1)S(1)} %collective-permute-done.6.refs_1_, bf16[4,128,256]{2,1,0:T(8,128)(2,1)S(1)} %collective-permute-done.7.refs_2_, ...), custom_call_target="tpu_custom_call" | custom-call | flops 2147483648 | bytes 10485760 | tf_op jit(solution)/shard_map/forward/pallas_call | solution.py:197
  45.3 1.6 %collective-permute-start.13 = (bf16[272,256]{1,0:T(8,128)(2,1)S(1)}, bf16[272,256]{1,0:T(8,128)(2,1)S(1)}, u32[]{:S(2)}, u32[]{:S(2)}) collective-permute-start(bf16[272,256]{1,0:T(8,128)(2,1)S(1)} %get-tuple-element.36), channel_id=1, source_target_pairs={{0,2},{1,3},{2,4},{3,5},{4,6},{5,7},{6,0},{7,1},{8,10},{9,11},{10,... | collective-permute-start | bytes 417800 | tf_op jit(solution)/shard_map/ppermute | solution.py:383
  46.9 2.9 %collective-permute-start.14 = (bf16[272,256]{1,0:T(8,128)(2,1)S(1)}, bf16[272,256]{1,0:T(8,128)(2,1)S(1)}, u32[]{:S(2)}, u32[]{:S(2)}) collective-permute-start(bf16[272,256]{1,0:T(8,128)(2,1)S(1)} %get-tuple-element.37), channel_id=1, source_target_pairs={{0,4},{1,5},{2,6},{3,7},{4,0},{5,1},{6,2},{7,3},{8,12},{9,13},{10,... | collective-permute-start | bytes 417800 | tf_op jit(solution)/shard_map/ppermute | solution.py:383
  52.7 4.2 %collective-permute-done.14.r2_ref = bf16[272,256]{1,0:T(8,128)(2,1)S(1)} collective-permute-done((bf16[272,256]{1,0:T(8,128)(2,1)S(1)}, bf16[272,256]{1,0:T(8,128)(2,1)S(1)}, u32[]{:S(2)}, u32[]{:S(2)}) %collective-permute-start.14) | collective-permute-done | bytes 139296 | tf_op jit(solution)/shard_map/ppermute | solution.py:383
  58.3 2.0 %collective-permute-start.23 = (bf16[528,256]{1,0:T(8,128)(2,1)S(1)}, bf16[528,256]{1,0:T(8,128)(2,1)S(1)}, u32[]{:S(2)}, u32[]{:S(2)}) collective-permute-start(bf16[528,256]{1,0:T(8,128)(2,1)S(1)} %get-tuple-element.43), channel_id=1, source_target_pairs={{0,32},{8,40},{16,48},{24,56},{32,0},{40,8},{48,16},{56,24},{64,96... | collective-permute-start | bytes 811016 | tf_op jit(solution)/shard_map/ppermute | solution.py:376
  60.3 2.2 %collective-permute-start.18 = (bf16[256,256]{1,0:T(8,128)(2,1)S(1)}, bf16[256,256]{1,0:T(8,128)(2,1)S(1)}, u32[]{:S(2)}, u32[]{:S(2)}) collective-permute-start(bf16[256,256]{1,0:T(8,128)(2,1)S(1)} %get-tuple-element.40.refs_0_), channel_id=1, source_target_pairs={{0,6},{1,7},{2,0},{3,1},{4,2},{5,3},{6,4},{7,5},{8,14},{9,15},{10,... | collective-permute-start | bytes 393224 | tf_op jit(solution)/shard_map/ppermute | solution.py:383
  64.3 3.5 %collective-permute-done.18.refs_3_ = bf16[256,256]{1,0:T(8,128)(2,1)S(1)} collective-permute-done((bf16[256,256]{1,0:T(8,128)(2,1)S(1)}, bf16[256,256]{1,0:T(8,128)(2,1)S(1)}, u32[]{:S(2)}, u32[]{:S(2)}) %collective-permute-start.18) | collective-permute-done | bytes 131104 | tf_op jit(solution)/shard_map/ppermute | solution.py:383
  67.8 2.3 %collective-permute-done.17.refs_2_ = bf16[256,256]{1,0:T(8,128)(2,1)S(1)} collective-permute-done((bf16[256,256]{1,0:T(8,128)(2,1)S(1)}, bf16[256,256]{1,0:T(8,128)(2,1)S(1)}, u32[]{:S(2)}, u32[]{:S(2)}) %collective-permute-start.17) | collective-permute-done | bytes 131104 | tf_op jit(solution)/shard_map/ppermute | solution.py:383
  71.5 3.5 %collective-permute-start.24 = (bf16[528,256]{1,0:T(8,128)(2,1)S(1)}, bf16[528,256]{1,0:T(8,128)(2,1)S(1)}, u32[]{:S(2)}, u32[]{:S(2)}) collective-permute-start(bf16[528,256]{1,0:T(8,128)(2,1)S(1)} %add_convert_fusion.1), channel_id=1, source_target_pairs={{0,64},{8,72},{16,80},{24,88},{32,96},{40,104},{48,112},{56,120},{... | collective-permute-start | bytes 811016 | tf_op jit(solution)/shard_map/ppermute | solution.py:376
  75.0 6.8 %backward.1 = bf16[4096,256]{1,0:T(8,128)(2,1)} custom-call(s32[4]{0:T(128)S(1)} %get-tuple-element.29.place_ref, bf16[256,256]{1,0:T(8,128)(2,1)S(1)} %get-tuple-element.40.refs_0_, bf16[256,256]{1,0:T(8,128)(2,1)S(1)} %collective-permute-done.16.refs_1_, bf16[256,256]{1,0:T(8,128)(2,1)S(1)} %collective-permute-done.17.refs_2_, ...), custom_call_target="tpu_custom_call" | custom-call | flops 4294967296 | bytes 20971520 | tf_op jit(solution)/shard_map/backward/pallas_call | solution.py:238
  82.2 7.3 %all-to-all-start = ((bf16[16,256,256]{2,1,0:T(8,128)(2,1)}), bf16[16,256,256]{2,1,0:T(8,128)(2,1)S(1)}, u32[]{:S(2)}, u32[]{:S(2)}) async-start(bf16[16,256,256]{2,1,0:T(8,128)(2,1)} %bitcast.19), calls=%async_computation | async-start | bytes 4194304 | tf_op jit(solution)/shard_map/all_to_all | solution.py:360
  93.8 3.9 %collective-permute-done.28 = bf16[272,256]{1,0:T(8,128)(2,1)S(1)} collective-permute-done((bf16[272,256]{1,0:T(8,128)(2,1)S(1)}, bf16[272,256]{1,0:T(8,128)(2,1)S(1)}, u32[]{:S(2)}, u32[]{:S(2)}) %collective-permute-start.28) | collective-permute-done | bytes 139296 | tf_op jit(solution)/shard_map/ppermute | solution.py:383
  97.7 3.7 %collective-permute-done.27 = bf16[272,256]{1,0:T(8,128)(2,1)S(1)} collective-permute-done((bf16[272,256]{1,0:T(8,128)(2,1)S(1)}, bf16[272,256]{1,0:T(8,128)(2,1)S(1)}, u32[]{:S(2)}, u32[]{:S(2)}) %collective-permute-start.27) | collective-permute-done | bytes 139296 | tf_op jit(solution)/shard_map/ppermute | solution.py:383
  101.4 3.2 %collective-permute-start.31 = (bf16[272,256]{1,0:T(8,128)(2,1)S(1)}, bf16[272,256]{1,0:T(8,128)(2,1)S(1)}, u32[]{:S(2)}, u32[]{:S(2)}) collective-permute-start(bf16[272,256]{1,0:T(8,128)(2,1)S(1)} %add_convert_fusion.2), channel_id=1, source_target_pairs={{0,24},{8,0},{16,8},{24,16},{32,56},{40,32},{48,40},{56,48},{64,88... | collective-permute-start | bytes 417800 | tf_op jit(solution)/shard_map/ppermute | solution.py:371
  104.6 2.3 %collective-permute-start.29 = (bf16[272,256]{1,0:T(8,128)(2,1)S(1)}, bf16[272,256]{1,0:T(8,128)(2,1)S(1)}, u32[]{:S(2)}, u32[]{:S(2)}) collective-permute-start(bf16[272,256]{1,0:T(8,128)(2,1)S(1)} %add_convert_fusion.2), channel_id=1, source_target_pairs={{0,16},{8,24},{16,0},{24,8},{32,48},{40,56},{48,32},{56,40},{64,80... | collective-permute-start | bytes 417800 | tf_op jit(solution)/shard_map/ppermute | solution.py:371
  107.0 13.1 %collective-permute-done.31 = bf16[272,256]{1,0:T(8,128)(2,1)S(1)} collective-permute-done((bf16[272,256]{1,0:T(8,128)(2,1)S(1)}, bf16[272,256]{1,0:T(8,128)(2,1)S(1)}, u32[]{:S(2)}, u32[]{:S(2)}) %collective-permute-start.31) | collective-permute-done | bytes 139296 | tf_op jit(solution)/shard_map/ppermute | solution.py:371
  120.1 2.1 %collective-permute-done.29 = bf16[272,256]{1,0:T(8,128)(2,1)S(1)} collective-permute-done((bf16[272,256]{1,0:T(8,128)(2,1)S(1)}, bf16[272,256]{1,0:T(8,128)(2,1)S(1)}, u32[]{:S(2)}, u32[]{:S(2)}) %collective-permute-start.29) | collective-permute-done | bytes 139296 | tf_op jit(solution)/shard_map/ppermute | solution.py:371
  (78 shorter events, 24.1 us)
Async XLA Ops:
  1.6 8.7 %collective-permute-start.2 = (bf16[128,256]{1,0:T(8,128)(2,1)S(1)}, bf16[128,256]{1,0:T(8,128)(2,1)S(1)}, u32[]{:S(2)}, u32[]{:S(2)}) collective-permute-start(bf16[128,256]{1,0:T(8,128)(2,1)S(1)} %get-tuple-element.27), channel_id=1, source_target_pairs={{0,96},{8,104},{16,112},{24,120},{32,0},{40,8},{48,16},{56,24},{64... | collective-permute-start | bytes 196616 | tf_op jit(solution)/shard_map/ppermute | solution.py:371
  4.5 7.1 %collective-permute-start.1 = (bf16[128,256]{1,0:T(8,128)(2,1)S(1)}, bf16[128,256]{1,0:T(8,128)(2,1)S(1)}, u32[]{:S(2)}, u32[]{:S(2)}) collective-permute-start(bf16[128,256]{1,0:T(8,128)(2,1)S(1)} %get-tuple-element.27), channel_id=1, source_target_pairs={{0,64},{8,72},{16,80},{24,88},{32,96},{40,104},{48,112},{56,120},{... | collective-permute-start | bytes 196616 | tf_op jit(solution)/shard_map/ppermute | solution.py:371
  16.6 11.4 %collective-permute-start.11 = (bf16[4,128,256]{2,1,0:T(8,128)(2,1)S(1)}, bf16[4,128,256]{2,1,0:T(8,128)(2,1)S(1)}, u32[]{:S(2)}, u32[]{:S(2)}) collective-permute-start(bf16[4,128,256]{2,1,0:T(8,128)(2,1)S(1)} %pad_maximum_fusion.1.refs_4_), channel_id=1, source_target_pairs={{0,96},{8,104},{16,112},{24,120},{32,0},{40,8},{48,16},{56,24},{64... | collective-permute-start | bytes 786440 | tf_op jit(solution)/shard_map/ppermute | solution.py:371
  19.0 17.2 %collective-permute-start.10 = (bf16[4,128,256]{2,1,0:T(8,128)(2,1)S(1)}, bf16[4,128,256]{2,1,0:T(8,128)(2,1)S(1)}, u32[]{:S(2)}, u32[]{:S(2)}) collective-permute-start(bf16[4,128,256]{2,1,0:T(8,128)(2,1)S(1)} %pad_maximum_fusion.1.refs_4_), channel_id=1, source_target_pairs={{0,64},{8,72},{16,80},{24,88},{32,96},{40,104},{48,112},{56,120},{... | collective-permute-start | bytes 786440 | tf_op jit(solution)/shard_map/ppermute | solution.py:371
  20.5 15.7 %collective-permute-start.9 = (bf16[4,128,256]{2,1,0:T(8,128)(2,1)S(1)}, bf16[4,128,256]{2,1,0:T(8,128)(2,1)S(1)}, u32[]{:S(2)}, u32[]{:S(2)}) collective-permute-start(bf16[4,128,256]{2,1,0:T(8,128)(2,1)S(1)} %pad_maximum_fusion.1.refs_4_), channel_id=1, source_target_pairs={{0,32},{8,40},{16,48},{24,56},{32,64},{40,72},{48,80},{56,88},{64,... | collective-permute-start | bytes 786440 | tf_op jit(solution)/shard_map/ppermute | solution.py:371
  20.5 15.7 %collective-permute-start.8 = (bf16[4,128,256]{2,1,0:T(8,128)(2,1)S(1)}, bf16[4,128,256]{2,1,0:T(8,128)(2,1)S(1)}, u32[]{:S(2)}, u32[]{:S(2)}) collective-permute-start(bf16[4,128,256]{2,1,0:T(8,128)(2,1)S(1)} %pad_maximum_fusion.gate_ref.refs_0_), channel_id=1, source_target_pairs={{0,24},{8,0},{16,8},{24,16},{32,56},{40,32},{48,40},{56,48},{64,88... | collective-permute-start | bytes 786440 | tf_op jit(solution)/shard_map/ppermute | solution.py:371
  21.3 14.9 %collective-permute-start.7 = (bf16[4,128,256]{2,1,0:T(8,128)(2,1)S(1)}, bf16[4,128,256]{2,1,0:T(8,128)(2,1)S(1)}, u32[]{:S(2)}, u32[]{:S(2)}) collective-permute-start(bf16[4,128,256]{2,1,0:T(8,128)(2,1)S(1)} %pad_maximum_fusion.gate_ref.refs_0_), channel_id=1, source_target_pairs={{0,16},{8,24},{16,0},{24,8},{32,48},{40,56},{48,32},{56,40},{64,80... | collective-permute-start | bytes 786440 | tf_op jit(solution)/shard_map/ppermute | solution.py:371
  27.9 8.3 %collective-permute-start.6 = (bf16[4,128,256]{2,1,0:T(8,128)(2,1)S(1)}, bf16[4,128,256]{2,1,0:T(8,128)(2,1)S(1)}, u32[]{:S(2)}, u32[]{:S(2)}) collective-permute-start(bf16[4,128,256]{2,1,0:T(8,128)(2,1)S(1)} %pad_maximum_fusion.gate_ref.refs_0_), channel_id=1, source_target_pairs={{0,8},{8,16},{16,24},{24,0},{32,40},{40,48},{48,56},{56,32},{64,72... | collective-permute-start | bytes 786440 | tf_op jit(solution)/shard_map/ppermute | solution.py:371
  45.3 7.4 %collective-permute-start.13 = (bf16[272,256]{1,0:T(8,128)(2,1)S(1)}, bf16[272,256]{1,0:T(8,128)(2,1)S(1)}, u32[]{:S(2)}, u32[]{:S(2)}) collective-permute-start(bf16[272,256]{1,0:T(8,128)(2,1)S(1)} %get-tuple-element.36), channel_id=1, source_target_pairs={{0,2},{1,3},{2,4},{3,5},{4,6},{5,7},{6,0},{7,1},{8,10},{9,11},{10,... | collective-permute-start | bytes 417800 | tf_op jit(solution)/shard_map/ppermute | solution.py:383
  46.9 9.9 %collective-permute-start.14 = (bf16[272,256]{1,0:T(8,128)(2,1)S(1)}, bf16[272,256]{1,0:T(8,128)(2,1)S(1)}, u32[]{:S(2)}, u32[]{:S(2)}) collective-permute-start(bf16[272,256]{1,0:T(8,128)(2,1)S(1)} %get-tuple-element.37), channel_id=1, source_target_pairs={{0,4},{1,5},{2,6},{3,7},{4,0},{5,1},{6,2},{7,3},{8,12},{9,13},{10,... | collective-permute-start | bytes 417800 | tf_op jit(solution)/shard_map/ppermute | solution.py:383
  49.8 7.0 %collective-permute-start.15 = (bf16[272,256]{1,0:T(8,128)(2,1)S(1)}, bf16[272,256]{1,0:T(8,128)(2,1)S(1)}, u32[]{:S(2)}, u32[]{:S(2)}) collective-permute-start(bf16[272,256]{1,0:T(8,128)(2,1)S(1)} %get-tuple-element.38), channel_id=1, source_target_pairs={{0,6},{1,7},{2,0},{3,1},{4,2},{5,3},{6,4},{7,5},{8,14},{9,15},{10,... | collective-permute-start | bytes 417800 | tf_op jit(solution)/shard_map/ppermute | solution.py:383
  58.3 13.2 %collective-permute-start.23 = (bf16[528,256]{1,0:T(8,128)(2,1)S(1)}, bf16[528,256]{1,0:T(8,128)(2,1)S(1)}, u32[]{:S(2)}, u32[]{:S(2)}) collective-permute-start(bf16[528,256]{1,0:T(8,128)(2,1)S(1)} %get-tuple-element.43), channel_id=1, source_target_pairs={{0,32},{8,40},{16,48},{24,56},{32,0},{40,8},{48,16},{56,24},{64,96... | collective-permute-start | bytes 811016 | tf_op jit(solution)/shard_map/ppermute | solution.py:376
  60.3 7.5 %collective-permute-start.18 = (bf16[256,256]{1,0:T(8,128)(2,1)S(1)}, bf16[256,256]{1,0:T(8,128)(2,1)S(1)}, u32[]{:S(2)}, u32[]{:S(2)}) collective-permute-start(bf16[256,256]{1,0:T(8,128)(2,1)S(1)} %get-tuple-element.40.refs_0_), channel_id=1, source_target_pairs={{0,6},{1,7},{2,0},{3,1},{4,2},{5,3},{6,4},{7,5},{8,14},{9,15},{10,... | collective-permute-start | bytes 393224 | tf_op jit(solution)/shard_map/ppermute | solution.py:383
  62.4 7.6 %collective-permute-start.17 = (bf16[256,256]{1,0:T(8,128)(2,1)S(1)}, bf16[256,256]{1,0:T(8,128)(2,1)S(1)}, u32[]{:S(2)}, u32[]{:S(2)}) collective-permute-start(bf16[256,256]{1,0:T(8,128)(2,1)S(1)} %get-tuple-element.40.refs_0_), channel_id=1, source_target_pairs={{0,4},{1,5},{2,6},{3,7},{4,0},{5,1},{6,2},{7,3},{8,12},{9,13},{10,... | collective-permute-start | bytes 393224 | tf_op jit(solution)/shard_map/ppermute | solution.py:383
  63.6 7.9 %collective-permute-start.16 = (bf16[256,256]{1,0:T(8,128)(2,1)S(1)}, bf16[256,256]{1,0:T(8,128)(2,1)S(1)}, u32[]{:S(2)}, u32[]{:S(2)}) collective-permute-start(bf16[256,256]{1,0:T(8,128)(2,1)S(1)} %get-tuple-element.40.refs_0_), channel_id=1, source_target_pairs={{0,2},{1,3},{2,4},{3,5},{4,6},{5,7},{6,0},{7,1},{8,10},{9,11},{10,... | collective-permute-start | bytes 393224 | tf_op jit(solution)/shard_map/ppermute | solution.py:383
  64.3 10.7 %collective-permute-start.19 = (bf16[256,256]{1,0:T(8,128)(2,1)S(1)}, bf16[256,256]{1,0:T(8,128)(2,1)S(1)}, u32[]{:S(2)}, u32[]{:S(2)}) collective-permute-start(bf16[256,256]{1,0:T(8,128)(2,1)S(1)} %get-tuple-element.40.refs_0_), channel_id=1, source_target_pairs={{0,1},{1,0},{2,3},{3,2},{4,5},{5,4},{6,7},{7,6},{8,9},{9,8},{10,11... | collective-permute-start | bytes 393224 | tf_op jit(solution)/shard_map/ppermute | solution.py:387
  67.8 7.2 %collective-permute-start.22 = (bf16[256,256]{1,0:T(8,128)(2,1)S(1)}, bf16[256,256]{1,0:T(8,128)(2,1)S(1)}, u32[]{:S(2)}, u32[]{:S(2)}) collective-permute-start(bf16[256,256]{1,0:T(8,128)(2,1)S(1)} %collective-permute-done.18.refs_3_), channel_id=1, source_target_pairs={{0,1},{1,0},{2,3},{3,2},{4,5},{5,4},{6,7},{7,6},{8,9},{9,8},{10,11... | collective-permute-start | bytes 393224 | tf_op jit(solution)/shard_map/ppermute | solution.py:387
  71.5 10.7 %collective-permute-start.24 = (bf16[528,256]{1,0:T(8,128)(2,1)S(1)}, bf16[528,256]{1,0:T(8,128)(2,1)S(1)}, u32[]{:S(2)}, u32[]{:S(2)}) collective-permute-start(bf16[528,256]{1,0:T(8,128)(2,1)S(1)} %add_convert_fusion.1), channel_id=1, source_target_pairs={{0,64},{8,72},{16,80},{24,88},{32,96},{40,104},{48,112},{56,120},{... | collective-permute-start | bytes 811016 | tf_op jit(solution)/shard_map/ppermute | solution.py:376
  82.2 42.5 %all-to-all-start = ((bf16[16,256,256]{2,1,0:T(8,128)(2,1)}), bf16[16,256,256]{2,1,0:T(8,128)(2,1)S(1)}, u32[]{:S(2)}, u32[]{:S(2)}) async-start(bf16[16,256,256]{2,1,0:T(8,128)(2,1)} %bitcast.19), calls=%async_computation | async-start | bytes 4194304 | tf_op jit(solution)/shard_map/all_to_all | solution.py:360
  91.7 9.6 %collective-permute-start.27 = (bf16[272,256]{1,0:T(8,128)(2,1)S(1)}, bf16[272,256]{1,0:T(8,128)(2,1)S(1)}, u32[]{:S(2)}, u32[]{:S(2)}) collective-permute-start(bf16[272,256]{1,0:T(8,128)(2,1)S(1)} %add_convert_fusion.3), channel_id=1, source_target_pairs={{0,2},{1,3},{2,4},{3,5},{4,6},{5,7},{6,0},{7,1},{8,10},{9,11},{10,... | collective-permute-start | bytes 417800 | tf_op jit(solution)/shard_map/ppermute | solution.py:383
  93.2 8.2 %collective-permute-start.26 = (bf16[272,256]{1,0:T(8,128)(2,1)S(1)}, bf16[272,256]{1,0:T(8,128)(2,1)S(1)}, u32[]{:S(2)}, u32[]{:S(2)}) collective-permute-start(bf16[272,256]{1,0:T(8,128)(2,1)S(1)} %add_convert_fusion.3), channel_id=1, source_target_pairs={{0,4},{1,5},{2,6},{3,7},{4,0},{5,1},{6,2},{7,3},{8,12},{9,13},{10,... | collective-permute-start | bytes 417800 | tf_op jit(solution)/shard_map/ppermute | solution.py:383
  101.4 18.6 %collective-permute-start.31 = (bf16[272,256]{1,0:T(8,128)(2,1)S(1)}, bf16[272,256]{1,0:T(8,128)(2,1)S(1)}, u32[]{:S(2)}, u32[]{:S(2)}) collective-permute-start(bf16[272,256]{1,0:T(8,128)(2,1)S(1)} %add_convert_fusion.2), channel_id=1, source_target_pairs={{0,24},{8,0},{16,8},{24,16},{32,56},{40,32},{48,40},{56,48},{64,88... | collective-permute-start | bytes 417800 | tf_op jit(solution)/shard_map/ppermute | solution.py:371
  104.6 15.4 %collective-permute-start.30 = (bf16[272,256]{1,0:T(8,128)(2,1)S(1)}, bf16[272,256]{1,0:T(8,128)(2,1)S(1)}, u32[]{:S(2)}, u32[]{:S(2)}) collective-permute-start(bf16[272,256]{1,0:T(8,128)(2,1)S(1)} %add_convert_fusion.2), channel_id=1, source_target_pairs={{0,8},{8,16},{16,24},{24,0},{32,40},{40,48},{48,56},{56,32},{64,72... | collective-permute-start | bytes 417800 | tf_op jit(solution)/shard_map/ppermute | solution.py:371
  104.6 17.5 %collective-permute-start.29 = (bf16[272,256]{1,0:T(8,128)(2,1)S(1)}, bf16[272,256]{1,0:T(8,128)(2,1)S(1)}, u32[]{:S(2)}, u32[]{:S(2)}) collective-permute-start(bf16[272,256]{1,0:T(8,128)(2,1)S(1)} %add_convert_fusion.2), channel_id=1, source_target_pairs={{0,16},{8,24},{16,0},{24,8},{32,48},{40,56},{48,32},{56,40},{64,80... | collective-permute-start | bytes 417800 | tf_op jit(solution)/shard_map/ppermute | solution.py:371
  (16 other events, 129.0 us)

commit v7 on v6

--- a/solution.py
+++ b/solution.py
@@ -149,25 +149,29 @@
     at_ref, deg_ref, out_ref, joined = refs[8:]
     half, rows = tops[0].shape[1:]
     width = 2 * half
-
-    @pl.when(pl.program_id(0) == 0)
-    def _():
-        for kx in range(4):
-            x = lax.rem(place_ref[2] + 4 - kx, 4)
-            for kz in range(4):
-                n = 4 * x + lax.rem(place_ref[3] + 4 - kz, 4)
-                lanes = pl.ds(pl.multiple_of(n * rows, rows), rows)
-                joined[0:half, lanes] = tops[kz][kx]
-                joined[half:width, lanes] = lows[kx][kz]
-
-    blocks = [
-        jnp.concatenate([at_ref[k, r] for r in range(at_ref.shape[1])], axis=1)
-        for k in range(at_ref.shape[0])
-    ]
-    part = jnp.dot(joined[...], jnp.concatenate(blocks, axis=0), preferred_element_type=F32)
-    out_ref[0, 0:width, :] = part.astype(out_ref.dtype)
-    degree = deg_ref[...] if out_ref.dtype == F32 else two_rows(deg_ref[...])
-    out_ref[0, width:, :] = spaced(degree, out_ref.dtype)
+    per = rows // 128
+    for kx in range(4):
+        x = lax.rem(place_ref[2] + 4 - kx, 4)
+        for kz in range(4):
+            n = 4 * x + lax.rem(place_ref[3] + 4 - kz, 4)
+            lanes = pl.ds(pl.multiple_of(n * rows, rows), rows)
+            joined[0:half, lanes] = tops[kz][kx]
+            joined[half:width, lanes] = lows[kx][kz]
+
+    def dest(j, carry):
+        chunk = 2 * lax.rem(place_ref[0] + j, 4) + place_ref[1]
+        blocks = [
+            jnp.concatenate([at_ref[k, per * chunk + r] for r in range(per)], axis=1)
+            for k in range(at_ref.shape[0] - 1)
+        ]
+        part = jnp.dot(joined[...], jnp.concatenate(blocks, axis=0), preferred_element_type=F32)
+        out_ref[j, 0:width, :] = part.astype(out_ref.dtype)
+        whole = deg_ref[:, pl.ds(pl.multiple_of(chunk * rows, rows), rows)]
+        degree = whole if out_ref.dtype == F32 else two_rows(whole)
+        out_ref[j, width:, :] = spaced(degree, out_ref.dtype)
+        return carry
+
+    lax.fori_loop(0, 4, dest, 0)
 
 
 def two_rows(whole):
@@ -186,26 +190,16 @@
 
 
 def forward(place, planes, at, degree, kind):
-    lines, half, rows = planes[0].shape
+    _, half, rows = planes[0].shape
     width = 2 * half
     sources = at.shape[0] - 1
-    per = rows // 128
-
-    def chunk(j, place):
-        return (0, 2 * lax.rem(place[0] + j, 4) + place[1], 0, 0)
-
+    vmem = pl.BlockSpec(memory_space=pltpu.VMEM)
     return pl.pallas_call(
         forward_kernel,
         out_shape=jax.ShapeDtypeStruct((4, width + EXTRA, rows), kind),
-        grid_spec=pltpu.PrefetchScalarGridSpec(
-            num_scalar_prefetch=1,
-            grid=(4,),
-            in_specs=[pl.BlockSpec((lines, half, rows), lambda j, *_: (0, 0, 0))] * 8
-            + [pl.BlockSpec((sources, per, 128, 128), chunk)]
-            + [pl.BlockSpec((1, rows), lambda j, place: chunk(j, place)[:2])],
-            out_specs=pl.BlockSpec((1, width + EXTRA, rows), lambda j, *_: (j, 0, 0)),
-            scratch_shapes=[pltpu.VMEM((width, sources * 128), BF)],
-        ),
+        in_specs=[pl.BlockSpec(memory_space=pltpu.SMEM)] + [vmem] * 10,
+        out_specs=vmem,
+        scratch_shapes=[pltpu.VMEM((width, sources * 128), BF)],
         compiler_params=params(20),
         cost_estimate=cost(8 * sources * 128 * rows * width, 10 << 20),
         name="forward",
@@ -213,39 +207,49 @@
 
 
 def backward_kernel(place_ref, *refs):
-    parts, at_ref, out_ref, grads = refs[:8], refs[8], refs[9], refs[10]
+    parts, at_ref, out_ref, grads, held, sems = refs[:8], *refs[8:]
     rows = parts[0].shape[0]
-
-    @pl.when(pl.program_id(0) == 0)
-    def _():
-        for k in range(4):
-            chunk = 2 * lax.rem(place_ref[0] + 4 - k, 4)
-            own = pl.multiple_of((chunk + place_ref[1]) * rows, rows)
-            other = pl.multiple_of((chunk + 1 - place_ref[1]) * rows, rows)
-            grads[pl.ds(own, rows), :] = parts[k][...]
-            grads[pl.ds(other, rows), :] = parts[4 + k][...]
-
-    for k in range(at_ref.shape[0]):
-        block = jnp.concatenate([at_ref[k, r] for r in range(at_ref.shape[1])], axis=1)
-        got = jnp.dot(block, grads[...], preferred_element_type=F32)
-        out_ref[k * 128 : (k + 1) * 128, :] = got.astype(BF)
+    for k in range(4):
+        chunk = 2 * lax.rem(place_ref[0] + 4 - k, 4)
+        own = pl.multiple_of((chunk + place_ref[1]) * rows, rows)
+        other = pl.multiple_of((chunk + 1 - place_ref[1]) * rows, rows)
+        grads[pl.ds(own, rows), :] = parts[k][...]
+        grads[pl.ds(other, rows), :] = parts[4 + k][...]
+    pieces, each, _ = held.shape
+
+    def copy(i):
+        into = out_ref.at[pl.ds(pl.multiple_of(i * each, each), each)]
+        return pltpu.make_async_copy(held.at[i], into, sems.at[i])
+
+    def piece(i, carry):
+        for k in range(each // 128):
+            at = i * (each // 128) + k
+            block = jnp.concatenate([at_ref[at, r] for r in range(at_ref.shape[1])], axis=1)
+            got = jnp.dot(block, grads[...], preferred_element_type=F32)
+            held[i, k * 128 : (k + 1) * 128, :] = got.astype(BF)
+        copy(i).start()
+        return carry
+
+    lax.fori_loop(0, pieces, piece, 0)
+    for i in range(pieces):
+        copy(i).wait()
 
 
 def backward(place, parts, at):
     sources, dests = at.shape[0] - 1, at.shape[1]
-    rows, width = parts[0].shape
-    per = 8
+    _, width = parts[0].shape
+    pieces = 8
+    vmem = pl.BlockSpec(memory_space=pltpu.VMEM)
     return pl.pallas_call(
         backward_kernel,
         out_shape=in_hbm((sources * 128, width), BF),
-        grid_spec=pltpu.PrefetchScalarGridSpec(
-            num_scalar_prefetch=1,
-            grid=(sources // per,),
-            in_specs=[pl.BlockSpec((rows, width), lambda i, *_: (0, 0))] * 8
-            + [pl.BlockSpec((per, dests, 128, 128), lambda i, *_: (i, 0, 0, 0))],
-            out_specs=pl.BlockSpec((per * 128, width), lambda i, *_: (i, 0)),
-            scratch_shapes=[pltpu.VMEM((dests * 128, width), BF)],
-        ),
+        in_specs=[pl.BlockSpec(memory_space=pltpu.SMEM)] + [vmem] * 9,
+        out_specs=pl.BlockSpec(memory_space=pltpu.HBM),
+        scratch_shapes=[
+            pltpu.VMEM((dests * 128, width), BF),
+            pltpu.VMEM((pieces, sources * 128 // pieces, width), BF),
+            pltpu.SemaphoreType.DMA((pieces,)),
+        ],
         compiler_params=params(20),
         cost_estimate=cost(2 * sources * 128 * dests * 128 * width, 20 << 20),
         name="backward",
@@ -425,11 +429,13 @@
     taken = send_core(give)
     keep = forward(mine, planes, at, degree, F32)
     own, *sent = mix(keep, taken)
-    got = [send_y(sent[k - 1], k) for k in (1, 2, 3)]
+    far = send_y(sent[1], 2)
+    got = [send_y(sent[0], 1), far, send_y(sent[2], 3)]
     layer_out, pre_grad, mean_t, mean_grad = middle(
         own, got, node_feats, w_self, w_neigh, bias.reshape(1, -1), cotangent
     )
-    same_core = [mean_grad] + [send_y(mean_grad, k) for k in (1, 2, 3)]
+    next_y, last_y = send_y(mean_grad, 1), send_y(mean_grad, 3)
+    same_core = [mean_grad, next_y, send_y(mean_grad, 2), last_y]
 
     part, self_part = weights(node_feats, pre_grad, mean_t, w_self)
     part = (part.astype(F32) + send_flip(part, 1).astype(F32)).astype(BF)

time: 127 us -> 126 us (level)
  transfers between devices with their start and end apart: 34 -> 34, of which waited for: 16 -> 15; matrix products, arithmetic and copies ran while one was open for 1% -> 1% of each run, Pallas kernels for 15% -> 16%
where the time goes in v7:
time: 126 us; the launch traced here: 124 us
  waiting for transfers between devices  48.6 us (39%)
  starting transfers between devices  46.4 us (37%)
  Pallas kernels  25.7 us (20%)
  local copies, waits for them, and re-layouts  1.5 us (1%)
  other arithmetic  1.33 us (1%)
    ppermute x15, waiting for transfers between devices, send_node(): return lax.ppermute(x, 'nodes', moves)  25.8 us
    ppermute x15, starting transfers between devices, send_node(): return lax.ppermute(x, 'nodes', moves)  21 us
    ppermute x9, waiting for transfers between devices, send_y(): return lax.ppermute(x, 'cols', along_y(step))  20.4 us
    ppermute x9, starting transfers between devices, send_y(): return lax.ppermute(x, 'cols', along_y(step))  12.6 us
    pallas_call x1, Pallas kernels, build(): pl.pallas_call(build_kernel, out_shape=(jax.ShapeDtypeStruct((sources + 1...  8.24 us
    pallas_call x2, Pallas kernels, forward(): pl.pallas_call(forward_kernel, out_shape=jax.ShapeDtypeStruct((4, width +...  7.61 us
    pallas_call x1, Pallas kernels, backward(): pl.pallas_call(backward_kernel, out_shape=in_hbm((sources * 128, width),...  7.33 us
    all_to_all x1, starting transfers between devices, swap(): return lax.all_to_all(x, axis, 0, 0, tiled=True)  7.09 us
  transfers between devices with their start and end apart: 34, of which 15 were waited for; matrix products, arithmetic and copies ran while one was open for 1% of the time, Pallas kernels for 16%

profile of v7, /device:TPU:0, one launch (start us, length us, event | category | flops | bytes accessed | tf_op | source)
XLA Modules:
  0.0 124.4 jit_solution(3720209721306818348)
XLA Ops:
  1.6 2.9 %collective-permute-start.2 = (bf16[128,256]{1,0:T(8,128)(2,1)S(1)}, bf16[128,256]{1,0:T(8,128)(2,1)S(1)}, u32[]{:S(2)}, u32[]{:S(2)}) collective-permute-start(bf16[128,256]{1,0:T(8,128)(2,1)S(1)} %get-tuple-element.27), channel_id=1, source_target_pairs={{0,96},{8,104},{16,112},{24,120},{32,0},{40,8},{48,16},{56,24},{64... | collective-permute-start | bytes 196616 | tf_op jit(solution)/shard_map/ppermute | solution.py:375
  6.2 4.0 %collective-permute-start.5 = (bf16[128,256]{1,0:T(8,128)(2,1)S(1)}, bf16[128,256]{1,0:T(8,128)(2,1)S(1)}, u32[]{:S(2)}, u32[]{:S(2)}) collective-permute-start(bf16[128,256]{1,0:T(8,128)(2,1)S(1)} %get-tuple-element.28), channel_id=1, source_target_pairs={{0,24},{8,0},{16,8},{24,16},{32,56},{40,32},{48,40},{56,48},{64,88... | collective-permute-start | bytes 196616 | tf_op jit(solution)/shard_map/ppermute | solution.py:375
  12.2 4.0 %collective-permute-done.4 = bf16[128,256]{1,0:T(8,128)(2,1)S(1)} collective-permute-done((bf16[128,256]{1,0:T(8,128)(2,1)S(1)}, bf16[128,256]{1,0:T(8,128)(2,1)S(1)}, u32[]{:S(2)}, u32[]{:S(2)}) %collective-permute-start.4) | collective-permute-done | bytes 65568 | tf_op jit(solution)/shard_map/ppermute | solution.py:375
  16.6 2.4 %collective-permute-start.11 = (bf16[4,128,256]{2,1,0:T(8,128)(2,1)S(1)}, bf16[4,128,256]{2,1,0:T(8,128)(2,1)S(1)}, u32[]{:S(2)}, u32[]{:S(2)}) collective-permute-start(bf16[4,128,256]{2,1,0:T(8,128)(2,1)S(1)} %pad_maximum_fusion.1.refs_4_), channel_id=1, source_target_pairs={{0,96},{8,104},{16,112},{24,120},{32,0},{40,8},{48,16},{56,24},{64... | collective-permute-start | bytes 786440 | tf_op jit(solution)/shard_map/ppermute | solution.py:375
  22.1 5.8 %collective-permute-done.11.refs_7_ = bf16[4,128,256]{2,1,0:T(8,128)(2,1)S(1)} collective-permute-done((bf16[4,128,256]{2,1,0:T(8,128)(2,1)S(1)}, bf16[4,128,256]{2,1,0:T(8,128)(2,1)S(1)}, u32[]{:S(2)}, u32[]{:S(2)}) %collective-permute-start.11) | collective-permute-done | bytes 262176 | tf_op jit(solution)/shard_map/ppermute | solution.py:375
  27.9 8.2 %build.1 = (bf16[33,16,128,128]{3,2,1,0:T(8,128)(2,1)S(1)}, f32[1,2048]{1,0:T(1,128)S(1)}) custom-call(s32[1,352]{1,0:T(1,128)} %rows_ref.1, s32[1,352]{1,0:T(1,128)} %cols_ref.1, s32[1,352,16,128]{3,2,1,0:T(8,128)} %bits_all.1, bf16[4,128,256]{2,1,0:T(8,128)(2,1)S(1)} %pad_maximum_fusion.gate_ref.refs_0_), custom_call_target="tpu_custom_call" | custom-call | bytes 31457280 | tf_op jit(solution)/shard_map/build/pallas_call | solution.py:124
  36.2 3.8 %forward.3 = bf16[4,272,256]{2,1,0:T(8,128)(2,1)S(1)} custom-call(s32[4]{0:T(128)S(1)} %get-tuple-element.34.place_ref, bf16[4,128,256]{2,1,0:T(8,128)(2,1)S(1)} %pad_maximum_fusion.gate_ref.refs_0_, bf16[4,128,256]{2,1,0:T(8,128)(2,1)S(1)} %collective-permute-done.6.refs_1_, bf16[4,128,256]{2,1,0:T(8,128)(2,1)S(1)} %collective-permute-done.7.refs_2_, ...), custom_call_target="tpu_custom_call" | custom-call | flops 2147483648 | bytes 10485760 | tf_op jit(solution)/shard_map/forward/pallas_call | solution.py:197
  40.2 3.8 %forward.2.keep_ref = f32[4,272,256]{2,1,0:T(8,128)S(1)} custom-call(s32[4]{0:T(128)S(1)} %get-tuple-element.29.place_ref, bf16[4,128,256]{2,1,0:T(8,128)(2,1)S(1)} %pad_maximum_fusion.gate_ref.refs_0_, bf16[4,128,256]{2,1,0:T(8,128)(2,1)S(1)} %collective-permute-done.6.refs_1_, bf16[4,128,256]{2,1,0:T(8,128)(2,1)S(1)} %collective-permute-done.7.refs_2_, ...), custom_call_target="tpu_custom_call" | custom-call | flops 2147483648 | bytes 10485760 | tf_op jit(solution)/shard_map/forward/pallas_call | solution.py:197
  44.1 1.6 %collective-permute-start.13 = (bf16[272,256]{1,0:T(8,128)(2,1)S(1)}, bf16[272,256]{1,0:T(8,128)(2,1)S(1)}, u32[]{:S(2)}, u32[]{:S(2)}) collective-permute-start(bf16[272,256]{1,0:T(8,128)(2,1)S(1)} %get-tuple-element.36), channel_id=1, source_target_pairs={{0,2},{1,3},{2,4},{3,5},{4,6},{5,7},{6,0},{7,1},{8,10},{9,11},{10,... | collective-permute-start | bytes 417800 | tf_op jit(solution)/shard_map/ppermute | solution.py:387
  45.8 2.9 %collective-permute-start.14 = (bf16[272,256]{1,0:T(8,128)(2,1)S(1)}, bf16[272,256]{1,0:T(8,128)(2,1)S(1)}, u32[]{:S(2)}, u32[]{:S(2)}) collective-permute-start(bf16[272,256]{1,0:T(8,128)(2,1)S(1)} %get-tuple-element.37), channel_id=1, source_target_pairs={{0,4},{1,5},{2,6},{3,7},{4,0},{5,1},{6,2},{7,3},{8,12},{9,13},{10,... | collective-permute-start | bytes 417800 | tf_op jit(solution)/shard_map/ppermute | solution.py:387
  51.5 4.2 %collective-permute-done.14.r2_ref = bf16[272,256]{1,0:T(8,128)(2,1)S(1)} collective-permute-done((bf16[272,256]{1,0:T(8,128)(2,1)S(1)}, bf16[272,256]{1,0:T(8,128)(2,1)S(1)}, u32[]{:S(2)}, u32[]{:S(2)}) %collective-permute-start.14) | collective-permute-done | bytes 139296 | tf_op jit(solution)/shard_map/ppermute | solution.py:387
  57.1 2.0 %collective-permute-start.23 = (bf16[528,256]{1,0:T(8,128)(2,1)S(1)}, bf16[528,256]{1,0:T(8,128)(2,1)S(1)}, u32[]{:S(2)}, u32[]{:S(2)}) collective-permute-start(bf16[528,256]{1,0:T(8,128)(2,1)S(1)} %get-tuple-element.43), channel_id=1, source_target_pairs={{0,32},{8,40},{16,48},{24,56},{32,0},{40,8},{48,16},{56,24},{64,96... | collective-permute-start | bytes 811016 | tf_op jit(solution)/shard_map/ppermute | solution.py:380
  59.1 2.1 %collective-permute-start.18 = (bf16[256,256]{1,0:T(8,128)(2,1)S(1)}, bf16[256,256]{1,0:T(8,128)(2,1)S(1)}, u32[]{:S(2)}, u32[]{:S(2)}) collective-permute-start(bf16[256,256]{1,0:T(8,128)(2,1)S(1)} %get-tuple-element.40.refs_0_), channel_id=1, source_target_pairs={{0,6},{1,7},{2,0},{3,1},{4,2},{5,3},{6,4},{7,5},{8,14},{9,15},{10,... | collective-permute-start | bytes 393224 | tf_op jit(solution)/shard_map/ppermute | solution.py:387
  63.1 3.5 %collective-permute-done.18.refs_3_ = bf16[256,256]{1,0:T(8,128)(2,1)S(1)} collective-permute-done((bf16[256,256]{1,0:T(8,128)(2,1)S(1)}, bf16[256,256]{1,0:T(8,128)(2,1)S(1)}, u32[]{:S(2)}, u32[]{:S(2)}) %collective-permute-start.18) | collective-permute-done | bytes 131104 | tf_op jit(solution)/shard_map/ppermute | solution.py:387
  66.6 2.3 %collective-permute-done.17.refs_2_ = bf16[256,256]{1,0:T(8,128)(2,1)S(1)} collective-permute-done((bf16[256,256]{1,0:T(8,128)(2,1)S(1)}, bf16[256,256]{1,0:T(8,128)(2,1)S(1)}, u32[]{:S(2)}, u32[]{:S(2)}) %collective-permute-start.17) | collective-permute-done | bytes 131104 | tf_op jit(solution)/shard_map/ppermute | solution.py:387
  70.3 3.3 %collective-permute-start.24 = (bf16[528,256]{1,0:T(8,128)(2,1)S(1)}, bf16[528,256]{1,0:T(8,128)(2,1)S(1)}, u32[]{:S(2)}, u32[]{:S(2)}) collective-permute-start(bf16[528,256]{1,0:T(8,128)(2,1)S(1)} %add_convert_fusion.1), channel_id=1, source_target_pairs={{0,64},{8,72},{16,80},{24,88},{32,96},{40,104},{48,112},{56,120},{... | collective-permute-start | bytes 811016 | tf_op jit(solution)/shard_map/ppermute | solution.py:380
  73.7 7.3 %backward.1 = bf16[4096,256]{1,0:T(8,128)(2,1)} custom-call(s32[4]{0:T(128)S(1)} %get-tuple-element.29.place_ref, bf16[256,256]{1,0:T(8,128)(2,1)S(1)} %get-tuple-element.40.refs_0_, bf16[256,256]{1,0:T(8,128)(2,1)S(1)} %collective-permute-done.16.refs_1_, bf16[256,256]{1,0:T(8,128)(2,1)S(1)} %collective-permute-done.17.refs_2_, ...), custom_call_target="tpu_custom_call" | custom-call | flops 4294967296 | bytes 20971520 | tf_op jit(solution)/shard_map/backward/pallas_call | solution.py:243
  81.0 7.1 %all-to-all-start = ((bf16[16,256,256]{2,1,0:T(8,128)(2,1)}), bf16[16,256,256]{2,1,0:T(8,128)(2,1)S(1)}, u32[]{:S(2)}, u32[]{:S(2)}) async-start(bf16[16,256,256]{2,1,0:T(8,128)(2,1)} %bitcast.19), calls=%async_computation | async-start | bytes 4194304 | tf_op jit(solution)/shard_map/all_to_all | solution.py:364
  92.6 3.9 %collective-permute-done.28 = bf16[272,256]{1,0:T(8,128)(2,1)S(1)} collective-permute-done((bf16[272,256]{1,0:T(8,128)(2,1)S(1)}, bf16[272,256]{1,0:T(8,128)(2,1)S(1)}, u32[]{:S(2)}, u32[]{:S(2)}) %collective-permute-start.28) | collective-permute-done | bytes 139296 | tf_op jit(solution)/shard_map/ppermute | solution.py:387
  96.5 3.7 %collective-permute-done.27 = bf16[272,256]{1,0:T(8,128)(2,1)S(1)} collective-permute-done((bf16[272,256]{1,0:T(8,128)(2,1)S(1)}, bf16[272,256]{1,0:T(8,128)(2,1)S(1)}, u32[]{:S(2)}, u32[]{:S(2)}) %collective-permute-start.27) | collective-permute-done | bytes 139296 | tf_op jit(solution)/shard_map/ppermute | solution.py:387
  100.3 3.2 %collective-permute-start.31 = (bf16[272,256]{1,0:T(8,128)(2,1)S(1)}, bf16[272,256]{1,0:T(8,128)(2,1)S(1)}, u32[]{:S(2)}, u32[]{:S(2)}) collective-permute-start(bf16[272,256]{1,0:T(8,128)(2,1)S(1)} %add_convert_fusion.2), channel_id=1, source_target_pairs={{0,24},{8,0},{16,8},{24,16},{32,56},{40,32},{48,40},{56,48},{64,88... | collective-permute-start | bytes 417800 | tf_op jit(solution)/shard_map/ppermute | solution.py:375
  103.5 2.3 %collective-permute-start.29 = (bf16[272,256]{1,0:T(8,128)(2,1)S(1)}, bf16[272,256]{1,0:T(8,128)(2,1)S(1)}, u32[]{:S(2)}, u32[]{:S(2)}) collective-permute-start(bf16[272,256]{1,0:T(8,128)(2,1)S(1)} %add_convert_fusion.2), channel_id=1, source_target_pairs={{0,16},{8,24},{16,0},{24,8},{32,48},{40,56},{48,32},{56,40},{64,80... | collective-permute-start | bytes 417800 | tf_op jit(solution)/shard_map/ppermute | solution.py:375
  105.8 12.9 %collective-permute-done.31 = bf16[272,256]{1,0:T(8,128)(2,1)S(1)} collective-permute-done((bf16[272,256]{1,0:T(8,128)(2,1)S(1)}, bf16[272,256]{1,0:T(8,128)(2,1)S(1)}, u32[]{:S(2)}, u32[]{:S(2)}) %collective-permute-start.31) | collective-permute-done | bytes 139296 | tf_op jit(solution)/shard_map/ppermute | solution.py:375
  118.7 2.2 %collective-permute-done.29 = bf16[272,256]{1,0:T(8,128)(2,1)S(1)} collective-permute-done((bf16[272,256]{1,0:T(8,128)(2,1)S(1)}, bf16[272,256]{1,0:T(8,128)(2,1)S(1)}, u32[]{:S(2)}, u32[]{:S(2)}) %collective-permute-start.29) | collective-permute-done | bytes 139296 | tf_op jit(solution)/shard_map/ppermute | solution.py:375
  (78 shorter events, 23.9 us)
Async XLA Ops:
  1.6 8.7 %collective-permute-start.2 = (bf16[128,256]{1,0:T(8,128)(2,1)S(1)}, bf16[128,256]{1,0:T(8,128)(2,1)S(1)}, u32[]{:S(2)}, u32[]{:S(2)}) collective-permute-start(bf16[128,256]{1,0:T(8,128)(2,1)S(1)} %get-tuple-element.27), channel_id=1, source_target_pairs={{0,96},{8,104},{16,112},{24,120},{32,0},{40,8},{48,16},{56,24},{64... | collective-permute-start | bytes 196616 | tf_op jit(solution)/shard_map/ppermute | solution.py:375
  4.5 7.1 %collective-permute-start.1 = (bf16[128,256]{1,0:T(8,128)(2,1)S(1)}, bf16[128,256]{1,0:T(8,128)(2,1)S(1)}, u32[]{:S(2)}, u32[]{:S(2)}) collective-permute-start(bf16[128,256]{1,0:T(8,128)(2,1)S(1)} %get-tuple-element.27), channel_id=1, source_target_pairs={{0,64},{8,72},{16,80},{24,88},{32,96},{40,104},{48,112},{56,120},{... | collective-permute-start | bytes 196616 | tf_op jit(solution)/shard_map/ppermute | solution.py:375
  16.6 11.4 %collective-permute-start.11 = (bf16[4,128,256]{2,1,0:T(8,128)(2,1)S(1)}, bf16[4,128,256]{2,1,0:T(8,128)(2,1)S(1)}, u32[]{:S(2)}, u32[]{:S(2)}) collective-permute-start(bf16[4,128,256]{2,1,0:T(8,128)(2,1)S(1)} %pad_maximum_fusion.1.refs_4_), channel_id=1, source_target_pairs={{0,96},{8,104},{16,112},{24,120},{32,0},{40,8},{48,16},{56,24},{64... | collective-permute-start | bytes 786440 | tf_op jit(solution)/shard_map/ppermute | solution.py:375
  19.0 17.2 %collective-permute-start.10 = (bf16[4,128,256]{2,1,0:T(8,128)(2,1)S(1)}, bf16[4,128,256]{2,1,0:T(8,128)(2,1)S(1)}, u32[]{:S(2)}, u32[]{:S(2)}) collective-permute-start(bf16[4,128,256]{2,1,0:T(8,128)(2,1)S(1)} %pad_maximum_fusion.1.refs_4_), channel_id=1, source_target_pairs={{0,64},{8,72},{16,80},{24,88},{32,96},{40,104},{48,112},{56,120},{... | collective-permute-start | bytes 786440 | tf_op jit(solution)/shard_map/ppermute | solution.py:375
  20.5 15.7 %collective-permute-start.9 = (bf16[4,128,256]{2,1,0:T(8,128)(2,1)S(1)}, bf16[4,128,256]{2,1,0:T(8,128)(2,1)S(1)}, u32[]{:S(2)}, u32[]{:S(2)}) collective-permute-start(bf16[4,128,256]{2,1,0:T(8,128)(2,1)S(1)} %pad_maximum_fusion.1.refs_4_), channel_id=1, source_target_pairs={{0,32},{8,40},{16,48},{24,56},{32,64},{40,72},{48,80},{56,88},{64,... | collective-permute-start | bytes 786440 | tf_op jit(solution)/shard_map/ppermute | solution.py:375
  20.5 15.7 %collective-permute-start.8 = (bf16[4,128,256]{2,1,0:T(8,128)(2,1)S(1)}, bf16[4,128,256]{2,1,0:T(8,128)(2,1)S(1)}, u32[]{:S(2)}, u32[]{:S(2)}) collective-permute-start(bf16[4,128,256]{2,1,0:T(8,128)(2,1)S(1)} %pad_maximum_fusion.gate_ref.refs_0_), channel_id=1, source_target_pairs={{0,24},{8,0},{16,8},{24,16},{32,56},{40,32},{48,40},{56,48},{64,88... | collective-permute-start | bytes 786440 | tf_op jit(solution)/shard_map/ppermute | solution.py:375
  21.3 14.9 %collective-permute-start.7 = (bf16[4,128,256]{2,1,0:T(8,128)(2,1)S(1)}, bf16[4,128,256]{2,1,0:T(8,128)(2,1)S(1)}, u32[]{:S(2)}, u32[]{:S(2)}) collective-permute-start(bf16[4,128,256]{2,1,0:T(8,128)(2,1)S(1)} %pad_maximum_fusion.gate_ref.refs_0_), channel_id=1, source_target_pairs={{0,16},{8,24},{16,0},{24,8},{32,48},{40,56},{48,32},{56,40},{64,80... | collective-permute-start | bytes 786440 | tf_op jit(solution)/shard_map/ppermute | solution.py:375
  27.9 8.3 %collective-permute-start.6 = (bf16[4,128,256]{2,1,0:T(8,128)(2,1)S(1)}, bf16[4,128,256]{2,1,0:T(8,128)(2,1)S(1)}, u32[]{:S(2)}, u32[]{:S(2)}) collective-permute-start(bf16[4,128,256]{2,1,0:T(8,128)(2,1)S(1)} %pad_maximum_fusion.gate_ref.refs_0_), channel_id=1, source_target_pairs={{0,8},{8,16},{16,24},{24,0},{32,40},{40,48},{48,56},{56,32},{64,72... | collective-permute-start | bytes 786440 | tf_op jit(solution)/shard_map/ppermute | solution.py:375
  44.1 7.4 %collective-permute-start.13 = (bf16[272,256]{1,0:T(8,128)(2,1)S(1)}, bf16[272,256]{1,0:T(8,128)(2,1)S(1)}, u32[]{:S(2)}, u32[]{:S(2)}) collective-permute-start(bf16[272,256]{1,0:T(8,128)(2,1)S(1)} %get-tuple-element.36), channel_id=1, source_target_pairs={{0,2},{1,3},{2,4},{3,5},{4,6},{5,7},{6,0},{7,1},{8,10},{9,11},{10,... | collective-permute-start | bytes 417800 | tf_op jit(solution)/shard_map/ppermute | solution.py:387
  45.8 9.9 %collective-permute-start.14 = (bf16[272,256]{1,0:T(8,128)(2,1)S(1)}, bf16[272,256]{1,0:T(8,128)(2,1)S(1)}, u32[]{:S(2)}, u32[]{:S(2)}) collective-permute-start(bf16[272,256]{1,0:T(8,128)(2,1)S(1)} %get-tuple-element.37), channel_id=1, source_target_pairs={{0,4},{1,5},{2,6},{3,7},{4,0},{5,1},{6,2},{7,3},{8,12},{9,13},{10,... | collective-permute-start | bytes 417800 | tf_op jit(solution)/shard_map/ppermute | solution.py:387
  48.7 7.0 %collective-permute-start.15 = (bf16[272,256]{1,0:T(8,128)(2,1)S(1)}, bf16[272,256]{1,0:T(8,128)(2,1)S(1)}, u32[]{:S(2)}, u32[]{:S(2)}) collective-permute-start(bf16[272,256]{1,0:T(8,128)(2,1)S(1)} %get-tuple-element.38), channel_id=1, source_target_pairs={{0,6},{1,7},{2,0},{3,1},{4,2},{5,3},{6,4},{7,5},{8,14},{9,15},{10,... | collective-permute-start | bytes 417800 | tf_op jit(solution)/shard_map/ppermute | solution.py:387
  57.1 13.2 %collective-permute-start.23 = (bf16[528,256]{1,0:T(8,128)(2,1)S(1)}, bf16[528,256]{1,0:T(8,128)(2,1)S(1)}, u32[]{:S(2)}, u32[]{:S(2)}) collective-permute-start(bf16[528,256]{1,0:T(8,128)(2,1)S(1)} %get-tuple-element.43), channel_id=1, source_target_pairs={{0,32},{8,40},{16,48},{24,56},{32,0},{40,8},{48,16},{56,24},{64,96... | collective-permute-start | bytes 811016 | tf_op jit(solution)/shard_map/ppermute | solution.py:380
  59.1 7.5 %collective-permute-start.18 = (bf16[256,256]{1,0:T(8,128)(2,1)S(1)}, bf16[256,256]{1,0:T(8,128)(2,1)S(1)}, u32[]{:S(2)}, u32[]{:S(2)}) collective-permute-start(bf16[256,256]{1,0:T(8,128)(2,1)S(1)} %get-tuple-element.40.refs_0_), channel_id=1, source_target_pairs={{0,6},{1,7},{2,0},{3,1},{4,2},{5,3},{6,4},{7,5},{8,14},{9,15},{10,... | collective-permute-start | bytes 393224 | tf_op jit(solution)/shard_map/ppermute | solution.py:387
  61.2 7.7 %collective-permute-start.17 = (bf16[256,256]{1,0:T(8,128)(2,1)S(1)}, bf16[256,256]{1,0:T(8,128)(2,1)S(1)}, u32[]{:S(2)}, u32[]{:S(2)}) collective-permute-start(bf16[256,256]{1,0:T(8,128)(2,1)S(1)} %get-tuple-element.40.refs_0_), channel_id=1, source_target_pairs={{0,4},{1,5},{2,6},{3,7},{4,0},{5,1},{6,2},{7,3},{8,12},{9,13},{10,... | collective-permute-start | bytes 393224 | tf_op jit(solution)/shard_map/ppermute | solution.py:387
  62.4 7.9 %collective-permute-start.16 = (bf16[256,256]{1,0:T(8,128)(2,1)S(1)}, bf16[256,256]{1,0:T(8,128)(2,1)S(1)}, u32[]{:S(2)}, u32[]{:S(2)}) collective-permute-start(bf16[256,256]{1,0:T(8,128)(2,1)S(1)} %get-tuple-element.40.refs_0_), channel_id=1, source_target_pairs={{0,2},{1,3},{2,4},{3,5},{4,6},{5,7},{6,0},{7,1},{8,10},{9,11},{10,... | collective-permute-start | bytes 393224 | tf_op jit(solution)/shard_map/ppermute | solution.py:387
  63.1 10.6 %collective-permute-start.19 = (bf16[256,256]{1,0:T(8,128)(2,1)S(1)}, bf16[256,256]{1,0:T(8,128)(2,1)S(1)}, u32[]{:S(2)}, u32[]{:S(2)}) collective-permute-start(bf16[256,256]{1,0:T(8,128)(2,1)S(1)} %get-tuple-element.40.refs_0_), channel_id=1, source_target_pairs={{0,1},{1,0},{2,3},{3,2},{4,5},{5,4},{6,7},{7,6},{8,9},{9,8},{10,11... | collective-permute-start | bytes 393224 | tf_op jit(solution)/shard_map/ppermute | solution.py:391
  66.6 7.1 %collective-permute-start.22 = (bf16[256,256]{1,0:T(8,128)(2,1)S(1)}, bf16[256,256]{1,0:T(8,128)(2,1)S(1)}, u32[]{:S(2)}, u32[]{:S(2)}) collective-permute-start(bf16[256,256]{1,0:T(8,128)(2,1)S(1)} %collective-permute-done.18.refs_3_), channel_id=1, source_target_pairs={{0,1},{1,0},{2,3},{3,2},{4,5},{5,4},{6,7},{7,6},{8,9},{9,8},{10,11... | collective-permute-start | bytes 393224 | tf_op jit(solution)/shard_map/ppermute | solution.py:391
  70.3 10.7 %collective-permute-start.24 = (bf16[528,256]{1,0:T(8,128)(2,1)S(1)}, bf16[528,256]{1,0:T(8,128)(2,1)S(1)}, u32[]{:S(2)}, u32[]{:S(2)}) collective-permute-start(bf16[528,256]{1,0:T(8,128)(2,1)S(1)} %add_convert_fusion.1), channel_id=1, source_target_pairs={{0,64},{8,72},{16,80},{24,88},{32,96},{40,104},{48,112},{56,120},{... | collective-permute-start | bytes 811016 | tf_op jit(solution)/shard_map/ppermute | solution.py:380
  81.0 42.4 %all-to-all-start = ((bf16[16,256,256]{2,1,0:T(8,128)(2,1)}), bf16[16,256,256]{2,1,0:T(8,128)(2,1)S(1)}, u32[]{:S(2)}, u32[]{:S(2)}) async-start(bf16[16,256,256]{2,1,0:T(8,128)(2,1)} %bitcast.19), calls=%async_computation | async-start | bytes 4194304 | tf_op jit(solution)/shard_map/all_to_all | solution.py:364
  90.6 9.6 %collective-permute-start.27 = (bf16[272,256]{1,0:T(8,128)(2,1)S(1)}, bf16[272,256]{1,0:T(8,128)(2,1)S(1)}, u32[]{:S(2)}, u32[]{:S(2)}) collective-permute-start(bf16[272,256]{1,0:T(8,128)(2,1)S(1)} %add_convert_fusion.3), channel_id=1, source_target_pairs={{0,2},{1,3},{2,4},{3,5},{4,6},{5,7},{6,0},{7,1},{8,10},{9,11},{10,... | collective-permute-start | bytes 417800 | tf_op jit(solution)/shard_map/ppermute | solution.py:387
  92.0 8.2 %collective-permute-start.26 = (bf16[272,256]{1,0:T(8,128)(2,1)S(1)}, bf16[272,256]{1,0:T(8,128)(2,1)S(1)}, u32[]{:S(2)}, u32[]{:S(2)}) collective-permute-start(bf16[272,256]{1,0:T(8,128)(2,1)S(1)} %add_convert_fusion.3), channel_id=1, source_target_pairs={{0,4},{1,5},{2,6},{3,7},{4,0},{5,1},{6,2},{7,3},{8,12},{9,13},{10,... | collective-permute-start | bytes 417800 | tf_op jit(solution)/shard_map/ppermute | solution.py:387
  100.3 18.4 %collective-permute-start.31 = (bf16[272,256]{1,0:T(8,128)(2,1)S(1)}, bf16[272,256]{1,0:T(8,128)(2,1)S(1)}, u32[]{:S(2)}, u32[]{:S(2)}) collective-permute-start(bf16[272,256]{1,0:T(8,128)(2,1)S(1)} %add_convert_fusion.2), channel_id=1, source_target_pairs={{0,24},{8,0},{16,8},{24,16},{32,56},{40,32},{48,40},{56,48},{64,88... | collective-permute-start | bytes 417800 | tf_op jit(solution)/shard_map/ppermute | solution.py:375
  103.5 15.2 %collective-permute-start.30 = (bf16[272,256]{1,0:T(8,128)(2,1)S(1)}, bf16[272,256]{1,0:T(8,128)(2,1)S(1)}, u32[]{:S(2)}, u32[]{:S(2)}) collective-permute-start(bf16[272,256]{1,0:T(8,128)(2,1)S(1)} %add_convert_fusion.2), channel_id=1, source_target_pairs={{0,8},{8,16},{16,24},{24,0},{32,40},{40,48},{48,56},{56,32},{64,72... | collective-permute-start | bytes 417800 | tf_op jit(solution)/shard_map/ppermute | solution.py:375
  103.5 17.4 %collective-permute-start.29 = (bf16[272,256]{1,0:T(8,128)(2,1)S(1)}, bf16[272,256]{1,0:T(8,128)(2,1)S(1)}, u32[]{:S(2)}, u32[]{:S(2)}) collective-permute-start(bf16[272,256]{1,0:T(8,128)(2,1)S(1)} %add_convert_fusion.2), channel_id=1, source_target_pairs={{0,16},{8,24},{16,0},{24,8},{32,48},{40,56},{48,32},{56,40},{64,80... | collective-permute-start | bytes 417800 | tf_op jit(solution)/shard_map/ppermute | solution.py:375
  (16 other events, 125.4 us)

commit v8 on v7

--- a/solution.py
+++ b/solution.py
@@ -102,7 +102,7 @@
     copies[1].wait()
     for k in range(pieces):
         copies[2 + k].wait()
-        lax.fori_loop(k * each, (k + 1) * each, add_tile, 0, unroll=2)
+        lax.fori_loop(k * each, (k + 1) * each, add_tile, 0, unroll=4)
 
     @pl.when(spill[0] >= 0)
     def _():
@@ -158,7 +158,7 @@
             joined[0:half, lanes] = tops[kz][kx]
             joined[half:width, lanes] = lows[kx][kz]
 
-    def dest(j, carry):
+    for j in range(4):
         chunk = 2 * lax.rem(place_ref[0] + j, 4) + place_ref[1]
         blocks = [
             jnp.concatenate([at_ref[k, per * chunk + r] for r in range(per)], axis=1)
@@ -169,9 +169,6 @@
         whole = deg_ref[:, pl.ds(pl.multiple_of(chunk * rows, rows), rows)]
         degree = whole if out_ref.dtype == F32 else two_rows(whole)
         out_ref[j, width:, :] = spaced(degree, out_ref.dtype)
-        return carry
-
-    lax.fori_loop(0, 4, dest, 0)
 
 
 def two_rows(whole):
@@ -238,7 +235,7 @@
 def backward(place, parts, at):
     sources, dests = at.shape[0] - 1, at.shape[1]
     _, width = parts[0].shape
-    pieces = 8
+    pieces = 4
     vmem = pl.BlockSpec(memory_space=pltpu.VMEM)
     return pl.pallas_call(
         backward_kernel,
@@ -360,6 +357,32 @@
     )(parts, self_part)
 
 
+def place_grads_kernel(place_ref, part_ref, other_ref, self_ref, neigh_ref, bias_ref):
+    width = self_ref.shape[0]
+    bias_ref[...] = part_ref[width : width + 1, :]
+    for core, (first, second) in enumerate(((part_ref, other_ref), (other_ref, part_ref))):
+
+        @pl.when(place_ref[1] == core)
+        def _():
+            self_ref[...] = first[0:width, :]
+            neigh_ref[...] = second[0:width, :]
+
+
+def place_grads(place, part, other):
+    width = part.shape[1]
+    vmem = pl.BlockSpec(memory_space=pltpu.VMEM)
+    shape = jax.ShapeDtypeStruct((width, width), F32)
+    return pl.pallas_call(
+        place_grads_kernel,
+        out_shape=(shape, shape, jax.ShapeDtypeStruct((1, width), F32)),
+        in_specs=[pl.BlockSpec(memory_space=pltpu.SMEM), vmem, vmem],
+        out_specs=(vmem, vmem, vmem),
+        compiler_params=params(16),
+        cost_estimate=cost(0, 1 << 20),
+        name="place_grads",
+    )(place, part, other)
+
+
 def swap(x, axis):
     return lax.all_to_all(x, axis, 0, 0, tiled=True)
 
@@ -446,20 +469,17 @@
     src, part, flipped = lax.optimization_barrier((src, part, flipped))
     parts = swap(src.reshape(nodes, rows_dev, width), "nodes")
 
-    part = (part.astype(F32) + flipped.astype(F32)).astype(BF)
+    part = part.astype(F32) + flipped.astype(F32)
     halves = (part[:width], part[width : 2 * width])
     kept = jnp.concatenate([jnp.where(zero, *halves), part[2 * width :]])
     given = jnp.concatenate([jnp.where(zero, *halves[::-1]), part[2 * width :]])
-    part = (kept.astype(F32) + send_core(given).astype(F32)).astype(BF)
+    part = kept + send_core(given)
     part = add_terms([part] + [send_y(part, k) for k in (1, 2, 3)]).astype(BF)
     part = add_terms([part] + [send_z(part, k) for k in (1, 2, 3)])
-    other = send_core(part)
-    bias_grad = part[width]
-    self_grad = jnp.where(zero, part[:width], other[:width])
-    neigh_grad = jnp.where(zero, other[:width], part[:width])
+    self_grad, neigh_grad, bias_grad = place_grads(mine, part, send_core(part))
 
     feat_grad = finish(parts, self_part)
-    return (layer_out, feat_grad, self_grad, neigh_grad, bias_grad)
+    return (layer_out, feat_grad, self_grad, neigh_grad, bias_grad[0])
 
 
 def solution(mesh):

time: 126 us -> 127 us (level)
  waiting for transfers between devices: 48.6 us -> 52.6 us
    ppermute x9, waiting for transfers between devices: 20.4 us -> 26.4 us  [send_y(): return lax.ppermute(x, 'cols', along_y(step))]
    ppermute x15, waiting for transfers between devices: 25.8 us -> 22.6 us  [send_node(): return lax.ppermute(x, 'nodes', moves)]
    pallas_call x0 -> x1, Pallas kernels: none -> 1.38 us  [place_grads(): pl.pallas_call(place_grads_kernel, out_shape=(shape, shape, jax.ShapeDtyp...]
    pallas_call x2, Pallas kernels: 7.61 us -> 6.34 us  [forward(): pl.pallas_call(forward_kernel, out_shape=jax.ShapeDtypeStruct((4, width +...]
  transfers between devices with their start and end apart: 34 -> 34, of which waited for: 15 -> 16; matrix products, arithmetic and copies ran while one was open for 1% -> 0% of each run, Pallas kernels for 16% -> 15%
where the time goes in v8:
time: 127 us; the launch traced here: 126 us
  waiting for transfers between devices  52.6 us (41%)
  starting transfers between devices  46.4 us (37%)
  Pallas kernels  24.6 us (19%)
    ppermute x9, waiting for transfers between devices, send_y(): return lax.ppermute(x, 'cols', along_y(step))  26.4 us
    ppermute x15, waiting for transfers between devices, send_node(): return lax.ppermute(x, 'nodes', moves)  22.6 us
    ppermute x15, starting transfers between devices, send_node(): return lax.ppermute(x, 'nodes', moves)  21 us
    ppermute x9, starting transfers between devices, send_y(): return lax.ppermute(x, 'cols', along_y(step))  12.6 us
    pallas_call x1, Pallas kernels, build(): pl.pallas_call(build_kernel, out_shape=(jax.ShapeDtypeStruct((sources + 1...  7.63 us
    all_to_all x1, starting transfers between devices, swap(): return lax.all_to_all(x, axis, 0, 0, tiled=True)  7.26 us
    pallas_call x1, Pallas kernels, backward(): pl.pallas_call(backward_kernel, out_shape=in_hbm((sources * 128, width),...  6.72 us
    pallas_call x2, Pallas kernels, forward(): pl.pallas_call(forward_kernel, out_shape=jax.ShapeDtypeStruct((4, width +...  6.34 us
  transfers between devices with their start and end apart: 34, of which 16 were waited for; matrix products, arithmetic and copies ran while one was open for 0% of the time, Pallas kernels for 15%

profile of v8, /device:TPU:0, one launch (start us, length us, event | category | flops | bytes accessed | tf_op | source)
XLA Modules:
  0.0 125.9 jit_solution(16619690533636105819)
XLA Ops:
  1.6 2.9 %collective-permute-start.2 = (bf16[128,256]{1,0:T(8,128)(2,1)S(1)}, bf16[128,256]{1,0:T(8,128)(2,1)S(1)}, u32[]{:S(2)}, u32[]{:S(2)}) collective-permute-start(bf16[128,256]{1,0:T(8,128)(2,1)S(1)} %get-tuple-element.30), channel_id=1, source_target_pairs={{0,96},{8,104},{16,112},{24,120},{32,0},{40,8},{48,16},{56,24},{64... | collective-permute-start | bytes 196616 | tf_op jit(solution)/shard_map/ppermute | solution.py:398
  6.2 4.0 %collective-permute-start.5 = (bf16[128,256]{1,0:T(8,128)(2,1)S(1)}, bf16[128,256]{1,0:T(8,128)(2,1)S(1)}, u32[]{:S(2)}, u32[]{:S(2)}) collective-permute-start(bf16[128,256]{1,0:T(8,128)(2,1)S(1)} %get-tuple-element.31), channel_id=1, source_target_pairs={{0,24},{8,0},{16,8},{24,16},{32,56},{40,32},{48,40},{56,48},{64,88... | collective-permute-start | bytes 196616 | tf_op jit(solution)/shard_map/ppermute | solution.py:398
  12.2 4.0 %collective-permute-done.4 = bf16[128,256]{1,0:T(8,128)(2,1)S(1)} collective-permute-done((bf16[128,256]{1,0:T(8,128)(2,1)S(1)}, bf16[128,256]{1,0:T(8,128)(2,1)S(1)}, u32[]{:S(2)}, u32[]{:S(2)}) %collective-permute-start.4) | collective-permute-done | bytes 65568 | tf_op jit(solution)/shard_map/ppermute | solution.py:398
  16.6 2.4 %collective-permute-start.11 = (bf16[4,128,256]{2,1,0:T(8,128)(2,1)S(1)}, bf16[4,128,256]{2,1,0:T(8,128)(2,1)S(1)}, u32[]{:S(2)}, u32[]{:S(2)}) collective-permute-start(bf16[4,128,256]{2,1,0:T(8,128)(2,1)S(1)} %pad_maximum_fusion.3.refs_4_), channel_id=1, source_target_pairs={{0,96},{8,104},{16,112},{24,120},{32,0},{40,8},{48,16},{56,24},{64... | collective-permute-start | bytes 786440 | tf_op jit(solution)/shard_map/ppermute | solution.py:398
  22.1 5.8 %collective-permute-done.11.refs_7_ = bf16[4,128,256]{2,1,0:T(8,128)(2,1)S(1)} collective-permute-done((bf16[4,128,256]{2,1,0:T(8,128)(2,1)S(1)}, bf16[4,128,256]{2,1,0:T(8,128)(2,1)S(1)}, u32[]{:S(2)}, u32[]{:S(2)}) %collective-permute-start.11) | collective-permute-done | bytes 262176 | tf_op jit(solution)/shard_map/ppermute | solution.py:398
  27.9 7.6 %build.1 = (bf16[33,16,128,128]{3,2,1,0:T(8,128)(2,1)S(1)}, f32[1,2048]{1,0:T(1,128)S(1)}) custom-call(s32[1,352]{1,0:T(1,128)} %rows_ref.1, s32[1,352]{1,0:T(1,128)} %cols_ref.1, s32[1,352,16,128]{3,2,1,0:T(8,128)} %bits_all.1, bf16[4,128,256]{2,1,0:T(8,128)(2,1)S(1)} %pad_maximum_fusion.2.gate_ref.refs_0_), custom_call_target="tpu_custom_call" | custom-call | bytes 31457280 | tf_op jit(solution)/shard_map/build/pallas_call | solution.py:124
  35.6 3.2 %forward.3 = bf16[4,272,256]{2,1,0:T(8,128)(2,1)S(1)} custom-call(s32[4]{0:T(128)S(1)} %get-tuple-element.37.place_ref, bf16[4,128,256]{2,1,0:T(8,128)(2,1)S(1)} %pad_maximum_fusion.2.gate_ref.refs_0_, bf16[4,128,256]{2,1,0:T(8,128)(2,1)S(1)} %collective-permute-done.6.refs_1_, bf16[4,128,256]{2,1,0:T(8,128)(2,1)S(1)} %collective-permute-done.7.refs_2_, ...), custom_call_target="tpu_custom_call" | custom-call | flops 2147483648 | bytes 10485760 | tf_op jit(solution)/shard_map/forward/pallas_call | solution.py:194
  39.0 3.2 %forward.2.keep_ref = f32[4,272,256]{2,1,0:T(8,128)S(1)} custom-call(s32[4]{0:T(128)S(1)} %get-tuple-element.32.place_ref, bf16[4,128,256]{2,1,0:T(8,128)(2,1)S(1)} %pad_maximum_fusion.2.gate_ref.refs_0_, bf16[4,128,256]{2,1,0:T(8,128)(2,1)S(1)} %collective-permute-done.6.refs_1_, bf16[4,128,256]{2,1,0:T(8,128)(2,1)S(1)} %collective-permute-done.7.refs_2_, ...), custom_call_target="tpu_custom_call" | custom-call | flops 2147483648 | bytes 10485760 | tf_op jit(solution)/shard_map/forward/pallas_call | solution.py:194
  42.3 1.6 %collective-permute-start.13 = (bf16[272,256]{1,0:T(8,128)(2,1)S(1)}, bf16[272,256]{1,0:T(8,128)(2,1)S(1)}, u32[]{:S(2)}, u32[]{:S(2)}) collective-permute-start(bf16[272,256]{1,0:T(8,128)(2,1)S(1)} %get-tuple-element.39), channel_id=1, source_target_pairs={{0,2},{1,3},{2,4},{3,5},{4,6},{5,7},{6,0},{7,1},{8,10},{9,11},{10,... | collective-permute-start | bytes 417800 | tf_op jit(solution)/shard_map/ppermute | solution.py:410
  43.9 2.9 %collective-permute-start.14 = (bf16[272,256]{1,0:T(8,128)(2,1)S(1)}, bf16[272,256]{1,0:T(8,128)(2,1)S(1)}, u32[]{:S(2)}, u32[]{:S(2)}) collective-permute-start(bf16[272,256]{1,0:T(8,128)(2,1)S(1)} %get-tuple-element.40), channel_id=1, source_target_pairs={{0,4},{1,5},{2,6},{3,7},{4,0},{5,1},{6,2},{7,3},{8,12},{9,13},{10,... | collective-permute-start | bytes 417800 | tf_op jit(solution)/shard_map/ppermute | solution.py:410
  49.7 4.2 %collective-permute-done.14.r2_ref = bf16[272,256]{1,0:T(8,128)(2,1)S(1)} collective-permute-done((bf16[272,256]{1,0:T(8,128)(2,1)S(1)}, bf16[272,256]{1,0:T(8,128)(2,1)S(1)}, u32[]{:S(2)}, u32[]{:S(2)}) %collective-permute-start.14) | collective-permute-done | bytes 139296 | tf_op jit(solution)/shard_map/ppermute | solution.py:410
  55.2 2.0 %collective-permute-start.23 = (bf16[528,256]{1,0:T(8,128)(2,1)S(1)}, bf16[528,256]{1,0:T(8,128)(2,1)S(1)}, u32[]{:S(2)}, u32[]{:S(2)}) collective-permute-start(bf16[528,256]{1,0:T(8,128)(2,1)S(1)} %get-tuple-element.46), channel_id=1, source_target_pairs={{0,32},{8,40},{16,48},{24,56},{32,0},{40,8},{48,16},{56,24},{64,96... | collective-permute-start | bytes 811016 | tf_op jit(solution)/shard_map/ppermute | solution.py:403
  57.2 2.1 %collective-permute-start.18 = (bf16[256,256]{1,0:T(8,128)(2,1)S(1)}, bf16[256,256]{1,0:T(8,128)(2,1)S(1)}, u32[]{:S(2)}, u32[]{:S(2)}) collective-permute-start(bf16[256,256]{1,0:T(8,128)(2,1)S(1)} %get-tuple-element.43.refs_0_), channel_id=1, source_target_pairs={{0,6},{1,7},{2,0},{3,1},{4,2},{5,3},{6,4},{7,5},{8,14},{9,15},{10,... | collective-permute-start | bytes 393224 | tf_op jit(solution)/shard_map/ppermute | solution.py:410
  61.2 3.5 %collective-permute-done.18.refs_3_ = bf16[256,256]{1,0:T(8,128)(2,1)S(1)} collective-permute-done((bf16[256,256]{1,0:T(8,128)(2,1)S(1)}, bf16[256,256]{1,0:T(8,128)(2,1)S(1)}, u32[]{:S(2)}, u32[]{:S(2)}) %collective-permute-start.18) | collective-permute-done | bytes 131104 | tf_op jit(solution)/shard_map/ppermute | solution.py:410
  64.7 2.3 %collective-permute-done.17.refs_2_ = bf16[256,256]{1,0:T(8,128)(2,1)S(1)} collective-permute-done((bf16[256,256]{1,0:T(8,128)(2,1)S(1)}, bf16[256,256]{1,0:T(8,128)(2,1)S(1)}, u32[]{:S(2)}, u32[]{:S(2)}) %collective-permute-start.17) | collective-permute-done | bytes 131104 | tf_op jit(solution)/shard_map/ppermute | solution.py:410
  68.5 3.3 %collective-permute-start.24 = (bf16[528,256]{1,0:T(8,128)(2,1)S(1)}, bf16[528,256]{1,0:T(8,128)(2,1)S(1)}, u32[]{:S(2)}, u32[]{:S(2)}) collective-permute-start(bf16[528,256]{1,0:T(8,128)(2,1)S(1)} %add_convert_fusion), channel_id=1, source_target_pairs={{0,64},{8,72},{16,80},{24,88},{32,96},{40,104},{48,112},{56,120},{... | collective-permute-start | bytes 811016 | tf_op jit(solution)/shard_map/ppermute | solution.py:403
  71.8 6.7 %backward.1 = bf16[4096,256]{1,0:T(8,128)(2,1)} custom-call(s32[4]{0:T(128)S(1)} %get-tuple-element.32.place_ref, bf16[256,256]{1,0:T(8,128)(2,1)S(1)} %get-tuple-element.43.refs_0_, bf16[256,256]{1,0:T(8,128)(2,1)S(1)} %collective-permute-done.16.refs_1_, bf16[256,256]{1,0:T(8,128)(2,1)S(1)} %collective-permute-done.17.refs_2_, ...), custom_call_target="tpu_custom_call" | custom-call | flops 4294967296 | bytes 20971520 | tf_op jit(solution)/shard_map/backward/pallas_call | solution.py:240
  79.0 7.3 %all-to-all-start = ((bf16[16,256,256]{2,1,0:T(8,128)(2,1)}), bf16[16,256,256]{2,1,0:T(8,128)(2,1)S(1)}, u32[]{:S(2)}, u32[]{:S(2)}) async-start(bf16[16,256,256]{2,1,0:T(8,128)(2,1)} %bitcast.19), calls=%async_computation | async-start | bytes 4194304 | tf_op jit(solution)/shard_map/all_to_all | solution.py:387
  90.8 6.9 %collective-permute-done.28 = f32[272,256]{1,0:T(8,128)S(1)} collective-permute-done((f32[272,256]{1,0:T(8,128)S(1)}, f32[272,256]{1,0:T(8,128)S(1)}, u32[]{:S(2)}, u32[]{:S(2)}) %collective-permute-start.28) | collective-permute-done | bytes 278560 | tf_op jit(solution)/shard_map/ppermute | solution.py:410
  97.6 6.7 %collective-permute-done.27 = f32[272,256]{1,0:T(8,128)S(1)} collective-permute-done((f32[272,256]{1,0:T(8,128)S(1)}, f32[272,256]{1,0:T(8,128)S(1)}, u32[]{:S(2)}, u32[]{:S(2)}) %collective-permute-start.27) | collective-permute-done | bytes 278560 | tf_op jit(solution)/shard_map/ppermute | solution.py:410
  104.4 3.2 %collective-permute-start.31 = (bf16[272,256]{1,0:T(8,128)(2,1)S(1)}, bf16[272,256]{1,0:T(8,128)(2,1)S(1)}, u32[]{:S(2)}, u32[]{:S(2)}) collective-permute-start(bf16[272,256]{1,0:T(8,128)(2,1)S(1)} %add_convert_fusion.1), channel_id=1, source_target_pairs={{0,24},{8,0},{16,8},{24,16},{32,56},{40,32},{48,40},{56,48},{64,88... | collective-permute-start | bytes 417800 | tf_op jit(solution)/shard_map/ppermute | solution.py:398
  107.6 2.3 %collective-permute-start.29 = (bf16[272,256]{1,0:T(8,128)(2,1)S(1)}, bf16[272,256]{1,0:T(8,128)(2,1)S(1)}, u32[]{:S(2)}, u32[]{:S(2)}) collective-permute-start(bf16[272,256]{1,0:T(8,128)(2,1)S(1)} %add_convert_fusion.1), channel_id=1, source_target_pairs={{0,16},{8,24},{16,0},{24,8},{32,48},{40,56},{48,32},{56,40},{64,80... | collective-permute-start | bytes 417800 | tf_op jit(solution)/shard_map/ppermute | solution.py:398
  109.9 7.7 %collective-permute-done.31 = bf16[272,256]{1,0:T(8,128)(2,1)S(1)} collective-permute-done((bf16[272,256]{1,0:T(8,128)(2,1)S(1)}, bf16[272,256]{1,0:T(8,128)(2,1)S(1)}, u32[]{:S(2)}, u32[]{:S(2)}) %collective-permute-start.31) | collective-permute-done | bytes 139296 | tf_op jit(solution)/shard_map/ppermute | solution.py:398
  117.6 4.2 %collective-permute-done.29 = bf16[272,256]{1,0:T(8,128)(2,1)S(1)} collective-permute-done((bf16[272,256]{1,0:T(8,128)(2,1)S(1)}, bf16[272,256]{1,0:T(8,128)(2,1)S(1)}, u32[]{:S(2)}, u32[]{:S(2)}) %collective-permute-start.29) | collective-permute-done | bytes 139296 | tf_op jit(solution)/shard_map/ppermute | solution.py:398
  (77 shorter events, 25.0 us)
Async XLA Ops:
  1.6 8.7 %collective-permute-start.2 = (bf16[128,256]{1,0:T(8,128)(2,1)S(1)}, bf16[128,256]{1,0:T(8,128)(2,1)S(1)}, u32[]{:S(2)}, u32[]{:S(2)}) collective-permute-start(bf16[128,256]{1,0:T(8,128)(2,1)S(1)} %get-tuple-element.30), channel_id=1, source_target_pairs={{0,96},{8,104},{16,112},{24,120},{32,0},{40,8},{48,16},{56,24},{64... | collective-permute-start | bytes 196616 | tf_op jit(solution)/shard_map/ppermute | solution.py:398
  4.5 7.1 %collective-permute-start.1 = (bf16[128,256]{1,0:T(8,128)(2,1)S(1)}, bf16[128,256]{1,0:T(8,128)(2,1)S(1)}, u32[]{:S(2)}, u32[]{:S(2)}) collective-permute-start(bf16[128,256]{1,0:T(8,128)(2,1)S(1)} %get-tuple-element.30), channel_id=1, source_target_pairs={{0,64},{8,72},{16,80},{24,88},{32,96},{40,104},{48,112},{56,120},{... | collective-permute-start | bytes 196616 | tf_op jit(solution)/shard_map/ppermute | solution.py:398
  16.6 11.4 %collective-permute-start.11 = (bf16[4,128,256]{2,1,0:T(8,128)(2,1)S(1)}, bf16[4,128,256]{2,1,0:T(8,128)(2,1)S(1)}, u32[]{:S(2)}, u32[]{:S(2)}) collective-permute-start(bf16[4,128,256]{2,1,0:T(8,128)(2,1)S(1)} %pad_maximum_fusion.3.refs_4_), channel_id=1, source_target_pairs={{0,96},{8,104},{16,112},{24,120},{32,0},{40,8},{48,16},{56,24},{64... | collective-permute-start | bytes 786440 | tf_op jit(solution)/shard_map/ppermute | solution.py:398
  19.0 16.6 %collective-permute-start.10 = (bf16[4,128,256]{2,1,0:T(8,128)(2,1)S(1)}, bf16[4,128,256]{2,1,0:T(8,128)(2,1)S(1)}, u32[]{:S(2)}, u32[]{:S(2)}) collective-permute-start(bf16[4,128,256]{2,1,0:T(8,128)(2,1)S(1)} %pad_maximum_fusion.3.refs_4_), channel_id=1, source_target_pairs={{0,64},{8,72},{16,80},{24,88},{32,96},{40,104},{48,112},{56,120},{... | collective-permute-start | bytes 786440 | tf_op jit(solution)/shard_map/ppermute | solution.py:398
  20.5 15.1 %collective-permute-start.9 = (bf16[4,128,256]{2,1,0:T(8,128)(2,1)S(1)}, bf16[4,128,256]{2,1,0:T(8,128)(2,1)S(1)}, u32[]{:S(2)}, u32[]{:S(2)}) collective-permute-start(bf16[4,128,256]{2,1,0:T(8,128)(2,1)S(1)} %pad_maximum_fusion.3.refs_4_), channel_id=1, source_target_pairs={{0,32},{8,40},{16,48},{24,56},{32,64},{40,72},{48,80},{56,88},{64,... | collective-permute-start | bytes 786440 | tf_op jit(solution)/shard_map/ppermute | solution.py:398
  20.5 15.1 %collective-permute-start.8 = (bf16[4,128,256]{2,1,0:T(8,128)(2,1)S(1)}, bf16[4,128,256]{2,1,0:T(8,128)(2,1)S(1)}, u32[]{:S(2)}, u32[]{:S(2)}) collective-permute-start(bf16[4,128,256]{2,1,0:T(8,128)(2,1)S(1)} %pad_maximum_fusion.2.gate_ref.refs_0_), channel_id=1, source_target_pairs={{0,24},{8,0},{16,8},{24,16},{32,56},{40,32},{48,40},{56,48},{64,88... | collective-permute-start | bytes 786440 | tf_op jit(solution)/shard_map/ppermute | solution.py:398
  21.3 14.3 %collective-permute-start.7 = (bf16[4,128,256]{2,1,0:T(8,128)(2,1)S(1)}, bf16[4,128,256]{2,1,0:T(8,128)(2,1)S(1)}, u32[]{:S(2)}, u32[]{:S(2)}) collective-permute-start(bf16[4,128,256]{2,1,0:T(8,128)(2,1)S(1)} %pad_maximum_fusion.2.gate_ref.refs_0_), channel_id=1, source_target_pairs={{0,16},{8,24},{16,0},{24,8},{32,48},{40,56},{48,32},{56,40},{64,80... | collective-permute-start | bytes 786440 | tf_op jit(solution)/shard_map/ppermute | solution.py:398
  27.9 7.7 %collective-permute-start.6 = (bf16[4,128,256]{2,1,0:T(8,128)(2,1)S(1)}, bf16[4,128,256]{2,1,0:T(8,128)(2,1)S(1)}, u32[]{:S(2)}, u32[]{:S(2)}) collective-permute-start(bf16[4,128,256]{2,1,0:T(8,128)(2,1)S(1)} %pad_maximum_fusion.2.gate_ref.refs_0_), channel_id=1, source_target_pairs={{0,8},{8,16},{16,24},{24,0},{32,40},{40,48},{48,56},{56,32},{64,72... | collective-permute-start | bytes 786440 | tf_op jit(solution)/shard_map/ppermute | solution.py:398
  42.3 7.4 %collective-permute-start.13 = (bf16[272,256]{1,0:T(8,128)(2,1)S(1)}, bf16[272,256]{1,0:T(8,128)(2,1)S(1)}, u32[]{:S(2)}, u32[]{:S(2)}) collective-permute-start(bf16[272,256]{1,0:T(8,128)(2,1)S(1)} %get-tuple-element.39), channel_id=1, source_target_pairs={{0,2},{1,3},{2,4},{3,5},{4,6},{5,7},{6,0},{7,1},{8,10},{9,11},{10,... | collective-permute-start | bytes 417800 | tf_op jit(solution)/shard_map/ppermute | solution.py:410
  43.9 9.9 %collective-permute-start.14 = (bf16[272,256]{1,0:T(8,128)(2,1)S(1)}, bf16[272,256]{1,0:T(8,128)(2,1)S(1)}, u32[]{:S(2)}, u32[]{:S(2)}) collective-permute-start(bf16[272,256]{1,0:T(8,128)(2,1)S(1)} %get-tuple-element.40), channel_id=1, source_target_pairs={{0,4},{1,5},{2,6},{3,7},{4,0},{5,1},{6,2},{7,3},{8,12},{9,13},{10,... | collective-permute-start | bytes 417800 | tf_op jit(solution)/shard_map/ppermute | solution.py:410
  55.2 13.2 %collective-permute-start.23 = (bf16[528,256]{1,0:T(8,128)(2,1)S(1)}, bf16[528,256]{1,0:T(8,128)(2,1)S(1)}, u32[]{:S(2)}, u32[]{:S(2)}) collective-permute-start(bf16[528,256]{1,0:T(8,128)(2,1)S(1)} %get-tuple-element.46), channel_id=1, source_target_pairs={{0,32},{8,40},{16,48},{24,56},{32,0},{40,8},{48,16},{56,24},{64,96... | collective-permute-start | bytes 811016 | tf_op jit(solution)/shard_map/ppermute | solution.py:403
  57.2 7.5 %collective-permute-start.18 = (bf16[256,256]{1,0:T(8,128)(2,1)S(1)}, bf16[256,256]{1,0:T(8,128)(2,1)S(1)}, u32[]{:S(2)}, u32[]{:S(2)}) collective-permute-start(bf16[256,256]{1,0:T(8,128)(2,1)S(1)} %get-tuple-element.43.refs_0_), channel_id=1, source_target_pairs={{0,6},{1,7},{2,0},{3,1},{4,2},{5,3},{6,4},{7,5},{8,14},{9,15},{10,... | collective-permute-start | bytes 393224 | tf_op jit(solution)/shard_map/ppermute | solution.py:410
  59.4 7.7 %collective-permute-start.17 = (bf16[256,256]{1,0:T(8,128)(2,1)S(1)}, bf16[256,256]{1,0:T(8,128)(2,1)S(1)}, u32[]{:S(2)}, u32[]{:S(2)}) collective-permute-start(bf16[256,256]{1,0:T(8,128)(2,1)S(1)} %get-tuple-element.43.refs_0_), channel_id=1, source_target_pairs={{0,4},{1,5},{2,6},{3,7},{4,0},{5,1},{6,2},{7,3},{8,12},{9,13},{10,... | collective-permute-start | bytes 393224 | tf_op jit(solution)/shard_map/ppermute | solution.py:410
  60.5 7.9 %collective-permute-start.16 = (bf16[256,256]{1,0:T(8,128)(2,1)S(1)}, bf16[256,256]{1,0:T(8,128)(2,1)S(1)}, u32[]{:S(2)}, u32[]{:S(2)}) collective-permute-start(bf16[256,256]{1,0:T(8,128)(2,1)S(1)} %get-tuple-element.43.refs_0_), channel_id=1, source_target_pairs={{0,2},{1,3},{2,4},{3,5},{4,6},{5,7},{6,0},{7,1},{8,10},{9,11},{10,... | collective-permute-start | bytes 393224 | tf_op jit(solution)/shard_map/ppermute | solution.py:410
  61.2 10.6 %collective-permute-start.19 = (bf16[256,256]{1,0:T(8,128)(2,1)S(1)}, bf16[256,256]{1,0:T(8,128)(2,1)S(1)}, u32[]{:S(2)}, u32[]{:S(2)}) collective-permute-start(bf16[256,256]{1,0:T(8,128)(2,1)S(1)} %get-tuple-element.43.refs_0_), channel_id=1, source_target_pairs={{0,1},{1,0},{2,3},{3,2},{4,5},{5,4},{6,7},{7,6},{8,9},{9,8},{10,11... | collective-permute-start | bytes 393224 | tf_op jit(solution)/shard_map/ppermute | solution.py:414
  64.7 7.0 %collective-permute-start.22 = (bf16[256,256]{1,0:T(8,128)(2,1)S(1)}, bf16[256,256]{1,0:T(8,128)(2,1)S(1)}, u32[]{:S(2)}, u32[]{:S(2)}) collective-permute-start(bf16[256,256]{1,0:T(8,128)(2,1)S(1)} %collective-permute-done.18.refs_3_), channel_id=1, source_target_pairs={{0,1},{1,0},{2,3},{3,2},{4,5},{5,4},{6,7},{7,6},{8,9},{9,8},{10,11... | collective-permute-start | bytes 393224 | tf_op jit(solution)/shard_map/ppermute | solution.py:414
  68.5 10.5 %collective-permute-start.24 = (bf16[528,256]{1,0:T(8,128)(2,1)S(1)}, bf16[528,256]{1,0:T(8,128)(2,1)S(1)}, u32[]{:S(2)}, u32[]{:S(2)}) collective-permute-start(bf16[528,256]{1,0:T(8,128)(2,1)S(1)} %add_convert_fusion), channel_id=1, source_target_pairs={{0,64},{8,72},{16,80},{24,88},{32,96},{40,104},{48,112},{56,120},{... | collective-permute-start | bytes 811016 | tf_op jit(solution)/shard_map/ppermute | solution.py:403
  79.0 46.0 %all-to-all-start = ((bf16[16,256,256]{2,1,0:T(8,128)(2,1)}), bf16[16,256,256]{2,1,0:T(8,128)(2,1)S(1)}, u32[]{:S(2)}, u32[]{:S(2)}) async-start(bf16[16,256,256]{2,1,0:T(8,128)(2,1)} %bitcast.19), calls=%async_computation | async-start | bytes 4194304 | tf_op jit(solution)/shard_map/all_to_all | solution.py:387
  88.1 9.6 %collective-permute-start.28 = (f32[272,256]{1,0:T(8,128)S(1)}, f32[272,256]{1,0:T(8,128)S(1)}, u32[]{:S(2)}, u32[]{:S(2)}) collective-permute-start(f32[272,256]{1,0:T(8,128)S(1)} %fusion), channel_id=1, source_target_pairs={{0,6},{1,7},{2,0},{3,1},{4,2},{5,3},{6,4},{7,5},{8,14},{9,15},{10,... | collective-permute-start | bytes 835592 | tf_op jit(solution)/shard_map/ppermute | solution.py:410
  88.7 15.6 %collective-permute-start.27 = (f32[272,256]{1,0:T(8,128)S(1)}, f32[272,256]{1,0:T(8,128)S(1)}, u32[]{:S(2)}, u32[]{:S(2)}) collective-permute-start(f32[272,256]{1,0:T(8,128)S(1)} %fusion), channel_id=1, source_target_pairs={{0,2},{1,3},{2,4},{3,5},{4,6},{5,7},{6,0},{7,1},{8,10},{9,11},{10,... | collective-permute-start | bytes 835592 | tf_op jit(solution)/shard_map/ppermute | solution.py:410
  90.2 14.1 %collective-permute-start.26 = (f32[272,256]{1,0:T(8,128)S(1)}, f32[272,256]{1,0:T(8,128)S(1)}, u32[]{:S(2)}, u32[]{:S(2)}) collective-permute-start(f32[272,256]{1,0:T(8,128)S(1)} %fusion), channel_id=1, source_target_pairs={{0,4},{1,5},{2,6},{3,7},{4,0},{5,1},{6,2},{7,3},{8,12},{9,13},{10,... | collective-permute-start | bytes 835592 | tf_op jit(solution)/shard_map/ppermute | solution.py:410
  104.4 13.2 %collective-permute-start.31 = (bf16[272,256]{1,0:T(8,128)(2,1)S(1)}, bf16[272,256]{1,0:T(8,128)(2,1)S(1)}, u32[]{:S(2)}, u32[]{:S(2)}) collective-permute-start(bf16[272,256]{1,0:T(8,128)(2,1)S(1)} %add_convert_fusion.1), channel_id=1, source_target_pairs={{0,24},{8,0},{16,8},{24,16},{32,56},{40,32},{48,40},{56,48},{64,88... | collective-permute-start | bytes 417800 | tf_op jit(solution)/shard_map/ppermute | solution.py:398
  107.6 10.0 %collective-permute-start.30 = (bf16[272,256]{1,0:T(8,128)(2,1)S(1)}, bf16[272,256]{1,0:T(8,128)(2,1)S(1)}, u32[]{:S(2)}, u32[]{:S(2)}) collective-permute-start(bf16[272,256]{1,0:T(8,128)(2,1)S(1)} %add_convert_fusion.1), channel_id=1, source_target_pairs={{0,8},{8,16},{16,24},{24,0},{32,40},{40,48},{48,56},{56,32},{64,72... | collective-permute-start | bytes 417800 | tf_op jit(solution)/shard_map/ppermute | solution.py:398
  107.6 14.3 %collective-permute-start.29 = (bf16[272,256]{1,0:T(8,128)(2,1)S(1)}, bf16[272,256]{1,0:T(8,128)(2,1)S(1)}, u32[]{:S(2)}, u32[]{:S(2)}) collective-permute-start(bf16[272,256]{1,0:T(8,128)(2,1)S(1)} %add_convert_fusion.1), channel_id=1, source_target_pairs={{0,16},{8,24},{16,0},{24,8},{32,48},{40,56},{48,32},{56,40},{64,80... | collective-permute-start | bytes 417800 | tf_op jit(solution)/shard_map/ppermute | solution.py:398
  (16 other events, 121.9 us)

commit v9 on v7

--- a/solution.py
+++ b/solution.py
@@ -102,7 +102,7 @@
     copies[1].wait()
     for k in range(pieces):
         copies[2 + k].wait()
-        lax.fori_loop(k * each, (k + 1) * each, add_tile, 0, unroll=2)
+        lax.fori_loop(k * each, (k + 1) * each, add_tile, 0, unroll=4)
 
     @pl.when(spill[0] >= 0)
     def _():
@@ -158,7 +158,7 @@
             joined[0:half, lanes] = tops[kz][kx]
             joined[half:width, lanes] = lows[kx][kz]
 
-    def dest(j, carry):
+    for j in range(4):
         chunk = 2 * lax.rem(place_ref[0] + j, 4) + place_ref[1]
         blocks = [
             jnp.concatenate([at_ref[k, per * chunk + r] for r in range(per)], axis=1)
@@ -169,9 +169,6 @@
         whole = deg_ref[:, pl.ds(pl.multiple_of(chunk * rows, rows), rows)]
         degree = whole if out_ref.dtype == F32 else two_rows(whole)
         out_ref[j, width:, :] = spaced(degree, out_ref.dtype)
-        return carry
-
-    lax.fori_loop(0, 4, dest, 0)
 
 
 def two_rows(whole):
@@ -238,7 +235,7 @@
 def backward(place, parts, at):
     sources, dests = at.shape[0] - 1, at.shape[1]
     _, width = parts[0].shape
-    pieces = 8
+    pieces = 4
     vmem = pl.BlockSpec(memory_space=pltpu.VMEM)
     return pl.pallas_call(
         backward_kernel,
@@ -375,9 +372,13 @@
     return lax.ppermute(x, "nodes", moves)
 
 
-def send_flip(x, bit):
+def send_x_flip(x, bit):
     moves = [(4 * i + j, 4 * (i ^ bit) + j) for i in range(4) for j in range(4)]
     return lax.ppermute(x, "nodes", moves)
+
+
+def pair_sum(one, other):
+    return one.astype(F32) + other.astype(F32)
 
 
 PARTNER = [(i, i ^ 1) for i in range(8)]
@@ -438,27 +439,29 @@
     same_core = [mean_grad, next_y, send_y(mean_grad, 2), last_y]
 
     part, self_part = weights(node_feats, pre_grad, mean_t, w_self)
-    part = (part.astype(F32) + send_flip(part, 1).astype(F32)).astype(BF)
+    part = pair_sum(part, send_x_flip(part, 1)).astype(BF)
     other_core = [send_core(g) for g in same_core]
-    flipped = send_flip(part, 2)
+    flipped = send_x_flip(part, 2)
 
     src = backward(mine, same_core + other_core, at)
     src, part, flipped = lax.optimization_barrier((src, part, flipped))
     parts = swap(src.reshape(nodes, rows_dev, width), "nodes")
 
-    part = (part.astype(F32) + flipped.astype(F32)).astype(BF)
+    part = pair_sum(part, flipped)
     halves = (part[:width], part[width : 2 * width])
     kept = jnp.concatenate([jnp.where(zero, *halves), part[2 * width :]])
     given = jnp.concatenate([jnp.where(zero, *halves[::-1]), part[2 * width :]])
-    part = (kept.astype(F32) + send_core(given).astype(F32)).astype(BF)
+    part = (kept + send_core(given)).astype(BF)
     part = add_terms([part] + [send_y(part, k) for k in (1, 2, 3)]).astype(BF)
-    part = add_terms([part] + [send_z(part, k) for k in (1, 2, 3)])
+    terms = [part] + [send_z(part, k) for k in (1, 2, 3)]
+
+    feat_grad = finish(parts, self_part)
+    feat_grad, terms = lax.optimization_barrier((feat_grad, terms))
+    part = add_terms(terms)
     other = send_core(part)
     bias_grad = part[width]
     self_grad = jnp.where(zero, part[:width], other[:width])
     neigh_grad = jnp.where(zero, other[:width], part[:width])
-
-    feat_grad = finish(parts, self_part)
     return (layer_out, feat_grad, self_grad, neigh_grad, bias_grad)
 
 

time: 126 us -> 122 us (0.968)
  Pallas kernels: 25.7 us -> 23.1 us
    ppermute x15, waiting for transfers between devices: 25.8 us -> 11.7 us  [send_node(): return lax.ppermute(x, 'nodes', moves)]
    all_to_all x1, waiting for transfers between devices: 0.01 us -> 13.1 us  [swap(): return lax.all_to_all(x, axis, 0, 0, tiled=True)]
    pallas_call x2, Pallas kernels: 7.61 us -> 6.32 us  [forward(): pl.pallas_call(forward_kernel, out_shape=jax.ShapeDtypeStruct((4, width +...]
  transfers between devices with their start and end apart: 34 -> 34, of which waited for: 15 -> 17; matrix products, arithmetic and copies ran while one was open for 1% -> 1% of each run, Pallas kernels for 16% -> 15%
where the time goes in v9:
time: 122 us; the launch traced here: 121 us
  waiting for transfers between devices  48.1 us (39%)
  starting transfers between devices  45.9 us (38%)
  Pallas kernels  23.1 us (19%)
  local copies, waits for them, and re-layouts  1.5 us (1%)
  other arithmetic  1.35 us (1%)
    ppermute x9, waiting for transfers between devices, send_y(): return lax.ppermute(x, 'cols', along_y(step))  20.4 us
    ppermute x15, starting transfers between devices, send_node(): return lax.ppermute(x, 'nodes', moves)  20.4 us
    all_to_all x1, waiting for transfers between devices, swap(): return lax.all_to_all(x, axis, 0, 0, tiled=True)  13.1 us
    ppermute x9, starting transfers between devices, send_y(): return lax.ppermute(x, 'cols', along_y(step))  12.6 us
    ppermute x15, waiting for transfers between devices, send_node(): return lax.ppermute(x, 'nodes', moves)  11.7 us
    pallas_call x1, Pallas kernels, build(): pl.pallas_call(build_kernel, out_shape=(jax.ShapeDtypeStruct((sources + 1...  7.63 us
    all_to_all x1, starting transfers between devices, swap(): return lax.all_to_all(x, axis, 0, 0, tiled=True)  7.27 us
    pallas_call x1, Pallas kernels, backward(): pl.pallas_call(backward_kernel, out_shape=in_hbm((sources * 128, width),...  6.69 us
  transfers between devices with their start and end apart: 34, of which 17 were waited for; matrix products, arithmetic and copies ran while one was open for 1% of the time, Pallas kernels for 15%

profile of v9, /device:TPU:0, one launch (start us, length us, event | category | flops | bytes accessed | tf_op | source)
XLA Modules:
  0.0 120.9 jit_solution(2467148319118024199)
XLA Ops:
  1.6 2.9 %collective-permute-start.2 = (bf16[128,256]{1,0:T(8,128)(2,1)S(1)}, bf16[128,256]{1,0:T(8,128)(2,1)S(1)}, u32[]{:S(2)}, u32[]{:S(2)}) collective-permute-start(bf16[128,256]{1,0:T(8,128)(2,1)S(1)} %get-tuple-element.32), channel_id=1, source_target_pairs={{0,96},{8,104},{16,112},{24,120},{32,0},{40,8},{48,16},{56,24},{64... | collective-permute-start | bytes 196616 | tf_op jit(solution)/shard_map/ppermute | solution.py:372
  6.2 4.0 %collective-permute-start.5 = (bf16[128,256]{1,0:T(8,128)(2,1)S(1)}, bf16[128,256]{1,0:T(8,128)(2,1)S(1)}, u32[]{:S(2)}, u32[]{:S(2)}) collective-permute-start(bf16[128,256]{1,0:T(8,128)(2,1)S(1)} %get-tuple-element.33), channel_id=1, source_target_pairs={{0,24},{8,0},{16,8},{24,16},{32,56},{40,32},{48,40},{56,48},{64,88... | collective-permute-start | bytes 196616 | tf_op jit(solution)/shard_map/ppermute | solution.py:372
  12.2 4.0 %collective-permute-done.4 = bf16[128,256]{1,0:T(8,128)(2,1)S(1)} collective-permute-done((bf16[128,256]{1,0:T(8,128)(2,1)S(1)}, bf16[128,256]{1,0:T(8,128)(2,1)S(1)}, u32[]{:S(2)}, u32[]{:S(2)}) %collective-permute-start.4) | collective-permute-done | bytes 65568 | tf_op jit(solution)/shard_map/ppermute | solution.py:372
  16.6 2.4 %collective-permute-start.11 = (bf16[4,128,256]{2,1,0:T(8,128)(2,1)S(1)}, bf16[4,128,256]{2,1,0:T(8,128)(2,1)S(1)}, u32[]{:S(2)}, u32[]{:S(2)}) collective-permute-start(bf16[4,128,256]{2,1,0:T(8,128)(2,1)S(1)} %pad_maximum_fusion.3.refs_4_), channel_id=1, source_target_pairs={{0,96},{8,104},{16,112},{24,120},{32,0},{40,8},{48,16},{56,24},{64... | collective-permute-start | bytes 786440 | tf_op jit(solution)/shard_map/ppermute | solution.py:372
  19.0 1.5 %collective-permute-start.10 = (bf16[4,128,256]{2,1,0:T(8,128)(2,1)S(1)}, bf16[4,128,256]{2,1,0:T(8,128)(2,1)S(1)}, u32[]{:S(2)}, u32[]{:S(2)}) collective-permute-start(bf16[4,128,256]{2,1,0:T(8,128)(2,1)S(1)} %pad_maximum_fusion.3.refs_4_), channel_id=1, source_target_pairs={{0,64},{8,72},{16,80},{24,88},{32,96},{40,104},{48,112},{56,120},{... | collective-permute-start | bytes 786440 | tf_op jit(solution)/shard_map/ppermute | solution.py:372
  22.1 5.8 %collective-permute-done.11.refs_7_ = bf16[4,128,256]{2,1,0:T(8,128)(2,1)S(1)} collective-permute-done((bf16[4,128,256]{2,1,0:T(8,128)(2,1)S(1)}, bf16[4,128,256]{2,1,0:T(8,128)(2,1)S(1)}, u32[]{:S(2)}, u32[]{:S(2)}) %collective-permute-start.11) | collective-permute-done | bytes 262176 | tf_op jit(solution)/shard_map/ppermute | solution.py:372
  27.9 7.6 %build.1 = (bf16[33,16,128,128]{3,2,1,0:T(8,128)(2,1)S(1)}, f32[1,2048]{1,0:T(1,128)S(1)}) custom-call(s32[1,352]{1,0:T(1,128)} %rows_ref.1, s32[1,352]{1,0:T(1,128)} %cols_ref.1, s32[1,352,16,128]{3,2,1,0:T(8,128)} %bits_all.1, bf16[4,128,256]{2,1,0:T(8,128)(2,1)S(1)} %pad_maximum_fusion.2.gate_ref.refs_0_), custom_call_target="tpu_custom_call" | custom-call | bytes 31457280 | tf_op jit(solution)/shard_map/build/pallas_call | solution.py:124
  35.6 3.2 %forward.3 = bf16[4,272,256]{2,1,0:T(8,128)(2,1)S(1)} custom-call(s32[4]{0:T(128)S(1)} %get-tuple-element.39.place_ref, bf16[4,128,256]{2,1,0:T(8,128)(2,1)S(1)} %pad_maximum_fusion.2.gate_ref.refs_0_, bf16[4,128,256]{2,1,0:T(8,128)(2,1)S(1)} %collective-permute-done.6.refs_1_, bf16[4,128,256]{2,1,0:T(8,128)(2,1)S(1)} %collective-permute-done.7.refs_2_, ...), custom_call_target="tpu_custom_call" | custom-call | flops 2147483648 | bytes 10485760 | tf_op jit(solution)/shard_map/forward/pallas_call | solution.py:194
  39.0 3.2 %forward.2.keep_ref = f32[4,272,256]{2,1,0:T(8,128)S(1)} custom-call(s32[4]{0:T(128)S(1)} %get-tuple-element.34.place_ref, bf16[4,128,256]{2,1,0:T(8,128)(2,1)S(1)} %pad_maximum_fusion.2.gate_ref.refs_0_, bf16[4,128,256]{2,1,0:T(8,128)(2,1)S(1)} %collective-permute-done.6.refs_1_, bf16[4,128,256]{2,1,0:T(8,128)(2,1)S(1)} %collective-permute-done.7.refs_2_, ...), custom_call_target="tpu_custom_call" | custom-call | flops 2147483648 | bytes 10485760 | tf_op jit(solution)/shard_map/forward/pallas_call | solution.py:194
  42.3 1.7 %collective-permute-start.13 = (bf16[272,256]{1,0:T(8,128)(2,1)S(1)}, bf16[272,256]{1,0:T(8,128)(2,1)S(1)}, u32[]{:S(2)}, u32[]{:S(2)}) collective-permute-start(bf16[272,256]{1,0:T(8,128)(2,1)S(1)} %get-tuple-element.41), channel_id=1, source_target_pairs={{0,2},{1,3},{2,4},{3,5},{4,6},{5,7},{6,0},{7,1},{8,10},{9,11},{10,... | collective-permute-start | bytes 417800 | tf_op jit(solution)/shard_map/ppermute | solution.py:388
  43.9 2.9 %collective-permute-start.14 = (bf16[272,256]{1,0:T(8,128)(2,1)S(1)}, bf16[272,256]{1,0:T(8,128)(2,1)S(1)}, u32[]{:S(2)}, u32[]{:S(2)}) collective-permute-start(bf16[272,256]{1,0:T(8,128)(2,1)S(1)} %get-tuple-element.42), channel_id=1, source_target_pairs={{0,4},{1,5},{2,6},{3,7},{4,0},{5,1},{6,2},{7,3},{8,12},{9,13},{10,... | collective-permute-start | bytes 417800 | tf_op jit(solution)/shard_map/ppermute | solution.py:388
  49.7 4.2 %collective-permute-done.14.r2_ref = bf16[272,256]{1,0:T(8,128)(2,1)S(1)} collective-permute-done((bf16[272,256]{1,0:T(8,128)(2,1)S(1)}, bf16[272,256]{1,0:T(8,128)(2,1)S(1)}, u32[]{:S(2)}, u32[]{:S(2)}) %collective-permute-start.14) | collective-permute-done | bytes 139296 | tf_op jit(solution)/shard_map/ppermute | solution.py:388
  55.2 2.0 %collective-permute-start.23 = (bf16[528,256]{1,0:T(8,128)(2,1)S(1)}, bf16[528,256]{1,0:T(8,128)(2,1)S(1)}, u32[]{:S(2)}, u32[]{:S(2)}) collective-permute-start(bf16[528,256]{1,0:T(8,128)(2,1)S(1)} %get-tuple-element.48), channel_id=1, source_target_pairs={{0,32},{8,40},{16,48},{24,56},{32,0},{40,8},{48,16},{56,24},{64,96... | collective-permute-start | bytes 811016 | tf_op jit(solution)/shard_map/ppermute | solution.py:377
  57.2 2.1 %collective-permute-start.18 = (bf16[256,256]{1,0:T(8,128)(2,1)S(1)}, bf16[256,256]{1,0:T(8,128)(2,1)S(1)}, u32[]{:S(2)}, u32[]{:S(2)}) collective-permute-start(bf16[256,256]{1,0:T(8,128)(2,1)S(1)} %get-tuple-element.45.refs_0_), channel_id=1, source_target_pairs={{0,6},{1,7},{2,0},{3,1},{4,2},{5,3},{6,4},{7,5},{8,14},{9,15},{10,... | collective-permute-start | bytes 393224 | tf_op jit(solution)/shard_map/ppermute | solution.py:388
  61.2 3.5 %collective-permute-done.18.refs_3_ = bf16[256,256]{1,0:T(8,128)(2,1)S(1)} collective-permute-done((bf16[256,256]{1,0:T(8,128)(2,1)S(1)}, bf16[256,256]{1,0:T(8,128)(2,1)S(1)}, u32[]{:S(2)}, u32[]{:S(2)}) %collective-permute-start.18) | collective-permute-done | bytes 131104 | tf_op jit(solution)/shard_map/ppermute | solution.py:388
  64.7 2.3 %collective-permute-done.17.refs_2_ = bf16[256,256]{1,0:T(8,128)(2,1)S(1)} collective-permute-done((bf16[256,256]{1,0:T(8,128)(2,1)S(1)}, bf16[256,256]{1,0:T(8,128)(2,1)S(1)}, u32[]{:S(2)}, u32[]{:S(2)}) %collective-permute-start.17) | collective-permute-done | bytes 131104 | tf_op jit(solution)/shard_map/ppermute | solution.py:388
  68.5 3.3 %collective-permute-start.24 = (bf16[528,256]{1,0:T(8,128)(2,1)S(1)}, bf16[528,256]{1,0:T(8,128)(2,1)S(1)}, u32[]{:S(2)}, u32[]{:S(2)}) collective-permute-start(bf16[528,256]{1,0:T(8,128)(2,1)S(1)} %add_convert_fusion), channel_id=1, source_target_pairs={{0,64},{8,72},{16,80},{24,88},{32,96},{40,104},{48,112},{56,120},{... | collective-permute-start | bytes 811016 | tf_op jit(solution)/shard_map/ppermute | solution.py:377
  71.8 6.7 %backward.1 = bf16[4096,256]{1,0:T(8,128)(2,1)} custom-call(s32[4]{0:T(128)S(1)} %get-tuple-element.34.place_ref, bf16[256,256]{1,0:T(8,128)(2,1)S(1)} %get-tuple-element.45.refs_0_, bf16[256,256]{1,0:T(8,128)(2,1)S(1)} %collective-permute-done.16.refs_1_, bf16[256,256]{1,0:T(8,128)(2,1)S(1)} %collective-permute-done.17.refs_2_, ...), custom_call_target="tpu_custom_call" | custom-call | flops 4294967296 | bytes 20971520 | tf_op jit(solution)/shard_map/backward/pallas_call | solution.py:240
  79.0 7.3 %all-to-all-start = ((bf16[16,256,256]{2,1,0:T(8,128)(2,1)}), bf16[16,256,256]{2,1,0:T(8,128)(2,1)S(1)}, u32[]{:S(2)}, u32[]{:S(2)}) async-start(bf16[16,256,256]{2,1,0:T(8,128)(2,1)} %bitcast.19), calls=%async_computation | async-start | bytes 4194304 | tf_op jit(solution)/shard_map/all_to_all | solution.py:361
  86.5 1.5 %collective-permute-done.25 = f32[272,256]{1,0:T(8,128)S(1)} collective-permute-done((f32[272,256]{1,0:T(8,128)S(1)}, f32[272,256]{1,0:T(8,128)S(1)}, u32[]{:S(2)}, u32[]{:S(2)}) %collective-permute-start.25) | collective-permute-done | bytes 278560 | tf_op jit(solution)/shard_map/ppermute | solution.py:392
  90.8 3.9 %collective-permute-done.28 = bf16[272,256]{1,0:T(8,128)(2,1)S(1)} collective-permute-done((bf16[272,256]{1,0:T(8,128)(2,1)S(1)}, bf16[272,256]{1,0:T(8,128)(2,1)S(1)}, u32[]{:S(2)}, u32[]{:S(2)}) %collective-permute-start.28) | collective-permute-done | bytes 139296 | tf_op jit(solution)/shard_map/ppermute | solution.py:388
  94.6 3.7 %collective-permute-done.27 = bf16[272,256]{1,0:T(8,128)(2,1)S(1)} collective-permute-done((bf16[272,256]{1,0:T(8,128)(2,1)S(1)}, bf16[272,256]{1,0:T(8,128)(2,1)S(1)}, u32[]{:S(2)}, u32[]{:S(2)}) %collective-permute-start.27) | collective-permute-done | bytes 139296 | tf_op jit(solution)/shard_map/ppermute | solution.py:388
  98.4 3.2 %collective-permute-start.31 = (bf16[272,256]{1,0:T(8,128)(2,1)S(1)}, bf16[272,256]{1,0:T(8,128)(2,1)S(1)}, u32[]{:S(2)}, u32[]{:S(2)}) collective-permute-start(bf16[272,256]{1,0:T(8,128)(2,1)S(1)} %add_convert_fusion.1), channel_id=1, source_target_pairs={{0,24},{8,0},{16,8},{24,16},{32,56},{40,32},{48,40},{56,48},{64,88... | collective-permute-start | bytes 417800 | tf_op jit(solution)/shard_map/ppermute | solution.py:372
  103.3 13.1 %all-to-all-done.parts_ref = bf16[16,256,256]{2,1,0:T(8,128)(2,1)S(1)} async-done(((bf16[16,256,256]{2,1,0:T(8,128)(2,1)}), bf16[16,256,256]{2,1,0:T(8,128)(2,1)S(1)}, u32[]{:S(2)}, u32[]{:S(2)}) %all-to-all-start) | async-done | bytes 2097184 | tf_op jit(solution)/shard_map/all_to_all | solution.py:361
  (78 shorter events, 24.0 us)
Async XLA Ops:
  1.6 8.7 %collective-permute-start.2 = (bf16[128,256]{1,0:T(8,128)(2,1)S(1)}, bf16[128,256]{1,0:T(8,128)(2,1)S(1)}, u32[]{:S(2)}, u32[]{:S(2)}) collective-permute-start(bf16[128,256]{1,0:T(8,128)(2,1)S(1)} %get-tuple-element.32), channel_id=1, source_target_pairs={{0,96},{8,104},{16,112},{24,120},{32,0},{40,8},{48,16},{56,24},{64... | collective-permute-start | bytes 196616 | tf_op jit(solution)/shard_map/ppermute | solution.py:372
  4.5 7.1 %collective-permute-start.1 = (bf16[128,256]{1,0:T(8,128)(2,1)S(1)}, bf16[128,256]{1,0:T(8,128)(2,1)S(1)}, u32[]{:S(2)}, u32[]{:S(2)}) collective-permute-start(bf16[128,256]{1,0:T(8,128)(2,1)S(1)} %get-tuple-element.32), channel_id=1, source_target_pairs={{0,64},{8,72},{16,80},{24,88},{32,96},{40,104},{48,112},{56,120},{... | collective-permute-start | bytes 196616 | tf_op jit(solution)/shard_map/ppermute | solution.py:372
  16.6 11.4 %collective-permute-start.11 = (bf16[4,128,256]{2,1,0:T(8,128)(2,1)S(1)}, bf16[4,128,256]{2,1,0:T(8,128)(2,1)S(1)}, u32[]{:S(2)}, u32[]{:S(2)}) collective-permute-start(bf16[4,128,256]{2,1,0:T(8,128)(2,1)S(1)} %pad_maximum_fusion.3.refs_4_), channel_id=1, source_target_pairs={{0,96},{8,104},{16,112},{24,120},{32,0},{40,8},{48,16},{56,24},{64... | collective-permute-start | bytes 786440 | tf_op jit(solution)/shard_map/ppermute | solution.py:372
  19.0 16.6 %collective-permute-start.10 = (bf16[4,128,256]{2,1,0:T(8,128)(2,1)S(1)}, bf16[4,128,256]{2,1,0:T(8,128)(2,1)S(1)}, u32[]{:S(2)}, u32[]{:S(2)}) collective-permute-start(bf16[4,128,256]{2,1,0:T(8,128)(2,1)S(1)} %pad_maximum_fusion.3.refs_4_), channel_id=1, source_target_pairs={{0,64},{8,72},{16,80},{24,88},{32,96},{40,104},{48,112},{56,120},{... | collective-permute-start | bytes 786440 | tf_op jit(solution)/shard_map/ppermute | solution.py:372
  20.5 15.1 %collective-permute-start.9 = (bf16[4,128,256]{2,1,0:T(8,128)(2,1)S(1)}, bf16[4,128,256]{2,1,0:T(8,128)(2,1)S(1)}, u32[]{:S(2)}, u32[]{:S(2)}) collective-permute-start(bf16[4,128,256]{2,1,0:T(8,128)(2,1)S(1)} %pad_maximum_fusion.3.refs_4_), channel_id=1, source_target_pairs={{0,32},{8,40},{16,48},{24,56},{32,64},{40,72},{48,80},{56,88},{64,... | collective-permute-start | bytes 786440 | tf_op jit(solution)/shard_map/ppermute | solution.py:372
  20.5 15.1 %collective-permute-start.8 = (bf16[4,128,256]{2,1,0:T(8,128)(2,1)S(1)}, bf16[4,128,256]{2,1,0:T(8,128)(2,1)S(1)}, u32[]{:S(2)}, u32[]{:S(2)}) collective-permute-start(bf16[4,128,256]{2,1,0:T(8,128)(2,1)S(1)} %pad_maximum_fusion.2.gate_ref.refs_0_), channel_id=1, source_target_pairs={{0,24},{8,0},{16,8},{24,16},{32,56},{40,32},{48,40},{56,48},{64,88... | collective-permute-start | bytes 786440 | tf_op jit(solution)/shard_map/ppermute | solution.py:372
  21.3 14.3 %collective-permute-start.7 = (bf16[4,128,256]{2,1,0:T(8,128)(2,1)S(1)}, bf16[4,128,256]{2,1,0:T(8,128)(2,1)S(1)}, u32[]{:S(2)}, u32[]{:S(2)}) collective-permute-start(bf16[4,128,256]{2,1,0:T(8,128)(2,1)S(1)} %pad_maximum_fusion.2.gate_ref.refs_0_), channel_id=1, source_target_pairs={{0,16},{8,24},{16,0},{24,8},{32,48},{40,56},{48,32},{56,40},{64,80... | collective-permute-start | bytes 786440 | tf_op jit(solution)/shard_map/ppermute | solution.py:372
  27.9 7.7 %collective-permute-start.6 = (bf16[4,128,256]{2,1,0:T(8,128)(2,1)S(1)}, bf16[4,128,256]{2,1,0:T(8,128)(2,1)S(1)}, u32[]{:S(2)}, u32[]{:S(2)}) collective-permute-start(bf16[4,128,256]{2,1,0:T(8,128)(2,1)S(1)} %pad_maximum_fusion.2.gate_ref.refs_0_), channel_id=1, source_target_pairs={{0,8},{8,16},{16,24},{24,0},{32,40},{40,48},{48,56},{56,32},{64,72... | collective-permute-start | bytes 786440 | tf_op jit(solution)/shard_map/ppermute | solution.py:372
  42.3 7.4 %collective-permute-start.13 = (bf16[272,256]{1,0:T(8,128)(2,1)S(1)}, bf16[272,256]{1,0:T(8,128)(2,1)S(1)}, u32[]{:S(2)}, u32[]{:S(2)}) collective-permute-start(bf16[272,256]{1,0:T(8,128)(2,1)S(1)} %get-tuple-element.41), channel_id=1, source_target_pairs={{0,2},{1,3},{2,4},{3,5},{4,6},{5,7},{6,0},{7,1},{8,10},{9,11},{10,... | collective-permute-start | bytes 417800 | tf_op jit(solution)/shard_map/ppermute | solution.py:388
  43.9 9.9 %collective-permute-start.14 = (bf16[272,256]{1,0:T(8,128)(2,1)S(1)}, bf16[272,256]{1,0:T(8,128)(2,1)S(1)}, u32[]{:S(2)}, u32[]{:S(2)}) collective-permute-start(bf16[272,256]{1,0:T(8,128)(2,1)S(1)} %get-tuple-element.42), channel_id=1, source_target_pairs={{0,4},{1,5},{2,6},{3,7},{4,0},{5,1},{6,2},{7,3},{8,12},{9,13},{10,... | collective-permute-start | bytes 417800 | tf_op jit(solution)/shard_map/ppermute | solution.py:388
  46.8 7.0 %collective-permute-start.15 = (bf16[272,256]{1,0:T(8,128)(2,1)S(1)}, bf16[272,256]{1,0:T(8,128)(2,1)S(1)}, u32[]{:S(2)}, u32[]{:S(2)}) collective-permute-start(bf16[272,256]{1,0:T(8,128)(2,1)S(1)} %get-tuple-element.43), channel_id=1, source_target_pairs={{0,6},{1,7},{2,0},{3,1},{4,2},{5,3},{6,4},{7,5},{8,14},{9,15},{10,... | collective-permute-start | bytes 417800 | tf_op jit(solution)/shard_map/ppermute | solution.py:388
  55.2 13.2 %collective-permute-start.23 = (bf16[528,256]{1,0:T(8,128)(2,1)S(1)}, bf16[528,256]{1,0:T(8,128)(2,1)S(1)}, u32[]{:S(2)}, u32[]{:S(2)}) collective-permute-start(bf16[528,256]{1,0:T(8,128)(2,1)S(1)} %get-tuple-element.48), channel_id=1, source_target_pairs={{0,32},{8,40},{16,48},{24,56},{32,0},{40,8},{48,16},{56,24},{64,96... | collective-permute-start | bytes 811016 | tf_op jit(solution)/shard_map/ppermute | solution.py:377
  57.2 7.5 %collective-permute-start.18 = (bf16[256,256]{1,0:T(8,128)(2,1)S(1)}, bf16[256,256]{1,0:T(8,128)(2,1)S(1)}, u32[]{:S(2)}, u32[]{:S(2)}) collective-permute-start(bf16[256,256]{1,0:T(8,128)(2,1)S(1)} %get-tuple-element.45.refs_0_), channel_id=1, source_target_pairs={{0,6},{1,7},{2,0},{3,1},{4,2},{5,3},{6,4},{7,5},{8,14},{9,15},{10,... | collective-permute-start | bytes 393224 | tf_op jit(solution)/shard_map/ppermute | solution.py:388
  59.4 7.7 %collective-permute-start.17 = (bf16[256,256]{1,0:T(8,128)(2,1)S(1)}, bf16[256,256]{1,0:T(8,128)(2,1)S(1)}, u32[]{:S(2)}, u32[]{:S(2)}) collective-permute-start(bf16[256,256]{1,0:T(8,128)(2,1)S(1)} %get-tuple-element.45.refs_0_), channel_id=1, source_target_pairs={{0,4},{1,5},{2,6},{3,7},{4,0},{5,1},{6,2},{7,3},{8,12},{9,13},{10,... | collective-permute-start | bytes 393224 | tf_op jit(solution)/shard_map/ppermute | solution.py:388
  60.5 7.9 %collective-permute-start.16 = (bf16[256,256]{1,0:T(8,128)(2,1)S(1)}, bf16[256,256]{1,0:T(8,128)(2,1)S(1)}, u32[]{:S(2)}, u32[]{:S(2)}) collective-permute-start(bf16[256,256]{1,0:T(8,128)(2,1)S(1)} %get-tuple-element.45.refs_0_), channel_id=1, source_target_pairs={{0,2},{1,3},{2,4},{3,5},{4,6},{5,7},{6,0},{7,1},{8,10},{9,11},{10,... | collective-permute-start | bytes 393224 | tf_op jit(solution)/shard_map/ppermute | solution.py:388
  61.2 10.6 %collective-permute-start.19 = (bf16[256,256]{1,0:T(8,128)(2,1)S(1)}, bf16[256,256]{1,0:T(8,128)(2,1)S(1)}, u32[]{:S(2)}, u32[]{:S(2)}) collective-permute-start(bf16[256,256]{1,0:T(8,128)(2,1)S(1)} %get-tuple-element.45.refs_0_), channel_id=1, source_target_pairs={{0,1},{1,0},{2,3},{3,2},{4,5},{5,4},{6,7},{7,6},{8,9},{9,8},{10,11... | collective-permute-start | bytes 393224 | tf_op jit(solution)/shard_map/ppermute | solution.py:392
  64.7 7.1 %collective-permute-start.22 = (bf16[256,256]{1,0:T(8,128)(2,1)S(1)}, bf16[256,256]{1,0:T(8,128)(2,1)S(1)}, u32[]{:S(2)}, u32[]{:S(2)}) collective-permute-start(bf16[256,256]{1,0:T(8,128)(2,1)S(1)} %collective-permute-done.18.refs_3_), channel_id=1, source_target_pairs={{0,1},{1,0},{2,3},{3,2},{4,5},{5,4},{6,7},{7,6},{8,9},{9,8},{10,11... | collective-permute-start | bytes 393224 | tf_op jit(solution)/shard_map/ppermute | solution.py:392
  68.5 10.5 %collective-permute-start.24 = (bf16[528,256]{1,0:T(8,128)(2,1)S(1)}, bf16[528,256]{1,0:T(8,128)(2,1)S(1)}, u32[]{:S(2)}, u32[]{:S(2)}) collective-permute-start(bf16[528,256]{1,0:T(8,128)(2,1)S(1)} %add_convert_fusion), channel_id=1, source_target_pairs={{0,64},{8,72},{16,80},{24,88},{32,96},{40,104},{48,112},{56,120},{... | collective-permute-start | bytes 811016 | tf_op jit(solution)/shard_map/ppermute | solution.py:377
  79.0 37.5 %all-to-all-start = ((bf16[16,256,256]{2,1,0:T(8,128)(2,1)}), bf16[16,256,256]{2,1,0:T(8,128)(2,1)S(1)}, u32[]{:S(2)}, u32[]{:S(2)}) async-start(bf16[16,256,256]{2,1,0:T(8,128)(2,1)} %bitcast.19), calls=%async_computation | async-start | bytes 4194304 | tf_op jit(solution)/shard_map/all_to_all | solution.py:361
  88.7 9.6 %collective-permute-start.27 = (bf16[272,256]{1,0:T(8,128)(2,1)S(1)}, bf16[272,256]{1,0:T(8,128)(2,1)S(1)}, u32[]{:S(2)}, u32[]{:S(2)}) collective-permute-start(bf16[272,256]{1,0:T(8,128)(2,1)S(1)} %fusion.1), channel_id=1, source_target_pairs={{0,2},{1,3},{2,4},{3,5},{4,6},{5,7},{6,0},{7,1},{8,10},{9,11},{10,... | collective-permute-start | bytes 417800 | tf_op jit(solution)/shard_map/ppermute | solution.py:388
  90.2 8.2 %collective-permute-start.26 = (bf16[272,256]{1,0:T(8,128)(2,1)S(1)}, bf16[272,256]{1,0:T(8,128)(2,1)S(1)}, u32[]{:S(2)}, u32[]{:S(2)}) collective-permute-start(bf16[272,256]{1,0:T(8,128)(2,1)S(1)} %fusion.1), channel_id=1, source_target_pairs={{0,4},{1,5},{2,6},{3,7},{4,0},{5,1},{6,2},{7,3},{8,12},{9,13},{10,... | collective-permute-start | bytes 417800 | tf_op jit(solution)/shard_map/ppermute | solution.py:388
  98.4 18.9 %collective-permute-start.31 = (bf16[272,256]{1,0:T(8,128)(2,1)S(1)}, bf16[272,256]{1,0:T(8,128)(2,1)S(1)}, u32[]{:S(2)}, u32[]{:S(2)}) collective-permute-start(bf16[272,256]{1,0:T(8,128)(2,1)S(1)} %add_convert_fusion.1), channel_id=1, source_target_pairs={{0,24},{8,0},{16,8},{24,16},{32,56},{40,32},{48,40},{56,48},{64,88... | collective-permute-start | bytes 417800 | tf_op jit(solution)/shard_map/ppermute | solution.py:372
  101.6 16.6 %collective-permute-start.30 = (bf16[272,256]{1,0:T(8,128)(2,1)S(1)}, bf16[272,256]{1,0:T(8,128)(2,1)S(1)}, u32[]{:S(2)}, u32[]{:S(2)}) collective-permute-start(bf16[272,256]{1,0:T(8,128)(2,1)S(1)} %add_convert_fusion.1), channel_id=1, source_target_pairs={{0,16},{8,24},{16,0},{24,8},{32,48},{40,56},{48,32},{56,40},{64,80... | collective-permute-start | bytes 417800 | tf_op jit(solution)/shard_map/ppermute | solution.py:372
  102.5 15.8 %collective-permute-start.29 = (bf16[272,256]{1,0:T(8,128)(2,1)S(1)}, bf16[272,256]{1,0:T(8,128)(2,1)S(1)}, u32[]{:S(2)}, u32[]{:S(2)}) collective-permute-start(bf16[272,256]{1,0:T(8,128)(2,1)S(1)} %add_convert_fusion.1), channel_id=1, source_target_pairs={{0,8},{8,16},{16,24},{24,0},{32,40},{40,48},{48,56},{56,32},{64,72... | collective-permute-start | bytes 417800 | tf_op jit(solution)/shard_map/ppermute | solution.py:372
  (16 other events, 121.5 us)

commit v10 on v9

--- a/solution.py
+++ b/solution.py
@@ -43,7 +43,7 @@
 
 
 def build_kernel(
-    rows_ref, cols_ref, bits_all, gate_ref, at_ref, deg_ref,
+    rows_ref, cols_ref, bits_all, gate_ref, clear_ref, at_ref, deg_ref,
     deg8, count, spill, row_ref, col_ref, bits_ref, sems,
 ):
     sources = at_ref.shape[0] - 1
@@ -67,12 +67,10 @@
 
     def clear(k, carry):
         for r in range(dests):
-            at_ref[k, r] = jnp.zeros((128, 128), BF)
             count[k * dests + r] = 0
         return carry
 
     lax.fori_loop(0, sources, clear, 0)
-    at_ref[sources, 0] = jnp.zeros((128, 128), BF)
     spill[0] = -1
     shifts = lax.broadcasted_iota(jnp.int32, (8, 128), 0)
 
@@ -116,7 +114,29 @@
         deg_ref[:, r * 128 : (r + 1) * 128] = jnp.sum(deg8[r], axis=0, keepdims=True)
 
 
-def build(rows, cols, bits, gate, sources, dests):
+def clear_kernel(gate_ref, at_ref):
+    def clear(k, carry):
+        for r in range(at_ref.shape[1]):
+            at_ref[k, r] = jnp.zeros((128, 128), BF)
+        return carry
+
+    lax.fori_loop(0, at_ref.shape[0], clear, 0)
+
+
+def cleared(gate, sources, dests):
+    return pl.pallas_call(
+        clear_kernel,
+        out_shape=jax.ShapeDtypeStruct((sources + 1, dests, 128, 128), BF),
+        in_specs=[pl.BlockSpec(memory_space=pl.ANY)],
+        out_specs=pl.BlockSpec(memory_space=pltpu.VMEM),
+        compiler_params=params(24),
+        cost_estimate=cost(0, 8 << 20),
+        name="clear",
+    )(gate)
+
+
+def build(rows, cols, bits, gate, at):
+    sources, dests = at.shape[0] - 1, at.shape[1]
     tiles = bits.shape[1]
     assert tiles <= 2 * EXACT and tiles % 8 == 0
     hbm = pl.BlockSpec(memory_space=pltpu.HBM)
@@ -127,7 +147,7 @@
             jax.ShapeDtypeStruct((sources + 1, dests, 128, 128), BF),
             jax.ShapeDtypeStruct((1, dests * 128), F32),
         ),
-        in_specs=[hbm, hbm, hbm, pl.BlockSpec(memory_space=pl.ANY)],
+        in_specs=[hbm, hbm, hbm, pl.BlockSpec(memory_space=pl.ANY), vmem],
         out_specs=(vmem, vmem),
         scratch_shapes=[
             pltpu.VMEM((dests, 8, 128), F32),
@@ -139,9 +159,10 @@
             pltpu.SemaphoreType.DMA((6,)),
         ],
         compiler_params=params(24),
+        input_output_aliases={4: 0},
         cost_estimate=cost(0, 30 << 20),
         name="build",
-    )(rows, cols, bits, gate)
+    )(rows, cols, bits, gate, at)
 
 
 def forward_kernel(place_ref, *refs):
@@ -419,12 +440,11 @@
     low = jnp.stack([low] + [send_z(low, k) for k in (1, 2, 3)])
     top, low, mine, theirs, zero = lax.optimization_barrier((top, low, mine, theirs, core == 0))
     planes = [top] + [send_z(top, k) for k in (1, 2, 3)]
-    planes += [low] + [send_x(low, k) for k in (1, 2, 3)]
-    at, degree = build(
-        *(pltpu.with_memory_space_constraint(t, pltpu.HBM) for t in (tile_row, tile_col, tile_bits)),
-        top,
-        nodes * rows_dev // 128, cols * rows_dev // 128
-    )
+    empty = cleared(low, nodes * rows_dev // 128, cols * rows_dev // 128)
+    late, empty, third = lax.optimization_barrier((low, empty, send_x(low, 3)))
+    planes += [low, send_x(late, 1), send_x(low, 2), third]
+    fixed = [pltpu.with_memory_space_constraint(t, pltpu.HBM) for t in (tile_row, tile_col, tile_bits)]
+    at, degree = build(*fixed, top, empty)
 
     give = forward(theirs, planes, at, degree, BF)
     taken = send_core(give)

time: 122 us -> 120 us (0.984)
  waiting for transfers between devices: 48.1 us -> 38.7 us
  starting transfers between devices: 45.9 us -> 51.7 us
    ppermute x9, waiting for transfers between devices: 20.4 us -> 14.9 us  [send_y(): return lax.ppermute(x, 'cols', along_y(step))]
    ppermute x15, starting transfers between devices: 20.4 us -> 25.1 us  [send_node(): return lax.ppermute(x, 'nodes', moves)]
    ppermute x9, starting transfers between devices: 12.6 us -> 16.7 us  [send_y(): return lax.ppermute(x, 'cols', along_y(step))]
    pallas_call x0 -> x1, Pallas kernels: none -> 2.25 us  [cleared(): pl.pallas_call(clear_kernel, out_shape=jax.ShapeDtypeStruct((sources + 1,...]
    all_to_all x1, waiting for transfers between devices: 13.1 us -> 10.9 us  [swap(): return lax.all_to_all(x, axis, 0, 0, tiled=True)]
    all_to_all x1, starting transfers between devices: 7.27 us -> 5.32 us  [swap(): return lax.all_to_all(x, axis, 0, 0, tiled=True)]
    ppermute x2, starting transfers between devices: 5.29 us -> 3.85 us  [send_x_flip(): return lax.ppermute(x, 'nodes', moves)]
    ppermute x15, waiting for transfers between devices: 11.7 us -> 10.4 us  [send_node(): return lax.ppermute(x, 'nodes', moves)]
  transfers between devices with their start and end apart: 34 -> 34, of which waited for: 17 -> 16; matrix products, arithmetic and copies ran while one was open for 1% -> 1% of each run, Pallas kernels for 15% -> 17%
where the time goes in v10:
time: 120 us; the launch traced here: 119 us
  starting transfers between devices  51.7 us (43%)
  waiting for transfers between devices  38.7 us (32%)
  Pallas kernels  24.3 us (20%)
  local copies, waits for them, and re-layouts  1.5 us (1%)
  other arithmetic  1.35 us (1%)
    ppermute x15, starting transfers between devices, send_node(): return lax.ppermute(x, 'nodes', moves)  25.1 us
    ppermute x9, starting transfers between devices, send_y(): return lax.ppermute(x, 'cols', along_y(step))  16.7 us
    ppermute x9, waiting for transfers between devices, send_y(): return lax.ppermute(x, 'cols', along_y(step))  14.9 us
    all_to_all x1, waiting for transfers between devices, swap(): return lax.all_to_all(x, axis, 0, 0, tiled=True)  10.9 us
    ppermute x15, waiting for transfers between devices, send_node(): return lax.ppermute(x, 'nodes', moves)  10.4 us
    pallas_call x1, Pallas kernels, backward(): pl.pallas_call(backward_kernel, out_shape=in_hbm((sources * 128, width),...  6.71 us
    pallas_call x1, Pallas kernels, build(): pl.pallas_call(build_kernel, out_shape=(jax.ShapeDtypeStruct((sources + 1...  6.51 us
    pallas_call x2, Pallas kernels, forward(): pl.pallas_call(forward_kernel, out_shape=jax.ShapeDtypeStruct((4, width +...  6.32 us
  transfers between devices with their start and end apart: 34, of which 16 were waited for; matrix products, arithmetic and copies ran while one was open for 1% of the time, Pallas kernels for 17%

profile of v10, /device:TPU:0, one launch (start us, length us, event | category | flops | bytes accessed | tf_op | source)
XLA Modules:
  0.0 118.5 jit_solution(4831145880381210937)
XLA Ops:
  1.6 2.1 %collective-permute-start.3 = (bf16[128,256]{1,0:T(8,128)(2,1)S(1)}, bf16[128,256]{1,0:T(8,128)(2,1)S(1)}, u32[]{:S(2)}, u32[]{:S(2)}) collective-permute-start(bf16[128,256]{1,0:T(8,128)(2,1)S(1)} %get-tuple-element.36), channel_id=1, source_target_pairs={{0,8},{8,16},{16,24},{24,0},{32,40},{40,48},{48,56},{56,32},{64,72... | collective-permute-start | bytes 196616 | tf_op jit(solution)/shard_map/ppermute | solution.py:393
  3.7 3.6 %collective-permute-start.4 = (bf16[128,256]{1,0:T(8,128)(2,1)S(1)}, bf16[128,256]{1,0:T(8,128)(2,1)S(1)}, u32[]{:S(2)}, u32[]{:S(2)}) collective-permute-start(bf16[128,256]{1,0:T(8,128)(2,1)S(1)} %get-tuple-element.36), channel_id=1, source_target_pairs={{0,16},{8,24},{16,0},{24,8},{32,48},{40,56},{48,32},{56,40},{64,80... | collective-permute-start | bytes 196616 | tf_op jit(solution)/shard_map/ppermute | solution.py:393
  9.8 2.7 %collective-permute-start.1 = (bf16[128,256]{1,0:T(8,128)(2,1)S(1)}, bf16[128,256]{1,0:T(8,128)(2,1)S(1)}, u32[]{:S(2)}, u32[]{:S(2)}) collective-permute-start(bf16[128,256]{1,0:T(8,128)(2,1)S(1)} %get-tuple-element.35), channel_id=1, source_target_pairs={{0,64},{8,72},{16,80},{24,88},{32,96},{40,104},{48,112},{56,120},{... | collective-permute-start | bytes 196616 | tf_op jit(solution)/shard_map/ppermute | solution.py:393
  16.9 2.7 %collective-permute-start.9 = (bf16[4,128,256]{2,1,0:T(8,128)(2,1)S(1)}, bf16[4,128,256]{2,1,0:T(8,128)(2,1)S(1)}, u32[]{:S(2)}, u32[]{:S(2)}) collective-permute-start(bf16[4,128,256]{2,1,0:T(8,128)(2,1)S(1)} %pad_maximum_fusion.3.gate_ref.refs_4_), channel_id=1, source_target_pairs={{0,96},{8,104},{16,112},{24,120},{32,0},{40,8},{48,16},{56,24},{64... | collective-permute-start | bytes 786440 | tf_op jit(solution)/shard_map/ppermute | solution.py:393
  19.6 2.3 %clear.1.clear_ref = bf16[33,16,128,128]{3,2,1,0:T(8,128)(2,1)S(1)} custom-call(bf16[4,128,256]{2,1,0:T(8,128)(2,1)S(1)} %pad_maximum_fusion.3.gate_ref.refs_4_), custom_call_target="tpu_custom_call" | custom-call | bytes 8388608 | tf_op jit(solution)/shard_map/clear/pallas_call | solution.py:127
  23.5 2.3 %collective-permute-start.8 = (bf16[4,128,256]{2,1,0:T(8,128)(2,1)S(1)}, bf16[4,128,256]{2,1,0:T(8,128)(2,1)S(1)}, u32[]{:S(2)}, u32[]{:S(2)}) collective-permute-start(bf16[4,128,256]{2,1,0:T(8,128)(2,1)S(1)} %pad_maximum_fusion.2.gate_ref.refs_0_), channel_id=1, source_target_pairs={{0,24},{8,0},{16,8},{24,16},{32,56},{40,32},{48,40},{56,48},{64,88... | collective-permute-start | bytes 786440 | tf_op jit(solution)/shard_map/ppermute | solution.py:393
  25.8 3.1 %collective-permute-done.9.refs_7_ = bf16[4,128,256]{2,1,0:T(8,128)(2,1)S(1)} collective-permute-done((bf16[4,128,256]{2,1,0:T(8,128)(2,1)S(1)}, bf16[4,128,256]{2,1,0:T(8,128)(2,1)S(1)}, u32[]{:S(2)}, u32[]{:S(2)}) %collective-permute-start.9) | collective-permute-done | bytes 262176 | tf_op jit(solution)/shard_map/ppermute | solution.py:393
  29.0 6.5 %build.1 = (bf16[33,16,128,128]{3,2,1,0:T(8,128)(2,1)S(1)}, f32[1,2048]{1,0:T(1,128)S(1)}) custom-call(s32[1,352]{1,0:T(1,128)} %rows_ref.1, s32[1,352]{1,0:T(1,128)} %cols_ref.1, s32[1,352,16,128]{3,2,1,0:T(8,128)} %bits_all.1, bf16[4,128,256]{2,1,0:T(8,128)(2,1)S(1)} %pad_maximum_fusion.2.gate_ref.refs_0_, ...), custom_call_target="tpu_custom_call", output_to_operand_aliasing={{0}: (4, {})} | custom-call | bytes 31457280 | tf_op jit(solution)/shard_map/build/pallas_call | solution.py:144
  37.0 3.2 %forward.3 = bf16[4,272,256]{2,1,0:T(8,128)(2,1)S(1)} custom-call(s32[4]{0:T(128)S(1)} %get-tuple-element.45.place_ref, bf16[4,128,256]{2,1,0:T(8,128)(2,1)S(1)} %pad_maximum_fusion.2.gate_ref.refs_0_, bf16[4,128,256]{2,1,0:T(8,128)(2,1)S(1)} %collective-permute-done.6.refs_1_, bf16[4,128,256]{2,1,0:T(8,128)(2,1)S(1)} %collective-permute-done.7.refs_2_, ...), custom_call_target="tpu_custom_call" | custom-call | flops 2147483648 | bytes 10485760 | tf_op jit(solution)/shard_map/forward/pallas_call | solution.py:215
  40.3 3.2 %forward.2.keep_ref = f32[4,272,256]{2,1,0:T(8,128)S(1)} custom-call(s32[4]{0:T(128)S(1)} %get-tuple-element.37.place_ref, bf16[4,128,256]{2,1,0:T(8,128)(2,1)S(1)} %pad_maximum_fusion.2.gate_ref.refs_0_, bf16[4,128,256]{2,1,0:T(8,128)(2,1)S(1)} %collective-permute-done.6.refs_1_, bf16[4,128,256]{2,1,0:T(8,128)(2,1)S(1)} %collective-permute-done.7.refs_2_, ...), custom_call_target="tpu_custom_call" | custom-call | flops 2147483648 | bytes 10485760 | tf_op jit(solution)/shard_map/forward/pallas_call | solution.py:215
  45.2 2.9 %collective-permute-start.14 = (bf16[272,256]{1,0:T(8,128)(2,1)S(1)}, bf16[272,256]{1,0:T(8,128)(2,1)S(1)}, u32[]{:S(2)}, u32[]{:S(2)}) collective-permute-start(bf16[272,256]{1,0:T(8,128)(2,1)S(1)} %get-tuple-element.48), channel_id=1, source_target_pairs={{0,4},{1,5},{2,6},{3,7},{4,0},{5,1},{6,2},{7,3},{8,12},{9,13},{10,... | collective-permute-start | bytes 417800 | tf_op jit(solution)/shard_map/ppermute | solution.py:409
  51.0 4.2 %collective-permute-done.14.r2_ref = bf16[272,256]{1,0:T(8,128)(2,1)S(1)} collective-permute-done((bf16[272,256]{1,0:T(8,128)(2,1)S(1)}, bf16[272,256]{1,0:T(8,128)(2,1)S(1)}, u32[]{:S(2)}, u32[]{:S(2)}) %collective-permute-start.14) | collective-permute-done | bytes 139296 | tf_op jit(solution)/shard_map/ppermute | solution.py:409
  58.0 2.4 %collective-permute-start.17 = (bf16[256,256]{1,0:T(8,128)(2,1)S(1)}, bf16[256,256]{1,0:T(8,128)(2,1)S(1)}, u32[]{:S(2)}, u32[]{:S(2)}) collective-permute-start(bf16[256,256]{1,0:T(8,128)(2,1)S(1)} %get-tuple-element.51.refs_0_), channel_id=1, source_target_pairs={{0,4},{1,5},{2,6},{3,7},{4,0},{5,1},{6,2},{7,3},{8,12},{9,13},{10,... | collective-permute-start | bytes 393224 | tf_op jit(solution)/shard_map/ppermute | solution.py:409
  63.6 2.8 %collective-permute-done.17.refs_2_ = bf16[256,256]{1,0:T(8,128)(2,1)S(1)} collective-permute-done((bf16[256,256]{1,0:T(8,128)(2,1)S(1)}, bf16[256,256]{1,0:T(8,128)(2,1)S(1)}, u32[]{:S(2)}, u32[]{:S(2)}) %collective-permute-start.17) | collective-permute-done | bytes 131104 | tf_op jit(solution)/shard_map/ppermute | solution.py:409
  67.0 3.8 %collective-permute-start.24 = (bf16[528,256]{1,0:T(8,128)(2,1)S(1)}, bf16[528,256]{1,0:T(8,128)(2,1)S(1)}, u32[]{:S(2)}, u32[]{:S(2)}) collective-permute-start(bf16[528,256]{1,0:T(8,128)(2,1)S(1)} %add_convert_fusion), channel_id=1, source_target_pairs={{0,64},{8,72},{16,80},{24,88},{32,96},{40,104},{48,112},{56,120},{... | collective-permute-start | bytes 811016 | tf_op jit(solution)/shard_map/ppermute | solution.py:398
  70.8 6.7 %backward.1 = bf16[4096,256]{1,0:T(8,128)(2,1)} custom-call(s32[4]{0:T(128)S(1)} %get-tuple-element.37.place_ref, bf16[256,256]{1,0:T(8,128)(2,1)S(1)} %get-tuple-element.51.refs_0_, bf16[256,256]{1,0:T(8,128)(2,1)S(1)} %collective-permute-done.16.refs_1_, bf16[256,256]{1,0:T(8,128)(2,1)S(1)} %collective-permute-done.17.refs_2_, ...), custom_call_target="tpu_custom_call" | custom-call | flops 4294967296 | bytes 20971520 | tf_op jit(solution)/shard_map/backward/pallas_call | solution.py:261
  77.5 5.3 %all-to-all-start = ((bf16[16,256,256]{2,1,0:T(8,128)(2,1)}), bf16[16,256,256]{2,1,0:T(8,128)(2,1)S(1)}, u32[]{:S(2)}, u32[]{:S(2)}) async-start(bf16[16,256,256]{2,1,0:T(8,128)(2,1)} %bitcast.19), calls=%async_computation | async-start | bytes 4194304 | tf_op jit(solution)/shard_map/all_to_all | solution.py:382
  84.7 2.3 %collective-permute-start.26 = (bf16[272,256]{1,0:T(8,128)(2,1)S(1)}, bf16[272,256]{1,0:T(8,128)(2,1)S(1)}, u32[]{:S(2)}, u32[]{:S(2)}) collective-permute-start(bf16[272,256]{1,0:T(8,128)(2,1)S(1)} %fusion.1), channel_id=1, source_target_pairs={{0,4},{1,5},{2,6},{3,7},{4,0},{5,1},{6,2},{7,3},{8,12},{9,13},{10,... | collective-permute-start | bytes 417800 | tf_op jit(solution)/shard_map/ppermute | solution.py:409
  90.2 2.5 %collective-permute-done.26 = bf16[272,256]{1,0:T(8,128)(2,1)S(1)} collective-permute-done((bf16[272,256]{1,0:T(8,128)(2,1)S(1)}, bf16[272,256]{1,0:T(8,128)(2,1)S(1)}, u32[]{:S(2)}, u32[]{:S(2)}) %collective-permute-start.26) | collective-permute-done | bytes 139296 | tf_op jit(solution)/shard_map/ppermute | solution.py:409
  92.8 2.2 %collective-permute-done.27 = bf16[272,256]{1,0:T(8,128)(2,1)S(1)} collective-permute-done((bf16[272,256]{1,0:T(8,128)(2,1)S(1)}, bf16[272,256]{1,0:T(8,128)(2,1)S(1)}, u32[]{:S(2)}, u32[]{:S(2)}) %collective-permute-start.27) | collective-permute-done | bytes 139296 | tf_op jit(solution)/shard_map/ppermute | solution.py:409
  95.0 2.0 %collective-permute-start.29 = (bf16[272,256]{1,0:T(8,128)(2,1)S(1)}, bf16[272,256]{1,0:T(8,128)(2,1)S(1)}, u32[]{:S(2)}, u32[]{:S(2)}) collective-permute-start(bf16[272,256]{1,0:T(8,128)(2,1)S(1)} %add_convert_fusion.1), channel_id=1, source_target_pairs={{0,8},{8,16},{16,24},{24,0},{32,40},{40,48},{48,56},{56,32},{64,72... | collective-permute-start | bytes 417800 | tf_op jit(solution)/shard_map/ppermute | solution.py:393
  97.0 2.7 %collective-permute-start.30 = (bf16[272,256]{1,0:T(8,128)(2,1)S(1)}, bf16[272,256]{1,0:T(8,128)(2,1)S(1)}, u32[]{:S(2)}, u32[]{:S(2)}) collective-permute-start(bf16[272,256]{1,0:T(8,128)(2,1)S(1)} %add_convert_fusion.1), channel_id=1, source_target_pairs={{0,16},{8,24},{16,0},{24,8},{32,48},{40,56},{48,32},{56,40},{64,80... | collective-permute-start | bytes 417800 | tf_op jit(solution)/shard_map/ppermute | solution.py:393
  101.2 10.9 %all-to-all-done.parts_ref = bf16[16,256,256]{2,1,0:T(8,128)(2,1)S(1)} async-done(((bf16[16,256,256]{2,1,0:T(8,128)(2,1)}), bf16[16,256,256]{2,1,0:T(8,128)(2,1)S(1)}, u32[]{:S(2)}, u32[]{:S(2)}) %all-to-all-start) | async-done | bytes 2097184 | tf_op jit(solution)/shard_map/all_to_all | solution.py:382
  113.0 3.0 %collective-permute-done.30 = bf16[272,256]{1,0:T(8,128)(2,1)S(1)} collective-permute-done((bf16[272,256]{1,0:T(8,128)(2,1)S(1)}, bf16[272,256]{1,0:T(8,128)(2,1)S(1)}, u32[]{:S(2)}, u32[]{:S(2)}) %collective-permute-start.30) | collective-permute-done | bytes 139296 | tf_op jit(solution)/shard_map/ppermute | solution.py:393
  (79 shorter events, 32.3 us)
Async XLA Ops:
  1.6 11.0 %collective-permute-start.3 = (bf16[128,256]{1,0:T(8,128)(2,1)S(1)}, bf16[128,256]{1,0:T(8,128)(2,1)S(1)}, u32[]{:S(2)}, u32[]{:S(2)}) collective-permute-start(bf16[128,256]{1,0:T(8,128)(2,1)S(1)} %get-tuple-element.36), channel_id=1, source_target_pairs={{0,8},{8,16},{16,24},{24,0},{32,40},{40,48},{48,56},{56,32},{64,72... | collective-permute-start | bytes 196616 | tf_op jit(solution)/shard_map/ppermute | solution.py:393
  3.7 10.3 %collective-permute-start.4 = (bf16[128,256]{1,0:T(8,128)(2,1)S(1)}, bf16[128,256]{1,0:T(8,128)(2,1)S(1)}, u32[]{:S(2)}, u32[]{:S(2)}) collective-permute-start(bf16[128,256]{1,0:T(8,128)(2,1)S(1)} %get-tuple-element.36), channel_id=1, source_target_pairs={{0,16},{8,24},{16,0},{24,8},{32,48},{40,56},{48,32},{56,40},{64,80... | collective-permute-start | bytes 196616 | tf_op jit(solution)/shard_map/ppermute | solution.py:393
  7.3 6.8 %collective-permute-start.5 = (bf16[128,256]{1,0:T(8,128)(2,1)S(1)}, bf16[128,256]{1,0:T(8,128)(2,1)S(1)}, u32[]{:S(2)}, u32[]{:S(2)}) collective-permute-start(bf16[128,256]{1,0:T(8,128)(2,1)S(1)} %get-tuple-element.36), channel_id=1, source_target_pairs={{0,24},{8,0},{16,8},{24,16},{32,56},{40,32},{48,40},{56,48},{64,88... | collective-permute-start | bytes 196616 | tf_op jit(solution)/shard_map/ppermute | solution.py:393
  16.9 12.1 %collective-permute-start.9 = (bf16[4,128,256]{2,1,0:T(8,128)(2,1)S(1)}, bf16[4,128,256]{2,1,0:T(8,128)(2,1)S(1)}, u32[]{:S(2)}, u32[]{:S(2)}) collective-permute-start(bf16[4,128,256]{2,1,0:T(8,128)(2,1)S(1)} %pad_maximum_fusion.3.gate_ref.refs_4_), channel_id=1, source_target_pairs={{0,96},{8,104},{16,112},{24,120},{32,0},{40,8},{48,16},{56,24},{64... | collective-permute-start | bytes 786440 | tf_op jit(solution)/shard_map/ppermute | solution.py:393
  21.9 13.6 %collective-permute-start.11 = (bf16[4,128,256]{2,1,0:T(8,128)(2,1)S(1)}, bf16[4,128,256]{2,1,0:T(8,128)(2,1)S(1)}, u32[]{:S(2)}, u32[]{:S(2)}) collective-permute-start(bf16[4,128,256]{2,1,0:T(8,128)(2,1)S(1)} %pad_maximum_fusion.3.gate_ref.refs_4_), channel_id=1, source_target_pairs={{0,64},{8,72},{16,80},{24,88},{32,96},{40,104},{48,112},{56,120},{... | collective-permute-start | bytes 786440 | tf_op jit(solution)/shard_map/ppermute | solution.py:393
  22.0 13.5 %collective-permute-start.6 = (bf16[4,128,256]{2,1,0:T(8,128)(2,1)S(1)}, bf16[4,128,256]{2,1,0:T(8,128)(2,1)S(1)}, u32[]{:S(2)}, u32[]{:S(2)}) collective-permute-start(bf16[4,128,256]{2,1,0:T(8,128)(2,1)S(1)} %pad_maximum_fusion.2.gate_ref.refs_0_), channel_id=1, source_target_pairs={{0,8},{8,16},{16,24},{24,0},{32,40},{40,48},{48,56},{56,32},{64,72... | collective-permute-start | bytes 786440 | tf_op jit(solution)/shard_map/ppermute | solution.py:393
  23.1 12.5 %collective-permute-start.7 = (bf16[4,128,256]{2,1,0:T(8,128)(2,1)S(1)}, bf16[4,128,256]{2,1,0:T(8,128)(2,1)S(1)}, u32[]{:S(2)}, u32[]{:S(2)}) collective-permute-start(bf16[4,128,256]{2,1,0:T(8,128)(2,1)S(1)} %pad_maximum_fusion.2.gate_ref.refs_0_), channel_id=1, source_target_pairs={{0,16},{8,24},{16,0},{24,8},{32,48},{40,56},{48,32},{56,40},{64,80... | collective-permute-start | bytes 786440 | tf_op jit(solution)/shard_map/ppermute | solution.py:393
  23.5 12.0 %collective-permute-start.8 = (bf16[4,128,256]{2,1,0:T(8,128)(2,1)S(1)}, bf16[4,128,256]{2,1,0:T(8,128)(2,1)S(1)}, u32[]{:S(2)}, u32[]{:S(2)}) collective-permute-start(bf16[4,128,256]{2,1,0:T(8,128)(2,1)S(1)} %pad_maximum_fusion.2.gate_ref.refs_0_), channel_id=1, source_target_pairs={{0,24},{8,0},{16,8},{24,16},{32,56},{40,32},{48,40},{56,48},{64,88... | collective-permute-start | bytes 786440 | tf_op jit(solution)/shard_map/ppermute | solution.py:393
  29.0 8.0 %collective-permute-start.10 = (bf16[4,128,256]{2,1,0:T(8,128)(2,1)S(1)}, bf16[4,128,256]{2,1,0:T(8,128)(2,1)S(1)}, u32[]{:S(2)}, u32[]{:S(2)}) collective-permute-start(bf16[4,128,256]{2,1,0:T(8,128)(2,1)S(1)} %pad_maximum_fusion.3.gate_ref.refs_4_), channel_id=1, source_target_pairs={{0,32},{8,40},{16,48},{24,56},{32,64},{40,72},{48,80},{56,88},{64,... | collective-permute-start | bytes 786440 | tf_op jit(solution)/shard_map/ppermute | solution.py:393
  43.6 7.4 %collective-permute-start.13 = (bf16[272,256]{1,0:T(8,128)(2,1)S(1)}, bf16[272,256]{1,0:T(8,128)(2,1)S(1)}, u32[]{:S(2)}, u32[]{:S(2)}) collective-permute-start(bf16[272,256]{1,0:T(8,128)(2,1)S(1)} %get-tuple-element.47), channel_id=1, source_target_pairs={{0,2},{1,3},{2,4},{3,5},{4,6},{5,7},{6,0},{7,1},{8,10},{9,11},{10,... | collective-permute-start | bytes 417800 | tf_op jit(solution)/shard_map/ppermute | solution.py:409
  45.2 9.9 %collective-permute-start.14 = (bf16[272,256]{1,0:T(8,128)(2,1)S(1)}, bf16[272,256]{1,0:T(8,128)(2,1)S(1)}, u32[]{:S(2)}, u32[]{:S(2)}) collective-permute-start(bf16[272,256]{1,0:T(8,128)(2,1)S(1)} %get-tuple-element.48), channel_id=1, source_target_pairs={{0,4},{1,5},{2,6},{3,7},{4,0},{5,1},{6,2},{7,3},{8,12},{9,13},{10,... | collective-permute-start | bytes 417800 | tf_op jit(solution)/shard_map/ppermute | solution.py:409
  48.1 7.0 %collective-permute-start.15 = (bf16[272,256]{1,0:T(8,128)(2,1)S(1)}, bf16[272,256]{1,0:T(8,128)(2,1)S(1)}, u32[]{:S(2)}, u32[]{:S(2)}) collective-permute-start(bf16[272,256]{1,0:T(8,128)(2,1)S(1)} %get-tuple-element.49), channel_id=1, source_target_pairs={{0,6},{1,7},{2,0},{3,1},{4,2},{5,3},{6,4},{7,5},{8,14},{9,15},{10,... | collective-permute-start | bytes 417800 | tf_op jit(solution)/shard_map/ppermute | solution.py:409
  56.6 10.4 %collective-permute-start.23 = (bf16[528,256]{1,0:T(8,128)(2,1)S(1)}, bf16[528,256]{1,0:T(8,128)(2,1)S(1)}, u32[]{:S(2)}, u32[]{:S(2)}) collective-permute-start(bf16[528,256]{1,0:T(8,128)(2,1)S(1)} %get-tuple-element.54), channel_id=1, source_target_pairs={{0,32},{8,40},{16,48},{24,56},{32,0},{40,8},{48,16},{56,24},{64,96... | collective-permute-start | bytes 811016 | tf_op jit(solution)/shard_map/ppermute | solution.py:398
  56.7 7.0 %collective-permute-start.16 = (bf16[256,256]{1,0:T(8,128)(2,1)S(1)}, bf16[256,256]{1,0:T(8,128)(2,1)S(1)}, u32[]{:S(2)}, u32[]{:S(2)}) collective-permute-start(bf16[256,256]{1,0:T(8,128)(2,1)S(1)} %get-tuple-element.51.refs_0_), channel_id=1, source_target_pairs={{0,2},{1,3},{2,4},{3,5},{4,6},{5,7},{6,0},{7,1},{8,10},{9,11},{10,... | collective-permute-start | bytes 393224 | tf_op jit(solution)/shard_map/ppermute | solution.py:409
  58.0 8.4 %collective-permute-start.17 = (bf16[256,256]{1,0:T(8,128)(2,1)S(1)}, bf16[256,256]{1,0:T(8,128)(2,1)S(1)}, u32[]{:S(2)}, u32[]{:S(2)}) collective-permute-start(bf16[256,256]{1,0:T(8,128)(2,1)S(1)} %get-tuple-element.51.refs_0_), channel_id=1, source_target_pairs={{0,4},{1,5},{2,6},{3,7},{4,0},{5,1},{6,2},{7,3},{8,12},{9,13},{10,... | collective-permute-start | bytes 393224 | tf_op jit(solution)/shard_map/ppermute | solution.py:409
  61.9 8.8 %collective-permute-start.19 = (bf16[256,256]{1,0:T(8,128)(2,1)S(1)}, bf16[256,256]{1,0:T(8,128)(2,1)S(1)}, u32[]{:S(2)}, u32[]{:S(2)}) collective-permute-start(bf16[256,256]{1,0:T(8,128)(2,1)S(1)} %get-tuple-element.51.refs_0_), channel_id=1, source_target_pairs={{0,1},{1,0},{2,3},{3,2},{4,5},{5,4},{6,7},{7,6},{8,9},{9,8},{10,11... | collective-permute-start | bytes 393224 | tf_op jit(solution)/shard_map/ppermute | solution.py:413
  63.6 7.1 %collective-permute-start.20 = (bf16[256,256]{1,0:T(8,128)(2,1)S(1)}, bf16[256,256]{1,0:T(8,128)(2,1)S(1)}, u32[]{:S(2)}, u32[]{:S(2)}) collective-permute-start(bf16[256,256]{1,0:T(8,128)(2,1)S(1)} %collective-permute-done.16.refs_1_), channel_id=1, source_target_pairs={{0,1},{1,0},{2,3},{3,2},{4,5},{5,4},{6,7},{7,6},{8,9},{9,8},{10,11... | collective-permute-start | bytes 393224 | tf_op jit(solution)/shard_map/ppermute | solution.py:413
  67.0 10.5 %collective-permute-start.24 = (bf16[528,256]{1,0:T(8,128)(2,1)S(1)}, bf16[528,256]{1,0:T(8,128)(2,1)S(1)}, u32[]{:S(2)}, u32[]{:S(2)}) collective-permute-start(bf16[528,256]{1,0:T(8,128)(2,1)S(1)} %add_convert_fusion), channel_id=1, source_target_pairs={{0,64},{8,72},{16,80},{24,88},{32,96},{40,104},{48,112},{56,120},{... | collective-permute-start | bytes 811016 | tf_op jit(solution)/shard_map/ppermute | solution.py:398
  77.5 34.5 %all-to-all-start = ((bf16[16,256,256]{2,1,0:T(8,128)(2,1)}), bf16[16,256,256]{2,1,0:T(8,128)(2,1)S(1)}, u32[]{:S(2)}, u32[]{:S(2)}) async-start(bf16[16,256,256]{2,1,0:T(8,128)(2,1)} %bitcast.19), calls=%async_computation | async-start | bytes 4194304 | tf_op jit(solution)/shard_map/all_to_all | solution.py:382
  84.7 8.1 %collective-permute-start.26 = (bf16[272,256]{1,0:T(8,128)(2,1)S(1)}, bf16[272,256]{1,0:T(8,128)(2,1)S(1)}, u32[]{:S(2)}, u32[]{:S(2)}) collective-permute-start(bf16[272,256]{1,0:T(8,128)(2,1)S(1)} %fusion.1), channel_id=1, source_target_pairs={{0,4},{1,5},{2,6},{3,7},{4,0},{5,1},{6,2},{7,3},{8,12},{9,13},{10,... | collective-permute-start | bytes 417800 | tf_op jit(solution)/shard_map/ppermute | solution.py:409
  87.0 8.0 %collective-permute-start.27 = (bf16[272,256]{1,0:T(8,128)(2,1)S(1)}, bf16[272,256]{1,0:T(8,128)(2,1)S(1)}, u32[]{:S(2)}, u32[]{:S(2)}) collective-permute-start(bf16[272,256]{1,0:T(8,128)(2,1)S(1)} %fusion.1), channel_id=1, source_target_pairs={{0,2},{1,3},{2,4},{3,5},{4,6},{5,7},{6,0},{7,1},{8,10},{9,11},{10,... | collective-permute-start | bytes 417800 | tf_op jit(solution)/shard_map/ppermute | solution.py:409
  95.0 17.9 %collective-permute-start.29 = (bf16[272,256]{1,0:T(8,128)(2,1)S(1)}, bf16[272,256]{1,0:T(8,128)(2,1)S(1)}, u32[]{:S(2)}, u32[]{:S(2)}) collective-permute-start(bf16[272,256]{1,0:T(8,128)(2,1)S(1)} %add_convert_fusion.1), channel_id=1, source_target_pairs={{0,8},{8,16},{16,24},{24,0},{32,40},{40,48},{48,56},{56,32},{64,72... | collective-permute-start | bytes 417800 | tf_op jit(solution)/shard_map/ppermute | solution.py:393
  97.0 18.9 %collective-permute-start.30 = (bf16[272,256]{1,0:T(8,128)(2,1)S(1)}, bf16[272,256]{1,0:T(8,128)(2,1)S(1)}, u32[]{:S(2)}, u32[]{:S(2)}) collective-permute-start(bf16[272,256]{1,0:T(8,128)(2,1)S(1)} %add_convert_fusion.1), channel_id=1, source_target_pairs={{0,16},{8,24},{16,0},{24,8},{32,48},{40,56},{48,32},{56,40},{64,80... | collective-permute-start | bytes 417800 | tf_op jit(solution)/shard_map/ppermute | solution.py:393
  99.7 16.3 %collective-permute-start.31 = (bf16[272,256]{1,0:T(8,128)(2,1)S(1)}, bf16[272,256]{1,0:T(8,128)(2,1)S(1)}, u32[]{:S(2)}, u32[]{:S(2)}) collective-permute-start(bf16[272,256]{1,0:T(8,128)(2,1)S(1)} %add_convert_fusion.1), channel_id=1, source_target_pairs={{0,24},{8,0},{16,8},{24,16},{32,56},{40,32},{48,40},{56,48},{64,88... | collective-permute-start | bytes 417800 | tf_op jit(solution)/shard_map/ppermute | solution.py:393
  (16 other events, 119.9 us)

commit v11 on v10

--- a/solution.py
+++ b/solution.py
@@ -9,6 +9,7 @@
 F32 = jnp.float32
 EXACT = 256
 EXTRA = 16
+FAR_FIRST = (0, 2, 1, 3)
 
 
 def params(mib):
@@ -227,12 +228,12 @@
 def backward_kernel(place_ref, *refs):
     parts, at_ref, out_ref, grads, held, sems = refs[:8], *refs[8:]
     rows = parts[0].shape[0]
-    for k in range(4):
+    for spot, k in enumerate(FAR_FIRST):
         chunk = 2 * lax.rem(place_ref[0] + 4 - k, 4)
         own = pl.multiple_of((chunk + place_ref[1]) * rows, rows)
         other = pl.multiple_of((chunk + 1 - place_ref[1]) * rows, rows)
-        grads[pl.ds(own, rows), :] = parts[k][...]
-        grads[pl.ds(other, rows), :] = parts[4 + k][...]
+        grads[pl.ds(own, rows), :] = parts[spot][...]
+        grads[pl.ds(other, rows), :] = parts[4 + spot][...]
     pieces, each, _ = held.shape
 
     def copy(i):
@@ -300,7 +301,7 @@
 
 
 def middle_kernel(
-    own_ref, r1_ref, r2_ref, r3_ref, x_ref, ws_ref, wn_ref, bias_ref, cot_ref,
+    own_ref, r2_ref, r1_ref, r3_ref, x_ref, ws_ref, wn_ref, bias_ref, cot_ref,
     out_ref, pre_ref, mean_ref, grad_ref,
 ):
     width = x_ref.shape[1]
@@ -451,12 +452,11 @@
     keep = forward(mine, planes, at, degree, F32)
     own, *sent = mix(keep, taken)
     far = send_y(sent[1], 2)
-    got = [send_y(sent[0], 1), far, send_y(sent[2], 3)]
+    got = [far, send_y(sent[0], 1), send_y(sent[2], 3)]
     layer_out, pre_grad, mean_t, mean_grad = middle(
         own, got, node_feats, w_self, w_neigh, bias.reshape(1, -1), cotangent
     )
-    next_y, last_y = send_y(mean_grad, 1), send_y(mean_grad, 3)
-    same_core = [mean_grad, next_y, send_y(mean_grad, 2), last_y]
+    same_core = [mean_grad] + [send_y(mean_grad, k) for k in FAR_FIRST[1:]]
 
     part, self_part = weights(node_feats, pre_grad, mean_t, w_self)
     part = pair_sum(part, send_x_flip(part, 1)).astype(BF)

time: 120 us -> 119 us (level)
  waiting for transfers between devices: 38.7 us -> 37.3 us
    ppermute x9, waiting for transfers between devices: 14.9 us -> 13.6 us  [send_y(): return lax.ppermute(x, 'cols', along_y(step))]
  transfers between devices with their start and end apart: 34 -> 34, of which waited for: 16 -> 17; matrix products, arithmetic and copies ran while one was open for 1% -> 1% of each run, Pallas kernels for 17% -> 17%
where the time goes in v11:
time: 119 us; the launch traced here: 118 us
  starting transfers between devices  52.4 us (44%)
  waiting for transfers between devices  37.3 us (31%)
  Pallas kernels  24.3 us (20%)
  local copies, waits for them, and re-layouts  1.5 us (1%)
  other arithmetic  1.35 us (1%)
    ppermute x15, starting transfers between devices, send_node(): return lax.ppermute(x, 'nodes', moves)  25.1 us
    ppermute x9, starting transfers between devices, send_y(): return lax.ppermute(x, 'cols', along_y(step))  17.3 us
    ppermute x9, waiting for transfers between devices, send_y(): return lax.ppermute(x, 'cols', along_y(step))  13.6 us
    all_to_all x1, waiting for transfers between devices, swap(): return lax.all_to_all(x, axis, 0, 0, tiled=True)  10.7 us
    ppermute x15, waiting for transfers between devices, send_node(): return lax.ppermute(x, 'nodes', moves)  10.5 us
    pallas_call x1, Pallas kernels, backward(): pl.pallas_call(backward_kernel, out_shape=in_hbm((sources * 128, width),...  6.69 us
    pallas_call x1, Pallas kernels, build(): pl.pallas_call(build_kernel, out_shape=(jax.ShapeDtypeStruct((sources + 1...  6.51 us
    pallas_call x2, Pallas kernels, forward(): pl.pallas_call(forward_kernel, out_shape=jax.ShapeDtypeStruct((4, width +...  6.32 us
  transfers between devices with their start and end apart: 34, of which 17 were waited for; matrix products, arithmetic and copies ran while one was open for 1% of the time, Pallas kernels for 17%

profile of v11, /device:TPU:0, one launch (start us, length us, event | category | flops | bytes accessed | tf_op | source)
XLA Modules:
  0.0 117.7 jit_solution(1746437948742815888)
XLA Ops:
  1.6 2.1 %collective-permute-start.3 = (bf16[128,256]{1,0:T(8,128)(2,1)S(1)}, bf16[128,256]{1,0:T(8,128)(2,1)S(1)}, u32[]{:S(2)}, u32[]{:S(2)}) collective-permute-start(bf16[128,256]{1,0:T(8,128)(2,1)S(1)} %get-tuple-element.36), channel_id=1, source_target_pairs={{0,8},{8,16},{16,24},{24,0},{32,40},{40,48},{48,56},{56,32},{64,72... | collective-permute-start | bytes 196616 | tf_op jit(solution)/shard_map/ppermute | solution.py:394
  3.7 3.6 %collective-permute-start.4 = (bf16[128,256]{1,0:T(8,128)(2,1)S(1)}, bf16[128,256]{1,0:T(8,128)(2,1)S(1)}, u32[]{:S(2)}, u32[]{:S(2)}) collective-permute-start(bf16[128,256]{1,0:T(8,128)(2,1)S(1)} %get-tuple-element.36), channel_id=1, source_target_pairs={{0,16},{8,24},{16,0},{24,8},{32,48},{40,56},{48,32},{56,40},{64,80... | collective-permute-start | bytes 196616 | tf_op jit(solution)/shard_map/ppermute | solution.py:394
  9.8 2.7 %collective-permute-start.1 = (bf16[128,256]{1,0:T(8,128)(2,1)S(1)}, bf16[128,256]{1,0:T(8,128)(2,1)S(1)}, u32[]{:S(2)}, u32[]{:S(2)}) collective-permute-start(bf16[128,256]{1,0:T(8,128)(2,1)S(1)} %get-tuple-element.35), channel_id=1, source_target_pairs={{0,64},{8,72},{16,80},{24,88},{32,96},{40,104},{48,112},{56,120},{... | collective-permute-start | bytes 196616 | tf_op jit(solution)/shard_map/ppermute | solution.py:394
  16.9 2.7 %collective-permute-start.9 = (bf16[4,128,256]{2,1,0:T(8,128)(2,1)S(1)}, bf16[4,128,256]{2,1,0:T(8,128)(2,1)S(1)}, u32[]{:S(2)}, u32[]{:S(2)}) collective-permute-start(bf16[4,128,256]{2,1,0:T(8,128)(2,1)S(1)} %pad_maximum_fusion.3.gate_ref.refs_4_), channel_id=1, source_target_pairs={{0,96},{8,104},{16,112},{24,120},{32,0},{40,8},{48,16},{56,24},{64... | collective-permute-start | bytes 786440 | tf_op jit(solution)/shard_map/ppermute | solution.py:394
  19.6 2.3 %clear.1.clear_ref = bf16[33,16,128,128]{3,2,1,0:T(8,128)(2,1)S(1)} custom-call(bf16[4,128,256]{2,1,0:T(8,128)(2,1)S(1)} %pad_maximum_fusion.3.gate_ref.refs_4_), custom_call_target="tpu_custom_call" | custom-call | bytes 8388608 | tf_op jit(solution)/shard_map/clear/pallas_call | solution.py:128
  23.5 2.3 %collective-permute-start.8 = (bf16[4,128,256]{2,1,0:T(8,128)(2,1)S(1)}, bf16[4,128,256]{2,1,0:T(8,128)(2,1)S(1)}, u32[]{:S(2)}, u32[]{:S(2)}) collective-permute-start(bf16[4,128,256]{2,1,0:T(8,128)(2,1)S(1)} %pad_maximum_fusion.2.gate_ref.refs_0_), channel_id=1, source_target_pairs={{0,24},{8,0},{16,8},{24,16},{32,56},{40,32},{48,40},{56,48},{64,88... | collective-permute-start | bytes 786440 | tf_op jit(solution)/shard_map/ppermute | solution.py:394
  25.8 3.1 %collective-permute-done.9.refs_7_ = bf16[4,128,256]{2,1,0:T(8,128)(2,1)S(1)} collective-permute-done((bf16[4,128,256]{2,1,0:T(8,128)(2,1)S(1)}, bf16[4,128,256]{2,1,0:T(8,128)(2,1)S(1)}, u32[]{:S(2)}, u32[]{:S(2)}) %collective-permute-start.9) | collective-permute-done | bytes 262176 | tf_op jit(solution)/shard_map/ppermute | solution.py:394
  29.0 6.5 %build.1 = (bf16[33,16,128,128]{3,2,1,0:T(8,128)(2,1)S(1)}, f32[1,2048]{1,0:T(1,128)S(1)}) custom-call(s32[1,352]{1,0:T(1,128)} %rows_ref.1, s32[1,352]{1,0:T(1,128)} %cols_ref.1, s32[1,352,16,128]{3,2,1,0:T(8,128)} %bits_all.1, bf16[4,128,256]{2,1,0:T(8,128)(2,1)S(1)} %pad_maximum_fusion.2.gate_ref.refs_0_, ...), custom_call_target="tpu_custom_call", output_to_operand_aliasing={{0}: (4, {})} | custom-call | bytes 31457280 | tf_op jit(solution)/shard_map/build/pallas_call | solution.py:145
  37.0 3.2 %forward.3 = bf16[4,272,256]{2,1,0:T(8,128)(2,1)S(1)} custom-call(s32[4]{0:T(128)S(1)} %get-tuple-element.45.place_ref, bf16[4,128,256]{2,1,0:T(8,128)(2,1)S(1)} %pad_maximum_fusion.2.gate_ref.refs_0_, bf16[4,128,256]{2,1,0:T(8,128)(2,1)S(1)} %collective-permute-done.6.refs_1_, bf16[4,128,256]{2,1,0:T(8,128)(2,1)S(1)} %collective-permute-done.7.refs_2_, ...), custom_call_target="tpu_custom_call" | custom-call | flops 2147483648 | bytes 10485760 | tf_op jit(solution)/shard_map/forward/pallas_call | solution.py:216
  40.3 3.2 %forward.2.keep_ref = f32[4,272,256]{2,1,0:T(8,128)S(1)} custom-call(s32[4]{0:T(128)S(1)} %get-tuple-element.37.place_ref, bf16[4,128,256]{2,1,0:T(8,128)(2,1)S(1)} %pad_maximum_fusion.2.gate_ref.refs_0_, bf16[4,128,256]{2,1,0:T(8,128)(2,1)S(1)} %collective-permute-done.6.refs_1_, bf16[4,128,256]{2,1,0:T(8,128)(2,1)S(1)} %collective-permute-done.7.refs_2_, ...), custom_call_target="tpu_custom_call" | custom-call | flops 2147483648 | bytes 10485760 | tf_op jit(solution)/shard_map/forward/pallas_call | solution.py:216
  43.6 3.3 %collective-permute-start.13 = (bf16[272,256]{1,0:T(8,128)(2,1)S(1)}, bf16[272,256]{1,0:T(8,128)(2,1)S(1)}, u32[]{:S(2)}, u32[]{:S(2)}) collective-permute-start(bf16[272,256]{1,0:T(8,128)(2,1)S(1)} %get-tuple-element.47), channel_id=1, source_target_pairs={{0,4},{1,5},{2,6},{3,7},{4,0},{5,1},{6,2},{7,3},{8,12},{9,13},{10,... | collective-permute-start | bytes 417800 | tf_op jit(solution)/shard_map/ppermute | solution.py:410
  47.5 2.6 %collective-permute-start.15 = (bf16[272,256]{1,0:T(8,128)(2,1)S(1)}, bf16[272,256]{1,0:T(8,128)(2,1)S(1)}, u32[]{:S(2)}, u32[]{:S(2)}) collective-permute-start(bf16[272,256]{1,0:T(8,128)(2,1)S(1)} %get-tuple-element.49), channel_id=1, source_target_pairs={{0,6},{1,7},{2,0},{3,1},{4,2},{5,3},{6,4},{7,5},{8,14},{9,15},{10,... | collective-permute-start | bytes 417800 | tf_op jit(solution)/shard_map/ppermute | solution.py:410
  51.6 2.6 %collective-permute-done.14.r1_ref = bf16[272,256]{1,0:T(8,128)(2,1)S(1)} collective-permute-done((bf16[272,256]{1,0:T(8,128)(2,1)S(1)}, bf16[272,256]{1,0:T(8,128)(2,1)S(1)}, u32[]{:S(2)}, u32[]{:S(2)}) %collective-permute-start.14) | collective-permute-done | bytes 139296 | tf_op jit(solution)/shard_map/ppermute | solution.py:410
  56.1 2.2 %collective-permute-start.16 = (bf16[256,256]{1,0:T(8,128)(2,1)S(1)}, bf16[256,256]{1,0:T(8,128)(2,1)S(1)}, u32[]{:S(2)}, u32[]{:S(2)}) collective-permute-start(bf16[256,256]{1,0:T(8,128)(2,1)S(1)} %get-tuple-element.51.refs_0_), channel_id=1, source_target_pairs={{0,4},{1,5},{2,6},{3,7},{4,0},{5,1},{6,2},{7,3},{8,12},{9,13},{10,... | collective-permute-start | bytes 393224 | tf_op jit(solution)/shard_map/ppermute | solution.py:410
  61.5 2.3 %collective-permute-done.16.refs_1_ = bf16[256,256]{1,0:T(8,128)(2,1)S(1)} collective-permute-done((bf16[256,256]{1,0:T(8,128)(2,1)S(1)}, bf16[256,256]{1,0:T(8,128)(2,1)S(1)}, u32[]{:S(2)}, u32[]{:S(2)}) %collective-permute-start.16) | collective-permute-done | bytes 131104 | tf_op jit(solution)/shard_map/ppermute | solution.py:410
  66.2 3.8 %collective-permute-start.24 = (bf16[528,256]{1,0:T(8,128)(2,1)S(1)}, bf16[528,256]{1,0:T(8,128)(2,1)S(1)}, u32[]{:S(2)}, u32[]{:S(2)}) collective-permute-start(bf16[528,256]{1,0:T(8,128)(2,1)S(1)} %add_convert_fusion), channel_id=1, source_target_pairs={{0,64},{8,72},{16,80},{24,88},{32,96},{40,104},{48,112},{56,120},{... | collective-permute-start | bytes 811016 | tf_op jit(solution)/shard_map/ppermute | solution.py:399
  70.0 6.7 %backward.1 = bf16[4096,256]{1,0:T(8,128)(2,1)} custom-call(s32[4]{0:T(128)S(1)} %get-tuple-element.37.place_ref, bf16[256,256]{1,0:T(8,128)(2,1)S(1)} %get-tuple-element.51.refs_0_, bf16[256,256]{1,0:T(8,128)(2,1)S(1)} %collective-permute-done.16.refs_1_, bf16[256,256]{1,0:T(8,128)(2,1)S(1)} %collective-permute-done.17.refs_2_, ...), custom_call_target="tpu_custom_call" | custom-call | flops 4294967296 | bytes 20971520 | tf_op jit(solution)/shard_map/backward/pallas_call | solution.py:262
  76.7 5.4 %all-to-all-start = ((bf16[16,256,256]{2,1,0:T(8,128)(2,1)}), bf16[16,256,256]{2,1,0:T(8,128)(2,1)S(1)}, u32[]{:S(2)}, u32[]{:S(2)}) async-start(bf16[16,256,256]{2,1,0:T(8,128)(2,1)} %bitcast.19), calls=%async_computation | async-start | bytes 4194304 | tf_op jit(solution)/shard_map/all_to_all | solution.py:383
  83.9 2.1 %collective-permute-start.26 = (bf16[272,256]{1,0:T(8,128)(2,1)S(1)}, bf16[272,256]{1,0:T(8,128)(2,1)S(1)}, u32[]{:S(2)}, u32[]{:S(2)}) collective-permute-start(bf16[272,256]{1,0:T(8,128)(2,1)S(1)} %fusion.1), channel_id=1, source_target_pairs={{0,4},{1,5},{2,6},{3,7},{4,0},{5,1},{6,2},{7,3},{8,12},{9,13},{10,... | collective-permute-start | bytes 417800 | tf_op jit(solution)/shard_map/ppermute | solution.py:410
  89.3 2.7 %collective-permute-done.26 = bf16[272,256]{1,0:T(8,128)(2,1)S(1)} collective-permute-done((bf16[272,256]{1,0:T(8,128)(2,1)S(1)}, bf16[272,256]{1,0:T(8,128)(2,1)S(1)}, u32[]{:S(2)}, u32[]{:S(2)}) %collective-permute-start.26) | collective-permute-done | bytes 139296 | tf_op jit(solution)/shard_map/ppermute | solution.py:410
  92.0 2.2 %collective-permute-done.27 = bf16[272,256]{1,0:T(8,128)(2,1)S(1)} collective-permute-done((bf16[272,256]{1,0:T(8,128)(2,1)S(1)}, bf16[272,256]{1,0:T(8,128)(2,1)S(1)}, u32[]{:S(2)}, u32[]{:S(2)}) %collective-permute-start.27) | collective-permute-done | bytes 139296 | tf_op jit(solution)/shard_map/ppermute | solution.py:410
  96.4 2.7 %collective-permute-start.30 = (bf16[272,256]{1,0:T(8,128)(2,1)S(1)}, bf16[272,256]{1,0:T(8,128)(2,1)S(1)}, u32[]{:S(2)}, u32[]{:S(2)}) collective-permute-start(bf16[272,256]{1,0:T(8,128)(2,1)S(1)} %add_convert_fusion.1), channel_id=1, source_target_pairs={{0,16},{8,24},{16,0},{24,8},{32,48},{40,56},{48,32},{56,40},{64,80... | collective-permute-start | bytes 417800 | tf_op jit(solution)/shard_map/ppermute | solution.py:394
  100.5 10.7 %all-to-all-done.parts_ref = bf16[16,256,256]{2,1,0:T(8,128)(2,1)S(1)} async-done(((bf16[16,256,256]{2,1,0:T(8,128)(2,1)}), bf16[16,256,256]{2,1,0:T(8,128)(2,1)S(1)}, u32[]{:S(2)}, u32[]{:S(2)}) %all-to-all-start) | async-done | bytes 2097184 | tf_op jit(solution)/shard_map/all_to_all | solution.py:383
  112.1 3.1 %collective-permute-done.30 = bf16[272,256]{1,0:T(8,128)(2,1)S(1)} collective-permute-done((bf16[272,256]{1,0:T(8,128)(2,1)S(1)}, bf16[272,256]{1,0:T(8,128)(2,1)S(1)}, u32[]{:S(2)}, u32[]{:S(2)}) %collective-permute-start.30) | collective-permute-done | bytes 139296 | tf_op jit(solution)/shard_map/ppermute | solution.py:394
  (79 shorter events, 33.0 us)
Async XLA Ops:
  1.6 11.0 %collective-permute-start.3 = (bf16[128,256]{1,0:T(8,128)(2,1)S(1)}, bf16[128,256]{1,0:T(8,128)(2,1)S(1)}, u32[]{:S(2)}, u32[]{:S(2)}) collective-permute-start(bf16[128,256]{1,0:T(8,128)(2,1)S(1)} %get-tuple-element.36), channel_id=1, source_target_pairs={{0,8},{8,16},{16,24},{24,0},{32,40},{40,48},{48,56},{56,32},{64,72... | collective-permute-start | bytes 196616 | tf_op jit(solution)/shard_map/ppermute | solution.py:394
  3.7 10.3 %collective-permute-start.4 = (bf16[128,256]{1,0:T(8,128)(2,1)S(1)}, bf16[128,256]{1,0:T(8,128)(2,1)S(1)}, u32[]{:S(2)}, u32[]{:S(2)}) collective-permute-start(bf16[128,256]{1,0:T(8,128)(2,1)S(1)} %get-tuple-element.36), channel_id=1, source_target_pairs={{0,16},{8,24},{16,0},{24,8},{32,48},{40,56},{48,32},{56,40},{64,80... | collective-permute-start | bytes 196616 | tf_op jit(solution)/shard_map/ppermute | solution.py:394
  7.3 6.8 %collective-permute-start.5 = (bf16[128,256]{1,0:T(8,128)(2,1)S(1)}, bf16[128,256]{1,0:T(8,128)(2,1)S(1)}, u32[]{:S(2)}, u32[]{:S(2)}) collective-permute-start(bf16[128,256]{1,0:T(8,128)(2,1)S(1)} %get-tuple-element.36), channel_id=1, source_target_pairs={{0,24},{8,0},{16,8},{24,16},{32,56},{40,32},{48,40},{56,48},{64,88... | collective-permute-start | bytes 196616 | tf_op jit(solution)/shard_map/ppermute | solution.py:394
  16.9 12.1 %collective-permute-start.9 = (bf16[4,128,256]{2,1,0:T(8,128)(2,1)S(1)}, bf16[4,128,256]{2,1,0:T(8,128)(2,1)S(1)}, u32[]{:S(2)}, u32[]{:S(2)}) collective-permute-start(bf16[4,128,256]{2,1,0:T(8,128)(2,1)S(1)} %pad_maximum_fusion.3.gate_ref.refs_4_), channel_id=1, source_target_pairs={{0,96},{8,104},{16,112},{24,120},{32,0},{40,8},{48,16},{56,24},{64... | collective-permute-start | bytes 786440 | tf_op jit(solution)/shard_map/ppermute | solution.py:394
  21.9 13.6 %collective-permute-start.11 = (bf16[4,128,256]{2,1,0:T(8,128)(2,1)S(1)}, bf16[4,128,256]{2,1,0:T(8,128)(2,1)S(1)}, u32[]{:S(2)}, u32[]{:S(2)}) collective-permute-start(bf16[4,128,256]{2,1,0:T(8,128)(2,1)S(1)} %pad_maximum_fusion.3.gate_ref.refs_4_), channel_id=1, source_target_pairs={{0,64},{8,72},{16,80},{24,88},{32,96},{40,104},{48,112},{56,120},{... | collective-permute-start | bytes 786440 | tf_op jit(solution)/shard_map/ppermute | solution.py:394
  22.0 13.5 %collective-permute-start.6 = (bf16[4,128,256]{2,1,0:T(8,128)(2,1)S(1)}, bf16[4,128,256]{2,1,0:T(8,128)(2,1)S(1)}, u32[]{:S(2)}, u32[]{:S(2)}) collective-permute-start(bf16[4,128,256]{2,1,0:T(8,128)(2,1)S(1)} %pad_maximum_fusion.2.gate_ref.refs_0_), channel_id=1, source_target_pairs={{0,8},{8,16},{16,24},{24,0},{32,40},{40,48},{48,56},{56,32},{64,72... | collective-permute-start | bytes 786440 | tf_op jit(solution)/shard_map/ppermute | solution.py:394
  23.1 12.5 %collective-permute-start.7 = (bf16[4,128,256]{2,1,0:T(8,128)(2,1)S(1)}, bf16[4,128,256]{2,1,0:T(8,128)(2,1)S(1)}, u32[]{:S(2)}, u32[]{:S(2)}) collective-permute-start(bf16[4,128,256]{2,1,0:T(8,128)(2,1)S(1)} %pad_maximum_fusion.2.gate_ref.refs_0_), channel_id=1, source_target_pairs={{0,16},{8,24},{16,0},{24,8},{32,48},{40,56},{48,32},{56,40},{64,80... | collective-permute-start | bytes 786440 | tf_op jit(solution)/shard_map/ppermute | solution.py:394
  23.5 12.0 %collective-permute-start.8 = (bf16[4,128,256]{2,1,0:T(8,128)(2,1)S(1)}, bf16[4,128,256]{2,1,0:T(8,128)(2,1)S(1)}, u32[]{:S(2)}, u32[]{:S(2)}) collective-permute-start(bf16[4,128,256]{2,1,0:T(8,128)(2,1)S(1)} %pad_maximum_fusion.2.gate_ref.refs_0_), channel_id=1, source_target_pairs={{0,24},{8,0},{16,8},{24,16},{32,56},{40,32},{48,40},{56,48},{64,88... | collective-permute-start | bytes 786440 | tf_op jit(solution)/shard_map/ppermute | solution.py:394
  29.0 8.0 %collective-permute-start.10 = (bf16[4,128,256]{2,1,0:T(8,128)(2,1)S(1)}, bf16[4,128,256]{2,1,0:T(8,128)(2,1)S(1)}, u32[]{:S(2)}, u32[]{:S(2)}) collective-permute-start(bf16[4,128,256]{2,1,0:T(8,128)(2,1)S(1)} %pad_maximum_fusion.3.gate_ref.refs_4_), channel_id=1, source_target_pairs={{0,32},{8,40},{16,48},{24,56},{32,64},{40,72},{48,80},{56,88},{64,... | collective-permute-start | bytes 786440 | tf_op jit(solution)/shard_map/ppermute | solution.py:394
  43.6 8.1 %collective-permute-start.13 = (bf16[272,256]{1,0:T(8,128)(2,1)S(1)}, bf16[272,256]{1,0:T(8,128)(2,1)S(1)}, u32[]{:S(2)}, u32[]{:S(2)}) collective-permute-start(bf16[272,256]{1,0:T(8,128)(2,1)S(1)} %get-tuple-element.47), channel_id=1, source_target_pairs={{0,4},{1,5},{2,6},{3,7},{4,0},{5,1},{6,2},{7,3},{8,12},{9,13},{10,... | collective-permute-start | bytes 417800 | tf_op jit(solution)/shard_map/ppermute | solution.py:410
  46.9 7.4 %collective-permute-start.14 = (bf16[272,256]{1,0:T(8,128)(2,1)S(1)}, bf16[272,256]{1,0:T(8,128)(2,1)S(1)}, u32[]{:S(2)}, u32[]{:S(2)}) collective-permute-start(bf16[272,256]{1,0:T(8,128)(2,1)S(1)} %get-tuple-element.48), channel_id=1, source_target_pairs={{0,2},{1,3},{2,4},{3,5},{4,6},{5,7},{6,0},{7,1},{8,10},{9,11},{10,... | collective-permute-start | bytes 417800 | tf_op jit(solution)/shard_map/ppermute | solution.py:410
  47.5 7.0 %collective-permute-start.15 = (bf16[272,256]{1,0:T(8,128)(2,1)S(1)}, bf16[272,256]{1,0:T(8,128)(2,1)S(1)}, u32[]{:S(2)}, u32[]{:S(2)}) collective-permute-start(bf16[272,256]{1,0:T(8,128)(2,1)S(1)} %get-tuple-element.49), channel_id=1, source_target_pairs={{0,6},{1,7},{2,0},{3,1},{4,2},{5,3},{6,4},{7,5},{8,14},{9,15},{10,... | collective-permute-start | bytes 417800 | tf_op jit(solution)/shard_map/ppermute | solution.py:410
  56.0 10.1 %collective-permute-start.23 = (bf16[528,256]{1,0:T(8,128)(2,1)S(1)}, bf16[528,256]{1,0:T(8,128)(2,1)S(1)}, u32[]{:S(2)}, u32[]{:S(2)}) collective-permute-start(bf16[528,256]{1,0:T(8,128)(2,1)S(1)} %get-tuple-element.54), channel_id=1, source_target_pairs={{0,32},{8,40},{16,48},{24,56},{32,0},{40,8},{48,16},{56,24},{64,96... | collective-permute-start | bytes 811016 | tf_op jit(solution)/shard_map/ppermute | solution.py:399
  56.1 7.7 %collective-permute-start.16 = (bf16[256,256]{1,0:T(8,128)(2,1)S(1)}, bf16[256,256]{1,0:T(8,128)(2,1)S(1)}, u32[]{:S(2)}, u32[]{:S(2)}) collective-permute-start(bf16[256,256]{1,0:T(8,128)(2,1)S(1)} %get-tuple-element.51.refs_0_), channel_id=1, source_target_pairs={{0,4},{1,5},{2,6},{3,7},{4,0},{5,1},{6,2},{7,3},{8,12},{9,13},{10,... | collective-permute-start | bytes 393224 | tf_op jit(solution)/shard_map/ppermute | solution.py:410
  58.2 7.3 %collective-permute-start.17 = (bf16[256,256]{1,0:T(8,128)(2,1)S(1)}, bf16[256,256]{1,0:T(8,128)(2,1)S(1)}, u32[]{:S(2)}, u32[]{:S(2)}) collective-permute-start(bf16[256,256]{1,0:T(8,128)(2,1)S(1)} %get-tuple-element.51.refs_0_), channel_id=1, source_target_pairs={{0,2},{1,3},{2,4},{3,5},{4,6},{5,7},{6,0},{7,1},{8,10},{9,11},{10,... | collective-permute-start | bytes 393224 | tf_op jit(solution)/shard_map/ppermute | solution.py:410
  61.5 8.5 %collective-permute-start.19 = (bf16[256,256]{1,0:T(8,128)(2,1)S(1)}, bf16[256,256]{1,0:T(8,128)(2,1)S(1)}, u32[]{:S(2)}, u32[]{:S(2)}) collective-permute-start(bf16[256,256]{1,0:T(8,128)(2,1)S(1)} %get-tuple-element.51.refs_0_), channel_id=1, source_target_pairs={{0,1},{1,0},{2,3},{3,2},{4,5},{5,4},{6,7},{7,6},{8,9},{9,8},{10,11... | collective-permute-start | bytes 393224 | tf_op jit(solution)/shard_map/ppermute | solution.py:414
  66.2 10.5 %collective-permute-start.24 = (bf16[528,256]{1,0:T(8,128)(2,1)S(1)}, bf16[528,256]{1,0:T(8,128)(2,1)S(1)}, u32[]{:S(2)}, u32[]{:S(2)}) collective-permute-start(bf16[528,256]{1,0:T(8,128)(2,1)S(1)} %add_convert_fusion), channel_id=1, source_target_pairs={{0,64},{8,72},{16,80},{24,88},{32,96},{40,104},{48,112},{56,120},{... | collective-permute-start | bytes 811016 | tf_op jit(solution)/shard_map/ppermute | solution.py:399
  76.7 34.5 %all-to-all-start = ((bf16[16,256,256]{2,1,0:T(8,128)(2,1)}), bf16[16,256,256]{2,1,0:T(8,128)(2,1)S(1)}, u32[]{:S(2)}, u32[]{:S(2)}) async-start(bf16[16,256,256]{2,1,0:T(8,128)(2,1)} %bitcast.19), calls=%async_computation | async-start | bytes 4194304 | tf_op jit(solution)/shard_map/all_to_all | solution.py:383
  83.9 8.1 %collective-permute-start.26 = (bf16[272,256]{1,0:T(8,128)(2,1)S(1)}, bf16[272,256]{1,0:T(8,128)(2,1)S(1)}, u32[]{:S(2)}, u32[]{:S(2)}) collective-permute-start(bf16[272,256]{1,0:T(8,128)(2,1)S(1)} %fusion.1), channel_id=1, source_target_pairs={{0,4},{1,5},{2,6},{3,7},{4,0},{5,1},{6,2},{7,3},{8,12},{9,13},{10,... | collective-permute-start | bytes 417800 | tf_op jit(solution)/shard_map/ppermute | solution.py:410
  86.0 8.1 %collective-permute-start.27 = (bf16[272,256]{1,0:T(8,128)(2,1)S(1)}, bf16[272,256]{1,0:T(8,128)(2,1)S(1)}, u32[]{:S(2)}, u32[]{:S(2)}) collective-permute-start(bf16[272,256]{1,0:T(8,128)(2,1)S(1)} %fusion.1), channel_id=1, source_target_pairs={{0,2},{1,3},{2,4},{3,5},{4,6},{5,7},{6,0},{7,1},{8,10},{9,11},{10,... | collective-permute-start | bytes 417800 | tf_op jit(solution)/shard_map/ppermute | solution.py:410
  87.6 6.7 %collective-permute-start.28 = (bf16[272,256]{1,0:T(8,128)(2,1)S(1)}, bf16[272,256]{1,0:T(8,128)(2,1)S(1)}, u32[]{:S(2)}, u32[]{:S(2)}) collective-permute-start(bf16[272,256]{1,0:T(8,128)(2,1)S(1)} %fusion.1), channel_id=1, source_target_pairs={{0,6},{1,7},{2,0},{3,1},{4,2},{5,3},{6,4},{7,5},{8,14},{9,15},{10,... | collective-permute-start | bytes 417800 | tf_op jit(solution)/shard_map/ppermute | solution.py:410
  94.4 17.7 %collective-permute-start.29 = (bf16[272,256]{1,0:T(8,128)(2,1)S(1)}, bf16[272,256]{1,0:T(8,128)(2,1)S(1)}, u32[]{:S(2)}, u32[]{:S(2)}) collective-permute-start(bf16[272,256]{1,0:T(8,128)(2,1)S(1)} %add_convert_fusion.1), channel_id=1, source_target_pairs={{0,8},{8,16},{16,24},{24,0},{32,40},{40,48},{48,56},{56,32},{64,72... | collective-permute-start | bytes 417800 | tf_op jit(solution)/shard_map/ppermute | solution.py:394
  96.4 18.8 %collective-permute-start.30 = (bf16[272,256]{1,0:T(8,128)(2,1)S(1)}, bf16[272,256]{1,0:T(8,128)(2,1)S(1)}, u32[]{:S(2)}, u32[]{:S(2)}) collective-permute-start(bf16[272,256]{1,0:T(8,128)(2,1)S(1)} %add_convert_fusion.1), channel_id=1, source_target_pairs={{0,16},{8,24},{16,0},{24,8},{32,48},{40,56},{48,32},{56,40},{64,80... | collective-permute-start | bytes 417800 | tf_op jit(solution)/shard_map/ppermute | solution.py:394
  99.0 16.2 %collective-permute-start.31 = (bf16[272,256]{1,0:T(8,128)(2,1)S(1)}, bf16[272,256]{1,0:T(8,128)(2,1)S(1)}, u32[]{:S(2)}, u32[]{:S(2)}) collective-permute-start(bf16[272,256]{1,0:T(8,128)(2,1)S(1)} %add_convert_fusion.1), channel_id=1, source_target_pairs={{0,24},{8,0},{16,8},{24,16},{32,56},{40,32},{48,40},{56,48},{64,88... | collective-permute-start | bytes 417800 | tf_op jit(solution)/shard_map/ppermute | solution.py:394
  (16 other events, 116.3 us)

commit v12 on v11

--- a/solution.py
+++ b/solution.py
@@ -177,8 +177,8 @@
         for kz in range(4):
             n = 4 * x + lax.rem(place_ref[3] + 4 - kz, 4)
             lanes = pl.ds(pl.multiple_of(n * rows, rows), rows)
-            joined[0:half, lanes] = tops[kz][kx]
-            joined[half:width, lanes] = lows[kx][kz]
+            joined[0:half, lanes] = tops[kz][FAR_FIRST.index(kx)]
+            joined[half:width, lanes] = lows[kx][FAR_FIRST.index(kz)]
 
     for j in range(4):
         chunk = 2 * lax.rem(place_ref[0] + j, 4) + place_ref[1]
@@ -437,8 +437,8 @@
     theirs = jnp.stack([y, 1 - core, node // 4, node % 4]).astype(jnp.int32)
 
     top, low = prepare(node_feats)
-    top = jnp.stack([top] + [send_x(top, k) for k in (1, 2, 3)])
-    low = jnp.stack([low] + [send_z(low, k) for k in (1, 2, 3)])
+    top = jnp.stack([top] + [send_x(top, k) for k in FAR_FIRST[1:]])
+    low = jnp.stack([low] + [send_z(low, k) for k in FAR_FIRST[1:]])
     top, low, mine, theirs, zero = lax.optimization_barrier((top, low, mine, theirs, core == 0))
     planes = [top] + [send_z(top, k) for k in (1, 2, 3)]
     empty = cleared(low, nodes * rows_dev // 128, cols * rows_dev // 128)

time: 119 us -> 119 us (level)
    ppermute x15, starting transfers between devices: 25.1 us -> 26.5 us  [send_node(): return lax.ppermute(x, 'nodes', moves)]
  transfers between devices with their start and end apart: 34 -> 34, of which waited for: 17 -> 15; matrix products, arithmetic and copies ran while one was open for 1% -> 1% of each run, Pallas kernels for 17% -> 17%
where the time goes in v12:
time: 119 us; the launch traced here: 118 us
  starting transfers between devices  53.2 us (45%)
  waiting for transfers between devices  36.9 us (31%)
  Pallas kernels  24.3 us (20%)
  local copies, waits for them, and re-layouts  1.5 us (1%)
  other arithmetic  1.35 us (1%)
    ppermute x15, starting transfers between devices, send_node(): return lax.ppermute(x, 'nodes', moves)  26.5 us
    ppermute x9, starting transfers between devices, send_y(): return lax.ppermute(x, 'cols', along_y(step))  17.3 us
    ppermute x9, waiting for transfers between devices, send_y(): return lax.ppermute(x, 'cols', along_y(step))  13.6 us
    all_to_all x1, waiting for transfers between devices, swap(): return lax.all_to_all(x, axis, 0, 0, tiled=True)  10.7 us
    ppermute x15, waiting for transfers between devices, send_node(): return lax.ppermute(x, 'nodes', moves)  10.1 us
    pallas_call x1, Pallas kernels, backward(): pl.pallas_call(backward_kernel, out_shape=in_hbm((sources * 128, width),...  6.69 us
    pallas_call x1, Pallas kernels, build(): pl.pallas_call(build_kernel, out_shape=(jax.ShapeDtypeStruct((sources + 1...  6.51 us
    pallas_call x2, Pallas kernels, forward(): pl.pallas_call(forward_kernel, out_shape=jax.ShapeDtypeStruct((4, width +...  6.32 us
  transfers between devices with their start and end apart: 34, of which 15 were waited for; matrix products, arithmetic and copies ran while one was open for 1% of the time, Pallas kernels for 17%

profile of v12, /device:TPU:0, one launch (start us, length us, event | category | flops | bytes accessed | tf_op | source)
XLA Modules:
  0.0 118.2 jit_solution(9885068583620908350)
XLA Ops:
  1.6 4.0 %collective-permute-start.3 = (bf16[128,256]{1,0:T(8,128)(2,1)S(1)}, bf16[128,256]{1,0:T(8,128)(2,1)S(1)}, u32[]{:S(2)}, u32[]{:S(2)}) collective-permute-start(bf16[128,256]{1,0:T(8,128)(2,1)S(1)} %get-tuple-element.36), channel_id=1, source_target_pairs={{0,16},{8,24},{16,0},{24,8},{32,48},{40,56},{48,32},{56,40},{64,80... | collective-permute-start | bytes 196616 | tf_op jit(solution)/shard_map/ppermute | solution.py:394
  6.7 2.2 %collective-permute-start.5 = (bf16[128,256]{1,0:T(8,128)(2,1)S(1)}, bf16[128,256]{1,0:T(8,128)(2,1)S(1)}, u32[]{:S(2)}, u32[]{:S(2)}) collective-permute-start(bf16[128,256]{1,0:T(8,128)(2,1)S(1)} %get-tuple-element.36), channel_id=1, source_target_pairs={{0,24},{8,0},{16,8},{24,16},{32,56},{40,32},{48,40},{56,48},{64,88... | collective-permute-start | bytes 196616 | tf_op jit(solution)/shard_map/ppermute | solution.py:394
  8.9 3.0 %collective-permute-start = (bf16[128,256]{1,0:T(8,128)(2,1)S(1)}, bf16[128,256]{1,0:T(8,128)(2,1)S(1)}, u32[]{:S(2)}, u32[]{:S(2)}) collective-permute-start(bf16[128,256]{1,0:T(8,128)(2,1)S(1)} %get-tuple-element.35), channel_id=1, source_target_pairs={{0,64},{8,72},{16,80},{24,88},{32,96},{40,104},{48,112},{56,120},{... | collective-permute-start | bytes 196616 | tf_op jit(solution)/shard_map/ppermute | solution.py:394
  12.6 2.7 %collective-permute-start.2 = (bf16[128,256]{1,0:T(8,128)(2,1)S(1)}, bf16[128,256]{1,0:T(8,128)(2,1)S(1)}, u32[]{:S(2)}, u32[]{:S(2)}) collective-permute-start(bf16[128,256]{1,0:T(8,128)(2,1)S(1)} %get-tuple-element.35), channel_id=1, source_target_pairs={{0,96},{8,104},{16,112},{24,120},{32,0},{40,8},{48,16},{56,24},{64... | collective-permute-start | bytes 196616 | tf_op jit(solution)/shard_map/ppermute | solution.py:394
  17.4 3.4 %collective-permute-start.9 = (bf16[4,128,256]{2,1,0:T(8,128)(2,1)S(1)}, bf16[4,128,256]{2,1,0:T(8,128)(2,1)S(1)}, u32[]{:S(2)}, u32[]{:S(2)}) collective-permute-start(bf16[4,128,256]{2,1,0:T(8,128)(2,1)S(1)} %pad_maximum_fusion.3.gate_ref.refs_4_), channel_id=1, source_target_pairs={{0,96},{8,104},{16,112},{24,120},{32,0},{40,8},{48,16},{56,24},{64... | collective-permute-start | bytes 786440 | tf_op jit(solution)/shard_map/ppermute | solution.py:394
  20.8 2.3 %clear.1.clear_ref = bf16[33,16,128,128]{3,2,1,0:T(8,128)(2,1)S(1)} custom-call(bf16[4,128,256]{2,1,0:T(8,128)(2,1)S(1)} %pad_maximum_fusion.3.gate_ref.refs_4_), custom_call_target="tpu_custom_call" | custom-call | bytes 8388608 | tf_op jit(solution)/shard_map/clear/pallas_call | solution.py:128
  26.5 3.4 %collective-permute-done.9.refs_7_ = bf16[4,128,256]{2,1,0:T(8,128)(2,1)S(1)} collective-permute-done((bf16[4,128,256]{2,1,0:T(8,128)(2,1)S(1)}, bf16[4,128,256]{2,1,0:T(8,128)(2,1)S(1)}, u32[]{:S(2)}, u32[]{:S(2)}) %collective-permute-start.9) | collective-permute-done | bytes 262176 | tf_op jit(solution)/shard_map/ppermute | solution.py:394
  30.0 6.5 %build.1 = (bf16[33,16,128,128]{3,2,1,0:T(8,128)(2,1)S(1)}, f32[1,2048]{1,0:T(1,128)S(1)}) custom-call(s32[1,352]{1,0:T(1,128)} %rows_ref.1, s32[1,352]{1,0:T(1,128)} %cols_ref.1, s32[1,352,16,128]{3,2,1,0:T(8,128)} %bits_all.1, bf16[4,128,256]{2,1,0:T(8,128)(2,1)S(1)} %pad_maximum_fusion.2.gate_ref.refs_0_, ...), custom_call_target="tpu_custom_call", output_to_operand_aliasing={{0}: (4, {})} | custom-call | bytes 31457280 | tf_op jit(solution)/shard_map/build/pallas_call | solution.py:145
  38.0 3.2 %forward.3 = bf16[4,272,256]{2,1,0:T(8,128)(2,1)S(1)} custom-call(s32[4]{0:T(128)S(1)} %get-tuple-element.45.place_ref, bf16[4,128,256]{2,1,0:T(8,128)(2,1)S(1)} %pad_maximum_fusion.2.gate_ref.refs_0_, bf16[4,128,256]{2,1,0:T(8,128)(2,1)S(1)} %collective-permute-done.6.refs_1_, bf16[4,128,256]{2,1,0:T(8,128)(2,1)S(1)} %collective-permute-done.7.refs_2_, ...), custom_call_target="tpu_custom_call" | custom-call | flops 2147483648 | bytes 10485760 | tf_op jit(solution)/shard_map/forward/pallas_call | solution.py:216
  41.3 3.2 %forward.2.keep_ref = f32[4,272,256]{2,1,0:T(8,128)S(1)} custom-call(s32[4]{0:T(128)S(1)} %get-tuple-element.37.place_ref, bf16[4,128,256]{2,1,0:T(8,128)(2,1)S(1)} %pad_maximum_fusion.2.gate_ref.refs_0_, bf16[4,128,256]{2,1,0:T(8,128)(2,1)S(1)} %collective-permute-done.6.refs_1_, bf16[4,128,256]{2,1,0:T(8,128)(2,1)S(1)} %collective-permute-done.7.refs_2_, ...), custom_call_target="tpu_custom_call" | custom-call | flops 2147483648 | bytes 10485760 | tf_op jit(solution)/shard_map/forward/pallas_call | solution.py:216
  44.6 3.3 %collective-permute-start.13 = (bf16[272,256]{1,0:T(8,128)(2,1)S(1)}, bf16[272,256]{1,0:T(8,128)(2,1)S(1)}, u32[]{:S(2)}, u32[]{:S(2)}) collective-permute-start(bf16[272,256]{1,0:T(8,128)(2,1)S(1)} %get-tuple-element.47), channel_id=1, source_target_pairs={{0,4},{1,5},{2,6},{3,7},{4,0},{5,1},{6,2},{7,3},{8,12},{9,13},{10,... | collective-permute-start | bytes 417800 | tf_op jit(solution)/shard_map/ppermute | solution.py:410
  48.6 2.6 %collective-permute-start.15 = (bf16[272,256]{1,0:T(8,128)(2,1)S(1)}, bf16[272,256]{1,0:T(8,128)(2,1)S(1)}, u32[]{:S(2)}, u32[]{:S(2)}) collective-permute-start(bf16[272,256]{1,0:T(8,128)(2,1)S(1)} %get-tuple-element.49), channel_id=1, source_target_pairs={{0,6},{1,7},{2,0},{3,1},{4,2},{5,3},{6,4},{7,5},{8,14},{9,15},{10,... | collective-permute-start | bytes 417800 | tf_op jit(solution)/shard_map/ppermute | solution.py:410
  52.7 2.6 %collective-permute-done.14.r1_ref = bf16[272,256]{1,0:T(8,128)(2,1)S(1)} collective-permute-done((bf16[272,256]{1,0:T(8,128)(2,1)S(1)}, bf16[272,256]{1,0:T(8,128)(2,1)S(1)}, u32[]{:S(2)}, u32[]{:S(2)}) %collective-permute-start.14) | collective-permute-done | bytes 139296 | tf_op jit(solution)/shard_map/ppermute | solution.py:410
  57.1 2.2 %collective-permute-start.16 = (bf16[256,256]{1,0:T(8,128)(2,1)S(1)}, bf16[256,256]{1,0:T(8,128)(2,1)S(1)}, u32[]{:S(2)}, u32[]{:S(2)}) collective-permute-start(bf16[256,256]{1,0:T(8,128)(2,1)S(1)} %get-tuple-element.51.refs_0_), channel_id=1, source_target_pairs={{0,4},{1,5},{2,6},{3,7},{4,0},{5,1},{6,2},{7,3},{8,12},{9,13},{10,... | collective-permute-start | bytes 393224 | tf_op jit(solution)/shard_map/ppermute | solution.py:410
  62.5 2.3 %collective-permute-done.16.refs_1_ = bf16[256,256]{1,0:T(8,128)(2,1)S(1)} collective-permute-done((bf16[256,256]{1,0:T(8,128)(2,1)S(1)}, bf16[256,256]{1,0:T(8,128)(2,1)S(1)}, u32[]{:S(2)}, u32[]{:S(2)}) %collective-permute-start.16) | collective-permute-done | bytes 131104 | tf_op jit(solution)/shard_map/ppermute | solution.py:410
  67.2 3.8 %collective-permute-start.24 = (bf16[528,256]{1,0:T(8,128)(2,1)S(1)}, bf16[528,256]{1,0:T(8,128)(2,1)S(1)}, u32[]{:S(2)}, u32[]{:S(2)}) collective-permute-start(bf16[528,256]{1,0:T(8,128)(2,1)S(1)} %add_convert_fusion), channel_id=1, source_target_pairs={{0,64},{8,72},{16,80},{24,88},{32,96},{40,104},{48,112},{56,120},{... | collective-permute-start | bytes 811016 | tf_op jit(solution)/shard_map/ppermute | solution.py:399
  71.0 6.7 %backward.1 = bf16[4096,256]{1,0:T(8,128)(2,1)} custom-call(s32[4]{0:T(128)S(1)} %get-tuple-element.37.place_ref, bf16[256,256]{1,0:T(8,128)(2,1)S(1)} %get-tuple-element.51.refs_0_, bf16[256,256]{1,0:T(8,128)(2,1)S(1)} %collective-permute-done.16.refs_1_, bf16[256,256]{1,0:T(8,128)(2,1)S(1)} %collective-permute-done.17.refs_2_, ...), custom_call_target="tpu_custom_call" | custom-call | flops 4294967296 | bytes 20971520 | tf_op jit(solution)/shard_map/backward/pallas_call | solution.py:262
  77.7 4.8 %all-to-all-start = ((bf16[16,256,256]{2,1,0:T(8,128)(2,1)}), bf16[16,256,256]{2,1,0:T(8,128)(2,1)S(1)}, u32[]{:S(2)}, u32[]{:S(2)}) async-start(bf16[16,256,256]{2,1,0:T(8,128)(2,1)} %bitcast.19), calls=%async_computation | async-start | bytes 4194304 | tf_op jit(solution)/shard_map/all_to_all | solution.py:383
  84.4 2.1 %collective-permute-start.26 = (bf16[272,256]{1,0:T(8,128)(2,1)S(1)}, bf16[272,256]{1,0:T(8,128)(2,1)S(1)}, u32[]{:S(2)}, u32[]{:S(2)}) collective-permute-start(bf16[272,256]{1,0:T(8,128)(2,1)S(1)} %fusion.1), channel_id=1, source_target_pairs={{0,4},{1,5},{2,6},{3,7},{4,0},{5,1},{6,2},{7,3},{8,12},{9,13},{10,... | collective-permute-start | bytes 417800 | tf_op jit(solution)/shard_map/ppermute | solution.py:410
  89.7 2.7 %collective-permute-done.26 = bf16[272,256]{1,0:T(8,128)(2,1)S(1)} collective-permute-done((bf16[272,256]{1,0:T(8,128)(2,1)S(1)}, bf16[272,256]{1,0:T(8,128)(2,1)S(1)}, u32[]{:S(2)}, u32[]{:S(2)}) %collective-permute-start.26) | collective-permute-done | bytes 139296 | tf_op jit(solution)/shard_map/ppermute | solution.py:410
  92.5 2.2 %collective-permute-done.27 = bf16[272,256]{1,0:T(8,128)(2,1)S(1)} collective-permute-done((bf16[272,256]{1,0:T(8,128)(2,1)S(1)}, bf16[272,256]{1,0:T(8,128)(2,1)S(1)}, u32[]{:S(2)}, u32[]{:S(2)}) %collective-permute-start.27) | collective-permute-done | bytes 139296 | tf_op jit(solution)/shard_map/ppermute | solution.py:410
  96.9 2.7 %collective-permute-start.30 = (bf16[272,256]{1,0:T(8,128)(2,1)S(1)}, bf16[272,256]{1,0:T(8,128)(2,1)S(1)}, u32[]{:S(2)}, u32[]{:S(2)}) collective-permute-start(bf16[272,256]{1,0:T(8,128)(2,1)S(1)} %add_convert_fusion.1), channel_id=1, source_target_pairs={{0,16},{8,24},{16,0},{24,8},{32,48},{40,56},{48,32},{56,40},{64,80... | collective-permute-start | bytes 417800 | tf_op jit(solution)/shard_map/ppermute | solution.py:394
  101.0 10.7 %all-to-all-done.parts_ref = bf16[16,256,256]{2,1,0:T(8,128)(2,1)S(1)} async-done(((bf16[16,256,256]{2,1,0:T(8,128)(2,1)}), bf16[16,256,256]{2,1,0:T(8,128)(2,1)S(1)}, u32[]{:S(2)}, u32[]{:S(2)}) %all-to-all-start) | async-done | bytes 2097184 | tf_op jit(solution)/shard_map/all_to_all | solution.py:383
  112.6 3.1 %collective-permute-done.30 = bf16[272,256]{1,0:T(8,128)(2,1)S(1)} collective-permute-done((bf16[272,256]{1,0:T(8,128)(2,1)S(1)}, bf16[272,256]{1,0:T(8,128)(2,1)S(1)}, u32[]{:S(2)}, u32[]{:S(2)}) %collective-permute-start.30) | collective-permute-done | bytes 139296 | tf_op jit(solution)/shard_map/ppermute | solution.py:394
  (79 shorter events, 31.8 us)
Async XLA Ops:
  1.6 11.0 %collective-permute-start.3 = (bf16[128,256]{1,0:T(8,128)(2,1)S(1)}, bf16[128,256]{1,0:T(8,128)(2,1)S(1)}, u32[]{:S(2)}, u32[]{:S(2)}) collective-permute-start(bf16[128,256]{1,0:T(8,128)(2,1)S(1)} %get-tuple-element.36), channel_id=1, source_target_pairs={{0,16},{8,24},{16,0},{24,8},{32,48},{40,56},{48,32},{56,40},{64,80... | collective-permute-start | bytes 196616 | tf_op jit(solution)/shard_map/ppermute | solution.py:394
  5.7 9.6 %collective-permute-start.4 = (bf16[128,256]{1,0:T(8,128)(2,1)S(1)}, bf16[128,256]{1,0:T(8,128)(2,1)S(1)}, u32[]{:S(2)}, u32[]{:S(2)}) collective-permute-start(bf16[128,256]{1,0:T(8,128)(2,1)S(1)} %get-tuple-element.36), channel_id=1, source_target_pairs={{0,8},{8,16},{16,24},{24,0},{32,40},{40,48},{48,56},{56,32},{64,72... | collective-permute-start | bytes 196616 | tf_op jit(solution)/shard_map/ppermute | solution.py:394
  6.7 8.6 %collective-permute-start.5 = (bf16[128,256]{1,0:T(8,128)(2,1)S(1)}, bf16[128,256]{1,0:T(8,128)(2,1)S(1)}, u32[]{:S(2)}, u32[]{:S(2)}) collective-permute-start(bf16[128,256]{1,0:T(8,128)(2,1)S(1)} %get-tuple-element.36), channel_id=1, source_target_pairs={{0,24},{8,0},{16,8},{24,16},{32,56},{40,32},{48,40},{56,48},{64,88... | collective-permute-start | bytes 196616 | tf_op jit(solution)/shard_map/ppermute | solution.py:394
  17.4 12.5 %collective-permute-start.9 = (bf16[4,128,256]{2,1,0:T(8,128)(2,1)S(1)}, bf16[4,128,256]{2,1,0:T(8,128)(2,1)S(1)}, u32[]{:S(2)}, u32[]{:S(2)}) collective-permute-start(bf16[4,128,256]{2,1,0:T(8,128)(2,1)S(1)} %pad_maximum_fusion.3.gate_ref.refs_4_), channel_id=1, source_target_pairs={{0,96},{8,104},{16,112},{24,120},{32,0},{40,8},{48,16},{56,24},{64... | collective-permute-start | bytes 786440 | tf_op jit(solution)/shard_map/ppermute | solution.py:394
  23.1 13.4 %collective-permute-start.11 = (bf16[4,128,256]{2,1,0:T(8,128)(2,1)S(1)}, bf16[4,128,256]{2,1,0:T(8,128)(2,1)S(1)}, u32[]{:S(2)}, u32[]{:S(2)}) collective-permute-start(bf16[4,128,256]{2,1,0:T(8,128)(2,1)S(1)} %pad_maximum_fusion.3.gate_ref.refs_4_), channel_id=1, source_target_pairs={{0,64},{8,72},{16,80},{24,88},{32,96},{40,104},{48,112},{56,120},{... | collective-permute-start | bytes 786440 | tf_op jit(solution)/shard_map/ppermute | solution.py:394
  23.2 13.3 %collective-permute-start.6 = (bf16[4,128,256]{2,1,0:T(8,128)(2,1)S(1)}, bf16[4,128,256]{2,1,0:T(8,128)(2,1)S(1)}, u32[]{:S(2)}, u32[]{:S(2)}) collective-permute-start(bf16[4,128,256]{2,1,0:T(8,128)(2,1)S(1)} %pad_maximum_fusion.2.gate_ref.refs_0_), channel_id=1, source_target_pairs={{0,8},{8,16},{16,24},{24,0},{32,40},{40,48},{48,56},{56,32},{64,72... | collective-permute-start | bytes 786440 | tf_op jit(solution)/shard_map/ppermute | solution.py:394
  23.3 13.2 %collective-permute-start.7 = (bf16[4,128,256]{2,1,0:T(8,128)(2,1)S(1)}, bf16[4,128,256]{2,1,0:T(8,128)(2,1)S(1)}, u32[]{:S(2)}, u32[]{:S(2)}) collective-permute-start(bf16[4,128,256]{2,1,0:T(8,128)(2,1)S(1)} %pad_maximum_fusion.2.gate_ref.refs_0_), channel_id=1, source_target_pairs={{0,16},{8,24},{16,0},{24,8},{32,48},{40,56},{48,32},{56,40},{64,80... | collective-permute-start | bytes 786440 | tf_op jit(solution)/shard_map/ppermute | solution.py:394
  24.7 11.8 %collective-permute-start.8 = (bf16[4,128,256]{2,1,0:T(8,128)(2,1)S(1)}, bf16[4,128,256]{2,1,0:T(8,128)(2,1)S(1)}, u32[]{:S(2)}, u32[]{:S(2)}) collective-permute-start(bf16[4,128,256]{2,1,0:T(8,128)(2,1)S(1)} %pad_maximum_fusion.2.gate_ref.refs_0_), channel_id=1, source_target_pairs={{0,24},{8,0},{16,8},{24,16},{32,56},{40,32},{48,40},{56,48},{64,88... | collective-permute-start | bytes 786440 | tf_op jit(solution)/shard_map/ppermute | solution.py:394
  30.0 8.0 %collective-permute-start.10 = (bf16[4,128,256]{2,1,0:T(8,128)(2,1)S(1)}, bf16[4,128,256]{2,1,0:T(8,128)(2,1)S(1)}, u32[]{:S(2)}, u32[]{:S(2)}) collective-permute-start(bf16[4,128,256]{2,1,0:T(8,128)(2,1)S(1)} %pad_maximum_fusion.3.gate_ref.refs_4_), channel_id=1, source_target_pairs={{0,32},{8,40},{16,48},{24,56},{32,64},{40,72},{48,80},{56,88},{64,... | collective-permute-start | bytes 786440 | tf_op jit(solution)/shard_map/ppermute | solution.py:394
  44.6 8.1 %collective-permute-start.13 = (bf16[272,256]{1,0:T(8,128)(2,1)S(1)}, bf16[272,256]{1,0:T(8,128)(2,1)S(1)}, u32[]{:S(2)}, u32[]{:S(2)}) collective-permute-start(bf16[272,256]{1,0:T(8,128)(2,1)S(1)} %get-tuple-element.47), channel_id=1, source_target_pairs={{0,4},{1,5},{2,6},{3,7},{4,0},{5,1},{6,2},{7,3},{8,12},{9,13},{10,... | collective-permute-start | bytes 417800 | tf_op jit(solution)/shard_map/ppermute | solution.py:410
  47.9 7.4 %collective-permute-start.14 = (bf16[272,256]{1,0:T(8,128)(2,1)S(1)}, bf16[272,256]{1,0:T(8,128)(2,1)S(1)}, u32[]{:S(2)}, u32[]{:S(2)}) collective-permute-start(bf16[272,256]{1,0:T(8,128)(2,1)S(1)} %get-tuple-element.48), channel_id=1, source_target_pairs={{0,2},{1,3},{2,4},{3,5},{4,6},{5,7},{6,0},{7,1},{8,10},{9,11},{10,... | collective-permute-start | bytes 417800 | tf_op jit(solution)/shard_map/ppermute | solution.py:410
  48.6 7.0 %collective-permute-start.15 = (bf16[272,256]{1,0:T(8,128)(2,1)S(1)}, bf16[272,256]{1,0:T(8,128)(2,1)S(1)}, u32[]{:S(2)}, u32[]{:S(2)}) collective-permute-start(bf16[272,256]{1,0:T(8,128)(2,1)S(1)} %get-tuple-element.49), channel_id=1, source_target_pairs={{0,6},{1,7},{2,0},{3,1},{4,2},{5,3},{6,4},{7,5},{8,14},{9,15},{10,... | collective-permute-start | bytes 417800 | tf_op jit(solution)/shard_map/ppermute | solution.py:410
  57.0 10.1 %collective-permute-start.23 = (bf16[528,256]{1,0:T(8,128)(2,1)S(1)}, bf16[528,256]{1,0:T(8,128)(2,1)S(1)}, u32[]{:S(2)}, u32[]{:S(2)}) collective-permute-start(bf16[528,256]{1,0:T(8,128)(2,1)S(1)} %get-tuple-element.54), channel_id=1, source_target_pairs={{0,32},{8,40},{16,48},{24,56},{32,0},{40,8},{48,16},{56,24},{64,96... | collective-permute-start | bytes 811016 | tf_op jit(solution)/shard_map/ppermute | solution.py:399
  57.1 7.7 %collective-permute-start.16 = (bf16[256,256]{1,0:T(8,128)(2,1)S(1)}, bf16[256,256]{1,0:T(8,128)(2,1)S(1)}, u32[]{:S(2)}, u32[]{:S(2)}) collective-permute-start(bf16[256,256]{1,0:T(8,128)(2,1)S(1)} %get-tuple-element.51.refs_0_), channel_id=1, source_target_pairs={{0,4},{1,5},{2,6},{3,7},{4,0},{5,1},{6,2},{7,3},{8,12},{9,13},{10,... | collective-permute-start | bytes 393224 | tf_op jit(solution)/shard_map/ppermute | solution.py:410
  59.2 7.3 %collective-permute-start.17 = (bf16[256,256]{1,0:T(8,128)(2,1)S(1)}, bf16[256,256]{1,0:T(8,128)(2,1)S(1)}, u32[]{:S(2)}, u32[]{:S(2)}) collective-permute-start(bf16[256,256]{1,0:T(8,128)(2,1)S(1)} %get-tuple-element.51.refs_0_), channel_id=1, source_target_pairs={{0,2},{1,3},{2,4},{3,5},{4,6},{5,7},{6,0},{7,1},{8,10},{9,11},{10,... | collective-permute-start | bytes 393224 | tf_op jit(solution)/shard_map/ppermute | solution.py:410
  62.5 8.5 %collective-permute-start.19 = (bf16[256,256]{1,0:T(8,128)(2,1)S(1)}, bf16[256,256]{1,0:T(8,128)(2,1)S(1)}, u32[]{:S(2)}, u32[]{:S(2)}) collective-permute-start(bf16[256,256]{1,0:T(8,128)(2,1)S(1)} %get-tuple-element.51.refs_0_), channel_id=1, source_target_pairs={{0,1},{1,0},{2,3},{3,2},{4,5},{5,4},{6,7},{7,6},{8,9},{9,8},{10,11... | collective-permute-start | bytes 393224 | tf_op jit(solution)/shard_map/ppermute | solution.py:414
  67.2 10.5 %collective-permute-start.24 = (bf16[528,256]{1,0:T(8,128)(2,1)S(1)}, bf16[528,256]{1,0:T(8,128)(2,1)S(1)}, u32[]{:S(2)}, u32[]{:S(2)}) collective-permute-start(bf16[528,256]{1,0:T(8,128)(2,1)S(1)} %add_convert_fusion), channel_id=1, source_target_pairs={{0,64},{8,72},{16,80},{24,88},{32,96},{40,104},{48,112},{56,120},{... | collective-permute-start | bytes 811016 | tf_op jit(solution)/shard_map/ppermute | solution.py:399
  77.7 34.0 %all-to-all-start = ((bf16[16,256,256]{2,1,0:T(8,128)(2,1)}), bf16[16,256,256]{2,1,0:T(8,128)(2,1)S(1)}, u32[]{:S(2)}, u32[]{:S(2)}) async-start(bf16[16,256,256]{2,1,0:T(8,128)(2,1)} %bitcast.19), calls=%async_computation | async-start | bytes 4194304 | tf_op jit(solution)/shard_map/all_to_all | solution.py:383
  84.4 8.1 %collective-permute-start.26 = (bf16[272,256]{1,0:T(8,128)(2,1)S(1)}, bf16[272,256]{1,0:T(8,128)(2,1)S(1)}, u32[]{:S(2)}, u32[]{:S(2)}) collective-permute-start(bf16[272,256]{1,0:T(8,128)(2,1)S(1)} %fusion.1), channel_id=1, source_target_pairs={{0,4},{1,5},{2,6},{3,7},{4,0},{5,1},{6,2},{7,3},{8,12},{9,13},{10,... | collective-permute-start | bytes 417800 | tf_op jit(solution)/shard_map/ppermute | solution.py:410
  86.5 8.1 %collective-permute-start.27 = (bf16[272,256]{1,0:T(8,128)(2,1)S(1)}, bf16[272,256]{1,0:T(8,128)(2,1)S(1)}, u32[]{:S(2)}, u32[]{:S(2)}) collective-permute-start(bf16[272,256]{1,0:T(8,128)(2,1)S(1)} %fusion.1), channel_id=1, source_target_pairs={{0,2},{1,3},{2,4},{3,5},{4,6},{5,7},{6,0},{7,1},{8,10},{9,11},{10,... | collective-permute-start | bytes 417800 | tf_op jit(solution)/shard_map/ppermute | solution.py:410
  88.1 6.7 %collective-permute-start.28 = (bf16[272,256]{1,0:T(8,128)(2,1)S(1)}, bf16[272,256]{1,0:T(8,128)(2,1)S(1)}, u32[]{:S(2)}, u32[]{:S(2)}) collective-permute-start(bf16[272,256]{1,0:T(8,128)(2,1)S(1)} %fusion.1), channel_id=1, source_target_pairs={{0,6},{1,7},{2,0},{3,1},{4,2},{5,3},{6,4},{7,5},{8,14},{9,15},{10,... | collective-permute-start | bytes 417800 | tf_op jit(solution)/shard_map/ppermute | solution.py:410
  94.9 17.7 %collective-permute-start.29 = (bf16[272,256]{1,0:T(8,128)(2,1)S(1)}, bf16[272,256]{1,0:T(8,128)(2,1)S(1)}, u32[]{:S(2)}, u32[]{:S(2)}) collective-permute-start(bf16[272,256]{1,0:T(8,128)(2,1)S(1)} %add_convert_fusion.1), channel_id=1, source_target_pairs={{0,8},{8,16},{16,24},{24,0},{32,40},{40,48},{48,56},{56,32},{64,72... | collective-permute-start | bytes 417800 | tf_op jit(solution)/shard_map/ppermute | solution.py:394
  96.9 18.8 %collective-permute-start.30 = (bf16[272,256]{1,0:T(8,128)(2,1)S(1)}, bf16[272,256]{1,0:T(8,128)(2,1)S(1)}, u32[]{:S(2)}, u32[]{:S(2)}) collective-permute-start(bf16[272,256]{1,0:T(8,128)(2,1)S(1)} %add_convert_fusion.1), channel_id=1, source_target_pairs={{0,16},{8,24},{16,0},{24,8},{32,48},{40,56},{48,32},{56,40},{64,80... | collective-permute-start | bytes 417800 | tf_op jit(solution)/shard_map/ppermute | solution.py:394
  99.5 16.2 %collective-permute-start.31 = (bf16[272,256]{1,0:T(8,128)(2,1)S(1)}, bf16[272,256]{1,0:T(8,128)(2,1)S(1)}, u32[]{:S(2)}, u32[]{:S(2)}) collective-permute-start(bf16[272,256]{1,0:T(8,128)(2,1)S(1)} %add_convert_fusion.1), channel_id=1, source_target_pairs={{0,24},{8,0},{16,8},{24,16},{32,56},{40,32},{48,40},{56,48},{64,88... | collective-permute-start | bytes 417800 | tf_op jit(solution)/shard_map/ppermute | solution.py:394
  (16 other events, 117.0 us)
